TPU v7x, 32 devices: a whole 2x2x4 slice. The times are simulated.
32 devices in a mesh: seq: 2 (over y), shard: 4 (over x, core), rep: 4 (over z).
Axes of the slice: x: 2, y: 2, z: 4, core: 2. Of those that a mesh axis runs over, the one named last changes fastest.
Arguments:
- tokens: bfloat16 [16, 580, 1024], P(('shard', 'rep'), 'seq'), may hold values from -6 to 6
- lengths: int32 [16], P(('shard', 'rep')), may hold values from 435 to 580, as said below
- qkv_weight: bfloat16 [1024, 3072], P('shard'), may hold values from -0.1875 to 0.1875
- query_bias: bfloat16 [1024], P('shard'), may hold values from -3 to 3
- value_bias: bfloat16 [1024], P('shard'), may hold values from -0.29882812 to 0.29882812
- out_weight: bfloat16 [1024, 1024], P('shard'), may hold values from -2 to 2
- out_bias: bfloat16 [1024], P('shard'), may hold values from -0.59765625 to 0.59765625
- first_gain: bfloat16 [1024], P('shard'), may hold values from 0.5 to 1.5
- first_shift: bfloat16 [1024], P('shard'), may hold values from -0.29882812 to 0.29882812
- second_gain: bfloat16 [1024], P('shard'), may hold values from 0.5 to 1.5
- second_shift: bfloat16 [1024], P('shard'), may hold values from -3 to 3
- up_weight: bfloat16 [1024, 4096], P('shard'), may hold values from -0.1875 to 0.1875
- up_bias: bfloat16 [4096], P('shard'), may hold values from -3 to 3
- down_weight: bfloat16 [4096, 1024], P('shard'), may hold values from -0.09375 to 0.09375
- down_bias: bfloat16 [1024], P('shard'), may hold values from -3 to 3
- cotangent: bfloat16 [16, 580, 1024], P(('shard', 'rep'), 'seq'), may hold values from -6 to 6
Outputs:
- block_out: bfloat16 [16, 580, 1024], P(('shard', 'rep'), 'seq')
- token_grad: float32 [16, 580, 1024], P(('shard', 'rep'), 'seq')
- grad_qkv_weight: float32 [1024, 3072], P('shard')
- grad_query_bias: float32 [1024], P('shard')
- grad_value_bias: float32 [1024], P('shard')
- grad_out_weight: float32 [1024, 1024], P('shard')
- grad_out_bias: float32 [1024], P('shard')
- grad_first_gain: float32 [1024], P('shard')
- grad_first_shift: float32 [1024], P('shard')
- grad_second_gain: float32 [1024], P('shard')
- grad_second_shift: float32 [1024], P('shard')
- grad_up_weight: float32 [1024, 4096], P('shard')
- grad_up_bias: float32 [4096], P('shard')
- grad_down_weight: float32 [4096, 1024], P('shard')
- grad_down_bias: float32 [1024], P('shard')
Inputs may be any that keep to these rules, and one draw needn't show every extreme that they name: Tokens of an image at positions lengths[image] and beyond are padding. Some image has 580 valid tokens and some has 435.
All inputs are finite; a program needn't handle non-finite values.
Results may differ from a plain program's by a relative error of at most 0.012.
Values may be sent and summed in bfloat16 or wider, within the bound.
No kernel may reach another device: no remote copies, remote signals or barrier semaphores. Data moves between devices by JAX's collectives and lax.ppermute only.
A program may use at most 192 MiB of HBM per device.

v0:
```python
import jax
import jax.numpy as jnp
from jax import lax
from jax.sharding import PartitionSpec as P

H = 16
HD = 64


def layer_norm(values, gain_vec, shift_vec):
    centered = values - jnp.mean(values, -1, keepdims=True)
    variance = jnp.mean(centered * centered, -1, keepdims=True)
    return centered * lax.rsqrt(variance + 1e-06) * gain_vec + shift_vec


def gelu_exact(values):
    return jax.nn.gelu(values, approximate=False)


def attention_scores(query_heads, key_heads, visible, score_scale):
    scores = (
        jnp.einsum("iqhd,ikhd->ihqk", query_heads, key_heads, preferred_element_type=jnp.float32)
        * score_scale
    )
    return jnp.where(visible[:, None, None, :], scores, -1000000000.0)


def single_out(values):
    return values.reshape((values.shape[0], 1) + values.shape[1:])


def merge_out(values):
    return values.reshape((values.shape[0] * values.shape[1],) + values.shape[2:])


def shards(
    tokens,
    lengths,
    qkv_weight,
    query_bias,
    value_bias,
    out_weight,
    out_bias,
    first_gain,
    first_shift,
    second_gain,
    second_shift,
    up_weight,
    up_bias,
    down_weight,
    down_bias,
    cotangent,
):
    images, rows_local, model_width = tokens.shape
    full_len = rows_local * lax.axis_size("seq")
    score_scale = HD ** (-0.5)
    gathered = (
        lax.all_gather(qkv_weight, "shard", axis=0, tiled=True),
        lax.all_gather(out_weight, "shard", axis=0, tiled=True),
        lax.all_gather(up_weight, "shard", axis=0, tiled=True),
        lax.all_gather(down_weight, "shard", axis=0, tiled=True),
        lax.all_gather(query_bias, "shard", axis=0, tiled=True),
        lax.all_gather(value_bias, "shard", axis=0, tiled=True),
        lax.all_gather(out_bias, "shard", axis=0, tiled=True),
        lax.all_gather(first_gain, "shard", axis=0, tiled=True),
        lax.all_gather(first_shift, "shard", axis=0, tiled=True),
        lax.all_gather(second_gain, "shard", axis=0, tiled=True),
        lax.all_gather(second_shift, "shard", axis=0, tiled=True),
        lax.all_gather(up_bias, "shard", axis=0, tiled=True),
        lax.all_gather(down_bias, "shard", axis=0, tiled=True),
    )
    wqkv, wout, wup, wdown = (gathered[0], gathered[1], gathered[2], gathered[3])
    vec_query, vec_value, vec_out, gain_one, shift_one, gain_two, shift_two, vec_up, vec_down = [
        item.astype(jnp.float32) for item in gathered[4:]
    ]
    flat_rows = tokens.reshape(-1, model_width).astype(jnp.float32)
    normed_first, pull_first = jax.vjp(layer_norm, flat_rows, gain_one, shift_one)
    first_low = normed_first.astype(jnp.bfloat16)
    projected = jnp.dot(first_low, wqkv, preferred_element_type=jnp.float32)
    queries = (projected[:, :model_width] + vec_query).astype(jnp.bfloat16)
    keys_local = projected[:, model_width : 2 * model_width].astype(jnp.bfloat16)
    values_local = (projected[:, 2 * model_width :] + vec_value).astype(jnp.bfloat16)
    keys_all, values_all = (
        lax.all_gather(
            keys_local.reshape(images, rows_local, model_width), "seq", axis=1, tiled=True
        ),
        lax.all_gather(
            values_local.reshape(images, rows_local, model_width), "seq", axis=1, tiled=True
        ),
    )
    query_heads = single_out(queries.reshape(images, rows_local, H, HD))
    key_heads = single_out(keys_all.reshape(images, full_len, H, HD))
    value_heads = single_out(values_all.reshape(images, full_len, H, HD))
    visible = single_out(jnp.arange(full_len, dtype=jnp.int32)[None, :] < lengths[:, None])

    def attend_forward(block):
        query_blk, key_blk, value_blk, visible_blk = block
        scores = attention_scores(query_blk, key_blk, visible_blk, score_scale)
        score_top = jnp.max(scores, -1, keepdims=True)
        shifted = jnp.exp(scores - score_top)
        exp_total = jnp.sum(shifted, -1, keepdims=True)
        log_total = score_top + jnp.log(exp_total)
        weights_low = (shifted / exp_total).astype(jnp.bfloat16)
        mixed_blk = jnp.einsum(
            "ihqk,ikhd->iqhd", weights_low, value_blk, preferred_element_type=jnp.float32
        )
        return (mixed_blk.astype(jnp.bfloat16), log_total)

    mixed_out, log_totals = lax.map(attend_forward, (query_heads, key_heads, value_heads, visible))
    mixed_low = mixed_out.reshape(-1, model_width)
    middle = flat_rows + jnp.dot(mixed_low, wout, preferred_element_type=jnp.float32) + vec_out
    normed_second, pull_second = jax.vjp(layer_norm, middle, gain_two, shift_two)
    second_low = normed_second.astype(jnp.bfloat16)
    hidden = jnp.dot(second_low, wup, preferred_element_type=jnp.float32) + vec_up
    activated, pull_gelu = jax.vjp(gelu_exact, hidden)
    act_low = activated.astype(jnp.bfloat16)
    result = middle + jnp.dot(act_low, wdown, preferred_element_type=jnp.float32) + vec_down
    block_out = result.astype(jnp.bfloat16).reshape(tokens.shape)
    back_qkv, back_out, back_up, back_down = (
        lax.all_gather(qkv_weight, "shard", axis=0, tiled=True),
        lax.all_gather(out_weight, "shard", axis=0, tiled=True),
        lax.all_gather(up_weight, "shard", axis=0, tiled=True),
        lax.all_gather(down_weight, "shard", axis=0, tiled=True),
    )
    incoming = cotangent.reshape(-1, model_width)
    incoming_f = incoming.astype(jnp.float32)
    grad_down = jnp.dot(act_low.T, incoming, preferred_element_type=jnp.float32)
    grad_down_bias = jnp.sum(incoming_f, 0)
    grad_act = jnp.dot(incoming, back_down.T, preferred_element_type=jnp.float32)
    hidden_low = pull_gelu(grad_act)[0].astype(jnp.bfloat16)
    grad_up = jnp.dot(second_low.T, hidden_low, preferred_element_type=jnp.float32)
    grad_up_bias = jnp.sum(hidden_low.astype(jnp.float32), 0)
    grad_second = jnp.dot(hidden_low, back_up.T, preferred_element_type=jnp.float32)
    middle_norm, grad_gain_two, grad_shift_two = pull_second(grad_second)
    grad_middle = incoming_f + middle_norm
    branch_low = grad_middle.astype(jnp.bfloat16)
    grad_out = jnp.dot(mixed_low.T, branch_low, preferred_element_type=jnp.float32)
    grad_out_bias = jnp.sum(branch_low.astype(jnp.float32), 0)
    grad_mixed = (
        jnp.dot(branch_low, back_out.T, preferred_element_type=jnp.float32)
        .astype(jnp.bfloat16)
        .reshape(images, rows_local, H, HD)
    )

    def attend_backward(block):
        query_blk, key_blk, value_blk, visible_blk, mixed_grad_blk, log_blk = block
        scores = attention_scores(query_blk, key_blk, visible_blk, score_scale)
        weights_exact = jnp.exp(scores - log_blk)
        grad_weights = jnp.einsum(
            "iqhd,ikhd->ihqk", mixed_grad_blk, value_blk, preferred_element_type=jnp.float32
        )
        row_inner = jnp.sum(weights_exact * grad_weights, -1, keepdims=True)
        grad_scores = (weights_exact * (grad_weights - row_inner)).astype(jnp.bfloat16)
        query_grad_blk = (
            jnp.einsum("ihqk,ikhd->iqhd", grad_scores, key_blk, preferred_element_type=jnp.float32)
            * score_scale
        )
        key_blk_part = (
            jnp.einsum(
                "ihqk,iqhd->ikhd", grad_scores, query_blk, preferred_element_type=jnp.float32
            )
            * score_scale
        )
        value_blk_part = jnp.einsum(
            "ihqk,iqhd->ikhd",
            weights_exact.astype(jnp.bfloat16),
            mixed_grad_blk,
            preferred_element_type=jnp.float32,
        )
        return (query_grad_blk, key_blk_part, value_blk_part)

    grad_queries, key_part, value_part = lax.map(
        attend_backward,
        (query_heads, key_heads, value_heads, visible, single_out(grad_mixed), log_totals),
    )
    key_part = merge_out(key_part)
    value_part = merge_out(value_part)
    grad_keys, grad_values = (
        lax.psum_scatter(key_part, "seq", scatter_dimension=1, tiled=True),
        lax.psum_scatter(value_part, "seq", scatter_dimension=1, tiled=True),
    )
    query_low = grad_queries.reshape(-1, model_width).astype(jnp.bfloat16)
    value_low = grad_values.reshape(-1, model_width).astype(jnp.bfloat16)
    grad_proj = jnp.concatenate(
        [query_low, grad_keys.reshape(-1, model_width).astype(jnp.bfloat16), value_low], axis=1
    )
    grad_qkv = jnp.dot(first_low.T, grad_proj, preferred_element_type=jnp.float32)
    grad_query_bias = jnp.sum(query_low.astype(jnp.float32), 0)
    grad_value_bias = jnp.sum(value_low.astype(jnp.float32), 0)
    grad_first = jnp.dot(grad_proj, back_qkv.T, preferred_element_type=jnp.float32)
    flat_norm, grad_gain_one, grad_shift_one = pull_first(grad_first)
    token_grad = (grad_middle + flat_norm).reshape(tokens.shape)
    owned_grads = (
        lax.psum_scatter(grad_qkv, "shard", scatter_dimension=0, tiled=True),
        lax.psum_scatter(grad_query_bias, "shard", scatter_dimension=0, tiled=True),
        lax.psum_scatter(grad_value_bias, "shard", scatter_dimension=0, tiled=True),
        lax.psum_scatter(grad_out, "shard", scatter_dimension=0, tiled=True),
        lax.psum_scatter(grad_out_bias, "shard", scatter_dimension=0, tiled=True),
        lax.psum_scatter(grad_gain_one, "shard", scatter_dimension=0, tiled=True),
        lax.psum_scatter(grad_shift_one, "shard", scatter_dimension=0, tiled=True),
        lax.psum_scatter(grad_gain_two, "shard", scatter_dimension=0, tiled=True),
        lax.psum_scatter(grad_shift_two, "shard", scatter_dimension=0, tiled=True),
        lax.psum_scatter(grad_up, "shard", scatter_dimension=0, tiled=True),
        lax.psum_scatter(grad_up_bias, "shard", scatter_dimension=0, tiled=True),
        lax.psum_scatter(grad_down, "shard", scatter_dimension=0, tiled=True),
        lax.psum_scatter(grad_down_bias, "shard", scatter_dimension=0, tiled=True),
    )
    summed = lax.psum(
        (
            owned_grads[0],
            owned_grads[1],
            owned_grads[2],
            owned_grads[3],
            owned_grads[4],
            owned_grads[5],
            owned_grads[6],
            owned_grads[7],
            owned_grads[8],
            owned_grads[9],
            owned_grads[10],
            owned_grads[11],
            owned_grads[12],
        ),
        ("seq", "rep"),
    )
    return (
        block_out,
        token_grad,
        summed[0],
        summed[1],
        summed[2],
        summed[3],
        summed[4],
        summed[5],
        summed[6],
        summed[7],
        summed[8],
        summed[9],
        summed[10],
        summed[11],
        summed[12],
    )


def solution(mesh):
    return jax.shard_map(
        shards,
        mesh=mesh,
        in_specs=(
            P(("shard", "rep"), "seq", None),
            P(("shard", "rep")),
            P("shard", None),
            P("shard"),
            P("shard"),
            P("shard", None),
            P("shard"),
            P("shard"),
            P("shard"),
            P("shard"),
            P("shard"),
            P("shard", None),
            P("shard"),
            P("shard", None),
            P("shard"),
            P(("shard", "rep"), "seq", None),
        ),
        out_specs=(
            P(("shard", "rep"), "seq", None),
            P(("shard", "rep"), "seq", None),
            P("shard", None),
            P("shard"),
            P("shard"),
            P("shard", None),
            P("shard"),
            P("shard"),
            P("shard"),
            P("shard"),
            P("shard"),
            P("shard", None),
            P("shard"),
            P("shard", None),
            P("shard"),
        ),
        check_vma=False,
    )
```

profile of v0, /device:TPU:0, one launch (start us, length us, event | category | flops | bytes accessed | tf_op | source)
XLA Modules:
  0.0 1235.7 jit_solution(14504747822557526560)
XLA Ops:
  9.3 6.0 all-gather.3
  15.3 5.4 all-gather.2
  20.7 1.3 convert_reduce_fusion.4
  22.0 1.4 fusion.32
  23.4 35.2 %all-gather.19.cloned.1.call-done = bf16[1024,3072]{1,0:T(8,128)(2,1)} async-done(((bf16[256,3072]{1,0:T(8,128)(2,1)}), bf16[1024,3072]{1,0:T(8,128)(2,1)}) %all-gather.19.cloned.1.call-update) | async-done | bytes 6291472 | tf_op jit(solution)/shard_map/all_gather | solution.py:58
  58.7 5.2 fusion.56
  63.9 1.8 copy-done.17
  65.7 0.9 fusion.40
  66.8 5.1 all-gather.4
  71.8 5.1 all-gather.6
  76.9 2.8 fusion.34
  82.3 5.1 all-gather.10
  87.3 5.1 all-gather.9
  92.4 5.1 all-gather.8
  97.5 5.5 all_gather.61
  103.3 4.9 copy.47
  108.2 3.6 reshape.246
  111.8 3.4 all-gather.27.cloned.1.call-done
  115.2 4.9 copy.45
  120.1 4.5 reshape.243
  124.6 2.3 fusion.6
  126.9 3.3 fusion
  130.2 1.2 copy-done
  131.4 3.9 fusion.23
  135.4 3.9 all-gather.21.cloned.1.call-done
  139.2 2.5 fusion.64
  142.1 56.9 %all-gather.23.cloned.1.call-done = bf16[1024,4096]{1,0:T(8,128)(2,1)} async-done(((bf16[256,4096]{1,0:T(8,128)(2,1)}), bf16[1024,4096]{1,0:T(8,128)(2,1)}) %all-gather.23.cloned.1.call-update) | async-done | bytes 8388624 | tf_op jit(solution)/shard_map/all_gather | solution.py:60
  198.9 18.0 %multiply_convert_fusion.1 = (bf16[290,4096]{1,0:T(8,128)(2,1)}, f32[290,4096]{1,0:T(8,128)}, f32[290,4096]{1,0:T(8,128)}) fusion(f32[4096]{0:T(1024)S(1)} %convert_element_type.150, bf16[1024,4096]{1,0:T(8,128)(2,1)} %all-gather.23.cloned.1.call-done, f32[290,1024]{1,0:T(8,128)S(1)} %get-tuple-element.157, f32[1024]{0:T(1024)S(1)} %bitcast.156, ...), kind=kOutput, calls=%fused_computation.17 | convolution fusion | flops 2512578560 | bytes 21481744 | tf_op jit(solution)/shard_map/dot_general | solution.py:114
  216.9 41.7 %all-gather.25.cloned.1.call-done = bf16[4096,1024]{1,0:T(8,128)(2,1)} async-done(((bf16[1024,1024]{1,0:T(8,128)(2,1)}), bf16[4096,1024]{1,0:T(8,128)(2,1)}) %all-gather.25.cloned.1.call-update) | async-done | bytes 8388624 | tf_op jit(solution)/shard_map/all_gather | solution.py:61
  258.7 10.7 convert_reduce_fusion
  269.3 6.4 multiply_reduce_fusion.1
  276.2 1.1 copy-done.5
  278.4 3.3 fusion.65
  283.6 3.2 convolution_convert_fusion
  286.8 1.5 copy.48
  288.3 8.7 fusion.13
  297.1 10.0 multiply_reduce_fusion
  307.1 6.5 multiply_convert_fusion
  313.6 2.6 copy-done.1
  316.2 2.8 multiply_bitcast_fusion
  319.0 125.6 %all-reduce.19 = (bf16[1,580,16,64]{1,3,2,0:T(8,128)(2,1)}, bf16[1,580,16,64]{1,3,2,0:T(8,128)(2,1)}) all-reduce(f32[1,580,16,64]{1,3,2,0:T(8,128)} %fusion.13, f32[1,580,16,64]{1,3,2,0:T(8,128)} %multiply_bitcast_fusion), channel_id=5, replica_groups=mesh['seq'=2,'shard'=4,'rep'=4] {'seq'}, use_global_device_ids=true, to_apply=%region_10.11.clone | all-reduce | flops 1187840 | bytes 7127040
  444.6 1.9 convert_reduce_fusion.1
  446.5 1.9 dynamic-slice_convert_fusion.1
  448.3 5.0 convert_reduce_fusion.2
  454.2 9.4 fusion.36
  463.7 13.5 %fusion.59 = f32[1024,4096]{1,0:T(8,128)} fusion(bf16[290,4096]{1,0:T(8,128)(2,1)} %copy-done.18, f32[290,1024]{1,0:T(8,128)S(1)} %get-tuple-element.157, f32[1024]{0:T(1024)S(1)} %bitcast.157, f32[1024]{0:T(1024)S(1)} %bitcast.155, f32[290]{0:T(512)S(1)} %fusion.48, f32[290]{0:T(512)S(1)} %broadcast_multiply_fusion), kind=kOutput, calls=%fused_computation.105 | convolution fusion | flops 2434181120 | bytes 20351248 | tf_op jit(solution)/shard_map/dot_general | solution.py:131
  477.3 1.1 copy-done.8
  478.4 10.4 fusion.41
  488.9 73.6 %reduce-scatter.7.cloned.1.call-done = f32[256,3072]{1,0:T(8,128)} async-done(((f32[1024,3072]{1,0:T(8,128)}), f32[256,3072]{1,0:T(8,128)}) %reduce-scatter.7.cloned.1.call-update) | async-done | bytes 3145744 | tf_op jit(solution)/shard_map/reduce_scatter | solution.py:194
  562.5 127.7 %reduce-scatter.11.cloned.1.call-done = f32[256,4096]{1,0:T(8,128)} async-done(((f32[1024,4096]{1,0:T(8,128)}), f32[256,4096]{1,0:T(8,128)}) %reduce-scatter.11.cloned.1.call-update) | async-done | bytes 4194320 | tf_op jit(solution)/shard_map/reduce_scatter | solution.py:203
  690.2 127.5 %reduce-scatter.13.cloned.1.call-done = f32[1024,1024]{1,0:T(8,128)} async-done(((f32[4096,1024]{1,0:T(8,128)}), f32[1024,1024]{1,0:T(8,128)}) %reduce-scatter.13.cloned.1.call-update) | async-done | bytes 4194320 | tf_op jit(solution)/shard_map/reduce_scatter | solution.py:205
  820.3 5.3 all-gather.11
  825.7 7.2 fusion.60
  833.6 1.6 convert_reduce_fusion.3
  835.3 11.6 all-reduce.13
  847.5 3.5 copy.49
  851.1 39.6 %all-reduce.11 = (f32[256]{0:T(256)}, f32[256]{0:T(256)}, f32[256]{0:T(256)}, f32[256]{0:T(256)}, f32[256]{0:T(256)}, /*index=5*/f32[256]{0:T(256)}, f32[256]{0:T(256)}, f32[1024]{0:T(1024)}, f32[256]{0:T(256)}) all-reduce(f32[256]{0:T(256)S(1)} %dynamic-slice.7, ...), channel_id=1, replica_groups=mesh['seq'=2,'shard'=4,'rep'=4] {'seq','rep'}, use_global_device_ids=true, to_apply=%region_17.18 | all-reduce | flops 3072 | bytes 24576 | tf_op jit(solution)/shard_map/psum | solution.py:208
  890.7 7.7 fusion.28
  898.4 319.8 %all-reduce.18.cloned.1.call-done = (f32[256,3072]{1,0:T(8,128)}, f32[256,1024]{1,0:T(8,128)}, f32[256,4096]{1,0:T(8,128)}, f32[1024,1024]{1,0:T(8,128)}) async-done(((f32[256,3072]{1,0:T(8,128)}, f32[256,1024]{1,0:T(8,128)}, f32[256,4096]{1,0:T(8,128)}, f32[1024,1024]{1,0:T(8,128)}), (f32[256,3072]{1,0:T(8,128)}, f32[256,1024]{1,0:T(8,128)}, f32[256,4096]{1,0:T(8,128)}, ...) | async-done | bytes 12582928 | tf_op jit(solution)/shard_map/psum | solution.py:208
  1218.2 4.0 copy.63
  1222.3 1.0 copy.64
  1223.2 2.1 copy.65
  1225.4 1.6 copy-done.11
  1226.9 2.0 copy.66
  (136 shorter events, 11.3 us)
Async XLA Ops:
  7.2 51.5 %all-gather.19.cloned.1.call-start = ((), (), s32[]{:S(2)}) async-start(), calls=%async_computation.4 | async-start | bytes 7864320 | tf_op jit(solution)/shard_map/all_gather | solution.py:58
  7.9 95.4 %all-gather.29.cloned.1.call-start = ((), (), s32[]{:S(2)}) async-start(), calls=%async_computation.13 | async-start | bytes 1818624 | tf_op jit(solution)/shard_map/all_gather | solution.py:84
  23.4 40.5 %copy-start.22 = (f32[290]{0:T(512)}, f32[290]{0:T(512)S(1)}, u32[]{:S(2)}) copy-start(f32[290]{0:T(512)S(1)} %fusion.32) | copy-start | bytes 3484
  58.7 8.1 copy-start.25
  58.7 8.1 copy-start.26
  63.9 1.8 copy-start.17
  66.7 48.6 %all-gather.27.cloned.1.call-start = ((), (), s32[]{:S(2)}) async-start(), calls=%async_computation.12 | async-start | bytes 1818624 | tf_op jit(solution)/shard_map/all_gather | solution.py:87
  76.9 5.3 copy-start.27
  76.9 5.3 copy-start.28
  76.9 5.3 copy-start.29
  76.9 20.5 %copy-start.24 = (bf16[1024]{0:T(1024)(128)(2,1)S(1)}, bf16[1024]{0:T(1024)(128)(2,1)}, u32[]{:S(2)}) copy-start(bf16[1024]{0:T(1024)(128)(2,1)} %param.28) | copy-start | bytes 6148
  79.8 59.5 %all-gather.21.cloned.1.call-start = ((), (), s32[]{:S(2)}) async-start(), calls=%async_computation.5 | async-start | bytes 2621440 | tf_op jit(solution)/shard_map/all_gather | solution.py:59
  80.3 118.6 %all-gather.23.cloned.1.call-start = ((), (), s32[]{:S(2)}) async-start(), calls=%async_computation.6 | async-start | bytes 10485760 | tf_op jit(solution)/shard_map/all_gather | solution.py:60
  80.9 177.7 %all-gather.25.cloned.1.call-start = ((), (), s32[]{:S(2)}) async-start(), calls=%async_computation.7 | async-start | bytes 10485760 | tf_op jit(solution)/shard_map/all_gather | solution.py:61
  81.5 407.4 %reduce-scatter.9.cloned.1.call-start = ((), (), s32[]{:S(2)}) async-start(), calls=%async_computation.9 | async-start | bytes 5242880 | tf_op jit(solution)/shard_map/reduce_scatter | solution.py:197
  111.8 15.1 %copy-start.3 = (bf16[580,16,64]{0,2,1:T(8,128)(2,1)}, bf16[580,16,64]{0,2,1:T(8,128)(2,1)S(1)}, u32[]{:S(2)}) copy-start(bf16[580,16,64]{0,2,1:T(8,128)(2,1)S(1)} %reshape.246) | copy-start | bytes 3563524
  126.9 4.5 copy-start
  126.9 4.5 copy-start.9
  131.4 7.8 copy-start.2
  269.3 6.4 copy-start.18
  269.3 7.9 copy-start.7
  276.2 1.1 copy-start.5
  277.5 0.8 copy-start.19
  281.6 0.7 copy-start.32
  281.6 1.9 copy-start.20
  281.7 280.9 %reduce-scatter.7.cloned.1.call-start = ((), (), s32[]{:S(2)}) async-start(), calls=%async_computation.8 | async-start | bytes 15728640 | tf_op jit(solution)/shard_map/reduce_scatter | solution.py:194
  288.3 8.7 copy-start.10
  288.3 18.7 %slice-start = ((s8[12124160]{0:T(1024)(128)(4,1)}), s8[4194304]{0:T(1024)(128)(4,1)S(1)}, s32[]{:S(2)}) async-start(s8[12124160]{0:T(1024)(128)(4,1)} %bitcast.131), calls=%async_computation.15 | async-start | bytes 8388608
  288.3 18.7 %slice-start.1 = ((s8[12124160]{0:T(1024)(128)(4,1)}), s8[4194304]{0:T(1024)(128)(4,1)S(1)}, s32[]{:S(2)}) async-start(s8[12124160]{0:T(1024)(128)(4,1)} %bitcast.131), calls=%async_computation.16 | async-start | bytes 8388608
  297.1 10.0 slice-start.2
  313.6 2.6 copy-start.1
  319.0 129.3 %copy-start.4 = (bf16[580,16,64]{0,2,1:T(8,128)(2,1)S(1)}, bf16[580,16,64]{0,2,1:T(8,128)(2,1)}, u32[]{:S(2)}) copy-start(bf16[580,16,64]{0,2,1:T(8,128)(2,1)} %copy-done.3) | copy-start | bytes 3563524
  446.4 6.9 copy-start.15
  448.3 5.0 copy-start.16
  453.4 0.9 copy-start.13
  463.6 226.5 %reduce-scatter.11.cloned.1.call-start = ((), (), s32[]{:S(2)}) async-start(), calls=%async_computation.10 | async-start | bytes 20971520 | tf_op jit(solution)/shard_map/reduce_scatter | solution.py:203
  477.2 1.2 copy-start.8
  477.3 340.4 %reduce-scatter.13.cloned.1.call-start = ((), (), s32[]{:S(2)}) async-start(), calls=%async_computation.11 | async-start | bytes 20971520 | tf_op jit(solution)/shard_map/reduce_scatter | solution.py:205
  488.8 729.4 %all-reduce.18.cloned.1.call-start = ((), (), s32[]{:S(2)}) async-start(), calls=%async_computation.14 | async-start | bytes 25165824 | tf_op jit(solution)/shard_map/psum | solution.py:208
  817.7 0.7 copy-start.31
  817.7 2.5 copy-start.30
  817.7 8.0 copy-start.14
  825.7 7.2 copy-start.23
  825.7 7.9 copy-start.6
  1218.2 4.0 copy-start.21
  1218.2 5.0 copy-start.12
  1223.2 3.7 copy-start.11
Sparse Core Ops, SparseCore 0:
  9.5 49.0 all-gather.18
  66.8 23.1 all-gather.28
  92.1 23.1 all-gather.26
  116.7 22.5 all-gather.20
  140.6 58.2 all-gather.22
  200.4 58.2 all-gather.24
  281.8 44.5 reduce-scatter.8
  463.8 98.7 reduce-scatter.6
  565.1 125.0 reduce-scatter.10
  692.6 125.0 reduce-scatter.12
  822.5 395.6 all-reduce.17
where the time goes:
time: 1240 us
  waiting for transfers between devices  792 us (64%)
  blocking collectives  224 us (18%)
  matrix products  130 us (10%)
  local copies, waits for them, and re-layouts  50.5 us (4%)
  other arithmetic  20.7 us (2%)
  between operations  17.3 us (1%)
    psum x1, waiting for transfers between devices, shards(): lax.psum((owned_grads[0], owned_grads[1], owned_grads[2], owned_grads[3],...  320 us
    unnamed x2, blocking collectives  137 us
    reduce_scatter x1, waiting for transfers between devices, shards(): lax.psum_scatter(grad_up, 'shard', scatter_dimension=0, tiled=True)  128 us
    reduce_scatter x1, waiting for transfers between devices, shards(): lax.psum_scatter(grad_down, 'shard', scatter_dimension=0, tiled=True)  128 us
    reduce_scatter x1, waiting for transfers between devices, shards(): lax.psum_scatter(grad_qkv, 'shard', scatter_dimension=0, tiled=True)  73.6 us
    all_gather x1, waiting for transfers between devices, shards(): lax.all_gather(up_weight, 'shard', axis=0, tiled=True)  56.9 us
    all_gather x1, waiting for transfers between devices, shards(): lax.all_gather(down_weight, 'shard', axis=0, tiled=True)  41.7 us
    psum x1, blocking collectives, shards(): lax.psum((owned_grads[0], owned_grads[1], owned_grads[2], owned_grads[3],...  39.6 us
  transfers between devices with their start and end apart: 11, of which 9 were waited for; matrix products, arithmetic and copies ran while one was open for 12% of the time, Pallas kernels for 0%

commit v1 on v0

v1 whole, which is shorter than its diff:
```python
import functools
import math

import jax
import jax.numpy as jnp
from jax import lax
from jax.experimental import pallas as pl
from jax.experimental.pallas import tpu as pltpu
from jax.sharding import PartitionSpec as P

H = 16
HD = 64
EPS = 1e-06
F32 = jnp.float32
BF16 = jnp.bfloat16
VMEM_LIMIT = 48 * 1024 * 1024


def dims(left, right, dot_left, dot_right):
    return lax.dot_general(
        left, right, (((dot_left,), (dot_right,)), ((), ())), preferred_element_type=F32
    )


def key_visible(length_ref, padded_half, rows):
    row = lax.broadcasted_iota(jnp.int32, (2 * padded_half, 1), 0)
    second = row >= padded_half
    inside = jnp.where(second, row - padded_half, row)
    position = jnp.where(second, inside + rows, inside)
    return (inside < rows) & (position < length_ref[0])


def attend_forward(padded_half, rows, length_ref, q_ref, k_ref, v_ref, mixed_ref, log_ref):
    visible = key_visible(length_ref, padded_half, rows)
    for head in range(2):
        lanes = slice(head * HD, (head + 1) * HD)
        scores = dims(k_ref[:, lanes], q_ref[:, lanes], 1, 1) * (HD ** -0.5)
        scores = jnp.where(visible, scores, -1000000000.0)
        top = jnp.max(scores, axis=0, keepdims=True)
        shifted = jnp.exp(scores - top)
        total = jnp.sum(shifted, axis=0, keepdims=True)
        weights = (shifted * (1.0 / total)).astype(BF16)
        log_ref[0, head : head + 1, :] = top + jnp.log(total)
        values = jnp.transpose(v_ref[:, lanes].astype(F32)).astype(BF16)
        mixed = dims(values, weights, 1, 0)
        mixed_ref[:, lanes] = jnp.transpose(mixed).astype(BF16)


def attend_backward(padded_half, rows, length_ref, q_ref, k_ref, v_ref, g_ref, log_ref, out_ref):
    visible = key_visible(length_ref, padded_half, rows)
    for head in range(2):
        lanes = slice(head * HD, (head + 1) * HD)
        queries, keys = q_ref[:, lanes], k_ref[:, lanes]
        values, grads = v_ref[:, lanes], g_ref[:, lanes]
        scores = dims(keys, queries, 1, 1) * (HD ** -0.5)
        weights = jnp.where(visible, jnp.exp(scores - log_ref[0, head : head + 1, :]), 0.0)
        grad_weights = dims(values, grads, 1, 1)
        inner = jnp.sum(weights * grad_weights, axis=0, keepdims=True)
        grad_scores = (weights * (grad_weights - inner)).astype(BF16)
        keys_t = jnp.transpose(keys.astype(F32)).astype(BF16)
        grad_q = jnp.transpose(dims(keys_t, grad_scores, 1, 0)) * (HD ** -0.5)
        out_ref[0, :, lanes] = grad_q.astype(BF16)
        out_ref[1, :, lanes] = (dims(grad_scores, queries, 1, 0) * (HD ** -0.5)).astype(BF16)
        out_ref[2, :, lanes] = dims(weights.astype(BF16), grads, 1, 0).astype(BF16)


def attention(length, qkv, rows, name):
    tokens, width = qkv.shape
    pairs = width // 3 // (2 * HD)
    part = lambda p: pl.BlockSpec((tokens, 2 * HD), lambda j, n, p=p: (0, p * pairs + j))
    return pl.pallas_call(
        functools.partial(attend_forward, tokens // 2, rows),
        grid_spec=pltpu.PrefetchScalarGridSpec(
            num_scalar_prefetch=1,
            grid=(pairs,),
            in_specs=[part(0), part(1), part(2)],
            out_specs=[
                pl.BlockSpec((tokens, 2 * HD), lambda j, n: (0, j)),
                pl.BlockSpec((1, 2, tokens), lambda j, n: (j, 0, 0)),
            ],
        ),
        out_shape=[
            jax.ShapeDtypeStruct((tokens, width // 3), BF16),
            jax.ShapeDtypeStruct((pairs, 2, tokens), F32),
        ],
        compiler_params=pltpu.CompilerParams(vmem_limit_bytes=VMEM_LIMIT),
        name=name,
    )(length, qkv, qkv, qkv)


def attention_grad(length, qkv, grad_mixed, log_total, rows, name):
    tokens, width = qkv.shape
    pairs = width // 3 // (2 * HD)
    part = lambda p: pl.BlockSpec((tokens, 2 * HD), lambda j, n, p=p: (0, p * pairs + j))
    return pl.pallas_call(
        functools.partial(attend_backward, tokens // 2, rows),
        grid_spec=pltpu.PrefetchScalarGridSpec(
            num_scalar_prefetch=1,
            grid=(pairs,),
            in_specs=[
                part(0),
                part(1),
                part(2),
                pl.BlockSpec((tokens, 2 * HD), lambda j, n: (0, j)),
                pl.BlockSpec((1, 2, tokens), lambda j, n: (j, 0, 0)),
            ],
            out_specs=pl.BlockSpec((3, tokens, 2 * HD), lambda j, n: (0, 0, j)),
        ),
        out_shape=jax.ShapeDtypeStruct((3, tokens, width // 3), BF16),
        compiler_params=pltpu.CompilerParams(vmem_limit_bytes=VMEM_LIMIT),
        name=name,
    )(length, qkv, qkv, qkv, grad_mixed, log_total)


def hidden_body(x_ref, w_ref, b_ref, act_ref, slope_ref):
    hidden = dims(x_ref[...], w_ref[...], 1, 0) + b_ref[...]
    normal = 0.5 * (1.0 + lax.erf(hidden * math.sqrt(0.5)))
    density = jnp.exp(-0.5 * hidden * hidden) * (1.0 / math.sqrt(2.0 * math.pi))
    act_ref[...] = (hidden * normal).astype(BF16)
    slope_ref[...] = (normal + hidden * density).astype(BF16)


def hidden_layer(inputs, weight, bias, tile):
    tokens, depth = inputs.shape
    width = weight.shape[1]
    return pl.pallas_call(
        hidden_body,
        grid=(width // tile,),
        in_specs=[
            pl.BlockSpec((tokens, depth), lambda j: (0, 0)),
            pl.BlockSpec((depth, tile), lambda j: (0, j)),
            pl.BlockSpec((1, tile), lambda j: (0, j)),
        ],
        out_specs=[pl.BlockSpec((tokens, tile), lambda j: (0, j))] * 2,
        out_shape=[jax.ShapeDtypeStruct((tokens, width), BF16)] * 2,
        compiler_params=pltpu.CompilerParams(vmem_limit_bytes=VMEM_LIMIT),
        name="hidden_layer",
    )(inputs, weight, bias)


def weight_grad_body(count, index_ref, left_ref, right_ref, *rest):
    total = dims(left_ref[...], right_ref[...], 0, 0)
    for added in rest[:count]:
        total = total + added[...].astype(F32)
    rest[count][...] = total.astype(BF16)


def weight_grad(left, right, blocks, height, added=()):
    tokens = left.shape[0]
    number = blocks.shape[0]
    if height % 128:
        narrow = [
            lax.dynamic_slice_in_dim(left, blocks[i] * height, height, 1) for i in range(number)
        ]
        left = jnp.concatenate(narrow, axis=1)
        blocks = jnp.zeros((1,), jnp.int32)
        number, height = 1, number * height
    parts = right.shape[0] if right.ndim == 3 else 1
    width = right.shape[-1]
    if right.ndim == 3:
        right_spec = pl.BlockSpec((pl.Squeezed(), tokens, width), lambda i, j, n: (j, 0, 0))
    else:
        parts = 2
        width = width // parts
        right_spec = pl.BlockSpec((tokens, width), lambda i, j, n: (0, j))
    tile = pl.BlockSpec((height, width), lambda i, j, n: (i, j))
    return pl.pallas_call(
        functools.partial(weight_grad_body, len(added)),
        grid_spec=pltpu.PrefetchScalarGridSpec(
            num_scalar_prefetch=1,
            grid=(number, parts),
            in_specs=[pl.BlockSpec((tokens, height), lambda i, j, n: (0, n[i])), right_spec]
            + [tile] * len(added),
            out_specs=tile,
        ),
        out_shape=jax.ShapeDtypeStruct((number * height, parts * width), BF16),
        compiler_params=pltpu.CompilerParams(vmem_limit_bytes=VMEM_LIMIT),
        name="weight_grad",
    )(blocks, left, right, *added)


def normalize(values):
    centered = values - jnp.mean(values, -1, keepdims=True)
    scale = lax.rsqrt(jnp.mean(centered * centered, -1, keepdims=True) + EPS)
    return centered * scale, scale


def normalize_grad(grad, gain, normal, scale):
    scaled = grad * gain
    return scale * (
        scaled
        - jnp.mean(scaled, -1, keepdims=True)
        - normal * jnp.mean(scaled * normal, -1, keepdims=True)
    )


def place(buffer, piece, position):
    start = (position,) + (0,) * (buffer.ndim - 1)
    return lax.dynamic_update_slice(buffer, piece[None], start)


def pick(array, index, axis=0):
    return lax.dynamic_index_in_dim(array, index, axis, keepdims=False)


def shards(
    tokens,
    lengths,
    qkv_weight,
    query_bias,
    value_bias,
    out_weight,
    out_bias,
    first_gain,
    first_shift,
    second_gain,
    second_shift,
    up_weight,
    up_bias,
    down_weight,
    down_bias,
    cotangent,
):
    _, rows, width = tokens.shape
    halves = lax.axis_size("seq")
    group = lax.axis_size("shard")
    replicas = lax.axis_size("rep")
    columns = group // 2
    half, member, copy_id = (lax.axis_index(name) for name in ("seq", "shard", "rep"))
    core, column = member % 2, member // 2
    owned = width // group
    owned_hidden = up_bias.shape[0]
    padded = -(-(rows + 1) // 16) * 16

    def over_core(value):
        return lax.ppermute(value, "shard", [(i, i ^ 1) for i in range(group)])

    def over_x(value, step):
        return lax.ppermute(value, "shard", [(i, (i + 2 * step) % group) for i in range(group)])

    def over_y(value):
        return lax.ppermute(value, "seq", [(i, halves - 1 - i) for i in range(halves)])

    def over_z(value, step):
        return lax.ppermute(value, "rep", [(i, i ^ step) for i in range(replicas)])

    swaps = []
    for s in range(halves):
        for h in range(group):
            if s != h % 2:
                swaps.append((s * group + h, (h % 2) * group + (h // 2) * 2 + s))

    def swap(value):
        return lax.ppermute(value, ("seq", "shard"), swaps)

    def by_core(mine, other, axis=0):
        return jnp.where(
            core == 0, jnp.stack([mine, other], axis), jnp.stack([other, mine], axis)
        )

    def whole_image(local):
        mine = jnp.where(half == core, local, swap(local))
        return by_core(mine, over_core(mine)).reshape(2 * padded, width)

    length = lengths[0]
    lane = lax.broadcasted_iota(jnp.int32, (padded - rows, width), 1)
    note = jnp.where(lane == 0, length // 16, jnp.where(lane == 1, length % 16, 0)).astype(BF16)
    image = whole_image(jnp.concatenate([tokens[0], note], axis=0))
    grad_tail = jnp.zeros((padded - rows, width), BF16)
    image_length = image[rows, 0].astype(jnp.int32) * 16 + image[rows, 1].astype(jnp.int32)
    image_length = image_length.reshape(1)

    def gather_x(shard):
        depth = shard.shape[0]
        split = shard.reshape((halves, depth // halves) + shard.shape[1:])
        buffer = jnp.zeros((columns * halves,) + split.shape[1:], shard.dtype)
        buffer = lax.dynamic_update_slice(
            buffer, split, (column * halves,) + (0,) * (split.ndim - 1)
        )
        first = pick(split, half)
        for step in range(1, columns):
            source = (column - step) % columns
            got = over_x(first, step)
            buffer = place(buffer, got, source * halves + half)
            buffer = place(buffer, over_y(got), source * halves + (halves - 1 - half))
        return buffer.reshape((columns, depth) + shard.shape[1:])

    def by_columns(gathered, blocks):
        depth, wide = gathered.shape[1:]
        one = wide // blocks // columns // 2
        cut = [
            jnp.concatenate(
                [
                    gathered[:, :, (2 * k + i) * one : (2 * k + i + 1) * one]
                    for k in range(blocks * columns)
                ],
                axis=2,
            )
            for i in range(2)
        ]
        keep = jnp.where(core == 0, cut[0], cut[1])
        send = jnp.where(core == 0, cut[1], cut[0])
        return by_core(keep, over_core(send), 1).reshape(columns * 2 * depth, wide // 2)

    vectors = jnp.concatenate(
        [
            query_bias,
            value_bias,
            out_bias,
            first_gain,
            first_shift,
            second_gain,
            second_shift,
            down_bias,
            up_bias,
        ]
    ).reshape(-1, 128)
    gathered_vec = jnp.zeros((columns,) + vectors.shape, BF16)
    gathered_vec = place(gathered_vec, vectors, column)
    for step in range(1, columns):
        gathered_vec = place(gathered_vec, over_x(vectors, step), (column - step) % columns)
    mine_vec = gathered_vec.reshape(columns, -1).astype(F32)
    all_vec = by_core(gathered_vec, over_core(gathered_vec), 1).reshape(columns * 2, -1)
    all_vec = all_vec.astype(F32)
    vec = lambda i: all_vec[:, i * owned : (i + 1) * owned].reshape(width)
    own_vec = lambda i: mine_vec[:, i * owned : (i + 1) * owned].reshape(width // 2)
    gain_one, shift_one, gain_two, shift_two = vec(3), vec(4), vec(5), vec(6)
    vec_out, vec_down = vec(2), vec(7)
    vec_up = mine_vec[:, 8 * owned :].reshape(1, columns * owned_hidden)
    vec_qkv = jnp.concatenate([own_vec(0), jnp.zeros((width // 2,), F32), own_vec(1)])

    wqkv = by_columns(gather_x(qkv_weight), 3)
    wout = gather_x(out_weight).reshape(width // 2, width)
    wup = by_columns(gather_x(up_weight), 1)
    wdown = gather_x(down_weight).reshape(columns * owned_hidden, width)
    incoming = whole_image(jnp.concatenate([cotangent[0], grad_tail], axis=0))

    image_f = image.astype(F32)
    normal_one, scale_one = normalize(image_f)
    first_low = (normal_one * gain_one + shift_one).astype(BF16)
    qkv = (jnp.dot(first_low, wqkv, preferred_element_type=F32) + vec_qkv).astype(BF16)
    mixed, log_total = attention(image_length, qkv, rows, "attention")
    branch = jnp.dot(mixed, wout, preferred_element_type=F32)
    middle = image_f + branch + over_core(branch.astype(BF16)).astype(F32) + vec_out
    normal_two, scale_two = normalize(middle)
    second_low = (normal_two * gain_two + shift_two).astype(BF16)
    act_low, slope = hidden_layer(second_low, wup, vec_up, 512)

    grad_act = jnp.dot(incoming, wdown.T, preferred_element_type=F32)
    hidden_low = (grad_act * slope.astype(F32)).astype(BF16)
    grad_second = jnp.dot(hidden_low, wup.T, preferred_element_type=F32)
    grad_second = grad_second + over_core(grad_second.astype(BF16)).astype(F32)
    incoming_f = incoming.astype(F32)
    grad_middle = incoming_f + normalize_grad(grad_second, gain_two, normal_two, scale_two)
    branch_low = grad_middle.astype(BF16)
    grad_mixed = jnp.dot(branch_low, wout.T, preferred_element_type=F32).astype(BF16)
    grad_qkv = attention_grad(image_length, qkv, grad_mixed, log_total, rows, "attention_grad")
    flat_grad = jnp.concatenate([grad_qkv[0], grad_qkv[1], grad_qkv[2]], axis=1)
    grad_first = jnp.dot(flat_grad, wqkv.T, preferred_element_type=F32)
    grad_first = grad_first + over_core(grad_first.astype(BF16)).astype(F32)
    token_grad = grad_middle + normalize_grad(grad_first, gain_one, normal_one, scale_one)

    partial = jnp.dot(act_low, wdown, preferred_element_type=F32).reshape(2, padded, width)
    from_other = over_core(pick(partial, 1 - core).astype(BF16)).astype(F32)
    own_middle = pick(middle.reshape(2, padded, width), core)
    block = (own_middle + pick(partial, core) + from_other + vec_down).astype(BF16)
    block = jnp.where(half == core, block, swap(block))
    block_out = block[:rows][None]
    own_grad = pick(token_grad.reshape(2, padded, width), core)
    moved = swap(own_grad.astype(BF16)).astype(F32)
    token_grad = jnp.where(half == core, own_grad, moved)[:rows][None]

    mine = lambda v: pick(v.reshape(columns, 2, owned), core, 1)
    summed = lambda v: jnp.sum(v, 0)
    vec_grads = jnp.concatenate(
        [
            summed(grad_qkv[0].astype(F32)).reshape(columns, owned),
            summed(grad_qkv[2].astype(F32)).reshape(columns, owned),
            mine(summed(branch_low.astype(F32))),
            mine(summed(grad_first * normal_one)),
            mine(summed(grad_first)),
            mine(summed(grad_second * normal_two)),
            mine(summed(grad_second)),
            mine(summed(incoming_f)),
            summed(hidden_low.astype(F32)).reshape(columns, owned_hidden),
        ],
        axis=1,
    )
    entries = vec_grads.shape[1]
    pieces = halves * replicas
    vec_grads = vec_grads.reshape(columns, halves, replicas, 1, entries // pieces)
    vec_grads = jnp.pad(
        vec_grads, ((0, 0), (0, 0), (0, 0), (0, 7), (0, width - entries // pieces))
    ).astype(BF16)

    def reduce_all(quadrant, lead, cross):
        other = halves - 1 - half
        sent = [quadrant((column + k) % columns, other, ()) for k in range(1, columns)]
        got = [over_x(v, k + 1) for k, v in enumerate(sent)]
        sent_b = [quadrant((column + k) % columns, half, ()) for k in range(1, columns)]
        got_b = [over_x(v, k + 1) for k, v in enumerate(sent_b)]
        from_y = over_y(quadrant(column, other, tuple(got)))
        total = quadrant(column, half, tuple(got_b) + (from_y,))
        total = total.reshape((lead, replicas, total.shape[0] // lead // replicas, total.shape[1]))
        step = 1
        while step < replicas:
            bit = (copy_id // step) % 2
            pairs = total.reshape((lead, total.shape[1] // 2, 2) + total.shape[2:])
            got = over_z(pick(pairs, 1 - bit, 2), step)
            total = (pick(pairs, bit, 2).astype(F32) + got.astype(F32)).astype(BF16)
            step *= 2
        total = total.reshape((lead,) + total.shape[2:])
        if cross:
            total = cross(total)
        else:
            total = total[0]
        total = total[None]
        while step > 1:
            step //= 2
            bit = (copy_id // step) % 2
            got = over_z(total, step)
            total = jnp.where(
                bit == 0, jnp.stack([total, got], 1), jnp.stack([got, total], 1)
            ).reshape((-1,) + total.shape[1:])
        got = over_y(total)
        return jnp.where(
            half == 0, jnp.stack([total, got], 0), jnp.stack([got, total], 0)
        )

    def cross_cores(blocks):
        def exchange(total):
            got = over_core(pick(total, 1 - core))
            own = pick(total, core)
            one = own.shape[1] // blocks
            left = jnp.where(core == 0, own, got)
            right = jnp.where(core == 0, got, own)
            cols = []
            for k in range(blocks):
                cols += [left[:, k * one : (k + 1) * one], right[:, k * one : (k + 1) * one]]
            return jnp.concatenate(cols, axis=1)

        return exchange

    def by_row(left, right):
        height = owned // halves

        def quadrant(x, y, added):
            blocks = jnp.stack([(x * 2 + i) * halves + y for i in range(2)]).astype(jnp.int32)
            return weight_grad(left, right, blocks, height, added)

        return quadrant

    def by_own(left, right, height):
        def quadrant(x, y, added):
            blocks = (x * halves + y).astype(jnp.int32).reshape(1)
            return weight_grad(left, right, blocks, height, added)

        return quadrant

    def out_quadrant(x, y, added):
        height = owned // halves
        blocks = (x * halves + y).astype(jnp.int32).reshape(1)
        core_part = weight_grad(mixed, branch_low, blocks, height)
        core_part = core_part.reshape(replicas, height // replicas, width)
        joined = jnp.concatenate([core_part, pick(pick(vec_grads, x), y)], axis=1)
        joined = joined.reshape(-1, width).astype(F32)
        for value in added:
            joined = joined + value.astype(F32)
        return joined.astype(BF16)

    grad_down = reduce_all(by_own(act_low, incoming, owned_hidden // halves), 1, None)
    grad_up = reduce_all(by_row(second_low, hidden_low), 2, cross_cores(columns))
    grad_qkv_w = reduce_all(by_row(first_low, grad_qkv), 2, cross_cores(3 * columns))
    grad_out = reduce_all(out_quadrant, 1, None)

    height = owned // pieces
    vec_out_grads = grad_out[:, :, height, : entries // pieces].astype(F32).reshape(entries)
    vec_of = lambda i: vec_out_grads[i * owned : (i + 1) * owned]
    grad_out = grad_out[:, :, :height].astype(F32).reshape(owned, width)
    return (
        block_out,
        token_grad,
        grad_qkv_w.astype(F32).reshape(owned, 3 * width),
        vec_of(0),
        vec_of(1),
        grad_out,
        vec_of(2),
        vec_of(3),
        vec_of(4),
        vec_of(5),
        vec_of(6),
        grad_up.astype(F32).reshape(owned, up_weight.shape[1]),
        vec_out_grads[8 * owned :],
        grad_down.astype(F32).reshape(owned_hidden, width),
        vec_of(7),
    )


def solution(mesh):
    return jax.shard_map(
        shards,
        mesh=mesh,
        in_specs=(
            P(("shard", "rep"), "seq", None),
            P(("shard", "rep")),
            P("shard", None),
            P("shard"),
            P("shard"),
            P("shard", None),
            P("shard"),
            P("shard"),
            P("shard"),
            P("shard"),
            P("shard"),
            P("shard", None),
            P("shard"),
            P("shard", None),
            P("shard"),
            P(("shard", "rep"), "seq", None),
        ),
        out_specs=(
            P(("shard", "rep"), "seq", None),
            P(("shard", "rep"), "seq", None),
            P("shard", None),
            P("shard"),
            P("shard"),
            P("shard", None),
            P("shard"),
            P("shard"),
            P("shard"),
            P("shard"),
            P("shard"),
            P("shard", None),
            P("shard"),
            P("shard", None),
            P("shard"),
        ),
        check_vma=False,
    )
```

time: 1240 us -> 510 us (0.41)
  waiting for transfers between devices: 792 us -> 216 us
  blocking collectives: 224 us -> 0 us
  matrix products: 130 us -> 26.6 us
  Pallas kernels: 0 us -> 75.9 us
  starting transfers between devices: 0.61 us -> 61.7 us
  other arithmetic: 20.7 us -> 58.2 us
  between operations: 17.3 us -> 4.65 us
    reduce_scatter x4 -> x0, waiting for transfers between devices: 329 us -> none  [the longest x1 128 us: shards(): lax.psum_scatter(grad_up, 'shard', scatter_dimension=0, tiled=True)]
    psum x1 -> x0, waiting for transfers between devices: 320 us -> none  [shards(): lax.psum((owned_grads[0], owned_grads[1], owned_grads[2], owned_grads[3],...]
    ppermute x0 -> x56, waiting for transfers between devices: none -> 216 us  [the longest x12 77 us: over_y(): lax.ppermute(value, 'seq', [(i, halves - 1 - i) for i in range(halves)])]
    all_gather x6 -> x0, waiting for transfers between devices: 141 us -> none  [the longest x1 56.9 us: shards(): lax.all_gather(up_weight, 'shard', axis=0, tiled=True)]
    unnamed x2 -> x0, blocking collectives: 137 us -> none
    dot_general x18 -> x7, matrix products: 130 us -> 26.6 us  [the longest x1 6.55 us: shards(): grad_act = jnp.dot(incoming, wdown.T, preferred_element_type=F32)]
    pallas_call x0 -> x19, Pallas kernels: none -> 75.9 us  [the longest x16 48.1 us: weight_grad(): pl.pallas_call(functools.partial(weight_grad_body, len(added)), grid_spec...]
    ppermute x0 -> x56, starting transfers between devices: none -> 61.7 us  [the longest x16 24.5 us: over_z(): return lax.ppermute(value, 'rep', [(i, i ^ step) for i in range(replicas)])]
  transfers between devices with their start and end apart: 11 -> 56, of which waited for: 9 -> 25; matrix products, arithmetic and copies ran while one was open for 12% -> 21% of each run, Pallas kernels for 0% -> 14%
where the time goes in v1:
time: 510 us; the launch traced here: 501 us
  waiting for transfers between devices  216 us (42%)
  Pallas kernels  75.9 us (15%)
  starting transfers between devices  61.7 us (12%)
  local copies, waits for them, and re-layouts  58.5 us (11%)
  other arithmetic  58.2 us (11%)
  matrix products  26.6 us (5%)
    ppermute x12, waiting for transfers between devices, over_y(): lax.ppermute(value, 'seq', [(i, halves - 1 - i) for i in range(halves)])  77 us
    ppermute x13, waiting for transfers between devices, over_x(): lax.ppermute(value, 'shard', [(i, (i + 2 * step) % group) for i in range(...  74.3 us
    ppermute x16, waiting for transfers between devices, over_z(): return lax.ppermute(value, 'rep', [(i, i ^ step) for i in range(replicas)])  62.4 us
    pallas_call x16, Pallas kernels, weight_grad(): pl.pallas_call(functools.partial(weight_grad_body, len(added)), grid_spec...  48.1 us
    unnamed x148, local copies, waits for them, and re-layouts  26.9 us
    ppermute x16, starting transfers between devices, over_z(): return lax.ppermute(value, 'rep', [(i, i ^ step) for i in range(replicas)])  24.5 us
    ppermute x13, starting transfers between devices, over_x(): lax.ppermute(value, 'shard', [(i, (i + 2 * step) % group) for i in range(...  14.7 us
    ppermute x12, starting transfers between devices, over_y(): lax.ppermute(value, 'seq', [(i, halves - 1 - i) for i in range(halves)])  14.2 us
  transfers between devices with their start and end apart: 56, of which 25 were waited for; matrix products, arithmetic and copies ran while one was open for 21% of the time, Pallas kernels for 14%

profile of v1, /device:TPU:0, one launch (start us, length us, event | category | flops | bytes accessed | tf_op | source)
XLA Modules:
  0.0 501.3 jit_solution(8745016460511711496)
XLA Ops:
  12.4 3.0 collective-permute-start.2
  29.6 2.5 broadcast_in_dim.91
  38.9 4.0 collective-permute-done.7
  42.9 2.8 collective-permute-start.8
  46.4 9.6 %collective-permute-done.8 = bf16[128,1024]{1,0:T(8,128)(2,1)S(1)} collective-permute-done((bf16[128,1024]{1,0:T(8,128)(2,1)S(1)}, bf16[128,1024]{1,0:T(8,128)(2,1)S(1)}, u32[]{:S(2)}, u32[]{:S(2)}) %collective-permute-start.8) | collective-permute-done | bytes 262176 | tf_op jit(solution)/shard_map/ppermute | solution.py:242
  62.9 2.5 collective-permute-done.10
  65.4 2.8 collective-permute-start.11
  68.2 19.7 %collective-permute-done.13 = bf16[512,1024]{1,0:T(8,128)(2,1)} collective-permute-done((bf16[512,1024]{1,0:T(8,128)(2,1)}, bf16[512,1024]{1,0:T(8,128)(2,1)}, u32[]{:S(2)}, u32[]{:S(2)}) %collective-permute-start.13) | collective-permute-done | bytes 1048608 | tf_op jit(solution)/shard_map/ppermute | solution.py:239
  94.9 9.5 %collective-permute-done.11 = bf16[128,4096]{1,0:T(8,128)(2,1)S(1)} collective-permute-done((bf16[128,4096]{1,0:T(8,128)(2,1)}, bf16[128,4096]{1,0:T(8,128)(2,1)S(1)}, u32[]{:S(2)}, u32[]{:S(2)}) %collective-permute-start.11) | collective-permute-done | bytes 1048608 | tf_op jit(solution)/shard_map/ppermute | solution.py:242
  111.0 8.6 %attention.1 = (bf16[608,512]{1,0:T(8,128)(2,1)S(1)}, f32[4,2,608]{2,1,0:T(2,128)S(1)}) custom-call(s32[1]{0:T(128)} %bitcast.5.length_ref, bf16[608,1536]{1,0:T(8,128)(2,1)S(1)} %add_convert_fusion.q_ref.k_ref.v_ref, bf16[608,1536]{1,0:T(8,128)(2,1)S(1)} %add_convert_fusion.q_ref.k_ref.v_ref, bf16[608,1536]{1,0:T(8,128)(2,1)S(1)} %add_convert_fusion.q_ref.k_ref.v_ref), custom_call_target="tpu_custom_call" | custom-call | tf_op jit(solution)/shard_map/attention/pallas_call | solution.py:71
  119.7 2.3 fusion.57
  122.5 2.3 bitcast_dynamic-update-slice_fusion.1
  124.8 2.3 convert_reduce_fusion.1
  127.9 2.3 bitcast_dynamic-update-slice_fusion
  130.2 4.6 maximum_select_fusion
  134.9 2.3 fusion.7
  139.1 2.2 multiply_reduce_fusion.2
  142.0 7.4 %hidden_layer.1 = (bf16[608,2048]{1,0:T(8,128)(2,1)S(1)}, bf16[608,2048]{1,0:T(8,128)(2,1)}) custom-call(bf16[608,1024]{1,0:T(8,128)(2,1)S(1)} %add_convert_fusion.1.x_ref.left_ref, bf16[1024,2048]{1,0:T(8,128)(2,1)} %bitcast.356, f32[1,2048]{1,0:T(1,128)S(1)} %bitcast.334), custom_call_target="tpu_custom_call" | custom-call | tf_op jit(solution)/shard_map/hidden_layer/pallas_call | solution.py:126
  149.4 6.6 %fusion.60 = (bf16[2048]{0:T(1024)(128)(2,1)S(1)}, bf16[608,2048]{1,0:T(8,128)(2,1)S(1)}) fusion(bf16[608,2048]{1,0:T(8,128)(2,1)} %get-tuple-element.21, bf16[608,1024]{1,0:T(8,128)(2,1)S(1)} %bitcast.318, bf16[2048,1024]{1,0:T(8,128)(2,1)} %bitcast.57), kind=kOutput, calls=%fused_computation.264 | convolution fusion | flops 2555115520 | bytes 10424320 | tf_op jit(solution)/shard_map/dot_general | solution.py:349
  155.9 4.6 fusion.58
  160.6 3.6 weight_grad.25
  164.7 4.5 fusion.61
  173.7 3.5 weight_grad.24
  184.3 6.2 %collective-permute-done.40.rest_0_ = bf16[256,2048]{1,0:T(8,128)(2,1)} collective-permute-done((bf16[256,2048]{1,0:T(8,128)(2,1)}, bf16[256,2048]{1,0:T(8,128)(2,1)}, u32[]{:S(2)}, u32[]{:S(2)}) %collective-permute-start.40) | collective-permute-done | bytes 1048608 | tf_op jit(solution)/shard_map/ppermute | solution.py:239
  190.5 5.1 %weight_grad.26 = bf16[256,2048]{1,0:T(8,128)(2,1)} custom-call(s32[2]{0:T(128)S(1)} %pad_add_fusion.2.index_ref, bf16[608,1024]{1,0:T(8,128)(2,1)S(1)} %add_convert_fusion.1.x_ref.left_ref, bf16[608,2048]{1,0:T(8,128)(2,1)S(1)} %copy-done.10, bf16[256,2048]{1,0:T(8,128)(2,1)} %collective-permute-done.40.rest_0_), custom_call_target="tpu_custom_call" | custom-call | tf_op jit(solution)/shard_map/weight_grad/pallas_call | solution.py:167
  195.9 2.5 multiply_reduce_fusion
  198.4 3.5 convert_reduce_fusion.2
  201.9 2.6 convolution_convert_fusion.g_ref
  204.5 11.8 %attention_grad.1.right_ref = bf16[3,608,512]{2,1,0:T(8,128)(2,1)S(1)} custom-call(s32[1]{0:T(128)} %bitcast.5.length_ref, bf16[608,1536]{1,0:T(8,128)(2,1)S(1)} %copy-done.1, bf16[608,1536]{1,0:T(8,128)(2,1)S(1)} %copy-done.1, bf16[608,1536]{1,0:T(8,128)(2,1)S(1)} %copy-done.1, bf16[608,512]{1,0:T(8,128)(2,1)S(1)} %convolution_convert_fusion.g_ref, ...), custom_call_target="tpu_custom_call" | custom-call | tf_op jit(solution)/shard_map/attention_grad/pallas_call | solution.py:95
  218.2 4.0 fusion.59
  227.4 7.6 %collective-permute-done.49.rest_0_ = bf16[512,1024]{1,0:T(8,128)(2,1)} collective-permute-done((bf16[512,1024]{1,0:T(8,128)(2,1)}, bf16[512,1024]{1,0:T(8,128)(2,1)}, u32[]{:S(2)}, u32[]{:S(2)}) %collective-permute-start.49) | collective-permute-done | bytes 1048608 | tf_op jit(solution)/shard_map/ppermute | solution.py:239
  235.5 3.1 weight_grad.30
  239.2 2.2 fusion.37
  250.2 5.0 weight_grad.27
  260.0 3.4 collective-permute-done.50.rest_1_
  263.4 3.0 weight_grad.31
  268.9 3.0 fusion.19
  271.9 2.4 fusion.18
  274.4 3.8 weight_grad.16
  278.2 3.8 weight_grad.17
  292.4 2.7 collective-permute-start.43
  296.3 33.1 %collective-permute-done.32 = bf16[160,1024]{1,0:T(8,128)(2,1)S(1)} collective-permute-done((bf16[160,1024]{1,0:T(8,128)(2,1)S(1)}, bf16[160,1024]{1,0:T(8,128)(2,1)S(1)}, u32[]{:S(2)}, u32[]{:S(2)}) %collective-permute-start.32) | collective-permute-done | bytes 327712 | tf_op jit(solution)/shard_map/ppermute | solution.py:239
  331.0 2.7 collective-permute-start.52
  333.8 11.7 %collective-permute-done.52 = bf16[1,1,128,1024]{3,2,1,0:T(8,128)(2,1)S(1)} collective-permute-done((bf16[1,1,128,1024]{3,2,1,0:T(8,128)(2,1)S(1)}, bf16[1,1,128,1024]{3,2,1,0:T(8,128)(2,1)S(1)}, u32[]{:S(2)}, u32[]{:S(2)}) %collective-permute-start.52) | collective-permute-done | bytes 262176 | tf_op jit(solution)/shard_map/ppermute | solution.py:245
  348.2 2.2 copy.68
  350.5 2.9 collective-permute-start.45
  353.4 3.2 collective-permute-done.33
  356.8 10.8 %collective-permute-done.53 = bf16[1,128,1024]{2,1,0:T(8,128)(2,1)S(1)} collective-permute-done((bf16[1,128,1024]{2,1,0:T(8,128)(2,1)S(1)}, bf16[1,128,1024]{2,1,0:T(8,128)(2,1)S(1)}, u32[]{:S(2)}, u32[]{:S(2)}) %collective-permute-start.53) | collective-permute-done | bytes 262176 | tf_op jit(solution)/shard_map/ppermute | solution.py:245
  367.9 6.3 %collective-permute-done.34 = bf16[1,2,40,1024]{3,2,1,0:T(8,128)(2,1)S(1)} collective-permute-done((bf16[1,2,40,1024]{3,2,1,0:T(8,128)(2,1)S(1)}, bf16[1,2,40,1024]{3,2,1,0:T(8,128)(2,1)S(1)}, u32[]{:S(2)}, u32[]{:S(2)}) %collective-permute-start.34) | collective-permute-done | bytes 163872 | tf_op jit(solution)/shard_map/ppermute | solution.py:245
  375.4 2.5 collective-permute-start.46
  378.0 3.9 collective-permute-done.35
  381.9 3.4 collective-permute-start.36
  385.4 8.7 %collective-permute-done.36 = bf16[1,40,1024]{2,1,0:T(8,128)(2,1)S(1)} collective-permute-done((bf16[1,40,1024]{2,1,0:T(8,128)(2,1)S(1)}, bf16[1,40,1024]{2,1,0:T(8,128)(2,1)S(1)}, u32[]{:S(2)}, u32[]{:S(2)}) %collective-permute-start.36) | collective-permute-done | bytes 81952 | tf_op jit(solution)/shard_map/ppermute | solution.py:245
  394.1 2.3 collective-permute-start.37
  396.5 4.9 weight_grad.18
  407.0 21.9 %collective-permute-done.38 = bf16[4,40,1024]{2,1,0:T(8,128)(2,1)S(1)} collective-permute-done((bf16[4,40,1024]{2,1,0:T(8,128)(2,1)S(1)}, bf16[4,40,1024]{2,1,0:T(8,128)(2,1)S(1)}, u32[]{:S(2)}, u32[]{:S(2)}) %collective-permute-start.38) | collective-permute-done | bytes 327712 | tf_op jit(solution)/shard_map/ppermute | solution.py:242
  429.1 4.7 weight_grad.19
  435.6 7.0 %collective-permute-done.25 = bf16[2,2,32,1536]{3,2,1,0:T(8,128)(2,1)S(1)} collective-permute-done((bf16[2,2,32,1536]{3,2,1,0:T(8,128)(2,1)S(1)}, bf16[2,2,32,1536]{3,2,1,0:T(8,128)(2,1)S(1)}, u32[]{:S(2)}, u32[]{:S(2)}) %collective-permute-start.25) | collective-permute-done | bytes 393248 | tf_op jit(solution)/shard_map/ppermute | solution.py:245
  445.2 5.3 %collective-permute-done.26 = bf16[2,1,32,1536]{3,2,1,0:T(8,128)(2,1)S(1)} collective-permute-done((bf16[2,1,32,1536]{3,2,1,0:T(8,128)(2,1)S(1)}, bf16[2,1,32,1536]{3,2,1,0:T(8,128)(2,1)S(1)}, u32[]{:S(2)}, u32[]{:S(2)}) %collective-permute-start.26) | collective-permute-done | bytes 196640 | tf_op jit(solution)/shard_map/ppermute | solution.py:245
  451.7 2.6 bitcast_convert_fusion
  455.7 16.2 %collective-permute-done.47 = bf16[4,32,4096]{2,1,0:T(8,128)(2,1)S(1)} collective-permute-done((bf16[4,32,4096]{2,1,0:T(8,128)(2,1)S(1)}, bf16[4,32,4096]{2,1,0:T(8,128)(2,1)S(1)}, u32[]{:S(2)}, u32[]{:S(2)}) %collective-permute-start.47) | collective-permute-done | bytes 1048608 | tf_op jit(solution)/shard_map/ppermute | solution.py:242
  472.8 8.8 %collective-permute-done.29 = bf16[2,32,3072]{2,1,0:T(8,128)(2,1)S(1)} collective-permute-done((bf16[2,32,3072]{2,1,0:T(8,128)(2,1)S(1)}, bf16[2,32,3072]{2,1,0:T(8,128)(2,1)S(1)}, u32[]{:S(2)}, u32[]{:S(2)}) %collective-permute-start.29) | collective-permute-done | bytes 393248 | tf_op jit(solution)/shard_map/ppermute | solution.py:245
  483.5 2.6 bitcast_convert_fusion.1
  486.2 12.5 %collective-permute-done.30 = bf16[4,32,3072]{2,1,0:T(8,128)(2,1)S(1)} collective-permute-done((bf16[4,32,3072]{2,1,0:T(8,128)(2,1)S(1)}, bf16[4,32,3072]{2,1,0:T(8,128)(2,1)S(1)}, u32[]{:S(2)}, u32[]{:S(2)}) %collective-permute-start.30) | collective-permute-done | bytes 786464 | tf_op jit(solution)/shard_map/ppermute | solution.py:242
  (375 shorter events, 127.4 us)
Async XLA Ops:
  0.6 16.8 %copy-start.44 = (bf16[256,1024]{1,0:T(8,128)(2,1)S(1)}, bf16[256,1024]{1,0:T(8,128)(2,1)}, u32[]{:S(2)}) copy-start(bf16[256,1024]{1,0:T(8,128)(2,1)} %param.21) | copy-start | bytes 1572868
  0.7 19.5 %copy-start.36 = (bf16[256,4096]{1,0:T(8,128)(2,1)S(1)}, bf16[256,4096]{1,0:T(8,128)(2,1)}, u32[]{:S(2)}) copy-start(bf16[256,4096]{1,0:T(8,128)(2,1)} %param.27) | copy-start | bytes 6291460
  3.6 54.7 %collective-permute-start = (bf16[304,1024]{1,0:T(8,128)(2,1)}, bf16[304,1024]{1,0:T(8,128)(2,1)}, u32[]{:S(2)}, u32[]{:S(2)}) collective-permute-start(bf16[304,1024]{1,0:T(8,128)(2,1)} %pad_maximum_fusion.2), channel_id=1, source_target_pairs={{4,16},{12,24},{16,4},{24,12},{5,17},{13,25},{17,5},{25,13},{6,18}... | collective-permute-start | bytes 1867784 | tf_op jit(solution)/shard_map/ppermute | solution.py:254
  12.4 23.3 %collective-permute-start.2 = (bf16[24,128]{1,0:T(8,128)(2,1)S(1)}, bf16[24,128]{1,0:T(8,128)(2,1)S(1)}, u32[]{:S(2)}, u32[]{:S(2)}) collective-permute-start(bf16[24,128]{1,0:T(8,128)(2,1)S(1)} %bitcast.438), channel_id=1, source_target_pairs={{0,8},{4,12},{8,0},{12,4},{1,9},{5,13},{9,1},{13,5},{2,10},{6,14},... | collective-permute-start | bytes 18440 | tf_op jit(solution)/shard_map/ppermute | solution.py:239
  17.4 43.9 %collective-permute-start.4 = (bf16[128,3072]{1,0:T(8,128)(2,1)}, bf16[128,3072]{1,0:T(8,128)(2,1)}, u32[]{:S(2)}, u32[]{:S(2)}) collective-permute-start(bf16[128,3072]{1,0:T(8,128)(2,1)} %dynamic-slice_bitcast_fusion.3), channel_id=1, source_target_pairs={{0,8},{4,12},{8,0},{12,4},{1,9},{5,13},{9,1},{13,5},{2,10},{6,14},... | collective-permute-start | bytes 2359304 | tf_op jit(solution)/shard_map/ppermute | solution.py:239
  18.2 24.7 %collective-permute-start.7 = (bf16[128,1024]{1,0:T(8,128)(2,1)}, bf16[128,1024]{1,0:T(8,128)(2,1)S(1)}, u32[]{:S(2)}, u32[]{:S(2)}) collective-permute-start(bf16[128,1024]{1,0:T(8,128)(2,1)} %dynamic-slice_bitcast_fusion.7), channel_id=1, source_target_pairs={{0,8},{4,12},{8,0},{12,4},{1,9},{5,13},{9,1},{13,5},{2,10},{6,14},... | collective-permute-start | bytes 786440 | tf_op jit(solution)/shard_map/ppermute | solution.py:239
  21.2 44.2 %collective-permute-start.10 = (bf16[128,4096]{1,0:T(8,128)(2,1)}, bf16[128,4096]{1,0:T(8,128)(2,1)}, u32[]{:S(2)}, u32[]{:S(2)}) collective-permute-start(bf16[128,4096]{1,0:T(8,128)(2,1)} %dynamic-slice_bitcast_fusion.2), channel_id=1, source_target_pairs={{0,8},{4,12},{8,0},{12,4},{1,9},{5,13},{9,1},{13,5},{2,10},{6,14},... | collective-permute-start | bytes 3145736 | tf_op jit(solution)/shard_map/ppermute | solution.py:239
  35.7 24.1 %copy-start.41 = (bf16[1,290,1024]{2,1,0:T(8,128)(2,1)S(1)}, bf16[1,290,1024]{2,1,0:T(8,128)(2,1)}, u32[]{:S(2)}) copy-start(bf16[1,290,1024]{2,1,0:T(8,128)(2,1)} %param.31) | copy-start | bytes 1781764
  35.8 2.4 collective-permute-start.3
  38.1 21.7 %collective-permute-start.17 = (bf16[304,1024]{1,0:T(8,128)(2,1)}, bf16[304,1024]{1,0:T(8,128)(2,1)S(1)}, u32[]{:S(2)}, u32[]{:S(2)}) collective-permute-start(bf16[304,1024]{1,0:T(8,128)(2,1)} %concatenate.224), channel_id=1, source_target_pairs={{4,16},{12,24},{16,4},{24,12},{5,17},{13,25},{17,5},{25,13},{6,18}... | collective-permute-start | bytes 1867784 | tf_op jit(solution)/shard_map/ppermute | solution.py:254
  42.9 13.2 %collective-permute-start.8 = (bf16[128,1024]{1,0:T(8,128)(2,1)S(1)}, bf16[128,1024]{1,0:T(8,128)(2,1)S(1)}, u32[]{:S(2)}, u32[]{:S(2)}) collective-permute-start(bf16[128,1024]{1,0:T(8,128)(2,1)S(1)} %collective-permute-done.7), channel_id=1, source_target_pairs={{0,16},{16,0},{1,17},{17,1},{2,18},{18,2},{3,19},{19,3},{4,20},{20... | collective-permute-start | bytes 786440 | tf_op jit(solution)/shard_map/ppermute | solution.py:242
  56.0 31.9 %collective-permute-start.13 = (bf16[512,1024]{1,0:T(8,128)(2,1)}, bf16[512,1024]{1,0:T(8,128)(2,1)}, u32[]{:S(2)}, u32[]{:S(2)}) collective-permute-start(bf16[512,1024]{1,0:T(8,128)(2,1)} %dynamic-slice_bitcast_fusion.1), channel_id=1, source_target_pairs={{0,8},{4,12},{8,0},{12,4},{1,9},{5,13},{9,1},{13,5},{2,10},{6,14},... | collective-permute-start | bytes 3145736 | tf_op jit(solution)/shard_map/ppermute | solution.py:239
  58.2 30.6 %copy-start.30 = (bf16[4,128,4096]{2,1,0:T(8,128)(2,1)S(1)}, bf16[4,128,4096]{2,1,0:T(8,128)(2,1)}, u32[]{:S(2)}) copy-start(bf16[4,128,4096]{2,1,0:T(8,128)(2,1)} %copy-done.29) | copy-start | bytes 12582916
  59.7 30.5 %collective-permute-start.1 = (bf16[304,1024]{1,0:T(8,128)(2,1)S(1)}, bf16[304,1024]{1,0:T(8,128)(2,1)S(1)}, u32[]{:S(2)}, u32[]{:S(2)}) collective-permute-start(bf16[304,1024]{1,0:T(8,128)(2,1)S(1)} %broadcast_select_fusion.2), channel_id=1, source_target_pairs={{0,4},{4,0},{8,12},{12,8},{1,5},{5,1},{9,13},{13,9},{2,6},{6,2},{1... | collective-permute-start | bytes 1867784 | tf_op jit(solution)/shard_map/ppermute | solution.py:236
  60.9 63.9 %collective-permute-start.18 = (bf16[304,1024]{1,0:T(8,128)(2,1)}, bf16[304,1024]{1,0:T(8,128)(2,1)}, u32[]{:S(2)}, u32[]{:S(2)}) collective-permute-start(bf16[304,1024]{1,0:T(8,128)(2,1)} %broadcast_select_fusion.1), channel_id=1, source_target_pairs={{0,4},{4,0},{8,12},{12,8},{1,5},{5,1},{9,13},{13,9},{2,6},{6,2},{1... | collective-permute-start | bytes 1867784 | tf_op jit(solution)/shard_map/ppermute | solution.py:236
  61.4 32.3 %collective-permute-start.5 = (bf16[128,3072]{1,0:T(8,128)(2,1)}, bf16[128,3072]{1,0:T(8,128)(2,1)S(1)}, u32[]{:S(2)}, u32[]{:S(2)}) collective-permute-start(bf16[128,3072]{1,0:T(8,128)(2,1)} %collective-permute-done.4), channel_id=1, source_target_pairs={{0,16},{16,0},{1,17},{17,1},{2,18},{18,2},{3,19},{19,3},{4,20},{20... | collective-permute-start | bytes 2359304 | tf_op jit(solution)/shard_map/ppermute | solution.py:242
  65.4 39.0 %collective-permute-start.11 = (bf16[128,4096]{1,0:T(8,128)(2,1)}, bf16[128,4096]{1,0:T(8,128)(2,1)S(1)}, u32[]{:S(2)}, u32[]{:S(2)}) collective-permute-start(bf16[128,4096]{1,0:T(8,128)(2,1)} %collective-permute-done.10), channel_id=1, source_target_pairs={{0,16},{16,0},{1,17},{17,1},{2,18},{18,2},{3,19},{19,3},{4,20},{20... | collective-permute-start | bytes 3145736 | tf_op jit(solution)/shard_map/ppermute | solution.py:242
  87.9 40.0 %collective-permute-start.14 = (bf16[512,1024]{1,0:T(8,128)(2,1)}, bf16[512,1024]{1,0:T(8,128)(2,1)}, u32[]{:S(2)}, u32[]{:S(2)}) collective-permute-start(bf16[512,1024]{1,0:T(8,128)(2,1)} %collective-permute-done.13), channel_id=1, source_target_pairs={{0,16},{16,0},{1,17},{17,1},{2,18},{18,2},{3,19},{19,3},{4,20},{20... | collective-permute-start | bytes 3145736 | tf_op jit(solution)/shard_map/ppermute | solution.py:242
  90.6 44.2 %copy-start.27 = (bf16[2,304,1024]{2,1,0:T(8,128)(2,1)}, bf16[2,304,1024]{2,1,0:T(8,128)(2,1)S(1)}, u32[]{:S(2)}) copy-start(bf16[2,304,1024]{2,1,0:T(8,128)(2,1)S(1)} %get-tuple-element.86) | copy-start | bytes 3735556
  94.4 13.5 %collective-permute-start.6 = (bf16[2,256,1536]{2,1,0:T(8,128)(2,1)S(1)}, bf16[2,256,1536]{2,1,0:T(8,128)(2,1)S(1)}, u32[]{:S(2)}, u32[]{:S(2)}) collective-permute-start(bf16[2,256,1536]{2,1,0:T(8,128)(2,1)S(1)} %broadcast_select_fusion), channel_id=1, source_target_pairs={{0,4},{4,0},{8,12},{12,8},{1,5},{5,1},{9,13},{13,9},{2,6},{6,2},{1... | collective-permute-start | bytes 4718600 | tf_op jit(solution)/shard_map/ppermute | solution.py:236
  107.9 22.3 %collective-permute-start.12 = (bf16[2,256,2048]{2,1,0:T(8,128)(2,1)}, bf16[2,256,2048]{2,1,0:T(8,128)(2,1)}, u32[]{:S(2)}, u32[]{:S(2)}) collective-permute-start(bf16[2,256,2048]{2,1,0:T(8,128)(2,1)} %maximum_select_fusion.2), channel_id=1, source_target_pairs={{0,4},{4,0},{8,12},{12,8},{1,5},{5,1},{9,13},{13,9},{2,6},{6,2},{1... | collective-permute-start | bytes 6291464 | tf_op jit(solution)/shard_map/ppermute | solution.py:236
  122.0 12.9 %collective-permute-start.9 = (bf16[608,1024]{1,0:T(8,128)(2,1)S(1)}, bf16[608,1024]{1,0:T(8,128)(2,1)S(1)}, u32[]{:S(2)}, u32[]{:S(2)}) collective-permute-start(bf16[608,1024]{1,0:T(8,128)(2,1)S(1)} %get-tuple-element.146), channel_id=1, source_target_pairs={{0,4},{4,0},{8,12},{12,8},{1,5},{5,1},{9,13},{13,9},{2,6},{6,2},{1... | collective-permute-start | bytes 3735560 | tf_op jit(solution)/shard_map/ppermute | solution.py:236
  127.1 71.3 %copy-start.2 = (bf16[2,304,1024]{2,1,0:T(8,128)(2,1)}, bf16[2,304,1024]{2,1,0:T(8,128)(2,1)S(1)}, u32[]{:S(2)}) copy-start(bf16[2,304,1024]{2,1,0:T(8,128)(2,1)S(1)} %get-tuple-element.79) | copy-start | bytes 3735556
  149.4 15.3 %copy-start.5 = (bf16[608,2048]{1,0:T(8,128)(2,1)}, bf16[608,2048]{1,0:T(8,128)(2,1)S(1)}, u32[]{:S(2)}) copy-start(bf16[608,2048]{1,0:T(8,128)(2,1)S(1)} %get-tuple-element.20.left_ref) | copy-start | bytes 7471108
  160.6 35.3 %collective-permute-start.19 = (bf16[608,1024]{1,0:T(8,128)(2,1)}, bf16[608,1024]{1,0:T(8,128)(2,1)}, u32[]{:S(2)}, u32[]{:S(2)}) collective-permute-start(bf16[608,1024]{1,0:T(8,128)(2,1)} %get-tuple-element.148), channel_id=1, source_target_pairs={{0,4},{4,0},{8,12},{12,8},{1,5},{5,1},{9,13},{13,9},{2,6},{6,2},{1... | collective-permute-start | bytes 3735560 | tf_op jit(solution)/shard_map/ppermute | solution.py:236
  164.1 26.3 %collective-permute-start.40 = (bf16[256,2048]{1,0:T(8,128)(2,1)}, bf16[256,2048]{1,0:T(8,128)(2,1)}, u32[]{:S(2)}, u32[]{:S(2)}) collective-permute-start(bf16[256,2048]{1,0:T(8,128)(2,1)} %weight_grad.25), channel_id=1, source_target_pairs={{0,8},{4,12},{8,0},{12,4},{1,9},{5,13},{9,1},{13,5},{2,10},{6,14},... | collective-permute-start | bytes 3145736 | tf_op jit(solution)/shard_map/ppermute | solution.py:239
  171.6 9.9 %collective-permute-start.15 = (bf16[304,1024]{1,0:T(8,128)(2,1)}, bf16[304,1024]{1,0:T(8,128)(2,1)S(1)}, u32[]{:S(2)}, u32[]{:S(2)}) collective-permute-start(bf16[304,1024]{1,0:T(8,128)(2,1)} %fusion.36), channel_id=1, source_target_pairs={{0,4},{4,0},{8,12},{12,8},{1,5},{5,1},{9,13},{13,9},{2,6},{6,2},{1... | collective-permute-start | bytes 1867784 | tf_op jit(solution)/shard_map/ppermute | solution.py:236
  177.3 73.0 %collective-permute-start.39 = (bf16[256,2048]{1,0:T(8,128)(2,1)}, bf16[256,2048]{1,0:T(8,128)(2,1)}, u32[]{:S(2)}, u32[]{:S(2)}) collective-permute-start(bf16[256,2048]{1,0:T(8,128)(2,1)} %weight_grad.24), channel_id=1, source_target_pairs={{0,8},{4,12},{8,0},{12,4},{1,9},{5,13},{9,1},{13,5},{2,10},{6,14},... | collective-permute-start | bytes 3145736 | tf_op jit(solution)/shard_map/ppermute | solution.py:239
  180.9 54.0 %collective-permute-start.49 = (bf16[512,1024]{1,0:T(8,128)(2,1)}, bf16[512,1024]{1,0:T(8,128)(2,1)}, u32[]{:S(2)}, u32[]{:S(2)}) collective-permute-start(bf16[512,1024]{1,0:T(8,128)(2,1)} %weight_grad.29), channel_id=1, source_target_pairs={{0,8},{4,12},{8,0},{12,4},{1,9},{5,13},{9,1},{13,5},{2,10},{6,14},... | collective-permute-start | bytes 3145736 | tf_op jit(solution)/shard_map/ppermute | solution.py:239
  182.7 56.0 %collective-permute-start.16 = (bf16[304,1024]{1,0:T(8,128)(2,1)}, bf16[304,1024]{1,0:T(8,128)(2,1)}, u32[]{:S(2)}, u32[]{:S(2)}) collective-permute-start(bf16[304,1024]{1,0:T(8,128)(2,1)} %fusion.28), channel_id=1, source_target_pairs={{4,16},{12,24},{16,4},{24,12},{5,17},{13,25},{17,5},{25,13},{6,18}... | collective-permute-start | bytes 1867784 | tf_op jit(solution)/shard_map/ppermute | solution.py:254
  195.6 54.7 %collective-permute-start.41 = (bf16[256,2048]{1,0:T(8,128)(2,1)}, bf16[256,2048]{1,0:T(8,128)(2,1)}, u32[]{:S(2)}, u32[]{:S(2)}) collective-permute-start(bf16[256,2048]{1,0:T(8,128)(2,1)} %weight_grad.26), channel_id=1, source_target_pairs={{0,16},{16,0},{1,17},{17,1},{2,18},{18,2},{3,19},{19,3},{4,20},{20... | collective-permute-start | bytes 3145736 | tf_op jit(solution)/shard_map/ppermute | solution.py:242
  222.2 46.8 %collective-permute-start.20 = (bf16[608,1024]{1,0:T(8,128)(2,1)}, bf16[608,1024]{1,0:T(8,128)(2,1)}, u32[]{:S(2)}, u32[]{:S(2)}) collective-permute-start(bf16[608,1024]{1,0:T(8,128)(2,1)} %get-tuple-element.150), channel_id=1, source_target_pairs={{0,4},{4,0},{8,12},{12,8},{1,5},{5,1},{9,13},{13,9},{2,6},{6,2},{1... | collective-permute-start | bytes 3735560 | tf_op jit(solution)/shard_map/ppermute | solution.py:236
  235.0 25.0 %collective-permute-start.48 = (bf16[512,1024]{1,0:T(8,128)(2,1)}, bf16[512,1024]{1,0:T(8,128)(2,1)}, u32[]{:S(2)}, u32[]{:S(2)}) collective-permute-start(bf16[512,1024]{1,0:T(8,128)(2,1)} %weight_grad.28), channel_id=1, source_target_pairs={{0,8},{4,12},{8,0},{12,4},{1,9},{5,13},{9,1},{13,5},{2,10},{6,14},... | collective-permute-start | bytes 3145736 | tf_op jit(solution)/shard_map/ppermute | solution.py:239
  238.6 24.7 %collective-permute-start.50 = (bf16[512,1024]{1,0:T(8,128)(2,1)}, bf16[512,1024]{1,0:T(8,128)(2,1)}, u32[]{:S(2)}, u32[]{:S(2)}) collective-permute-start(bf16[512,1024]{1,0:T(8,128)(2,1)} %weight_grad.30), channel_id=1, source_target_pairs={{0,16},{16,0},{1,17},{17,1},{2,18},{18,2},{3,19},{19,3},{4,20},{20... | collective-permute-start | bytes 3145736 | tf_op jit(solution)/shard_map/ppermute | solution.py:242
  257.1 32.5 %collective-permute-start.42 = (bf16[2,2,32,2048]{3,2,1,0:T(8,128)(2,1)}, bf16[2,2,32,2048]{3,2,1,0:T(8,128)(2,1)}, u32[]{:S(2)}, u32[]{:S(2)}) collective-permute-start(bf16[2,2,32,2048]{3,2,1,0:T(8,128)(2,1)} %dynamic-slice_bitcast_fusion.5), channel_id=1, source_target_pairs={{0,1},{1,0},{2,3},{3,2},{4,5},{5,4},{6,7},{7,6},{8,9},{9,8},{10,11... | collective-permute-start | bytes 1572872 | tf_op jit(solution)/shard_map/ppermute | solution.py:245
  267.3 25.0 %collective-permute-start.51 = (bf16[1,2,128,1024]{3,2,1,0:T(8,128)(2,1)}, bf16[1,2,128,1024]{3,2,1,0:T(8,128)(2,1)}, u32[]{:S(2)}, u32[]{:S(2)}) collective-permute-start(bf16[1,2,128,1024]{3,2,1,0:T(8,128)(2,1)} %dynamic-slice_bitcast_fusion.4), channel_id=1, source_target_pairs={{0,1},{1,0},{2,3},{3,2},{4,5},{5,4},{6,7},{7,6},{8,9},{9,8},{10,11... | collective-permute-start | bytes 1572872 | tf_op jit(solution)/shard_map/ppermute | solution.py:245
  283.5 63.4 %collective-permute-start.21 = (bf16[304,1024]{1,0:T(8,128)(2,1)}, bf16[304,1024]{1,0:T(8,128)(2,1)}, u32[]{:S(2)}, u32[]{:S(2)}) collective-permute-start(bf16[304,1024]{1,0:T(8,128)(2,1)} %get-tuple-element.83), channel_id=1, source_target_pairs={{4,16},{12,24},{16,4},{24,12},{5,17},{13,25},{17,5},{25,13},{6,18}... | collective-permute-start | bytes 1867784 | tf_op jit(solution)/shard_map/ppermute | solution.py:254
  285.0 144.1 %collective-permute-start.22 = (bf16[256,1536]{1,0:T(8,128)(2,1)}, bf16[256,1536]{1,0:T(8,128)(2,1)}, u32[]{:S(2)}, u32[]{:S(2)}) collective-permute-start(bf16[256,1536]{1,0:T(8,128)(2,1)} %weight_grad.16), channel_id=1, source_target_pairs={{0,8},{4,12},{8,0},{12,4},{1,9},{5,13},{9,1},{13,5},{2,10},{6,14},... | collective-permute-start | bytes 2359304 | tf_op jit(solution)/shard_map/ppermute | solution.py:239
  286.5 110.0 %collective-permute-start.23 = (bf16[256,1536]{1,0:T(8,128)(2,1)}, bf16[256,1536]{1,0:T(8,128)(2,1)}, u32[]{:S(2)}, u32[]{:S(2)}) collective-permute-start(bf16[256,1536]{1,0:T(8,128)(2,1)} %weight_grad.17), channel_id=1, source_target_pairs={{0,8},{4,12},{8,0},{12,4},{1,9},{5,13},{9,1},{13,5},{2,10},{6,14},... | collective-permute-start | bytes 2359304 | tf_op jit(solution)/shard_map/ppermute | solution.py:239
  289.6 39.8 %collective-permute-start.32 = (bf16[160,1024]{1,0:T(8,128)(2,1)S(1)}, bf16[160,1024]{1,0:T(8,128)(2,1)S(1)}, u32[]{:S(2)}, u32[]{:S(2)}) collective-permute-start(bf16[160,1024]{1,0:T(8,128)(2,1)S(1)} %bitcast.410), channel_id=1, source_target_pairs={{0,8},{4,12},{8,0},{12,4},{1,9},{5,13},{9,1},{13,5},{2,10},{6,14},... | collective-permute-start | bytes 983048 | tf_op jit(solution)/shard_map/ppermute | solution.py:239
  292.4 38.6 %collective-permute-start.43 = (bf16[2,1,32,2048]{3,2,1,0:T(8,128)(2,1)S(1)}, bf16[2,1,32,2048]{3,2,1,0:T(8,128)(2,1)S(1)}, u32[]{:S(2)}, u32[]{:S(2)}) collective-permute-start(bf16[2,1,32,2048]{3,2,1,0:T(8,128)(2,1)S(1)} %constant_dynamic-slice_fusion.1), channel_id=1, source_target_pairs={{0,2},{1,3},{2,0},{3,1},{4,6},{5,7},{6,4},{7,5},{8,10},{9,11},{10,... | collective-permute-start | bytes 786440 | tf_op jit(solution)/shard_map/ppermute | solution.py:245
  296.3 50.7 %copy-start.35 = (f32[304,1024]{1,0:T(8,128)S(1)}, f32[304,1024]{1,0:T(8,128)}, u32[]{:S(2)}) copy-start(f32[304,1024]{1,0:T(8,128)} %get-tuple-element.84) | copy-start | bytes 3735556
  329.4 21.1 %collective-permute-start.31 = (bf16[160,1024]{1,0:T(8,128)(2,1)S(1)}, bf16[160,1024]{1,0:T(8,128)(2,1)S(1)}, u32[]{:S(2)}, u32[]{:S(2)}) collective-permute-start(bf16[160,1024]{1,0:T(8,128)(2,1)S(1)} %bitcast.409), channel_id=1, source_target_pairs={{0,8},{4,12},{8,0},{12,4},{1,9},{5,13},{9,1},{13,5},{2,10},{6,14},... | collective-permute-start | bytes 983048 | tf_op jit(solution)/shard_map/ppermute | solution.py:239
  331.0 14.4 %collective-permute-start.52 = (bf16[1,1,128,1024]{3,2,1,0:T(8,128)(2,1)S(1)}, bf16[1,1,128,1024]{3,2,1,0:T(8,128)(2,1)S(1)}, u32[]{:S(2)}, u32[]{:S(2)}) collective-permute-start(bf16[1,1,128,1024]{3,2,1,0:T(8,128)(2,1)S(1)} %constant_dynamic-slice_fusion), channel_id=1, source_target_pairs={{0,2},{1,3},{2,0},{3,1},{4,6},{5,7},{6,4},{7,5},{8,10},{9,11},{10,... | collective-permute-start | bytes 786440 | tf_op jit(solution)/shard_map/ppermute | solution.py:245
  345.4 1.3 collective-permute-start.44
  346.8 9.8 %collective-permute-start.33 = (bf16[160,1024]{1,0:T(8,128)(2,1)S(1)}, bf16[160,1024]{1,0:T(8,128)(2,1)S(1)}, u32[]{:S(2)}, u32[]{:S(2)}) collective-permute-start(bf16[160,1024]{1,0:T(8,128)(2,1)S(1)} %fusion.33), channel_id=1, source_target_pairs={{0,16},{16,0},{1,17},{17,1},{2,18},{18,2},{3,19},{19,3},{4,20},{20... | collective-permute-start | bytes 983048 | tf_op jit(solution)/shard_map/ppermute | solution.py:242
  346.9 20.7 %collective-permute-start.53 = (bf16[1,128,1024]{2,1,0:T(8,128)(2,1)S(1)}, bf16[1,128,1024]{2,1,0:T(8,128)(2,1)S(1)}, u32[]{:S(2)}, u32[]{:S(2)}) collective-permute-start(bf16[1,128,1024]{2,1,0:T(8,128)(2,1)S(1)} %bitcast.378), channel_id=1, source_target_pairs={{0,2},{1,3},{2,0},{3,1},{4,6},{5,7},{6,4},{7,5},{8,10},{9,11},{10,... | collective-permute-start | bytes 786440 | tf_op jit(solution)/shard_map/ppermute | solution.py:245
  350.5 24.8 %collective-permute-start.45 = (bf16[1,32,4096]{2,1,0:T(8,128)(2,1)S(1)}, bf16[1,32,4096]{2,1,0:T(8,128)(2,1)S(1)}, u32[]{:S(2)}, u32[]{:S(2)}) collective-permute-start(bf16[1,32,4096]{2,1,0:T(8,128)(2,1)S(1)} %get-tuple-element.121), channel_id=1, source_target_pairs={{0,2},{1,3},{2,0},{3,1},{4,6},{5,7},{6,4},{7,5},{8,10},{9,11},{10,... | collective-permute-start | bytes 786440 | tf_op jit(solution)/shard_map/ppermute | solution.py:245
  356.8 17.4 %collective-permute-start.34 = (bf16[1,2,40,1024]{3,2,1,0:T(8,128)(2,1)S(1)}, bf16[1,2,40,1024]{3,2,1,0:T(8,128)(2,1)S(1)}, u32[]{:S(2)}, u32[]{:S(2)}) collective-permute-start(bf16[1,2,40,1024]{3,2,1,0:T(8,128)(2,1)S(1)} %dynamic-slice_bitcast_fusion.8), channel_id=1, source_target_pairs={{0,1},{1,0},{2,3},{3,2},{4,5},{5,4},{6,7},{7,6},{8,9},{9,8},{10,11... | collective-permute-start | bytes 491528 | tf_op jit(solution)/shard_map/ppermute | solution.py:245
  367.7 36.7 %collective-permute-start.54 = (bf16[2,128,1024]{2,1,0:T(8,128)(2,1)S(1)}, bf16[2,128,1024]{2,1,0:T(8,128)(2,1)S(1)}, u32[]{:S(2)}, u32[]{:S(2)}) collective-permute-start(bf16[2,128,1024]{2,1,0:T(8,128)(2,1)S(1)} %maximum_select_fusion.15), channel_id=1, source_target_pairs={{0,1},{1,0},{2,3},{3,2},{4,5},{5,4},{6,7},{7,6},{8,9},{9,8},{10,11... | collective-permute-start | bytes 1572872 | tf_op jit(solution)/shard_map/ppermute | solution.py:245
  374.2 7.6 %collective-permute-start.35 = (bf16[1,1,40,1024]{3,2,1,0:T(8,128)(2,1)S(1)}, bf16[1,1,40,1024]{3,2,1,0:T(8,128)(2,1)S(1)}, u32[]{:S(2)}, u32[]{:S(2)}) collective-permute-start(bf16[1,1,40,1024]{3,2,1,0:T(8,128)(2,1)S(1)} %constant_dynamic-slice_fusion.2), channel_id=1, source_target_pairs={{0,2},{1,3},{2,0},{3,1},{4,6},{5,7},{6,4},{7,5},{8,10},{9,11},{10,... | collective-permute-start | bytes 245768 | tf_op jit(solution)/shard_map/ppermute | solution.py:245
  375.4 30.2 %collective-permute-start.46 = (bf16[2,32,4096]{2,1,0:T(8,128)(2,1)S(1)}, bf16[2,32,4096]{2,1,0:T(8,128)(2,1)S(1)}, u32[]{:S(2)}, u32[]{:S(2)}) collective-permute-start(bf16[2,32,4096]{2,1,0:T(8,128)(2,1)S(1)} %maximum_select_fusion.13), channel_id=1, source_target_pairs={{0,1},{1,0},{2,3},{3,2},{4,5},{5,4},{6,7},{7,6},{8,9},{9,8},{10,11... | collective-permute-start | bytes 1572872 | tf_op jit(solution)/shard_map/ppermute | solution.py:245
  381.9 12.2 %collective-permute-start.36 = (bf16[1,40,1024]{2,1,0:T(8,128)(2,1)S(1)}, bf16[1,40,1024]{2,1,0:T(8,128)(2,1)S(1)}, u32[]{:S(2)}, u32[]{:S(2)}) collective-permute-start(bf16[1,40,1024]{2,1,0:T(8,128)(2,1)S(1)} %bitcast.404), channel_id=1, source_target_pairs={{0,2},{1,3},{2,0},{3,1},{4,6},{5,7},{6,4},{7,5},{8,10},{9,11},{10,... | collective-permute-start | bytes 245768 | tf_op jit(solution)/shard_map/ppermute | solution.py:245
  394.1 9.1 %collective-permute-start.37 = (bf16[2,40,1024]{2,1,0:T(8,128)(2,1)S(1)}, bf16[2,40,1024]{2,1,0:T(8,128)(2,1)S(1)}, u32[]{:S(2)}, u32[]{:S(2)}) collective-permute-start(bf16[2,40,1024]{2,1,0:T(8,128)(2,1)S(1)} %maximum_select_fusion.20), channel_id=1, source_target_pairs={{0,1},{1,0},{2,3},{3,2},{4,5},{5,4},{6,7},{7,6},{8,9},{9,8},{10,11... | collective-permute-start | bytes 491528 | tf_op jit(solution)/shard_map/ppermute | solution.py:245
  401.4 27.7 %collective-permute-start.24 = (bf16[256,1536]{1,0:T(8,128)(2,1)S(1)}, bf16[256,1536]{1,0:T(8,128)(2,1)S(1)}, u32[]{:S(2)}, u32[]{:S(2)}) collective-permute-start(bf16[256,1536]{1,0:T(8,128)(2,1)S(1)} %weight_grad.18), channel_id=1, source_target_pairs={{0,16},{16,0},{1,17},{17,1},{2,18},{18,2},{3,19},{19,3},{4,20},{20... | collective-permute-start | bytes 2359304 | tf_op jit(solution)/shard_map/ppermute | solution.py:242
  403.3 25.6 %collective-permute-start.38 = (bf16[4,40,1024]{2,1,0:T(8,128)(2,1)S(1)}, bf16[4,40,1024]{2,1,0:T(8,128)(2,1)S(1)}, u32[]{:S(2)}, u32[]{:S(2)}) collective-permute-start(bf16[4,40,1024]{2,1,0:T(8,128)(2,1)S(1)} %bitcast.395), channel_id=1, source_target_pairs={{0,16},{16,0},{1,17},{17,1},{2,18},{18,2},{3,19},{19,3},{4,20},{20... | collective-permute-start | bytes 983048 | tf_op jit(solution)/shard_map/ppermute | solution.py:242
  404.6 46.8 %collective-permute-start.55 = (bf16[4,128,1024]{2,1,0:T(8,128)(2,1)S(1)}, bf16[4,128,1024]{2,1,0:T(8,128)(2,1)S(1)}, u32[]{:S(2)}, u32[]{:S(2)}) collective-permute-start(bf16[4,128,1024]{2,1,0:T(8,128)(2,1)S(1)} %bitcast.363), channel_id=1, source_target_pairs={{0,16},{16,0},{1,17},{17,1},{2,18},{18,2},{3,19},{19,3},{4,20},{20... | collective-permute-start | bytes 3145736 | tf_op jit(solution)/shard_map/ppermute | solution.py:242
  405.8 66.1 %collective-permute-start.47 = (bf16[4,32,4096]{2,1,0:T(8,128)(2,1)S(1)}, bf16[4,32,4096]{2,1,0:T(8,128)(2,1)S(1)}, u32[]{:S(2)}, u32[]{:S(2)}) collective-permute-start(bf16[4,32,4096]{2,1,0:T(8,128)(2,1)S(1)} %bitcast.365), channel_id=1, source_target_pairs={{0,16},{16,0},{1,17},{17,1},{2,18},{18,2},{3,19},{19,3},{4,20},{20... | collective-permute-start | bytes 3145736 | tf_op jit(solution)/shard_map/ppermute | solution.py:242
  433.8 8.8 %collective-permute-start.25 = (bf16[2,2,32,1536]{3,2,1,0:T(8,128)(2,1)S(1)}, bf16[2,2,32,1536]{3,2,1,0:T(8,128)(2,1)S(1)}, u32[]{:S(2)}, u32[]{:S(2)}) collective-permute-start(bf16[2,2,32,1536]{3,2,1,0:T(8,128)(2,1)S(1)} %dynamic-slice_bitcast_fusion.6), channel_id=1, source_target_pairs={{0,1},{1,0},{2,3},{3,2},{4,5},{5,4},{6,7},{7,6},{8,9},{9,8},{10,11... | collective-permute-start | bytes 1179656 | tf_op jit(solution)/shard_map/ppermute | solution.py:245
  442.8 7.7 %collective-permute-start.26 = (bf16[2,1,32,1536]{3,2,1,0:T(8,128)(2,1)S(1)}, bf16[2,1,32,1536]{3,2,1,0:T(8,128)(2,1)S(1)}, u32[]{:S(2)}, u32[]{:S(2)}) collective-permute-start(bf16[2,1,32,1536]{3,2,1,0:T(8,128)(2,1)S(1)} %constant_dynamic-slice_fusion.9), channel_id=1, source_target_pairs={{0,2},{1,3},{2,0},{3,1},{4,6},{5,7},{6,4},{7,5},{8,10},{9,11},{10,... | collective-permute-start | bytes 589832 | tf_op jit(solution)/shard_map/ppermute | solution.py:245
  450.6 3.7 collective-permute-start.27
  454.5 17.8 %collective-permute-start.28 = (bf16[1,32,3072]{2,1,0:T(8,128)(2,1)S(1)}, bf16[1,32,3072]{2,1,0:T(8,128)(2,1)S(1)}, u32[]{:S(2)}, u32[]{:S(2)}) collective-permute-start(bf16[1,32,3072]{2,1,0:T(8,128)(2,1)S(1)} %bitcast.384), channel_id=1, source_target_pairs={{0,2},{1,3},{2,0},{3,1},{4,6},{5,7},{6,4},{7,5},{8,10},{9,11},{10,... | collective-permute-start | bytes 589832 | tf_op jit(solution)/shard_map/ppermute | solution.py:245
  472.3 9.3 %collective-permute-start.29 = (bf16[2,32,3072]{2,1,0:T(8,128)(2,1)S(1)}, bf16[2,32,3072]{2,1,0:T(8,128)(2,1)S(1)}, u32[]{:S(2)}, u32[]{:S(2)}) collective-permute-start(bf16[2,32,3072]{2,1,0:T(8,128)(2,1)S(1)} %maximum_select_fusion.17), channel_id=1, source_target_pairs={{0,1},{1,0},{2,3},{3,2},{4,5},{5,4},{6,7},{7,6},{8,9},{9,8},{10,11... | collective-permute-start | bytes 1179656 | tf_op jit(solution)/shard_map/ppermute | solution.py:245
  481.8 16.9 %collective-permute-start.30 = (bf16[4,32,3072]{2,1,0:T(8,128)(2,1)S(1)}, bf16[4,32,3072]{2,1,0:T(8,128)(2,1)S(1)}, u32[]{:S(2)}, u32[]{:S(2)}) collective-permute-start(bf16[4,32,3072]{2,1,0:T(8,128)(2,1)S(1)} %bitcast.371), channel_id=1, source_target_pairs={{0,16},{16,0},{1,17},{17,1},{2,18},{18,2},{3,19},{19,3},{4,20},{20... | collective-permute-start | bytes 2359304 | tf_op jit(solution)/shard_map/ppermute | solution.py:242
  (38 other events, 162.7 us)

commit v2 on v1

v2 whole, which is shorter than its diff:
```python
import functools
import math

import jax
import jax.numpy as jnp
from jax import lax
from jax.experimental import pallas as pl
from jax.experimental.pallas import tpu as pltpu
from jax.sharding import PartitionSpec as P

H = 16
HD = 64
EPS = 1e-06
F32 = jnp.float32
BF16 = jnp.bfloat16
VMEM_LIMIT = 48 * 1024 * 1024


def dims(left, right, dot_left, dot_right):
    return lax.dot_general(
        left, right, (((dot_left,), (dot_right,)), ((), ())), preferred_element_type=F32
    )


def whole(*shape):
    return pl.BlockSpec(shape, lambda *index: (0,) * len(shape))


def run(body, name, grid, place, operands, in_specs, outs, scratch=()):
    return pl.pallas_call(
        body,
        grid_spec=pltpu.PrefetchScalarGridSpec(
            num_scalar_prefetch=1,
            grid=grid,
            in_specs=in_specs,
            out_specs=[out[2] for out in outs],
            scratch_shapes=list(scratch),
        ),
        out_shape=[jax.ShapeDtypeStruct(out[0], out[1]) for out in outs],
        compiler_params=pltpu.CompilerParams(vmem_limit_bytes=VMEM_LIMIT),
        name=name,
    )(place, *operands)


def numbers(*values):
    return jnp.stack([jnp.asarray(value, jnp.int32) for value in values])


def key_visible(note_ref, padded_half, rows):
    note = note_ref[...].astype(F32)[rows % 16 : rows % 16 + 1, :]
    length = note[:, 0:1] * 16.0 + note[:, 1:2]
    row = lax.broadcasted_iota(jnp.int32, (2 * padded_half, 1), 0)
    second = row >= padded_half
    inside = jnp.where(second, row - padded_half, row)
    position = jnp.where(second, inside + rows, inside)
    return (inside < rows) & (position.astype(F32) < length)


def attend_forward(padded_half, rows, place_ref, note_ref, q_ref, k_ref, v_ref, mixed_ref, log_ref):
    visible = key_visible(note_ref, padded_half, rows)
    for head in range(2):
        lanes = slice(head * HD, (head + 1) * HD)
        scores = dims(k_ref[:, lanes], q_ref[:, lanes], 1, 1) * (HD ** -0.5)
        scores = jnp.where(visible, scores, -1000000000.0)
        top = jnp.max(scores, axis=0, keepdims=True)
        shifted = jnp.exp(scores - top)
        total = jnp.sum(shifted, axis=0, keepdims=True)
        weights = (shifted * (1.0 / total)).astype(BF16)
        log_ref[0, head : head + 1, :] = top + jnp.log(total)
        values = jnp.transpose(v_ref[:, lanes].astype(F32)).astype(BF16)
        mixed = dims(values, weights, 1, 0)
        mixed_ref[:, lanes] = jnp.transpose(mixed).astype(BF16)


def attend_backward(
    padded_half, rows, place_ref, note_ref, q_ref, k_ref, v_ref, g_ref, log_ref, out_ref, sum_ref
):
    visible = key_visible(note_ref, padded_half, rows)
    for head in range(2):
        lanes = slice(head * HD, (head + 1) * HD)
        queries, keys = q_ref[:, lanes], k_ref[:, lanes]
        values, grads = v_ref[:, lanes], g_ref[:, lanes]
        scores = dims(keys, queries, 1, 1) * (HD ** -0.5)
        weights = jnp.where(visible, jnp.exp(scores - log_ref[0, head : head + 1, :]), 0.0)
        grad_weights = dims(values, grads, 1, 1)
        inner = jnp.sum(weights * grad_weights, axis=0, keepdims=True)
        grad_scores = (weights * (grad_weights - inner)).astype(BF16)
        keys_t = jnp.transpose(keys.astype(F32)).astype(BF16)
        grad_q = (jnp.transpose(dims(keys_t, grad_scores, 1, 0)) * (HD ** -0.5)).astype(BF16)
        grad_v = dims(weights.astype(BF16), grads, 1, 0).astype(BF16)
        out_ref[0, :, lanes] = grad_q
        out_ref[1, :, lanes] = (dims(grad_scores, queries, 1, 0) * (HD ** -0.5)).astype(BF16)
        out_ref[2, :, lanes] = grad_v
        sum_ref[0, 0:1, lanes] = jnp.sum(grad_q.astype(F32), axis=0, keepdims=True)
        sum_ref[0, 1:2, lanes] = jnp.sum(grad_v.astype(F32), axis=0, keepdims=True)


def attention(place, image, qkv, rows):
    tokens, width = qkv.shape
    pairs = width // 3 // (2 * HD)
    part = lambda p: pl.BlockSpec((tokens, 2 * HD), lambda j, n, p=p: (0, p * pairs + j))
    return run(
        functools.partial(attend_forward, tokens // 2, rows),
        "attention",
        (pairs,),
        place,
        (image, qkv, qkv, qkv),
        [pl.BlockSpec((16, 128), lambda j, n: (rows // 16, 0)), part(0), part(1), part(2)],
        [
            ((tokens, width // 3), BF16, pl.BlockSpec((tokens, 2 * HD), lambda j, n: (0, j))),
            ((pairs, 2, tokens), F32, pl.BlockSpec((1, 2, tokens), lambda j, n: (j, 0, 0))),
        ],
    )


def attention_grad(place, image, qkv, grad_mixed, log_total, rows):
    tokens, width = qkv.shape
    pairs = width // 3 // (2 * HD)
    part = lambda p: pl.BlockSpec((tokens, 2 * HD), lambda j, n, p=p: (0, p * pairs + j))
    return run(
        functools.partial(attend_backward, tokens // 2, rows),
        "attention_grad",
        (pairs,),
        place,
        (image, qkv, qkv, qkv, grad_mixed, log_total),
        [
            pl.BlockSpec((16, 128), lambda j, n: (rows // 16, 0)),
            part(0),
            part(1),
            part(2),
            pl.BlockSpec((tokens, 2 * HD), lambda j, n: (0, j)),
            pl.BlockSpec((1, 2, tokens), lambda j, n: (j, 0, 0)),
        ],
        [
            (
                (3, tokens, width // 3),
                BF16,
                pl.BlockSpec((3, tokens, 2 * HD), lambda j, n: (0, 0, j)),
            ),
            ((pairs, 8, 2 * HD), F32, pl.BlockSpec((1, 8, 2 * HD), lambda j, n: (j, 0, 0))),
        ],
    )


def norm_one_body(place_ref, own_ref, other_ref, gain_ref, shift_ref, image_ref, low_ref):
    def write(values_ref):
        normal, _ = normalize(values_ref[...].astype(F32))
        image_ref[...] = values_ref[...]
        low_ref[...] = (normal * gain_ref[...] + shift_ref[...]).astype(BF16)

    mine = pl.program_id(0) == place_ref[0]
    pl.when(mine)(lambda: write(own_ref))
    pl.when(jnp.logical_not(mine))(lambda: write(other_ref))


def norm_one(place, own, other, gain, shift):
    padded, width = own.shape
    rows = pl.BlockSpec((padded, width), lambda i, n: (i, 0))
    shape = (2 * padded, width)
    return run(
        norm_one_body,
        "norm_one",
        (2,),
        place,
        (own, other, gain, shift),
        [whole(padded, width)] * 2 + [whole(1, width)] * 2,
        [(shape, BF16, rows)] * 2,
    )


def norm_two_body(
    place_ref, image_ref, own_ref, other_ref, bias_ref, gain_ref, shift_ref, middle_ref, low_ref
):
    branch = own_ref[...].astype(F32) + other_ref[...].astype(F32)
    middle = image_ref[...].astype(F32) + branch + bias_ref[...]
    normal, _ = normalize(middle)
    middle_ref[...] = middle
    low_ref[...] = (normal * gain_ref[...] + shift_ref[...]).astype(BF16)


def norm_two(place, image, own, other, bias, gain, shift):
    tokens, width = image.shape
    rows = pl.BlockSpec((tokens // 2, width), lambda i, n: (i, 0))
    return run(
        norm_two_body,
        "norm_two",
        (2,),
        place,
        (image, own, other, bias, gain, shift),
        [rows] * 3 + [whole(1, width)] * 3,
        [((tokens, width), F32, rows), ((tokens, width), BF16, rows)],
    )


def add_sums(sum_ref, values):
    @pl.when(pl.program_id(0) == 0)
    def _():
        sum_ref[...] = jnp.zeros_like(sum_ref)

    for k, value in enumerate(values):
        sum_ref[k : k + 1, :] += jnp.sum(value, axis=0, keepdims=True)


def norm_two_back_body(
    place_ref, incoming_ref, own_ref, other_ref, middle_ref, gain_ref, grad_ref, low_ref, sum_ref
):
    incoming = incoming_ref[...].astype(F32)
    grad = own_ref[...].astype(F32) + other_ref[...].astype(F32)
    normal, scale = normalize(middle_ref[...])
    grad_middle = incoming + normalize_grad(grad, gain_ref[...], normal, scale)
    low = grad_middle.astype(BF16)
    grad_ref[...] = grad_middle
    low_ref[...] = low
    add_sums(sum_ref, (grad * normal, grad, low.astype(F32), incoming))


def norm_two_back(place, incoming, own, other, middle, gain):
    tokens, width = incoming.shape
    rows = pl.BlockSpec((tokens // 2, width), lambda i, n: (i, 0))
    return run(
        norm_two_back_body,
        "norm_two_back",
        (2,),
        place,
        (incoming, own, other, middle, gain),
        [rows] * 4 + [whole(1, width)],
        [((tokens, width), F32, rows), ((tokens, width), BF16, rows), ((8, width), F32, whole(8, width))],
    )


def norm_one_back_body(
    place_ref, grad_ref, own_ref, other_ref, image_ref, gain_ref, kept_ref, low_ref, sum_ref
):
    grad = own_ref[...].astype(F32) + other_ref[...].astype(F32)
    normal, scale = normalize(image_ref[...].astype(F32))
    total = grad_ref[...] + normalize_grad(grad, gain_ref[...], normal, scale)
    add_sums(sum_ref, (grad * normal, grad))

    @pl.when(pl.program_id(0) == place_ref[0])
    def _():
        kept_ref[...] = total
        low_ref[...] = total.astype(BF16)


def norm_one_back(place, grad_middle, own, other, image, gain):
    tokens, width = image.shape
    padded = tokens // 2
    rows = pl.BlockSpec((padded, width), lambda i, n: (i, 0))
    return run(
        norm_one_back_body,
        "norm_one_back",
        (2,),
        place,
        (grad_middle, own, other, image, gain),
        [rows] * 4 + [whole(1, width)],
        [
            ((padded, width), F32, whole(padded, width)),
            ((padded, width), BF16, whole(padded, width)),
            ((8, width), F32, whole(8, width)),
        ],
    )


def split_body(part_rows, place_ref, keep_in, send_in, keep, send, *parts):
    keep[...] = keep_in[...]
    send[...] = send_in[...]
    if parts:
        first = pl.multiple_of(place_ref[1] * part_rows, part_rows)
        parts[0][...] = keep_in[pl.ds(first, part_rows), :]
        parts[1][...] = send_in[pl.ds(first, part_rows), :]


def split_columns(place, shard, number, part_rows, name):
    depth, wide = shard.shape
    one = wide // number // 2
    out = lambda rows: ((rows, wide // 2), BF16, pl.BlockSpec((rows, one), lambda j, n: (0, j)))
    return run(
        functools.partial(split_body, part_rows),
        name,
        (number,),
        place,
        (shard, shard),
        [
            pl.BlockSpec((depth, one), lambda j, n: (0, 2 * j + n[0])),
            pl.BlockSpec((depth, one), lambda j, n: (0, 2 * j + 1 - n[0])),
        ],
        [out(depth)] * 2 + ([out(part_rows)] * 2 if part_rows else []),
    )


def pair_body(rows, place_ref, own_ref, other_ref, out_ref):
    first = pl.multiple_of(place_ref[1] * rows, rows)
    zero = place_ref[0] == 0
    own, other = own_ref[pl.ds(first, rows), :], other_ref[pl.ds(first, rows), :]
    out_ref[:rows, :] = jnp.where(zero, own, other)
    out_ref[rows:, :] = jnp.where(zero, other, own)


def pair_part(place, own, other, rows):
    depth, wide = own.shape
    tile = wide // 2
    return run(
        functools.partial(pair_body, rows),
        "pair_part",
        (2,),
        place,
        (own, other),
        [pl.BlockSpec((depth, tile), lambda j, n: (0, j))] * 2,
        [((2 * rows, wide), BF16, pl.BlockSpec((2 * rows, tile), lambda j, n: (0, j)))],
    )[0]


def join_body(blocks, count, finish, place_ref, left_ref, bias_ref, *refs):
    pieces, joined_ref, outs = refs[:count], refs[count], refs[count + 1 :]
    for k, (number, source, rows) in enumerate(blocks):
        first = pl.multiple_of(place_ref[k] * rows, rows)
        joined_ref[pl.ds(first, rows), :] = pieces[number][source : source + rows, :]
    total = dims(left_ref[...], joined_ref[...], 1, 0) + bias_ref[...]
    for out, value in zip(outs, finish(total)):
        out[...] = value.astype(out.dtype)


def join_dot(line, left, pieces, bias, finish, results, tile, name):
    arrays = []
    for piece in pieces:
        if not any(piece[0] is array for array in arrays):
            arrays.append(piece[0])
    number = lambda array: [array is other for other in arrays].index(True)
    blocks = [(number(array), source, rows) for array, source, rows, _ in pieces]
    place = line.gate(numbers(*[piece[3] for piece in pieces]))
    tokens, depth = left.shape
    wide = arrays[0].shape[1]
    spec = lambda rows: pl.BlockSpec((rows, tile), lambda j, n: (0, j))
    return line.mark(
        run(
            functools.partial(join_body, blocks, len(arrays), finish),
            name,
            (wide // tile,),
            place,
            (left, bias) + tuple(arrays),
            [whole(tokens, depth), spec(1)] + [spec(array.shape[0]) for array in arrays],
            [((depth, wide), BF16, spec(depth))] + [((tokens, wide), BF16, spec(tokens))] * results,
        )
    )


def activate(hidden):
    normal = 0.5 * (1.0 + lax.erf(hidden * math.sqrt(0.5)))
    density = jnp.exp(-0.5 * hidden * hidden) * (1.0 / math.sqrt(2.0 * math.pi))
    return hidden * normal, normal + hidden * density


def feed_back_body(
    own_blocks, count, place_ref, incoming_ref, act_ref, slope_ref, own_ref, *refs
):
    others, (low_ref, sum_ref, part_ref), (weight_ref, total_ref) = (
        refs[:count],
        refs[count : count + 3],
        refs[count + 3 :],
    )
    step = pl.program_id(0)

    @pl.when(step < own_blocks)
    def _():
        weight_ref[...] = own_ref[...]

    for k in range(count):

        @pl.when(step == own_blocks + k)
        def _(k=k):
            weight_ref[...] = others[k][...]

    grad = dims(incoming_ref[...], weight_ref[...], 1, 1) * slope_ref[...].astype(F32)
    low = grad.astype(BF16)
    low_ref[...] = low
    sum_ref[...] = jnp.sum(low.astype(F32), axis=0, keepdims=True)
    part = dims(act_ref[...], weight_ref[...], 1, 0)
    total = jnp.where(step == 0, part, total_ref[...] + part)
    total_ref[...] = total

    @pl.when(step == own_blocks + count - 1)
    def _():
        part_ref[...] = total.astype(BF16)


def feed_back(place, incoming, act, slope, own, others):
    tokens, width = incoming.shape
    hidden = act.shape[1]
    tile = others[0].shape[0]
    own_blocks = own.shape[0] // tile
    steps = own_blocks + len(others)
    block = pl.BlockSpec((tokens, tile), lambda s, n: (0, n[s]))
    return run(
        functools.partial(feed_back_body, own_blocks, len(others)),
        "feed_back",
        (steps,),
        place,
        (incoming, act, slope, own) + tuple(others),
        [
            whole(tokens, width),
            block,
            block,
            pl.BlockSpec((tile, width), lambda s, n: (jnp.minimum(s, own_blocks - 1), 0)),
        ]
        + [whole(tile, width)] * len(others),
        [
            ((tokens, hidden), BF16, block),
            ((1, hidden), F32, pl.BlockSpec((1, tile), lambda s, n: (0, n[s]))),
            ((tokens, width), BF16, whole(tokens, width)),
        ],
        [pltpu.VMEM((tile, width), BF16), pltpu.VMEM((tokens, width), F32)],
    )


def dot_rows_body(place_ref, left_ref, weight_ref, out_ref):
    parts = left_ref.shape[0] if len(left_ref.shape) == 3 else 1
    if parts == 1:
        total = dims(left_ref[...], weight_ref[...], 1, 1)
    else:
        one = left_ref.shape[2]
        total = dims(left_ref[0], weight_ref[:, :one], 1, 1)
        for p in range(1, parts):
            total = total + dims(left_ref[p], weight_ref[:, p * one : (p + 1) * one], 1, 1)
    out_ref[...] = total.astype(BF16)


def dot_rows(place, left, weight, tile, name):
    tokens = left.shape[-2]
    rows, depth = weight.shape
    return run(
        dot_rows_body,
        name,
        (rows // tile,),
        place,
        (left, weight),
        [whole(*left.shape), pl.BlockSpec((tile, depth), lambda j, n: (j, 0))],
        [((tokens, rows), BF16, pl.BlockSpec((tokens, tile), lambda j, n: (0, j)))],
    )[0]


def pack_body(columns, owned, replicas, share, place_ref, two_ref, one_ref, qv_ref, up_ref, out_ref):
    zero = place_ref[0] == 0
    pairs = qv_ref.shape[0] // columns
    hidden = up_ref.shape[1] // columns
    out_ref[...] = jnp.zeros_like(out_ref)
    for x in range(columns):
        parts = [qv_ref[x * pairs + p, row : row + 1, :] for row in range(2) for p in range(pairs)]
        for ref, row in ((two_ref, 2), (one_ref, 0), (one_ref, 1), (two_ref, 0), (two_ref, 1), (two_ref, 3)):
            first, second = (
                ref[row : row + 1, (2 * x + c) * owned : (2 * x + c + 1) * owned] for c in range(2)
            )
            parts.append(jnp.where(zero, first, second))
        parts.append(up_ref[:, x * hidden : (x + 1) * hidden])
        row = jnp.concatenate(parts, axis=1)
        for p in range(out_ref.shape[1] // 8):
            out_ref[x, 8 * p : 8 * p + 1, :share] = row[:, p * share : (p + 1) * share]


def out_grad_body(count, replicas, place_ref, left_ref, right_ref, vec_ref, *rest):
    total = dims(left_ref[...], right_ref[...], 0, 0)
    height = total.shape[0] // replicas
    every = height + 8
    for z in range(replicas):
        for first, value in (
            (z * every, total[z * height : (z + 1) * height]),
            (z * every + height, vec_ref[0, 8 * z : 8 * z + 8, :]),
        ):
            rows = slice(first, first + value.shape[0])
            for added in rest[:count]:
                value = value + added[rows, :].astype(F32)
            rest[count][rows, :] = value.astype(BF16)


def out_grad(place, left, right, vectors, height, replicas, added=()):
    tokens, width = right.shape
    every = height + 8 * replicas
    if height % 128:
        left = lax.dynamic_slice_in_dim(left, place[0] * height, height, 1)
        place = place * numbers(0, 1, 1)
    return run(
        functools.partial(out_grad_body, len(added), replicas),
        "out_grad",
        (1,),
        place,
        (left, right, vectors) + tuple(added),
        [
            pl.BlockSpec((tokens, height), lambda i, n: (0, n[0])),
            whole(tokens, width),
            pl.BlockSpec((1, 8 * replicas, width), lambda i, n: (n[1], n[2], 0)),
        ]
        + [whole(every, width)] * len(added),
        [((every, width), BF16, whole(every, width))],
    )[0]


def weight_grad_body(count, index_ref, left_ref, right_ref, *rest):
    total = dims(left_ref[...], right_ref[...], 0, 0)
    for added in rest[:count]:
        total = total + added[...].astype(F32)
    rest[count][...] = total.astype(BF16)


def weight_grad(left, right, blocks, height, added=()):
    tokens = left.shape[0]
    number = blocks.shape[0]
    if height % 128:
        narrow = [
            lax.dynamic_slice_in_dim(left, blocks[i] * height, height, 1) for i in range(number)
        ]
        left = jnp.concatenate(narrow, axis=1)
        blocks = jnp.zeros((1,), jnp.int32)
        number, height = 1, number * height
    parts = right.shape[0] if right.ndim == 3 else 1
    width = right.shape[-1]
    if right.ndim == 3:
        right_spec = pl.BlockSpec((pl.Squeezed(), tokens, width), lambda i, j, n: (j, 0, 0))
    else:
        parts = 2
        width = width // parts
        right_spec = pl.BlockSpec((tokens, width), lambda i, j, n: (0, j))
    tile = pl.BlockSpec((height, width), lambda i, j, n: (i, j))
    return pl.pallas_call(
        functools.partial(weight_grad_body, len(added)),
        grid_spec=pltpu.PrefetchScalarGridSpec(
            num_scalar_prefetch=1,
            grid=(number, parts),
            in_specs=[pl.BlockSpec((tokens, height), lambda i, j, n: (0, n[i])), right_spec]
            + [tile] * len(added),
            out_specs=tile,
        ),
        out_shape=jax.ShapeDtypeStruct((number * height, parts * width), BF16),
        compiler_params=pltpu.CompilerParams(vmem_limit_bytes=VMEM_LIMIT),
        name="weight_grad",
    )(blocks, left, right, *added)


class Line:
    def __init__(self):
        self.last = None

    def gate(self, value):
        if self.last is None:
            return value
        return lax.optimization_barrier((value, self.last))[0]

    def mark(self, value):
        self.last = value
        return value

    def pass_on(self, value):
        return self.mark(self.gate(value))


def normalize(values):
    centered = values - jnp.mean(values, -1, keepdims=True)
    scale = lax.rsqrt(jnp.mean(centered * centered, -1, keepdims=True) + EPS)
    return centered * scale, scale


def normalize_grad(grad, gain, normal, scale):
    scaled = grad * gain
    return scale * (
        scaled
        - jnp.mean(scaled, -1, keepdims=True)
        - normal * jnp.mean(scaled * normal, -1, keepdims=True)
    )


def place(buffer, piece, position):
    start = (position,) + (0,) * (buffer.ndim - 1)
    return lax.dynamic_update_slice(buffer, piece[None], start)


def pick(array, index, axis=0):
    return lax.dynamic_index_in_dim(array, index, axis, keepdims=False)


def shards(
    tokens,
    lengths,
    qkv_weight,
    query_bias,
    value_bias,
    out_weight,
    out_bias,
    first_gain,
    first_shift,
    second_gain,
    second_shift,
    up_weight,
    up_bias,
    down_weight,
    down_bias,
    cotangent,
):
    _, rows, width = tokens.shape
    halves = lax.axis_size("seq")
    group = lax.axis_size("shard")
    replicas = lax.axis_size("rep")
    columns = group // 2
    half, member, copy_id = (lax.axis_index(name) for name in ("seq", "shard", "rep"))
    core, column = member % 2, member // 2
    owned = width // group
    owned_hidden = up_bias.shape[0]
    padded = -(-(rows + 1) // 16) * 16

    def over_core(value):
        return lax.ppermute(value, "shard", [(i, i ^ 1) for i in range(group)])

    def over_x(value, step):
        return lax.ppermute(value, "shard", [(i, (i + 2 * step) % group) for i in range(group)])

    def over_x_core(value, step):
        pairs = [(i, ((i + 2 * step) % group) ^ 1) for i in range(group)]
        return lax.ppermute(value, "shard", pairs)

    def over_y(value):
        return lax.ppermute(value, "seq", [(i, halves - 1 - i) for i in range(halves)])

    def over_z(value, step):
        return lax.ppermute(value, "rep", [(i, i ^ step) for i in range(replicas)])

    swaps = []
    for s in range(halves):
        for h in range(group):
            if s != h % 2:
                swaps.append((s * group + h, (h % 2) * group + (h // 2) * 2 + s))

    def swap(value):
        return lax.ppermute(value, ("seq", "shard"), swaps)

    def by_core(mine, other, axis=0):
        return jnp.where(
            core == 0, jnp.stack([mine, other], axis), jnp.stack([other, mine], axis)
        )

    line = Line()
    steps = range(1, columns)
    other_half = halves - 1 - half
    side = copy_id % 2
    quarter = half * 2 + side

    length = lengths[0]
    lane = lax.broadcasted_iota(jnp.int32, (padded - rows, width), 1)
    note = jnp.where(lane == 0, length // 16, jnp.where(lane == 1, length % 16, 0)).astype(BF16)
    own_tokens = line.mark(jnp.concatenate([tokens[0], note], axis=0))
    other_tokens = swap(own_tokens)

    qkv_keep, qkv_send, qkv_part, qkv_cross = line.mark(
        split_columns(
            line.gate(numbers(core, half)), qkv_weight, 3 * columns, owned // halves, "split_qkv"
        )
    )
    qkv_x = [(over_x(qkv_part, k), over_x_core(qkv_cross, k)) for k in steps]
    qkv_core = over_core(qkv_send)

    vectors = jnp.concatenate(
        [
            line.gate(query_bias),
            value_bias,
            out_bias,
            first_gain,
            first_shift,
            second_gain,
            second_shift,
            down_bias,
            up_bias,
        ]
    ).reshape(-1, 128)
    line.mark(vectors)
    vec_x = [over_x(vectors, k) for k in steps]

    own_half = lambda shard: pick(
        shard.reshape(halves, shard.shape[0] // halves, shard.shape[1]), half
    )
    up_keep, up_send = line.mark(
        split_columns(line.gate(numbers(core, half)), up_weight, columns, 0, "split_up")
    )

    gathered_vec = jnp.zeros((columns,) + vectors.shape, BF16)
    gathered_vec = place(gathered_vec, vectors, column)
    for k in steps:
        gathered_vec = place(gathered_vec, vec_x[k - 1], (column - k) % columns)
    gathered_vec = line.mark(line.gate(gathered_vec))
    vec_core = over_core(gathered_vec)
    out_part = line.mark(own_half(line.gate(out_weight)))
    out_x = [over_x(out_part, k) for k in steps]

    own_image = line.pass_on(jnp.where(half == core, own_tokens, other_tokens))
    other_image = over_core(own_image)
    up_core = over_core(line.pass_on(up_send))

    mine_vec = gathered_vec.reshape(columns, -1).astype(F32)
    all_vec = by_core(gathered_vec, vec_core, 1).reshape(columns * 2, -1)
    all_vec = all_vec.astype(F32)
    vec = lambda i: all_vec[:, i * owned : (i + 1) * owned].reshape(1, width)
    own_vec = lambda i: mine_vec[:, i * owned : (i + 1) * owned].reshape(1, width // 2)
    gain_one, shift_one, gain_two, shift_two = vec(3), vec(4), vec(5), vec(6)
    vec_out, vec_down = vec(2), vec(7)
    vec_up = mine_vec[:, 8 * owned :].reshape(1, columns * owned_hidden)
    vec_qkv = jnp.concatenate(
        [own_vec(0), jnp.zeros((1, width // 2), F32), own_vec(1)], axis=1
    )
    image, first_low = line.mark(
        norm_one(line.gate(numbers(core)), own_image, other_image, gain_one, shift_one)
    )
    eighth = owned // halves // 2
    up_part = line.mark(pair_part(line.gate(numbers(core, quarter)), up_keep, up_core, eighth))
    up_x = [over_x(up_part, k) for k in steps]

    source = lambda k: (column - k) % columns
    qkv_pieces = [
        (qkv_keep, 0, owned, member),
        (qkv_core, 0, owned, member + 1 - 2 * core),
    ]
    part = owned // halves
    for k in steps:
        for value, c in ((qkv_x[k - 1][0], core), (qkv_x[k - 1][1], 1 - core)):
            value = line.pass_on(value)
            at = (2 * source(k) + c) * halves
            qkv_pieces += [(value, 0, part, at + half), (over_y(value), 0, part, at + other_half)]
    own_cotangent = line.mark(
        jnp.concatenate([line.gate(cotangent[0]), jnp.zeros((padded - rows, width), BF16)], axis=0)
    )
    other_cotangent = swap(own_cotangent)
    out_pieces = [(out_weight, 0, owned, column)]
    for k in steps:
        value = line.pass_on(out_x[k - 1])
        at = source(k) * halves
        out_pieces += [(value, 0, part, at + half), (over_y(value), 0, part, at + other_half)]
    down_part = line.mark(own_half(line.gate(down_weight)))
    down_x = [over_x(down_part, k) for k in steps]
    up_pieces = [(up_keep, 0, owned, member), (up_core, 0, owned, member + 1 - 2 * core)]

    def up_rows(value, k, h, s):
        for c in range(2):
            at = (2 * source(k) + c) * halves * 2 + h * 2 + s
            up_pieces.append((value, c * eighth, eighth, at))

    up_y = []
    for k in steps:
        value = line.pass_on(up_x[k - 1])
        up_rows(value, k, half, side)
        up_rows(over_z(value, 1), k, half, 1 - side)
        up_y.append(over_y(value))

    wqkv, qkv = join_dot(
        line, first_low, qkv_pieces, vec_qkv, lambda total: (total,), 1, width // 2, "project"
    )
    mixed, log_total = line.mark(attention(line.gate(numbers(core)), image, qkv, rows))
    for k in steps:
        value = line.pass_on(up_y[k - 1])
        up_rows(value, k, other_half, side)
        up_rows(over_z(value, 1), k, other_half, 1 - side)
    no_bias = jnp.zeros((1, width), F32)
    wout, branch = join_dot(
        line, mixed, out_pieces, no_bias, lambda total: (total,), 1, width // 2, "project_out"
    )
    branch_other = over_core(branch)
    middle, second_low = line.mark(
        norm_two(
            line.gate(numbers(core)), image, branch, branch_other, vec_out, gain_two, shift_two
        )
    )
    down_others = []
    for k in steps:
        value = line.pass_on(down_x[k - 1])
        down_others += [(value, source(k) * halves + half), (over_y(value), source(k) * halves + other_half)]
    wup, act_low, slope = join_dot(line, second_low, up_pieces, vec_up, activate, 2, 512, "hidden")
    own_incoming = line.pass_on(jnp.where(half == core, own_cotangent, other_cotangent))
    incoming = by_core(own_incoming, over_core(own_incoming)).reshape(2 * padded, width)

    class Total:
        def __init__(self, quadrant, lead, cross):
            self.quadrant, self.lead, self.cross = quadrant, lead, cross

        def along_x(self, y):
            sent = [self.quadrant((column + k) % columns, y, ()) for k in steps]
            return tuple(over_x(v, k) for k, v in zip(steps, sent))

        def first(self):
            self.got = self.along_x(other_half)

        def second(self):
            self.got_b = self.along_x(half)

        def third(self):
            self.from_y = over_y(self.quadrant(column, other_half, self.got))

        def fourth(self):
            total = self.quadrant(column, half, self.got_b + (self.from_y,))
            height = total.shape[0] // self.lead // replicas
            self.total = total.reshape(self.lead, replicas, height, total.shape[1])
            self.got_z = [over_z(pick(self.total, copy_id ^ s, 1), s) for s in range(1, replicas)]

        def fifth(self):
            total = line.gate(pick(self.total, copy_id, 1)).astype(F32)
            for value in self.got_z:
                total = total + value.astype(F32)
            total = line.mark(total.astype(BF16))
            return self.cross(total) if self.cross else total[0]

    def collect(total):
        return lax.all_gather(total, ("seq", "rep"), axis=0, tiled=False)

    def cross_cores(blocks):
        def exchange(total):
            got = over_core(pick(total, 1 - core))
            own = pick(total, core)
            one = own.shape[1] // blocks
            left = jnp.where(core == 0, own, got)
            right = jnp.where(core == 0, got, own)
            cols = []
            for k in range(blocks):
                cols += [left[:, k * one : (k + 1) * one], right[:, k * one : (k + 1) * one]]
            return cols

        return exchange

    def by_row(left, right):
        height = owned // halves

        def quadrant(x, y, added):
            blocks = numbers(*[(x * 2 + i) * halves + y for i in range(2)])
            return line.mark(weight_grad(left, right, line.gate(blocks), height, added))

        return quadrant

    def down_quadrant(x, y, added):
        blocks = line.gate(numbers(x * halves + y))
        return line.mark(weight_grad(act_low, incoming, blocks, owned_hidden // halves, added))

    def out_quadrant(x, y, added):
        at = line.gate(numbers(x * halves + y, x, y))
        return line.mark(
            out_grad(at, mixed, branch_low, vec_grads, owned // halves, replicas, added)
        )

    pieces = halves * replicas
    total_down = Total(down_quadrant, 1, None)
    total_down.first()
    total_down.second()

    at = [column * halves + h for h in range(halves)] + [place_ for _, place_ in down_others]
    hidden_low, up_sums, partial = line.mark(
        feed_back(
            line.gate(numbers(*at)),
            incoming,
            act_low,
            slope,
            down_weight,
            [value for value, _ in down_others],
        )
    )
    total_up = Total(by_row(second_low, hidden_low), 2, cross_cores(columns))
    grad_second = line.mark(
        dot_rows(line.gate(numbers(core)), hidden_low, wup, width // 2, "grad_second")
    )
    grad_second_other = over_core(grad_second)
    total_up.first()
    total_up.second()
    grad_middle, branch_low, sums_two = line.mark(
        norm_two_back(
            line.gate(numbers(core)), incoming, grad_second, grad_second_other, middle, gain_two
        )
    )
    grad_mixed = line.mark(
        dot_rows(line.gate(numbers(core)), branch_low, wout, width // 2, "grad_mixed")
    )
    total_down.third()
    grad_qkv, qv_sums = line.mark(
        attention_grad(line.gate(numbers(core)), image, qkv, grad_mixed, log_total, rows)
    )
    grad_first = line.mark(
        dot_rows(line.gate(numbers(core)), grad_qkv, wqkv, width // 2, "grad_first")
    )
    grad_first_other = over_core(grad_first)
    total_qkv = Total(by_row(first_low, grad_qkv), 2, cross_cores(3 * columns))
    total_qkv.first()
    total_qkv.second()
    total_down.fourth()
    own_grad, own_grad_low, sums_one = line.mark(
        norm_one_back(
            line.gate(numbers(core)), grad_middle, grad_first, grad_first_other, image, gain_one
        )
    )

    entries = 8 * owned + owned_hidden
    vec_grads = line.mark(
        run(
            functools.partial(pack_body, columns, owned, replicas, entries // pieces),
            "pack_vectors",
            (1,),
            line.gate(numbers(core)),
            (sums_two, sums_one, qv_sums, up_sums),
            [
                whole(8, width),
                whole(8, width),
                whole(*qv_sums.shape),
                whole(*up_sums.shape),
            ],
            [((columns, 8 * pieces, width), F32, whole(columns, 8 * pieces, width))],
        )[0]
    )
    total_out = Total(out_quadrant, 1, None)
    total_out.first()
    total_out.second()
    total_up.third()

    halves_of = lambda value: value.reshape(2, padded, width)
    from_other = over_core(line.pass_on(pick(halves_of(partial), 1 - core)))
    grad_down = collect(total_down.fifth())
    block = pick(halves_of(middle), core) + pick(halves_of(partial), core).astype(F32)
    block = line.mark((line.gate(block) + from_other.astype(F32) + vec_down).astype(BF16))
    block_moved = swap(block)
    moved = swap(line.pass_on(own_grad_low))
    total_up.fourth()
    total_qkv.third()
    up_cols = total_up.fifth()
    grad_up = collect(jnp.concatenate(up_cols, axis=1))
    total_qkv.fourth()
    total_out.third()
    block_out = line.mark(jnp.where(half == core, line.gate(block), block_moved)[:rows][None])
    token_grad = line.mark(
        jnp.where(half == core, line.gate(own_grad), moved.astype(F32))[:rows][None]
    )
    total_out.fourth()
    qkv_cols = total_qkv.fifth()
    out_rows = total_out.fifth()
    height = out_rows.shape[0] - 8
    each = 2 * columns
    joined = [jnp.concatenate(qkv_cols[each * p : each * p + each], axis=1) for p in range(3)]
    joined = collect(jnp.concatenate(joined + [out_rows], axis=0))
    grad_down = line.mark(line.gate(grad_down).astype(F32).reshape(owned_hidden, width))
    grad_up = line.mark(line.gate(grad_up).astype(F32).reshape(owned, up_weight.shape[1]))
    joined = line.gate(joined).reshape(pieces, -1, width)
    grad_qkv_w = jnp.concatenate(
        [joined[:, p * height : (p + 1) * height] for p in range(3)], axis=2
    )
    grad_qkv_w = grad_qkv_w.astype(F32).reshape(owned, 3 * width)
    grad_out = joined[:, 3 * height : 4 * height].astype(F32).reshape(owned, width)
    vec_out_grads = joined[:, 4 * height, : entries // pieces].astype(F32).reshape(entries)
    vec_of = lambda i: vec_out_grads[i * owned : (i + 1) * owned]
    return (
        block_out,
        token_grad,
        grad_qkv_w,
        vec_of(0),
        vec_of(1),
        grad_out,
        vec_of(2),
        vec_of(3),
        vec_of(4),
        vec_of(5),
        vec_of(6),
        grad_up,
        vec_out_grads[8 * owned :],
        grad_down,
        vec_of(7),
    )


def solution(mesh):
    return jax.shard_map(
        shards,
        mesh=mesh,
        in_specs=(
            P(("shard", "rep"), "seq", None),
            P(("shard", "rep")),
            P("shard", None),
            P("shard"),
            P("shard"),
            P("shard", None),
            P("shard"),
            P("shard"),
            P("shard"),
            P("shard"),
            P("shard"),
            P("shard", None),
            P("shard"),
            P("shard", None),
            P("shard"),
            P(("shard", "rep"), "seq", None),
        ),
        out_specs=(
            P(("shard", "rep"), "seq", None),
            P(("shard", "rep"), "seq", None),
            P("shard", None),
            P("shard"),
            P("shard"),
            P("shard", None),
            P("shard"),
            P("shard"),
            P("shard"),
            P("shard"),
            P("shard"),
            P("shard", None),
            P("shard"),
            P("shard", None),
            P("shard"),
        ),
        check_vma=False,
    )
```

time: 510 us -> 486 us (0.953); the launches traced: 501 us -> 484 us
  Pallas kernels: 75.9 us -> 125 us
  other arithmetic: 58.2 us -> 25.1 us
  matrix products: 26.6 us -> 0 us
  local copies, waits for them, and re-layouts: 58.5 us -> 40.8 us
  starting transfers between devices: 61.7 us -> 73.7 us
  waiting for transfers between devices: 216 us -> 204 us
  between operations: 4.65 us -> 15.5 us
    pallas_call x3 -> x21, Pallas kernels: 27.8 us -> 84.4 us  [run(): pl.pallas_call(body, grid_spec=pltpu.PrefetchScalarGridSpec(num_scalar_pr...]
    all_gather x0 -> x3, waiting for transfers between devices: none -> 41.1 us  [collect(): return lax.all_gather(total, ('seq', 'rep'), axis=0, tiled=False)]
    dot_general x7 -> x0, matrix products: 26.6 us -> none  [the longest x1 6.55 us: shards(): grad_act = jnp.dot(incoming, wdown.T, preferred_element_type=F32)]
    ppermute x12 -> x9, waiting for transfers between devices: 77 us -> 53.2 us  [over_y(): lax.ppermute(value, 'seq', [(i, halves - 1 - i) for i in range(halves)])]
    ppermute x16 -> x14, waiting for transfers between devices: 62.4 us -> 39 us  [over_z(): return lax.ppermute(value, 'rep', [(i, i ^ step) for i in range(replicas)])]
    reduce_sum x9 -> x0, other arithmetic: 16.6 us -> none  [the longest x5 11.5 us: shards(): summed = lambda v: jnp.sum(v, 0)]
    ppermute x16 -> x14, starting transfers between devices: 24.5 us -> 40 us  [over_z(): return lax.ppermute(value, 'rep', [(i, i ^ step) for i in range(replicas)])]
    ppermute x13, waiting for transfers between devices: 74.3 us -> 62.1 us  [over_x(): lax.ppermute(value, 'shard', [(i, (i + 2 * step) % group) for i in range(...]
  transfers between devices with their start and end apart: 56 -> 55, of which waited for: 25 -> 23; matrix products, arithmetic and copies ran while one was open for 21% -> 7% of each run, Pallas kernels for 14% -> 22%
where the time goes in v2:
time: 486 us; the launch traced here: 484 us
  waiting for transfers between devices  204 us (42%)
  Pallas kernels  125 us (26%)
  starting transfers between devices  73.7 us (15%)
  local copies, waits for them, and re-layouts  40.8 us (8%)
  other arithmetic  25.1 us (5%)
  between operations  15.5 us (3%)
    pallas_call x21, Pallas kernels, run(): pl.pallas_call(body, grid_spec=pltpu.PrefetchScalarGridSpec(num_scalar_pr...  84.4 us
    ppermute x13, waiting for transfers between devices, over_x(): lax.ppermute(value, 'shard', [(i, (i + 2 * step) % group) for i in range(...  62.1 us
    ppermute x9, waiting for transfers between devices, over_y(): lax.ppermute(value, 'seq', [(i, halves - 1 - i) for i in range(halves)])  53.2 us
    all_gather x3, waiting for transfers between devices, collect(): return lax.all_gather(total, ('seq', 'rep'), axis=0, tiled=False)  41.1 us
    pallas_call x12, Pallas kernels, weight_grad(): pl.pallas_call(functools.partial(weight_grad_body, len(added)), grid_spec...  40.4 us
    ppermute x14, starting transfers between devices, over_z(): return lax.ppermute(value, 'rep', [(i, i ^ step) for i in range(replicas)])  40 us
    ppermute x14, waiting for transfers between devices, over_z(): return lax.ppermute(value, 'rep', [(i, i ^ step) for i in range(replicas)])  39 us
    unnamed x175, local copies, waits for them, and re-layouts  27.7 us
  transfers between devices with their start and end apart: 55, of which 23 were waited for; matrix products, arithmetic and copies ran while one was open for 7% of the time, Pallas kernels for 22%

profile of v2, /device:TPU:0, one launch (start us, length us, event | category | flops | bytes accessed | tf_op | source)
XLA Modules:
  0.0 484.1 jit_solution(15822558012062471541)
XLA Ops:
  8.0 2.0 pad_maximum_fusion
  13.0 3.1 split_qkv.1
  18.7 3.0 collective-permute-start.1
  21.7 1.8 split_up.1
  23.5 1.9 dynamic-slice_bitcast_fusion.10
  26.7 2.1 collective-permute-start.4
  37.4 2.7 pair_part.1
  43.0 6.4 %collective-permute-done.7.refs_4_ = bf16[128,1536]{1,0:T(8,128)(2,1)} collective-permute-done((bf16[128,1536]{1,0:T(8,128)(2,1)}, bf16[128,1536]{1,0:T(8,128)(2,1)}, u32[]{:S(2)}, u32[]{:S(2)}) %collective-permute-start.7) | collective-permute-done | bytes 393248 | tf_op jit(solution)/shard_map/ppermute | solution.py:615
  49.4 2.0 concatenate.39
  51.3 15.3 %collective-permute-done.6.refs_1_ = bf16[128,1024]{1,0:T(8,128)(2,1)S(1)} collective-permute-done((bf16[128,1024]{1,0:T(8,128)(2,1)}, bf16[128,1024]{1,0:T(8,128)(2,1)S(1)}, u32[]{:S(2)}, u32[]{:S(2)}) %collective-permute-start.6) | collective-permute-done | bytes 262176 | tf_op jit(solution)/shard_map/ppermute | solution.py:611
  66.7 2.3 dynamic-slice_bitcast_fusion
  73.1 19.2 %collective-permute-done.12.refs_5_ = bf16[128,1536]{1,0:T(8,128)(2,1)S(1)} collective-permute-done((bf16[128,1536]{1,0:T(8,128)(2,1)}, bf16[128,1536]{1,0:T(8,128)(2,1)S(1)}, u32[]{:S(2)}, u32[]{:S(2)}) %collective-permute-start.12) | collective-permute-done | bytes 393248 | tf_op jit(solution)/shard_map/ppermute | solution.py:618
  92.4 8.4 %collective-permute-done.11.refs_3_ = bf16[128,1536]{1,0:T(8,128)(2,1)S(1)} collective-permute-done((bf16[128,1536]{1,0:T(8,128)(2,1)}, bf16[128,1536]{1,0:T(8,128)(2,1)S(1)}, u32[]{:S(2)}, u32[]{:S(2)}) %collective-permute-start.11) | collective-permute-done | bytes 393248 | tf_op jit(solution)/shard_map/ppermute | solution.py:618
  100.8 5.8 %project.1 = (bf16[1024,1536]{1,0:T(8,128)(2,1)}, bf16[608,1536]{1,0:T(8,128)(2,1)}) custom-call(s32[6]{0:T(128)S(1)} %stack.237.place_ref, bf16[608,1024]{1,0:T(8,128)(2,1)S(1)} %get-tuple-element.119.left_ref, f32[1,1536]{1,0:T(1,128)S(1)} %fusion.3.bias_ref, bf16[256,1536]{1,0:T(8,128)(2,1)S(1)} %copy-done.47, ...), custom_call_target="tpu_custom_call" | custom-call | tf_op jit(solution)/shard_map/project/pallas_call | solution.py:30
  108.1 8.5 %attention.1 = (bf16[608,512]{1,0:T(8,128)(2,1)S(1)}, f32[4,2,608]{2,1,0:T(2,128)S(1)}) custom-call(s32[1]{0:T(128)} %bitcast.place_ref, bf16[608,1024]{1,0:T(8,128)(2,1)S(1)} %get-tuple-element.118.note_ref.image_ref, bf16[608,1536]{1,0:T(8,128)(2,1)S(1)} %copy-done, bf16[608,1536]{1,0:T(8,128)(2,1)S(1)} %copy-done, bf16[608,1536]{1,0:T(8,128)(2,1)S(1)} %copy-done), custom_call_target="tpu_custom_call" | custom-call | tf_op jit(solution)/shard_map/attention/pallas_call | solution.py:30
  116.7 1.9 project_out.1
  124.0 3.3 norm_two.1
  127.3 18.2 %collective-permute-done.16.refs_0_ = bf16[512,1024]{1,0:T(8,128)(2,1)} collective-permute-done((bf16[512,1024]{1,0:T(8,128)(2,1)}, bf16[512,1024]{1,0:T(8,128)(2,1)}, u32[]{:S(2)}, u32[]{:S(2)}) %collective-permute-start.16) | collective-permute-done | bytes 1048608 | tf_op jit(solution)/shard_map/ppermute | solution.py:611
  147.2 8.7 %hidden.1 = (bf16[1024,2048]{1,0:T(8,128)(2,1)}, bf16[608,2048]{1,0:T(8,128)(2,1)}, bf16[608,2048]{1,0:T(8,128)(2,1)}) custom-call(s32[10]{0:T(128)S(1)} %stack.251.place_ref, bf16[608,1024]{1,0:T(8,128)(2,1)S(1)} %get-tuple-element.139.left_ref, f32[1,2048]{1,0:T(1,128)S(1)} %bitcast.193, bf16[256,2048]{1,0:T(8,128)(2,1)S(1)} %copy-done.32, ...), custom_call_target="tpu_custom_call" | custom-call | tf_op jit(solution)/shard_map/hidden/pallas_call | solution.py:30
  158.6 1.9 copy-done.4
  160.5 2.2 weight_grad.12
  164.2 6.2 %collective-permute-done.20.refs_1_ = bf16[512,1024]{1,0:T(8,128)(2,1)S(1)} collective-permute-done((bf16[512,1024]{1,0:T(8,128)(2,1)}, bf16[512,1024]{1,0:T(8,128)(2,1)S(1)}, u32[]{:S(2)}, u32[]{:S(2)}) %collective-permute-start.20) | collective-permute-done | bytes 1048608 | tf_op jit(solution)/shard_map/ppermute | solution.py:618
  170.4 10.3 %feed_back.1 = (bf16[608,2048]{1,0:T(8,128)(2,1)}, f32[1,2048]{1,0:T(1,128)S(1)}, bf16[608,1024]{1,0:T(8,128)(2,1)S(1)}) custom-call(s32[4]{0:T(128)S(1)} %pad_add_fusion.3.place_ref, bf16[608,1024]{1,0:T(8,128)(2,1)S(1)} %bitcast.178, bf16[608,2048]{1,0:T(8,128)(2,1)} %get-tuple-element.143.left_ref.act_ref, ...), custom_call_target="tpu_custom_call" | custom-call | tf_op jit(solution)/shard_map/feed_back/pallas_call | solution.py:30
  181.8 1.7 copy-done.2
  183.5 5.7 %grad_second.1.own_ref = bf16[608,1024]{1,0:T(8,128)(2,1)} custom-call(s32[1]{0:T(128)} %bitcast.place_ref, bf16[608,2048]{1,0:T(8,128)(2,1)S(1)} %copy-done.2, bf16[1024,2048]{1,0:T(8,128)(2,1)} %get-tuple-element.142.weight_ref), custom_call_target="tpu_custom_call" | custom-call | tf_op jit(solution)/shard_map/grad_second/pallas_call | solution.py:30
  192.5 3.5 weight_grad.14
  196.1 2.7 weight_grad.15
  198.8 5.5 %norm_two_back.1 = (f32[608,1024]{1,0:T(8,128)}, bf16[608,1024]{1,0:T(8,128)(2,1)S(1)}, f32[8,1024]{1,0:T(8,128)S(1)}) custom-call(s32[1]{0:T(128)} %bitcast.place_ref, bf16[608,1024]{1,0:T(8,128)(2,1)S(1)} %bitcast.179, bf16[608,1024]{1,0:T(8,128)(2,1)} %grad_second.1.own_ref, bf16[608,1024]{1,0:T(8,128)(2,1)} %collective-permute-done.21.other_ref, ...), custom_call_target="tpu_custom_call" | custom-call | tf_op jit(solution)/shard_map/norm_two_back/pallas_call | solution.py:30
  205.4 10.1 %collective-permute-done.22.rest_0_ = bf16[512,1024]{1,0:T(8,128)(2,1)} collective-permute-done((bf16[512,1024]{1,0:T(8,128)(2,1)}, bf16[512,1024]{1,0:T(8,128)(2,1)}, u32[]{:S(2)}, u32[]{:S(2)}) %collective-permute-start.22) | collective-permute-done | bytes 1048608 | tf_op jit(solution)/shard_map/ppermute | solution.py:611
  215.5 3.3 weight_grad.16
  219.2 11.9 %attention_grad.1 = (bf16[3,608,512]{2,1,0:T(8,128)(2,1)S(1)}, f32[4,8,128]{2,1,0:T(8,128)S(1)}) custom-call(s32[1]{0:T(128)} %bitcast.place_ref, bf16[608,1024]{1,0:T(8,128)(2,1)S(1)} %copy-done.23, bf16[608,1536]{1,0:T(8,128)(2,1)S(1)} %copy-done.1, bf16[608,1536]{1,0:T(8,128)(2,1)S(1)} %copy-done.1, bf16[608,1536]{1,0:T(8,128)(2,1)S(1)} %copy-done.1, ...), custom_call_target="tpu_custom_call" | custom-call | tf_op jit(solution)/shard_map/attention_grad/pallas_call | solution.py:30
  231.1 5.3 %grad_first.1.own_ref = bf16[608,1024]{1,0:T(8,128)(2,1)} custom-call(s32[1]{0:T(128)} %bitcast.place_ref, bf16[3,608,512]{2,1,0:T(8,128)(2,1)S(1)} %get-tuple-element.162.left_ref.right_ref, bf16[1024,1536]{1,0:T(8,128)(2,1)} %get-tuple-element.128.weight_ref), custom_call_target="tpu_custom_call" | custom-call | tf_op jit(solution)/shard_map/grad_first/pallas_call | solution.py:30
  240.6 2.6 weight_grad.17
  244.2 3.9 weight_grad.18
  248.1 2.8 weight_grad.19
  253.5 2.6 collective-permute-start.28
  256.5 2.0 dynamic-slice_bitcast_fusion.1
  259.1 4.2 norm_one_back.1
  266.8 4.1 weight_grad.20
  272.6 2.6 collective-permute-done.28
  275.2 2.0 add_convert_fusion.2
  279.7 2.2 add_convert_fusion
  281.9 3.4 collective-permute-done.31.rest_0_
  285.2 12.8 %collective-permute-done.32.rest_1_ = bf16[256,2048]{1,0:T(8,128)(2,1)S(1)} collective-permute-done((bf16[256,2048]{1,0:T(8,128)(2,1)S(1)}, bf16[256,2048]{1,0:T(8,128)(2,1)S(1)}, u32[]{:S(2)}, u32[]{:S(2)}) %collective-permute-start.32) | collective-permute-done | bytes 1048608 | tf_op jit(solution)/shard_map/ppermute | solution.py:618
  300.3 4.8 weight_grad.21
  305.8 3.5 collective-permute-start.35
  309.6 3.9 weight_grad.22
  313.5 9.5 %collective-permute-done.34 = bf16[2,32,2048]{2,1,0:T(8,128)(2,1)S(1)} collective-permute-done((bf16[2,32,2048]{2,1,0:T(8,128)(2,1)S(1)}, bf16[2,32,2048]{2,1,0:T(8,128)(2,1)S(1)}, u32[]{:S(2)}, u32[]{:S(2)}) %collective-permute-start.34) | collective-permute-done | bytes 262176 | tf_op jit(solution)/shard_map/ppermute | solution.py:621
  323.0 15.7 %collective-permute-done.35 = bf16[2,32,2048]{2,1,0:T(8,128)(2,1)S(1)} collective-permute-done((bf16[2,32,2048]{2,1,0:T(8,128)(2,1)S(1)}, bf16[2,32,2048]{2,1,0:T(8,128)(2,1)S(1)}, u32[]{:S(2)}, u32[]{:S(2)}) %collective-permute-start.35) | collective-permute-done | bytes 262176 | tf_op jit(solution)/shard_map/ppermute | solution.py:621
  342.5 1.7 collective-permute-start.39
  345.1 14.6 %collective-permute-done.37.rest_0_ = bf16[256,1536]{1,0:T(8,128)(2,1)} collective-permute-done((bf16[256,1536]{1,0:T(8,128)(2,1)}, bf16[256,1536]{1,0:T(8,128)(2,1)}, u32[]{:S(2)}, u32[]{:S(2)}) %collective-permute-start.37) | collective-permute-done | bytes 786464 | tf_op jit(solution)/shard_map/ppermute | solution.py:611
  361.1 5.2 %weight_grad.23 = bf16[256,1536]{1,0:T(8,128)(2,1)S(1)} custom-call(s32[2]{0:T(128)S(1)} %get-tuple-element.183.index_ref, bf16[608,1024]{1,0:T(8,128)(2,1)S(1)} %copy-done.18, bf16[3,608,512]{2,1,0:T(8,128)(2,1)S(1)} %copy-done.11, bf16[256,1536]{1,0:T(8,128)(2,1)} %collective-permute-done.37.rest_0_, bf16[256,1536]{1,0:T(8,128)(2,1)} %collective-permute-done.38.rest_1_), custom_call_target="tpu_custom_call" | custom-call | tf_op jit(solution)/shard_map/weight_grad/pallas_call | solution.py:522
  367.7 1.7 collective-permute-start.43
  370.4 11.3 %collective-permute-start.44 = (bf16[2,32,1536]{2,1,0:T(8,128)(2,1)S(1)}, bf16[2,32,1536]{2,1,0:T(8,128)(2,1)S(1)}, u32[]{:S(2)}, u32[]{:S(2)}) collective-permute-start(bf16[2,32,1536]{2,1,0:T(8,128)(2,1)S(1)} %get-tuple-element.238), channel_id=1, source_target_pairs={{0,1},{1,0},{2,3},{3,2},{4,5},{5,4},{6,7},{7,6},{8,9},{9,8},{10,11... | collective-permute-start | bytes 589832 | tf_op jit(solution)/shard_map/ppermute | solution.py:621
  384.3 6.5 %collective-permute-done.43.rest_1_ = bf16[160,1024]{1,0:T(8,128)(2,1)S(1)} collective-permute-done((bf16[160,1024]{1,0:T(8,128)(2,1)S(1)}, bf16[160,1024]{1,0:T(8,128)(2,1)S(1)}, u32[]{:S(2)}, u32[]{:S(2)}) %collective-permute-start.43) | collective-permute-done | bytes 327712 | tf_op jit(solution)/shard_map/ppermute | solution.py:618
  391.8 13.0 %collective-permute-start.48 = (bf16[1,40,1024]{2,1,0:T(8,128)(2,1)S(1)}, bf16[1,40,1024]{2,1,0:T(8,128)(2,1)S(1)}, u32[]{:S(2)}, u32[]{:S(2)}) collective-permute-start(bf16[1,40,1024]{2,1,0:T(8,128)(2,1)S(1)} %get-tuple-element.244), channel_id=1, source_target_pairs={{0,1},{1,0},{2,3},{3,2},{4,5},{5,4},{6,7},{7,6},{8,9},{9,8},{10,11... | collective-permute-start | bytes 245768 | tf_op jit(solution)/shard_map/ppermute | solution.py:621
  407.3 3.6 collective-permute-done.46
  412.1 6.3 %collective-permute-done.49 = bf16[1,40,1024]{2,1,0:T(8,128)(2,1)S(1)} collective-permute-done((bf16[1,40,1024]{2,1,0:T(8,128)(2,1)S(1)}, bf16[1,40,1024]{2,1,0:T(8,128)(2,1)S(1)}, u32[]{:S(2)}, u32[]{:S(2)}) %collective-permute-start.49) | collective-permute-done | bytes 81952 | tf_op jit(solution)/shard_map/ppermute | solution.py:621
  419.2 2.2 copy.32
  421.5 4.1 bitcast_convert_fusion.1
  425.6 4.1 bitcast_convert_fusion
  429.7 41.1 %all-gather.8.cloned.1.call-done = bf16[1088,1024]{1,0:T(8,128)(2,1)} async-done(((bf16[136,1024]{1,0:T(8,128)(2,1)}), bf16[1088,1024]{1,0:T(8,128)(2,1)}) %all-gather.8.cloned.1.call-update) | async-done | bytes 2228240 | tf_op jit(solution)/shard_map/all_gather | solution.py:804
  470.7 1.7 fusion.5
  475.6 2.0 maximum_convert_fusion
  (320 shorter events, 80.1 us)
Async XLA Ops:
  7.2 414.3 %all-gather.6.cloned.1.call-start = ((), (), s32[]{:S(2)}) async-start(), calls=%async_computation | async-start | bytes 2359296 | tf_op jit(solution)/shard_map/all_gather | solution.py:804
  9.9 15.5 %collective-permute-start = (bf16[304,1024]{1,0:T(8,128)(2,1)}, bf16[304,1024]{1,0:T(8,128)(2,1)}, u32[]{:S(2)}, u32[]{:S(2)}) collective-permute-start(bf16[304,1024]{1,0:T(8,128)(2,1)} %pad_maximum_fusion), channel_id=1, source_target_pairs={{4,16},{12,24},{16,4},{24,12},{5,17},{13,25},{17,5},{25,13},{6,18}... | collective-permute-start | bytes 1867784 | tf_op jit(solution)/shard_map/ppermute | solution.py:630
  18.7 4.9 %collective-permute-start.1 = (bf16[24,128]{1,0:T(8,128)(2,1)S(1)}, bf16[24,128]{1,0:T(8,128)(2,1)S(1)}, u32[]{:S(2)}, u32[]{:S(2)}) collective-permute-start(bf16[24,128]{1,0:T(8,128)(2,1)S(1)} %bitcast.223), channel_id=1, source_target_pairs={{0,8},{4,12},{8,0},{12,4},{1,9},{5,13},{9,1},{13,5},{2,10},{6,14},... | collective-permute-start | bytes 18440 | tf_op jit(solution)/shard_map/ppermute | solution.py:611
  26.7 10.7 %collective-permute-start.4 = (bf16[256,2048]{1,0:T(8,128)(2,1)}, bf16[256,2048]{1,0:T(8,128)(2,1)}, u32[]{:S(2)}, u32[]{:S(2)}) collective-permute-start(bf16[256,2048]{1,0:T(8,128)(2,1)} %get-tuple-element.116), channel_id=1, source_target_pairs={{0,4},{4,0},{8,12},{12,8},{1,5},{5,1},{9,13},{13,9},{2,6},{6,2},{1... | collective-permute-start | bytes 3145736 | tf_op jit(solution)/shard_map/ppermute | solution.py:608
  28.8 4.6 collective-permute-start.2
  29.7 13.2 %collective-permute-start.8 = (bf16[128,1536]{1,0:T(8,128)(2,1)}, bf16[128,1536]{1,0:T(8,128)(2,1)}, u32[]{:S(2)}, u32[]{:S(2)}) collective-permute-start(bf16[128,1536]{1,0:T(8,128)(2,1)} %get-tuple-element.107), channel_id=1, source_target_pairs={{0,8},{4,12},{8,0},{12,4},{1,9},{5,13},{9,1},{13,5},{2,10},{6,14},... | collective-permute-start | bytes 1179656 | tf_op jit(solution)/shard_map/ppermute | solution.py:611
  30.4 18.9 %collective-permute-start.7 = (bf16[128,1536]{1,0:T(8,128)(2,1)}, bf16[128,1536]{1,0:T(8,128)(2,1)}, u32[]{:S(2)}, u32[]{:S(2)}) collective-permute-start(bf16[128,1536]{1,0:T(8,128)(2,1)} %get-tuple-element.108), channel_id=1, source_target_pairs={{0,12},{4,8},{8,4},{12,0},{1,13},{5,9},{9,5},{13,1},{2,14},{6,10},... | collective-permute-start | bytes 1179656 | tf_op jit(solution)/shard_map/ppermute | solution.py:615
  31.5 1.2 collective-permute-start.3
  37.4 63.4 %copy-start.16 = (bf16[608,1024]{1,0:T(8,128)(2,1)}, bf16[608,1024]{1,0:T(8,128)(2,1)S(1)}, u32[]{:S(2)}) copy-start(bf16[608,1024]{1,0:T(8,128)(2,1)S(1)} %get-tuple-element.119.left_ref) | copy-start | bytes 3735556
  37.4 86.6 %copy-start.22 = (bf16[608,1024]{1,0:T(8,128)(2,1)}, bf16[608,1024]{1,0:T(8,128)(2,1)S(1)}, u32[]{:S(2)}) copy-start(bf16[608,1024]{1,0:T(8,128)(2,1)S(1)} %get-tuple-element.118.note_ref.image_ref) | copy-start | bytes 3735556
  40.2 28.8 %collective-permute-start.5 = (bf16[128,2048]{1,0:T(8,128)(2,1)}, bf16[128,2048]{1,0:T(8,128)(2,1)}, u32[]{:S(2)}, u32[]{:S(2)}) collective-permute-start(bf16[128,2048]{1,0:T(8,128)(2,1)} %pair_part.1), channel_id=1, source_target_pairs={{0,8},{4,12},{8,0},{12,4},{1,9},{5,13},{9,1},{13,5},{2,10},{6,14},... | collective-permute-start | bytes 1572872 | tf_op jit(solution)/shard_map/ppermute | solution.py:611
  40.9 25.8 %collective-permute-start.6 = (bf16[128,1024]{1,0:T(8,128)(2,1)}, bf16[128,1024]{1,0:T(8,128)(2,1)S(1)}, u32[]{:S(2)}, u32[]{:S(2)}) collective-permute-start(bf16[128,1024]{1,0:T(8,128)(2,1)} %dynamic-slice_bitcast_fusion.10), channel_id=1, source_target_pairs={{0,8},{4,12},{8,0},{12,4},{1,9},{5,13},{9,1},{13,5},{2,10},{6,14},... | collective-permute-start | bytes 786440 | tf_op jit(solution)/shard_map/ppermute | solution.py:611
  42.2 30.9 %collective-permute-start.10 = (bf16[256,1536]{1,0:T(8,128)(2,1)}, bf16[256,1536]{1,0:T(8,128)(2,1)S(1)}, u32[]{:S(2)}, u32[]{:S(2)}) collective-permute-start(bf16[256,1536]{1,0:T(8,128)(2,1)} %get-tuple-element.106), channel_id=1, source_target_pairs={{0,4},{4,0},{8,12},{12,8},{1,5},{5,1},{9,13},{13,9},{2,6},{6,2},{1... | collective-permute-start | bytes 2359304 | tf_op jit(solution)/shard_map/ppermute | solution.py:608
  51.3 21.8 %copy-start.62 = (f32[1536]{0:T(1024)S(1)}, f32[1536]{0:T(1024)}, u32[]{:S(2)}) copy-start(f32[1536]{0:T(1024)} %pad.50.clone) | copy-start | bytes 18436
  51.3 49.5 %copy-start.47 = (bf16[256,1536]{1,0:T(8,128)(2,1)S(1)}, bf16[256,1536]{1,0:T(8,128)(2,1)}, u32[]{:S(2)}) copy-start(bf16[256,1536]{1,0:T(8,128)(2,1)} %copy-done.46) | copy-start | bytes 2359300
  68.9 47.7 %collective-permute-start.9 = (bf16[128,2048]{1,0:T(8,128)(2,1)}, bf16[128,2048]{1,0:T(8,128)(2,1)}, u32[]{:S(2)}, u32[]{:S(2)}) collective-permute-start(bf16[128,2048]{1,0:T(8,128)(2,1)} %collective-permute-done.5.refs_2_), channel_id=1, source_target_pairs={{0,16},{16,0},{1,17},{17,1},{2,18},{18,2},{3,19},{19,3},{4,20},{20... | collective-permute-start | bytes 1572872 | tf_op jit(solution)/shard_map/ppermute | solution.py:618
  69.4 37.2 %copy-start.61 = (f32[1,2,24,128]{3,1,2,0:T(2,128)}, f32[1,2,24,128]{3,1,2,0:T(2,128)S(1)}, u32[]{:S(2)}) copy-start(f32[1,2,24,128]{3,1,2,0:T(2,128)S(1)} %copy.47) | copy-start | bytes 73732
  69.4 23.0 %collective-permute-start.12 = (bf16[128,1536]{1,0:T(8,128)(2,1)}, bf16[128,1536]{1,0:T(8,128)(2,1)S(1)}, u32[]{:S(2)}, u32[]{:S(2)}) collective-permute-start(bf16[128,1536]{1,0:T(8,128)(2,1)} %collective-permute-done.7.refs_4_), channel_id=1, source_target_pairs={{0,16},{16,0},{1,17},{17,1},{2,18},{18,2},{3,19},{19,3},{4,20},{20... | collective-permute-start | bytes 1179656 | tf_op jit(solution)/shard_map/ppermute | solution.py:618
  71.1 29.7 %collective-permute-start.11 = (bf16[128,1536]{1,0:T(8,128)(2,1)}, bf16[128,1536]{1,0:T(8,128)(2,1)S(1)}, u32[]{:S(2)}, u32[]{:S(2)}) collective-permute-start(bf16[128,1536]{1,0:T(8,128)(2,1)} %collective-permute-done.8.refs_2_), channel_id=1, source_target_pairs={{0,16},{16,0},{1,17},{17,1},{2,18},{18,2},{3,19},{19,3},{4,20},{20... | collective-permute-start | bytes 1179656 | tf_op jit(solution)/shard_map/ppermute | solution.py:618
  71.5 45.2 %collective-permute-start.13 = (bf16[128,1024]{1,0:T(8,128)(2,1)S(1)}, bf16[128,1024]{1,0:T(8,128)(2,1)S(1)}, u32[]{:S(2)}, u32[]{:S(2)}) collective-permute-start(bf16[128,1024]{1,0:T(8,128)(2,1)S(1)} %collective-permute-done.6.refs_1_), channel_id=1, source_target_pairs={{0,16},{16,0},{1,17},{17,1},{2,18},{18,2},{3,19},{19,3},{4,20},{20... | collective-permute-start | bytes 786440 | tf_op jit(solution)/shard_map/ppermute | solution.py:618
  116.6 148.6 %copy-start.25 = (bf16[608,512]{1,0:T(8,128)(2,1)}, bf16[608,512]{1,0:T(8,128)(2,1)S(1)}, u32[]{:S(2)}) copy-start(bf16[608,512]{1,0:T(8,128)(2,1)S(1)} %get-tuple-element.131.left_ref) | copy-start | bytes 1867780
  119.6 4.4 collective-permute-start.14
  119.6 25.9 %collective-permute-start.16 = (bf16[512,1024]{1,0:T(8,128)(2,1)}, bf16[512,1024]{1,0:T(8,128)(2,1)}, u32[]{:S(2)}, u32[]{:S(2)}) collective-permute-start(bf16[512,1024]{1,0:T(8,128)(2,1)} %dynamic-slice_bitcast_fusion), channel_id=1, source_target_pairs={{0,8},{4,12},{8,0},{12,4},{1,9},{5,13},{9,1},{13,5},{2,10},{6,14},... | collective-permute-start | bytes 3145736 | tf_op jit(solution)/shard_map/ppermute | solution.py:611
  120.3 26.3 %collective-permute-start.15 = (bf16[304,1024]{1,0:T(8,128)(2,1)}, bf16[304,1024]{1,0:T(8,128)(2,1)}, u32[]{:S(2)}, u32[]{:S(2)}) collective-permute-start(bf16[304,1024]{1,0:T(8,128)(2,1)} %concatenate.39), channel_id=1, source_target_pairs={{4,16},{12,24},{16,4},{24,12},{5,17},{13,25},{17,5},{25,13},{6,18}... | collective-permute-start | bytes 1867784 | tf_op jit(solution)/shard_map/ppermute | solution.py:630
  121.8 25.1 %collective-permute-start.17 = (bf16[128,2048]{1,0:T(8,128)(2,1)}, bf16[128,2048]{1,0:T(8,128)(2,1)}, u32[]{:S(2)}, u32[]{:S(2)}) collective-permute-start(bf16[128,2048]{1,0:T(8,128)(2,1)} %collective-permute-done.5.refs_2_), channel_id=1, source_target_pairs={{0,1},{1,0},{2,3},{3,2},{4,5},{5,4},{6,7},{7,6},{8,9},{9,8},{10,11... | collective-permute-start | bytes 1572872 | tf_op jit(solution)/shard_map/ppermute | solution.py:621
  123.4 23.8 %collective-permute-start.18 = (bf16[128,2048]{1,0:T(8,128)(2,1)}, bf16[128,2048]{1,0:T(8,128)(2,1)}, u32[]{:S(2)}, u32[]{:S(2)}) collective-permute-start(bf16[128,2048]{1,0:T(8,128)(2,1)} %collective-permute-done.9.refs_4_), channel_id=1, source_target_pairs={{0,1},{1,0},{2,3},{3,2},{4,5},{5,4},{6,7},{7,6},{8,9},{9,8},{10,11... | collective-permute-start | bytes 1572872 | tf_op jit(solution)/shard_map/ppermute | solution.py:621
  124.0 22.6 %copy-start.57 = (bf16[1,290,1024]{2,1,0:T(8,128)(2,1)S(1)}, bf16[1,290,1024]{2,1,0:T(8,128)(2,1)}, u32[]{:S(2)}) copy-start(bf16[1,290,1024]{2,1,0:T(8,128)(2,1)} %param.31) | copy-start | bytes 1781764
  127.3 28.7 %copy-start.12 = (bf16[608,1024]{1,0:T(8,128)(2,1)}, bf16[608,1024]{1,0:T(8,128)(2,1)S(1)}, u32[]{:S(2)}) copy-start(bf16[608,1024]{1,0:T(8,128)(2,1)S(1)} %get-tuple-element.139.left_ref) | copy-start | bytes 3735556
  145.5 24.9 %collective-permute-start.20 = (bf16[512,1024]{1,0:T(8,128)(2,1)}, bf16[512,1024]{1,0:T(8,128)(2,1)S(1)}, u32[]{:S(2)}, u32[]{:S(2)}) collective-permute-start(bf16[512,1024]{1,0:T(8,128)(2,1)} %collective-permute-done.16.refs_0_), channel_id=1, source_target_pairs={{0,16},{16,0},{1,17},{17,1},{2,18},{18,2},{3,19},{19,3},{4,20},{20... | collective-permute-start | bytes 3145736 | tf_op jit(solution)/shard_map/ppermute | solution.py:618
  155.9 2.4 collective-permute-start.19
  189.1 9.7 %collective-permute-start.21 = (bf16[608,1024]{1,0:T(8,128)(2,1)}, bf16[608,1024]{1,0:T(8,128)(2,1)}, u32[]{:S(2)}, u32[]{:S(2)}) collective-permute-start(bf16[608,1024]{1,0:T(8,128)(2,1)} %grad_second.1.own_ref), channel_id=1, source_target_pairs={{0,4},{4,0},{8,12},{12,8},{1,5},{5,1},{9,13},{13,9},{2,6},{6,2},{1... | collective-permute-start | bytes 3735560 | tf_op jit(solution)/shard_map/ppermute | solution.py:608
  189.1 26.3 %collective-permute-start.22 = (bf16[512,1024]{1,0:T(8,128)(2,1)}, bf16[512,1024]{1,0:T(8,128)(2,1)}, u32[]{:S(2)}, u32[]{:S(2)}) collective-permute-start(bf16[512,1024]{1,0:T(8,128)(2,1)} %weight_grad.12), channel_id=1, source_target_pairs={{0,8},{4,12},{8,0},{12,4},{1,9},{5,13},{9,1},{13,5},{2,10},{6,14},... | collective-permute-start | bytes 3145736 | tf_op jit(solution)/shard_map/ppermute | solution.py:611
  190.0 58.1 %collective-permute-start.23 = (bf16[512,1024]{1,0:T(8,128)(2,1)}, bf16[512,1024]{1,0:T(8,128)(2,1)}, u32[]{:S(2)}, u32[]{:S(2)}) collective-permute-start(bf16[512,1024]{1,0:T(8,128)(2,1)} %copy-done.43), channel_id=1, source_target_pairs={{0,8},{4,12},{8,0},{12,4},{1,9},{5,13},{9,1},{13,5},{2,10},{6,14},... | collective-permute-start | bytes 3145736 | tf_op jit(solution)/shard_map/ppermute | solution.py:611
  218.7 29.3 %collective-permute-start.24 = (bf16[512,1024]{1,0:T(8,128)(2,1)}, bf16[512,1024]{1,0:T(8,128)(2,1)}, u32[]{:S(2)}, u32[]{:S(2)}) collective-permute-start(bf16[512,1024]{1,0:T(8,128)(2,1)} %weight_grad.16), channel_id=1, source_target_pairs={{0,16},{16,0},{1,17},{17,1},{2,18},{18,2},{3,19},{19,3},{4,20},{20... | collective-permute-start | bytes 3145736 | tf_op jit(solution)/shard_map/ppermute | solution.py:618
  236.4 22.1 %collective-permute-start.25 = (bf16[608,1024]{1,0:T(8,128)(2,1)}, bf16[608,1024]{1,0:T(8,128)(2,1)}, u32[]{:S(2)}, u32[]{:S(2)}) collective-permute-start(bf16[608,1024]{1,0:T(8,128)(2,1)} %grad_first.1.own_ref), channel_id=1, source_target_pairs={{0,4},{4,0},{8,12},{12,8},{1,5},{5,1},{9,13},{13,9},{2,6},{6,2},{1... | collective-permute-start | bytes 3735560 | tf_op jit(solution)/shard_map/ppermute | solution.py:608
  236.4 29.9 %collective-permute-start.26 = (bf16[256,2048]{1,0:T(8,128)(2,1)}, bf16[256,2048]{1,0:T(8,128)(2,1)}, u32[]{:S(2)}, u32[]{:S(2)}) collective-permute-start(bf16[256,2048]{1,0:T(8,128)(2,1)} %weight_grad.14), channel_id=1, source_target_pairs={{0,8},{4,12},{8,0},{12,4},{1,9},{5,13},{9,1},{13,5},{2,10},{6,14},... | collective-permute-start | bytes 3145736 | tf_op jit(solution)/shard_map/ppermute | solution.py:611
  252.0 20.6 %collective-permute-start.27 = (bf16[1,128,1024]{2,1,0:T(8,128)(2,1)}, bf16[1,128,1024]{2,1,0:T(8,128)(2,1)}, u32[]{:S(2)}, u32[]{:S(2)}) collective-permute-start(bf16[1,128,1024]{2,1,0:T(8,128)(2,1)} %get-tuple-element.234), channel_id=1, source_target_pairs={{0,1},{1,0},{2,3},{3,2},{4,5},{5,4},{6,7},{7,6},{8,9},{9,8},{10,11... | collective-permute-start | bytes 786440 | tf_op jit(solution)/shard_map/ppermute | solution.py:621
  253.5 21.6 %collective-permute-start.28 = (bf16[1,128,1024]{2,1,0:T(8,128)(2,1)}, bf16[1,128,1024]{2,1,0:T(8,128)(2,1)}, u32[]{:S(2)}, u32[]{:S(2)}) collective-permute-start(bf16[1,128,1024]{2,1,0:T(8,128)(2,1)} %get-tuple-element.233), channel_id=1, source_target_pairs={{0,2},{1,3},{2,0},{3,1},{4,6},{5,7},{6,4},{7,5},{8,10},{9,11},{10,... | collective-permute-start | bytes 786440 | tf_op jit(solution)/shard_map/ppermute | solution.py:621
  256.1 19.0 %collective-permute-start.29 = (bf16[1,128,1024]{2,1,0:T(8,128)(2,1)}, bf16[1,128,1024]{2,1,0:T(8,128)(2,1)}, u32[]{:S(2)}, u32[]{:S(2)}) collective-permute-start(bf16[1,128,1024]{2,1,0:T(8,128)(2,1)} %get-tuple-element.232), channel_id=1, source_target_pairs={{0,3},{1,2},{2,1},{3,0},{4,7},{5,6},{6,5},{7,4},{8,11},{9,10},{10,... | collective-permute-start | bytes 786440 | tf_op jit(solution)/shard_map/ppermute | solution.py:621
  258.5 26.7 %collective-permute-start.31 = (bf16[256,2048]{1,0:T(8,128)(2,1)}, bf16[256,2048]{1,0:T(8,128)(2,1)}, u32[]{:S(2)}, u32[]{:S(2)}) collective-permute-start(bf16[256,2048]{1,0:T(8,128)(2,1)} %copy-done.40), channel_id=1, source_target_pairs={{0,8},{4,12},{8,0},{12,4},{1,9},{5,13},{9,1},{13,5},{2,10},{6,14},... | collective-permute-start | bytes 3145736 | tf_op jit(solution)/shard_map/ppermute | solution.py:611
  270.9 27.1 %collective-permute-start.32 = (bf16[256,2048]{1,0:T(8,128)(2,1)S(1)}, bf16[256,2048]{1,0:T(8,128)(2,1)S(1)}, u32[]{:S(2)}, u32[]{:S(2)}) collective-permute-start(bf16[256,2048]{1,0:T(8,128)(2,1)S(1)} %weight_grad.20), channel_id=1, source_target_pairs={{0,16},{16,0},{1,17},{17,1},{2,18},{18,2},{3,19},{19,3},{4,20},{20... | collective-permute-start | bytes 3145736 | tf_op jit(solution)/shard_map/ppermute | solution.py:618
  277.2 148.4 %all-gather.10.cloned.1.call-start = ((), (), s32[]{:S(2)}) async-start(), calls=%async_computation.2 | async-start | bytes 2359296 | tf_op jit(solution)/shard_map/all_gather | solution.py:804
  277.2 2.5 collective-permute-start.30
  278.9 30.7 %collective-permute-start.33 = (bf16[256,1536]{1,0:T(8,128)(2,1)S(1)}, bf16[256,1536]{1,0:T(8,128)(2,1)S(1)}, u32[]{:S(2)}, u32[]{:S(2)}) collective-permute-start(bf16[256,1536]{1,0:T(8,128)(2,1)S(1)} %copy-done.49), channel_id=1, source_target_pairs={{0,8},{4,12},{8,0},{12,4},{1,9},{5,13},{9,1},{13,5},{2,10},{6,14},... | collective-permute-start | bytes 2359304 | tf_op jit(solution)/shard_map/ppermute | solution.py:611
  305.1 17.9 %collective-permute-start.34 = (bf16[2,32,2048]{2,1,0:T(8,128)(2,1)S(1)}, bf16[2,32,2048]{2,1,0:T(8,128)(2,1)S(1)}, u32[]{:S(2)}, u32[]{:S(2)}) collective-permute-start(bf16[2,32,2048]{2,1,0:T(8,128)(2,1)S(1)} %get-tuple-element.230), channel_id=1, source_target_pairs={{0,1},{1,0},{2,3},{3,2},{4,5},{5,4},{6,7},{7,6},{8,9},{9,8},{10,11... | collective-permute-start | bytes 786440 | tf_op jit(solution)/shard_map/ppermute | solution.py:621
  305.8 32.9 %collective-permute-start.35 = (bf16[2,32,2048]{2,1,0:T(8,128)(2,1)S(1)}, bf16[2,32,2048]{2,1,0:T(8,128)(2,1)S(1)}, u32[]{:S(2)}, u32[]{:S(2)}) collective-permute-start(bf16[2,32,2048]{2,1,0:T(8,128)(2,1)S(1)} %get-tuple-element.229), channel_id=1, source_target_pairs={{0,2},{1,3},{2,0},{3,1},{4,6},{5,7},{6,4},{7,5},{8,10},{9,11},{10,... | collective-permute-start | bytes 786440 | tf_op jit(solution)/shard_map/ppermute | solution.py:621
  309.3 29.4 %collective-permute-start.36 = (bf16[2,32,2048]{2,1,0:T(8,128)(2,1)S(1)}, bf16[2,32,2048]{2,1,0:T(8,128)(2,1)S(1)}, u32[]{:S(2)}, u32[]{:S(2)}) collective-permute-start(bf16[2,32,2048]{2,1,0:T(8,128)(2,1)S(1)} %get-tuple-element.228), channel_id=1, source_target_pairs={{0,3},{1,2},{2,1},{3,0},{4,7},{5,6},{6,5},{7,4},{8,11},{9,10},{10,... | collective-permute-start | bytes 786440 | tf_op jit(solution)/shard_map/ppermute | solution.py:621
  338.9 2.1 collective-permute-start.51
  339.0 20.8 %collective-permute-start.37 = (bf16[256,1536]{1,0:T(8,128)(2,1)}, bf16[256,1536]{1,0:T(8,128)(2,1)}, u32[]{:S(2)}, u32[]{:S(2)}) collective-permute-start(bf16[256,1536]{1,0:T(8,128)(2,1)} %weight_grad.18), channel_id=1, source_target_pairs={{0,8},{4,12},{8,0},{12,4},{1,9},{5,13},{9,1},{13,5},{2,10},{6,14},... | collective-permute-start | bytes 2359304 | tf_op jit(solution)/shard_map/ppermute | solution.py:611
  340.3 20.7 %collective-permute-start.38 = (bf16[256,1536]{1,0:T(8,128)(2,1)}, bf16[256,1536]{1,0:T(8,128)(2,1)}, u32[]{:S(2)}, u32[]{:S(2)}) collective-permute-start(bf16[256,1536]{1,0:T(8,128)(2,1)} %weight_grad.22), channel_id=1, source_target_pairs={{0,16},{16,0},{1,17},{17,1},{2,18},{18,2},{3,19},{19,3},{4,20},{20... | collective-permute-start | bytes 2359304 | tf_op jit(solution)/shard_map/ppermute | solution.py:618
  341.8 129.0 %all-gather.8.cloned.1.call-start = ((), (), s32[]{:S(2)}) async-start(), calls=%async_computation.1 | async-start | bytes 2506752 | tf_op jit(solution)/shard_map/all_gather | solution.py:804
  341.8 27.6 %collective-permute-start.40 = (bf16[304,1024]{1,0:T(8,128)(2,1)}, bf16[304,1024]{1,0:T(8,128)(2,1)S(1)}, u32[]{:S(2)}, u32[]{:S(2)}) collective-permute-start(bf16[304,1024]{1,0:T(8,128)(2,1)} %add_convert_fusion), channel_id=1, source_target_pairs={{4,16},{12,24},{16,4},{24,12},{5,17},{13,25},{17,5},{25,13},{6,18}... | collective-permute-start | bytes 1867784 | tf_op jit(solution)/shard_map/ppermute | solution.py:630
  342.5 24.1 %collective-permute-start.39 = (bf16[160,1024]{1,0:T(8,128)(2,1)}, bf16[160,1024]{1,0:T(8,128)(2,1)S(1)}, u32[]{:S(2)}, u32[]{:S(2)}) collective-permute-start(bf16[160,1024]{1,0:T(8,128)(2,1)} %copy-done.54), channel_id=1, source_target_pairs={{0,8},{4,12},{8,0},{12,4},{1,9},{5,13},{9,1},{13,5},{2,10},{6,14},... | collective-permute-start | bytes 983048 | tf_op jit(solution)/shard_map/ppermute | solution.py:611
  344.4 38.3 %collective-permute-start.41 = (bf16[304,1024]{1,0:T(8,128)(2,1)}, bf16[304,1024]{1,0:T(8,128)(2,1)S(1)}, u32[]{:S(2)}, u32[]{:S(2)}) collective-permute-start(bf16[304,1024]{1,0:T(8,128)(2,1)} %copy-done.55), channel_id=1, source_target_pairs={{4,16},{12,24},{16,4},{24,12},{5,17},{13,25},{17,5},{25,13},{6,18}... | collective-permute-start | bytes 1867784 | tf_op jit(solution)/shard_map/ppermute | solution.py:630
  345.1 21.6 %copy-start.28 = (f32[2,64,1024]{2,1,0:T(8,128)S(1)}, f32[2,64,1024]{2,1,0:T(8,128)}, u32[]{:S(2)}) copy-start(f32[2,64,1024]{2,1,0:T(8,128)} %copy-done.27) | copy-start | bytes 1572868
  359.8 24.5 %collective-permute-start.42 = (bf16[160,1024]{1,0:T(8,128)(2,1)S(1)}, bf16[160,1024]{1,0:T(8,128)(2,1)S(1)}, u32[]{:S(2)}, u32[]{:S(2)}) collective-permute-start(bf16[160,1024]{1,0:T(8,128)(2,1)S(1)} %copy-done.53), channel_id=1, source_target_pairs={{0,8},{4,12},{8,0},{12,4},{1,9},{5,13},{9,1},{13,5},{2,10},{6,14},... | collective-permute-start | bytes 983048 | tf_op jit(solution)/shard_map/ppermute | solution.py:611
  367.7 23.1 %collective-permute-start.43 = (bf16[160,1024]{1,0:T(8,128)(2,1)S(1)}, bf16[160,1024]{1,0:T(8,128)(2,1)S(1)}, u32[]{:S(2)}, u32[]{:S(2)}) collective-permute-start(bf16[160,1024]{1,0:T(8,128)(2,1)S(1)} %out_grad.6), channel_id=1, source_target_pairs={{0,16},{16,0},{1,17},{17,1},{2,18},{18,2},{3,19},{19,3},{4,20},{20... | collective-permute-start | bytes 983048 | tf_op jit(solution)/shard_map/ppermute | solution.py:618
  370.4 35.5 %collective-permute-start.44 = (bf16[2,32,1536]{2,1,0:T(8,128)(2,1)S(1)}, bf16[2,32,1536]{2,1,0:T(8,128)(2,1)S(1)}, u32[]{:S(2)}, u32[]{:S(2)}) collective-permute-start(bf16[2,32,1536]{2,1,0:T(8,128)(2,1)S(1)} %get-tuple-element.238), channel_id=1, source_target_pairs={{0,1},{1,0},{2,3},{3,2},{4,5},{5,4},{6,7},{7,6},{8,9},{9,8},{10,11... | collective-permute-start | bytes 589832 | tf_op jit(solution)/shard_map/ppermute | solution.py:621
  381.6 25.7 %collective-permute-start.45 = (bf16[2,32,1536]{2,1,0:T(8,128)(2,1)S(1)}, bf16[2,32,1536]{2,1,0:T(8,128)(2,1)S(1)}, u32[]{:S(2)}, u32[]{:S(2)}) collective-permute-start(bf16[2,32,1536]{2,1,0:T(8,128)(2,1)S(1)} %get-tuple-element.237), channel_id=1, source_target_pairs={{0,2},{1,3},{2,0},{3,1},{4,6},{5,7},{6,4},{7,5},{8,10},{9,11},{10,... | collective-permute-start | bytes 589832 | tf_op jit(solution)/shard_map/ppermute | solution.py:621
  382.7 28.2 %collective-permute-start.46 = (bf16[2,32,1536]{2,1,0:T(8,128)(2,1)S(1)}, bf16[2,32,1536]{2,1,0:T(8,128)(2,1)S(1)}, u32[]{:S(2)}, u32[]{:S(2)}) collective-permute-start(bf16[2,32,1536]{2,1,0:T(8,128)(2,1)S(1)} %get-tuple-element.236), channel_id=1, source_target_pairs={{0,3},{1,2},{2,1},{3,0},{4,7},{5,6},{6,5},{7,4},{8,11},{9,10},{10,... | collective-permute-start | bytes 589832 | tf_op jit(solution)/shard_map/ppermute | solution.py:621
  391.8 20.3 %collective-permute-start.48 = (bf16[1,40,1024]{2,1,0:T(8,128)(2,1)S(1)}, bf16[1,40,1024]{2,1,0:T(8,128)(2,1)S(1)}, u32[]{:S(2)}, u32[]{:S(2)}) collective-permute-start(bf16[1,40,1024]{2,1,0:T(8,128)(2,1)S(1)} %get-tuple-element.244), channel_id=1, source_target_pairs={{0,1},{1,0},{2,3},{3,2},{4,5},{5,4},{6,7},{7,6},{8,9},{9,8},{10,11... | collective-permute-start | bytes 245768 | tf_op jit(solution)/shard_map/ppermute | solution.py:621
  404.8 13.5 %collective-permute-start.49 = (bf16[1,40,1024]{2,1,0:T(8,128)(2,1)S(1)}, bf16[1,40,1024]{2,1,0:T(8,128)(2,1)S(1)}, u32[]{:S(2)}, u32[]{:S(2)}) collective-permute-start(bf16[1,40,1024]{2,1,0:T(8,128)(2,1)S(1)} %get-tuple-element.243), channel_id=1, source_target_pairs={{0,2},{1,3},{2,0},{3,1},{4,6},{5,7},{6,4},{7,5},{8,10},{9,11},{10,... | collective-permute-start | bytes 245768 | tf_op jit(solution)/shard_map/ppermute | solution.py:621
  405.9 12.5 %collective-permute-start.50 = (bf16[1,40,1024]{2,1,0:T(8,128)(2,1)S(1)}, bf16[1,40,1024]{2,1,0:T(8,128)(2,1)S(1)}, u32[]{:S(2)}, u32[]{:S(2)}) collective-permute-start(bf16[1,40,1024]{2,1,0:T(8,128)(2,1)S(1)} %get-tuple-element.242), channel_id=1, source_target_pairs={{0,3},{1,2},{2,1},{3,0},{4,7},{5,6},{6,5},{7,4},{8,11},{9,10},{10,... | collective-permute-start | bytes 245768 | tf_op jit(solution)/shard_map/ppermute | solution.py:621
  411.0 7.4 %collective-permute-start.47 = (bf16[32,1536]{1,0:T(8,128)(2,1)S(1)}, bf16[32,1536]{1,0:T(8,128)(2,1)S(1)}, u32[]{:S(2)}, u32[]{:S(2)}) collective-permute-start(bf16[32,1536]{1,0:T(8,128)(2,1)S(1)} %dynamic-slice_bitcast_fusion.16), channel_id=1, source_target_pairs={{0,4},{4,0},{8,12},{12,8},{1,5},{5,1},{9,13},{13,9},{2,6},{6,2},{1... | collective-permute-start | bytes 294920 | tf_op jit(solution)/shard_map/ppermute | solution.py:608
  (67 other events, 413.4 us)
Sparse Core Ops, SparseCore 0:
  277.3 69.4 all-gather.5
  349.5 68.6 all-gather.9
  420.9 49.8 all-gather.7

commit v3 on v2

--- a/solution.py
+++ b/solution.py
@@ -14,6 +14,7 @@
 F32 = jnp.float32
 BF16 = jnp.bfloat16
 VMEM_LIMIT = 48 * 1024 * 1024
+HINT = pl.CostEstimate(flops=200_000_000_000, transcendentals=0, bytes_accessed=20_000_000)
 
 
 def dims(left, right, dot_left, dot_right):
@@ -38,6 +39,7 @@
         ),
         out_shape=[jax.ShapeDtypeStruct(out[0], out[1]) for out in outs],
         compiler_params=pltpu.CompilerParams(vmem_limit_bytes=VMEM_LIMIT),
+        cost_estimate=HINT,
         name=name,
     )(place, *operands)
 
@@ -530,8 +532,13 @@
         ),
         out_shape=jax.ShapeDtypeStruct((number * height, parts * width), BF16),
         compiler_params=pltpu.CompilerParams(vmem_limit_bytes=VMEM_LIMIT),
+        cost_estimate=HINT,
         name="weight_grad",
     )(blocks, left, right, *added)
+
+
+def tick_body(place_ref, out_ref):
+    out_ref[...] = jnp.full(out_ref.shape, place_ref[0], jnp.int32)
 
 
 class Line:
@@ -547,7 +554,14 @@
         self.last = value
         return value
 
+    def tick(self):
+        place = self.gate(jnp.zeros((1,), jnp.int32))
+        self.last = run(
+            tick_body, "tick", (1,), place, (), [], [((8, 128), jnp.int32, whole(8, 128))]
+        )[0]
+
     def pass_on(self, value):
+        self.tick()
         return self.mark(self.gate(value))
 
 
@@ -652,22 +666,23 @@
         )
     )
     qkv_x = [(over_x(qkv_part, k), over_x_core(qkv_cross, k)) for k in steps]
-    qkv_core = over_core(qkv_send)
-
-    vectors = jnp.concatenate(
-        [
-            line.gate(query_bias),
-            value_bias,
-            out_bias,
-            first_gain,
-            first_shift,
-            second_gain,
-            second_shift,
-            down_bias,
-            up_bias,
-        ]
-    ).reshape(-1, 128)
-    line.mark(vectors)
+
+    singles = [
+        query_bias,
+        value_bias,
+        out_bias,
+        first_gain,
+        first_shift,
+        second_gain,
+        second_shift,
+        down_bias,
+    ]
+    singles += [up_bias[i * owned : (i + 1) * owned] for i in range(owned_hidden // owned)]
+    row_of = lax.broadcasted_iota(jnp.int32, (16, owned), 0)
+    vectors = jnp.zeros((16, owned), BF16)
+    for i, single in enumerate(singles):
+        vectors = jnp.where(row_of == i, jnp.broadcast_to(single[None], (16, owned)), vectors)
+    vectors = line.mark(line.gate(vectors))
     vec_x = [over_x(vectors, k) for k in steps]
 
     own_half = lambda shard: pick(
@@ -676,60 +691,70 @@
     up_keep, up_send = line.mark(
         split_columns(line.gate(numbers(core, half)), up_weight, columns, 0, "split_up")
     )
-
-    gathered_vec = jnp.zeros((columns,) + vectors.shape, BF16)
-    gathered_vec = place(gathered_vec, vectors, column)
-    for k in steps:
-        gathered_vec = place(gathered_vec, vec_x[k - 1], (column - k) % columns)
-    gathered_vec = line.mark(line.gate(gathered_vec))
-    vec_core = over_core(gathered_vec)
-    out_part = line.mark(own_half(line.gate(out_weight)))
-    out_x = [over_x(out_part, k) for k in steps]
-
-    own_image = line.pass_on(jnp.where(half == core, own_tokens, other_tokens))
-    other_image = over_core(own_image)
-    up_core = over_core(line.pass_on(up_send))
-
-    mine_vec = gathered_vec.reshape(columns, -1).astype(F32)
-    all_vec = by_core(gathered_vec, vec_core, 1).reshape(columns * 2, -1)
-    all_vec = all_vec.astype(F32)
-    vec = lambda i: all_vec[:, i * owned : (i + 1) * owned].reshape(1, width)
-    own_vec = lambda i: mine_vec[:, i * owned : (i + 1) * owned].reshape(1, width // 2)
-    gain_one, shift_one, gain_two, shift_two = vec(3), vec(4), vec(5), vec(6)
-    vec_out, vec_down = vec(2), vec(7)
-    vec_up = mine_vec[:, 8 * owned :].reshape(1, columns * owned_hidden)
-    vec_qkv = jnp.concatenate(
-        [own_vec(0), jnp.zeros((1, width // 2), F32), own_vec(1)], axis=1
-    )
-    image, first_low = line.mark(
-        norm_one(line.gate(numbers(core)), own_image, other_image, gain_one, shift_one)
-    )
-    eighth = owned // halves // 2
-    up_part = line.mark(pair_part(line.gate(numbers(core, quarter)), up_keep, up_core, eighth))
-    up_x = [over_x(up_part, k) for k in steps]
-
+    qkv_core = line.pass_on(over_core(line.gate(qkv_send)))
     source = lambda k: (column - k) % columns
     qkv_pieces = [
         (qkv_keep, 0, owned, member),
         (qkv_core, 0, owned, member + 1 - 2 * core),
     ]
     part = owned // halves
+
+    def relay_qkv(index, c):
+        for k in steps:
+            value = line.pass_on(qkv_x[k - 1][index])
+            at = (2 * source(k) + c) * halves
+            qkv_pieces.append((value, 0, part, at + half))
+            qkv_pieces.append((over_y(value), 0, part, at + other_half))
+
+    own_image = line.pass_on(jnp.where(half == core, own_tokens, line.pass_on(other_tokens)))
+    other_image = line.pass_on(over_core(own_image))
+    relay_qkv(0, core)
+    up_core = line.pass_on(over_core(line.gate(up_send)))
+    eighth = owned // halves // 2
+    up_part = line.mark(pair_part(line.gate(numbers(core, quarter)), up_keep, up_core, eighth))
+    out_part = line.mark(own_half(line.gate(out_weight)))
+    relay_qkv(1, 1 - core)
+    out_x = [over_x(line.gate(out_part), k) for k in steps]
+
+    gathered_vec = jnp.zeros((columns,) + vectors.shape, BF16)
+    gathered_vec = place(gathered_vec, vectors, column)
     for k in steps:
-        for value, c in ((qkv_x[k - 1][0], core), (qkv_x[k - 1][1], 1 - core)):
-            value = line.pass_on(value)
-            at = (2 * source(k) + c) * halves
-            qkv_pieces += [(value, 0, part, at + half), (over_y(value), 0, part, at + other_half)]
+        gathered_vec = place(gathered_vec, line.pass_on(vec_x[k - 1]), (column - k) % columns)
+    line.mark(gathered_vec)
+    vec_core = line.pass_on(over_core(gathered_vec))
+    up_x = [over_x(line.gate(up_part), k) for k in steps]
+
+    mine_vec = gathered_vec.astype(F32)
+    all_vec = by_core(gathered_vec, vec_core, 1).reshape(columns * 2, 16, owned)
+    all_vec = all_vec.astype(F32)
+    vec = lambda i: all_vec[:, i].reshape(1, width)
+    own_vec = lambda i: mine_vec[:, i].reshape(1, width // 2)
+    gain_one, shift_one, gain_two, shift_two = vec(3), vec(4), vec(5), vec(6)
+    vec_out, vec_down = vec(2), vec(7)
+    vec_up = mine_vec[:, 8 : 8 + owned_hidden // owned].reshape(1, columns * owned_hidden)
+    vec_qkv = jnp.concatenate(
+        [own_vec(0), jnp.zeros((1, width // 2), F32), own_vec(1)], axis=1
+    )
+    image, first_low = line.mark(
+        norm_one(line.gate(numbers(core)), own_image, other_image, gain_one, shift_one)
+    )
     own_cotangent = line.mark(
         jnp.concatenate([line.gate(cotangent[0]), jnp.zeros((padded - rows, width), BF16)], axis=0)
     )
-    other_cotangent = swap(own_cotangent)
+    chunks = 2
+    down_part = line.mark(
+        own_half(line.gate(down_weight)).reshape(chunks, -1, width)
+    )
     out_pieces = [(out_weight, 0, owned, column)]
     for k in steps:
         value = line.pass_on(out_x[k - 1])
         at = source(k) * halves
         out_pieces += [(value, 0, part, at + half), (over_y(value), 0, part, at + other_half)]
-    down_part = line.mark(own_half(line.gate(down_weight)))
-    down_x = [over_x(down_part, k) for k in steps]
+    down_x = [[over_x(line.gate(down_part[0]), k) for k in steps]]
+
+    wqkv, qkv = join_dot(
+        line, first_low, qkv_pieces, vec_qkv, lambda total: (total,), 1, width // 2, "project"
+    )
     up_pieces = [(up_keep, 0, owned, member), (up_core, 0, owned, member + 1 - 2 * core)]
 
     def up_rows(value, k, h, s):
@@ -737,83 +762,151 @@
             at = (2 * source(k) + c) * halves * 2 + h * 2 + s
             up_pieces.append((value, c * eighth, eighth, at))
 
-    up_y = []
+    up_y, up_z, down_others = [], [], []
+    no_bias = jnp.zeros((1, width), F32)
+
+    def relay_down(c):
+        for k in steps:
+            value = line.pass_on(down_x[c][k - 1])
+            at = source(k) * halves * chunks + c
+            down_others.append((value, at + half * chunks))
+            down_others.append((over_y(value), at + other_half * chunks))
+
+    other_cotangent = swap(line.gate(own_cotangent))
     for k in steps:
         value = line.pass_on(up_x[k - 1])
         up_rows(value, k, half, side)
-        up_rows(over_z(value, 1), k, half, 1 - side)
+        up_z.append(over_z(value, 1))
         up_y.append(over_y(value))
-
-    wqkv, qkv = join_dot(
-        line, first_low, qkv_pieces, vec_qkv, lambda total: (total,), 1, width // 2, "project"
-    )
     mixed, log_total = line.mark(attention(line.gate(numbers(core)), image, qkv, rows))
+    wout, branch = join_dot(
+        line, mixed, out_pieces, no_bias, lambda total: (total,), 1, width // 2, "project_out"
+    )
+    branch_other = over_core(branch)
+    for k in steps:
+        up_rows(line.pass_on(up_z[k - 1]), k, half, 1 - side)
     for k in steps:
         value = line.pass_on(up_y[k - 1])
         up_rows(value, k, other_half, side)
-        up_rows(over_z(value, 1), k, other_half, 1 - side)
-    no_bias = jnp.zeros((1, width), F32)
-    wout, branch = join_dot(
-        line, mixed, out_pieces, no_bias, lambda total: (total,), 1, width // 2, "project_out"
-    )
-    branch_other = over_core(branch)
+        up_y[k - 1] = over_z(value, 1)
+    relay_down(0)
+    line.tick()
+    down_x.append([over_x(line.gate(down_part[1]), k) for k in steps])
     middle, second_low = line.mark(
         norm_two(
             line.gate(numbers(core)), image, branch, branch_other, vec_out, gain_two, shift_two
         )
     )
-    down_others = []
+    other_cotangent = line.pass_on(other_cotangent)
+    own_incoming = line.mark(jnp.where(half == core, own_cotangent, other_cotangent))
+    incoming_other = over_core(own_incoming)
+    incoming_other = line.pass_on(incoming_other)
+    incoming = line.mark(by_core(own_incoming, incoming_other).reshape(2 * padded, width))
     for k in steps:
-        value = line.pass_on(down_x[k - 1])
-        down_others += [(value, source(k) * halves + half), (over_y(value), source(k) * halves + other_half)]
+        up_rows(line.pass_on(up_y[k - 1]), k, other_half, 1 - side)
     wup, act_low, slope = join_dot(line, second_low, up_pieces, vec_up, activate, 2, 512, "hidden")
-    own_incoming = line.pass_on(jnp.where(half == core, own_cotangent, other_cotangent))
-    incoming = by_core(own_incoming, over_core(own_incoming)).reshape(2 * padded, width)
 
     class Total:
         def __init__(self, quadrant, lead, cross):
             self.quadrant, self.lead, self.cross = quadrant, lead, cross
+            self.crossed = not cross
+            self.halving, self.done, self.step = True, False, 1
 
         def along_x(self, y):
-            sent = [self.quadrant((column + k) % columns, y, ()) for k in steps]
-            return tuple(over_x(v, k) for k, v in zip(steps, sent))
+            return [self.quadrant((column + k) % columns, y, ()) for k in steps]
+
+        def make_first(self):
+            self.sent = self.along_x(other_half)
+
+        def make_second(self):
+            self.sent_b = self.along_x(half)
 
         def first(self):
-            self.got = self.along_x(other_half)
+            self.got = tuple(over_x(line.gate(v), k) for k, v in zip(steps, self.sent))
 
         def second(self):
-            self.got_b = self.along_x(half)
+            self.got_b = tuple(over_x(line.gate(v), k) for k, v in zip(steps, self.sent_b))
 
         def third(self):
+            line.tick()
             self.from_y = over_y(self.quadrant(column, other_half, self.got))
 
         def fourth(self):
+            line.tick()
             total = self.quadrant(column, half, self.got_b + (self.from_y,))
             height = total.shape[0] // self.lead // replicas
             self.total = total.reshape(self.lead, replicas, height, total.shape[1])
-            self.got_z = [over_z(pick(self.total, copy_id ^ s, 1), s) for s in range(1, replicas)]
-
-        def fifth(self):
-            total = line.gate(pick(self.total, copy_id, 1)).astype(F32)
-            for value in self.got_z:
-                total = total + value.astype(F32)
-            total = line.mark(total.astype(BF16))
-            return self.cross(total) if self.cross else total[0]
-
-    def collect(total):
-        return lax.all_gather(total, ("seq", "rep"), axis=0, tiled=False)
+            self.halve()
+
+        def bit(self):
+            return (copy_id // self.step) % 2
+
+        def halve(self):
+            shape = self.total.shape
+            pairs = self.total.reshape((self.lead, shape[1] // 2, 2) + shape[2:])
+            self.own = pick(pairs, self.bit(), 2)
+            self.from_z = over_z(line.mark(pick(pairs, 1 - self.bit(), 2)), self.step)
+
+        def double(self):
+            self.step //= 2
+            self.from_z = over_z(self.total, self.step)
+
+        def turn(self):
+            line.tick()
+            if self.halving:
+                own = line.gate(self.own).astype(F32)
+                self.total = line.mark((own + self.from_z.astype(F32)).astype(BF16))
+                self.step *= 2
+                if self.step < replicas:
+                    self.halve()
+                    return
+                self.halving = False
+                total = self.total.reshape((self.lead,) + self.total.shape[2:])
+                if self.cross:
+                    self.own = pick(total, core)
+                    self.from_core = over_core(line.mark(pick(total, 1 - core)))
+                    return
+                self.total = total
+                self.double()
+            elif not self.crossed:
+                self.crossed = True
+                own, got = line.gate(self.own), self.from_core
+                self.total = line.mark(self.cross(own, got))[None]
+                self.double()
+            elif self.step:
+                self.total = line.mark(
+                    jnp.where(
+                        self.bit() == 0,
+                        jnp.stack([line.gate(self.total), self.from_z], 1),
+                        jnp.stack([self.from_z, self.total], 1),
+                    ).reshape((-1,) + self.total.shape[1:])
+                )
+                if self.step > 1:
+                    self.double()
+                else:
+                    self.step = 0
+                    self.from_y = over_y(self.total)
+
+        def finish(self):
+            while self.step:
+                self.turn()
+            line.tick()
+            total, got = line.gate(self.total), self.from_y
+            return line.mark(
+                jnp.where(half == 0, jnp.stack([total, got], 0), jnp.stack([got, total], 0)).astype(
+                    F32
+                )
+            )
 
     def cross_cores(blocks):
-        def exchange(total):
-            got = over_core(pick(total, 1 - core))
-            own = pick(total, core)
+        def exchange(own, got):
             one = own.shape[1] // blocks
             left = jnp.where(core == 0, own, got)
             right = jnp.where(core == 0, got, own)
             cols = []
             for k in range(blocks):
                 cols += [left[:, k * one : (k + 1) * one], right[:, k * one : (k + 1) * one]]
-            return cols
+            return jnp.concatenate(cols, axis=1)
 
         return exchange
 
@@ -838,10 +931,12 @@
 
     pieces = halves * replicas
     total_down = Total(down_quadrant, 1, None)
+    total_down.make_first()
     total_down.first()
-    total_down.second()
-
-    at = [column * halves + h for h in range(halves)] + [place_ for _, place_ in down_others]
+    total_down.make_second()
+    relay_down(1)
+    blocks = halves * chunks
+    at = [column * blocks + h for h in range(blocks)] + [place_ for _, place_ in down_others]
     hidden_low, up_sums, partial = line.mark(
         feed_back(
             line.gate(numbers(*at)),
@@ -852,13 +947,15 @@
             [value for value, _ in down_others],
         )
     )
-    total_up = Total(by_row(second_low, hidden_low), 2, cross_cores(columns))
+    total_down.second()
     grad_second = line.mark(
         dot_rows(line.gate(numbers(core)), hidden_low, wup, width // 2, "grad_second")
     )
     grad_second_other = over_core(grad_second)
+    total_up = Total(by_row(second_low, hidden_low), 2, cross_cores(columns))
+    total_up.make_first()
+    total_down.third()
     total_up.first()
-    total_up.second()
     grad_middle, branch_low, sums_two = line.mark(
         norm_two_back(
             line.gate(numbers(core)), incoming, grad_second, grad_second_other, middle, gain_two
@@ -867,7 +964,7 @@
     grad_mixed = line.mark(
         dot_rows(line.gate(numbers(core)), branch_low, wout, width // 2, "grad_mixed")
     )
-    total_down.third()
+    total_up.make_second()
     grad_qkv, qv_sums = line.mark(
         attention_grad(line.gate(numbers(core)), image, qkv, grad_mixed, log_total, rows)
     )
@@ -876,15 +973,14 @@
     )
     grad_first_other = over_core(grad_first)
     total_qkv = Total(by_row(first_low, grad_qkv), 2, cross_cores(3 * columns))
-    total_qkv.first()
-    total_qkv.second()
+    total_qkv.make_first()
     total_down.fourth()
+    total_up.second()
     own_grad, own_grad_low, sums_one = line.mark(
         norm_one_back(
             line.gate(numbers(core)), grad_middle, grad_first, grad_first_other, image, gain_one
         )
     )
-
     entries = 8 * owned + owned_hidden
     vec_grads = line.mark(
         run(
@@ -903,43 +999,55 @@
         )[0]
     )
     total_out = Total(out_quadrant, 1, None)
-    total_out.first()
-    total_out.second()
-    total_up.third()
-
+    total_out.make_first()
+    total_out.make_second()
+    total_down.turn()
+    total_qkv.first()
     halves_of = lambda value: value.reshape(2, padded, width)
     from_other = over_core(line.pass_on(pick(halves_of(partial), 1 - core)))
-    grad_down = collect(total_down.fifth())
     block = pick(halves_of(middle), core) + pick(halves_of(partial), core).astype(F32)
     block = line.mark((line.gate(block) + from_other.astype(F32) + vec_down).astype(BF16))
-    block_moved = swap(block)
-    moved = swap(line.pass_on(own_grad_low))
+    total_down.turn()
+    total_qkv.make_second()
+    total_qkv.second()
+    total_qkv.third()
+    total_up.third()
+    total_down.turn()
     total_up.fourth()
-    total_qkv.third()
-    up_cols = total_up.fifth()
-    grad_up = collect(jnp.concatenate(up_cols, axis=1))
+    total_out.first()
+    total_up.turn()
+    total_down.turn()
+    total_up.turn()
+    grad_down = total_down.finish().reshape(owned_hidden, width)
     total_qkv.fourth()
+    total_out.second()
+    total_up.turn()
+    total_up.turn()
+    block_moved = swap(line.gate(block))
     total_out.third()
+    total_out.fourth()
+    total_qkv.turn()
+    total_up.turn()
+    total_qkv.turn()
+    total_qkv.turn()
+    total_out.turn()
+    total_qkv.turn()
+    moved = swap(line.gate(own_grad_low))
+    total_out.turn()
     block_out = line.mark(jnp.where(half == core, line.gate(block), block_moved)[:rows][None])
+    total_qkv.turn()
+    total_out.turn()
+    grad_up = total_up.finish().reshape(owned, up_weight.shape[1])
     token_grad = line.mark(
         jnp.where(half == core, line.gate(own_grad), moved.astype(F32))[:rows][None]
     )
-    total_out.fourth()
-    qkv_cols = total_qkv.fifth()
-    out_rows = total_out.fifth()
-    height = out_rows.shape[0] - 8
-    each = 2 * columns
-    joined = [jnp.concatenate(qkv_cols[each * p : each * p + each], axis=1) for p in range(3)]
-    joined = collect(jnp.concatenate(joined + [out_rows], axis=0))
-    grad_down = line.mark(line.gate(grad_down).astype(F32).reshape(owned_hidden, width))
-    grad_up = line.mark(line.gate(grad_up).astype(F32).reshape(owned, up_weight.shape[1]))
-    joined = line.gate(joined).reshape(pieces, -1, width)
-    grad_qkv_w = jnp.concatenate(
-        [joined[:, p * height : (p + 1) * height] for p in range(3)], axis=2
-    )
-    grad_qkv_w = grad_qkv_w.astype(F32).reshape(owned, 3 * width)
-    grad_out = joined[:, 3 * height : 4 * height].astype(F32).reshape(owned, width)
-    vec_out_grads = joined[:, 4 * height, : entries // pieces].astype(F32).reshape(entries)
+    grad_qkv_w = total_qkv.finish().reshape(owned, 3 * width)
+    total_out.turn()
+    out_rows = total_out.finish()
+    height = out_rows.shape[2] - 8
+    grad_out = out_rows[:, :, :height].reshape(owned, width)
+
+    vec_out_grads = out_rows[:, :, height, : entries // pieces].reshape(entries)
     vec_of = lambda i: vec_out_grads[i * owned : (i + 1) * owned]
     return (
         block_out,

time: 486 us -> 400 us (0.82)
  waiting for transfers between devices: 204 us -> 109 us
  other arithmetic: 25.1 us -> 43.7 us
  between operations: 15.5 us -> 3.13 us
  Pallas kernels: 125 us -> 134 us
  starting transfers between devices: 73.7 us -> 68 us
    ppermute x13 -> x14, waiting for transfers between devices: 62.1 us -> 19.3 us  [over_x(): lax.ppermute(value, 'shard', [(i, (i + 2 * step) % group) for i in range(...]
    all_gather x3 -> x0, waiting for transfers between devices: 41.1 us -> none  [collect(): return lax.all_gather(total, ('seq', 'rep'), axis=0, tiled=False)]
    ppermute x14 -> x18, starting transfers between devices: 40 us -> 21.8 us  [over_z(): return lax.ppermute(value, 'rep', [(i, i ^ step) for i in range(replicas)])]
    ppermute x9 -> x14, waiting for transfers between devices: 53.2 us -> 35.9 us  [over_y(): lax.ppermute(value, 'seq', [(i, halves - 1 - i) for i in range(halves)])]
    select_n x1 -> x18, other arithmetic: 1.3 us -> 18.1 us  [the longest x12 12.8 us: turn(): jnp.where(self.bit() == 0, jnp.stack([line.gate(self.total), self.from_z]...]
    ppermute x14 -> x18, waiting for transfers between devices: 39 us -> 53.4 us  [over_z(): return lax.ppermute(value, 'rep', [(i, i ^ step) for i in range(replicas)])]
    reshape x3 -> x0, other arithmetic: 9.29 us -> none  [the longest x1 4.1 us: shards(): line.gate(grad_up).astype(F32).reshape(owned, up_weight.shape[1])]
    convert_element_type x6 -> x12, other arithmetic: 5.08 us -> 13.9 us  [the longest x4 7.51 us: finish(): jnp.where(half == 0, jnp.stack([total, got], 0), jnp.stack([got, total], 0))]
  transfers between devices with their start and end apart: 55 -> 62, of which waited for: 23 -> 14; matrix products, arithmetic and copies ran while one was open for 7% -> 15% of each run, Pallas kernels for 22% -> 34%
where the time goes in v3:
time: 400 us; the launch traced here: 394 us
  Pallas kernels  134 us (34%)
  waiting for transfers between devices  109 us (27%)
  starting transfers between devices  68 us (17%)
  other arithmetic  43.7 us (11%)
  local copies, waits for them, and re-layouts  36.2 us (9%)
    pallas_call x21, Pallas kernels, run(): pl.pallas_call(body, grid_spec=pltpu.PrefetchScalarGridSpec(num_scalar_pr...  88.4 us
    ppermute x18, waiting for transfers between devices, over_z(): return lax.ppermute(value, 'rep', [(i, i ^ step) for i in range(replicas)])  53.4 us
    pallas_call x12, Pallas kernels, weight_grad(): pl.pallas_call(functools.partial(weight_grad_body, len(added)), grid_spec...  45.8 us
    ppermute x14, waiting for transfers between devices, over_y(): lax.ppermute(value, 'seq', [(i, halves - 1 - i) for i in range(halves)])  35.9 us
    ppermute x18, starting transfers between devices, over_z(): return lax.ppermute(value, 'rep', [(i, i ^ step) for i in range(replicas)])  21.8 us
    ppermute x14, waiting for transfers between devices, over_x(): lax.ppermute(value, 'shard', [(i, (i + 2 * step) % group) for i in range(...  19.3 us
    unnamed x175, local copies, waits for them, and re-layouts  19.3 us
    ppermute x14, starting transfers between devices, over_x(): lax.ppermute(value, 'shard', [(i, (i + 2 * step) % group) for i in range(...  18 us
  transfers between devices with their start and end apart: 62, of which 14 were waited for; matrix products, arithmetic and copies ran while one was open for 15% of the time, Pallas kernels for 34%

profile of v3, /device:TPU:0, one launch (start us, length us, event | category | flops | bytes accessed | tf_op | source)
XLA Modules:
  0.0 394.0 jit_solution(15044678711931979257)
XLA Ops:
  2.0 1.9 pad_maximum_fusion.2
  7.0 2.9 split_qkv.1
  9.9 3.0 collective-permute-start.4
  12.9 1.9 collective-permute-start.6
  21.0 9.1 %collective-permute-done = bf16[16,256]{1,0:T(8,128)(2,1)} collective-permute-done((bf16[16,256]{1,0:T(8,128)(2,1)}, bf16[16,256]{1,0:T(8,128)(2,1)}, u32[]{:S(2)}, u32[]{:S(2)}) %collective-permute-start) | collective-permute-done | bytes 8224 | tf_op jit(solution)/shard_map/ppermute | solution.py:625
  43.9 2.0 collective-permute-start.7
  46.0 2.1 norm_one.1
  49.0 2.7 dynamic-slice_bitcast_fusion.1
  54.8 4.3 %collective-permute-done.12.refs_5_ = bf16[128,1536]{1,0:T(8,128)(2,1)} collective-permute-done((bf16[128,1536]{1,0:T(8,128)(2,1)}, bf16[128,1536]{1,0:T(8,128)(2,1)}, u32[]{:S(2)}, u32[]{:S(2)}) %collective-permute-start.12) | collective-permute-done | bytes 393248 | tf_op jit(solution)/shard_map/ppermute | solution.py:632
  59.1 6.3 %project.1 = (bf16[1024,1536]{1,0:T(8,128)(2,1)}, bf16[608,1536]{1,0:T(8,128)(2,1)}) custom-call(s32[6]{0:T(128)S(1)} %stack.433.place_ref, bf16[608,1024]{1,0:T(8,128)(2,1)S(1)} %get-tuple-element.101.left_ref, f32[1,1536]{1,0:T(1,128)S(1)} %fusion.6.bias_ref, bf16[256,1536]{1,0:T(8,128)(2,1)S(1)} %copy-done.44, ...), custom_call_target="tpu_custom_call" | custom-call | flops 199999995904 | bytes 20000000 | tf_op jit(solution)/shard_map/project/pallas_call | solution.py:31
  71.4 8.7 %attention.1 = (bf16[608,512]{1,0:T(8,128)(2,1)S(1)}, f32[4,2,608]{2,1,0:T(2,128)S(1)}) custom-call(s32[1]{0:T(128)} %bitcast.place_ref, bf16[608,1024]{1,0:T(8,128)(2,1)S(1)} %get-tuple-element.100.note_ref.image_ref, bf16[608,1536]{1,0:T(8,128)(2,1)S(1)} %copy-done.18, bf16[608,1536]{1,0:T(8,128)(2,1)S(1)} %copy-done.18, bf16[608,1536]{1,0:T(8,128)(2,1)S(1)} %copy-done.18), custom_call_target="tpu_custom_call" | custom-call | flops 199999995904 | bytes 20000000 | tf_op jit(solution)/shard_map/attention/pallas_call | solution.py:31
  80.1 2.8 project_out.1
  91.1 9.8 %collective-permute-done.15.refs_2_ = bf16[256,1024]{1,0:T(8,128)(2,1)} collective-permute-done((bf16[256,1024]{1,0:T(8,128)(2,1)}, bf16[256,1024]{1,0:T(8,128)(2,1)}, u32[]{:S(2)}, u32[]{:S(2)}) %collective-permute-start.15) | collective-permute-done | bytes 524320 | tf_op jit(solution)/shard_map/ppermute | solution.py:625
  104.4 2.1 norm_two.1
  107.2 8.3 %hidden.1 = (bf16[1024,2048]{1,0:T(8,128)(2,1)}, bf16[608,2048]{1,0:T(8,128)(2,1)}, bf16[608,2048]{1,0:T(8,128)(2,1)}) custom-call(s32[10]{0:T(128)S(1)} %stack.455.place_ref, bf16[608,1024]{1,0:T(8,128)(2,1)S(1)} %get-tuple-element.129.left_ref, f32[1,2048]{1,0:T(1,128)S(1)} %reshape.478.bias_ref, bf16[256,2048]{1,0:T(8,128)(2,1)S(1)} %copy-done.40, ...), custom_call_target="tpu_custom_call" | custom-call | flops 199999995904 | bytes 20000000 | tf_op jit(solution)/shard_map/hidden/pallas_call | solution.py:31
  117.3 2.2 weight_grad.12
  121.0 2.2 weight_grad.14
  123.1 12.0 %feed_back.1 = (bf16[608,2048]{1,0:T(8,128)(2,1)}, f32[1,2048]{1,0:T(1,128)S(1)}, bf16[608,1024]{1,0:T(8,128)(2,1)S(1)}) custom-call(s32[8]{0:T(128)S(1)} %stack.442.place_ref, bf16[608,1024]{1,0:T(8,128)(2,1)S(1)} %bitcast.191, bf16[608,2048]{1,0:T(8,128)(2,1)} %get-tuple-element.130.act_ref.left_ref, bf16[608,2048]{1,0:T(8,128)(2,1)} %get-tuple-element.131.slope_ref, ...), custom_call_target="tpu_custom_call" | custom-call | flops 199999995904 | bytes 20000000 | tf_op jit(solution)/shard_map/feed_back/pallas_call | solution.py:31
  138.8 5.7 %grad_second.1.own_ref = bf16[608,1024]{1,0:T(8,128)(2,1)} custom-call(s32[1]{0:T(128)} %bitcast.place_ref, bf16[608,2048]{1,0:T(8,128)(2,1)S(1)} %copy-done.14, bf16[1024,2048]{1,0:T(8,128)(2,1)} %get-tuple-element.134.weight_ref), custom_call_target="tpu_custom_call" | custom-call | flops 199999995904 | bytes 20000000 | tf_op jit(solution)/shard_map/grad_second/pallas_call | solution.py:31
  145.5 3.5 weight_grad.21
  149.7 2.5 add_convert_fusion
  152.2 3.2 weight_grad.13
  157.4 5.4 %norm_two_back.1 = (f32[608,1024]{1,0:T(8,128)}, bf16[608,1024]{1,0:T(8,128)(2,1)S(1)}, f32[8,1024]{1,0:T(8,128)S(1)}) custom-call(s32[1]{0:T(128)} %bitcast.place_ref, bf16[608,1024]{1,0:T(8,128)(2,1)S(1)} %bitcast.193, bf16[608,1024]{1,0:T(8,128)(2,1)} %grad_second.1.own_ref, bf16[608,1024]{1,0:T(8,128)(2,1)} %collective-permute-done.25.other_ref, ...), custom_call_target="tpu_custom_call" | custom-call | flops 199999995904 | bytes 20000000 | tf_op jit(solution)/shard_map/norm_two_back/pallas_call | solution.py:31
  164.8 3.5 weight_grad.16
  168.3 11.9 %attention_grad.1 = (bf16[3,608,512]{2,1,0:T(8,128)(2,1)S(1)}, f32[4,8,128]{2,1,0:T(8,128)S(1)}) custom-call(s32[1]{0:T(128)} %bitcast.place_ref, bf16[608,1024]{1,0:T(8,128)(2,1)S(1)} %copy-done.24, bf16[608,1536]{1,0:T(8,128)(2,1)S(1)} %copy-done.19, bf16[608,1536]{1,0:T(8,128)(2,1)S(1)} %copy-done.19, bf16[608,1536]{1,0:T(8,128)(2,1)S(1)} %copy-done.19, ...), custom_call_target="tpu_custom_call" | custom-call | flops 199999995904 | bytes 20000000 | tf_op jit(solution)/shard_map/attention_grad/pallas_call | solution.py:31
  180.3 5.3 %grad_first.1.own_ref = bf16[608,1024]{1,0:T(8,128)(2,1)} custom-call(s32[1]{0:T(128)} %bitcast.place_ref, bf16[3,608,512]{2,1,0:T(8,128)(2,1)S(1)} %get-tuple-element.151.left_ref.right_ref, bf16[1024,1536]{1,0:T(8,128)(2,1)} %get-tuple-element.126.weight_ref), custom_call_target="tpu_custom_call" | custom-call | flops 199999995904 | bytes 20000000 | tf_op jit(solution)/shard_map/grad_first/pallas_call | solution.py:31
  185.6 3.9 weight_grad.18
  189.4 2.8 weight_grad.15
  194.3 4.9 %weight_grad.22 = bf16[256,2048]{1,0:T(8,128)(2,1)} custom-call(s32[2]{0:T(128)S(1)} %pad_add_fusion.5.index_ref, bf16[608,1024]{1,0:T(8,128)(2,1)S(1)} %copy-done.27, bf16[608,2048]{1,0:T(8,128)(2,1)S(1)} %copy-done.15, bf16[256,2048]{1,0:T(8,128)(2,1)} %collective-permute-done.36.rest_0_), custom_call_target="tpu_custom_call" | custom-call | flops 199999995904 | bytes 20000000 | tf_op jit(solution)/shard_map/weight_grad/pallas_call | solution.py:524
  200.8 4.1 %norm_one_back.1 = (f32[304,1024]{1,0:T(8,128)S(1)}, bf16[304,1024]{1,0:T(8,128)(2,1)S(1)}, f32[8,1024]{1,0:T(8,128)S(1)}) custom-call(s32[1]{0:T(128)} %bitcast.place_ref, f32[608,1024]{1,0:T(8,128)} %get-tuple-element.145.grad_ref, bf16[608,1024]{1,0:T(8,128)(2,1)} %grad_first.1.own_ref, bf16[608,1024]{1,0:T(8,128)(2,1)} %collective-permute-done.28.other_ref, ...), custom_call_target="tpu_custom_call" | custom-call | flops 199999995904 | bytes 20000000 | tf_op jit(solution)/shard_map/norm_one_back/pallas_call | solution.py:31
  210.0 2.6 collective-permute-start.30
  215.1 9.8 %collective-permute-done.30 = bf16[1,1,128,1024]{3,2,1,0:T(8,128)(2,1)} collective-permute-done((bf16[1,1,128,1024]{3,2,1,0:T(8,128)(2,1)}, bf16[1,1,128,1024]{3,2,1,0:T(8,128)(2,1)}, u32[]{:S(2)}, u32[]{:S(2)}) %collective-permute-start.30) | collective-permute-done | bytes 262176 | tf_op jit(solution)/shard_map/ppermute | solution.py:635
  226.6 3.8 weight_grad.17
  231.8 5.0 %weight_grad.23 = bf16[256,2048]{1,0:T(8,128)(2,1)S(1)} custom-call(s32[2]{0:T(128)S(1)} %pad_add_fusion.4.index_ref, bf16[608,1024]{1,0:T(8,128)(2,1)S(1)} %copy-done.28, bf16[608,2048]{1,0:T(8,128)(2,1)} %get-tuple-element.138.left_ref.right_ref, bf16[256,2048]{1,0:T(8,128)(2,1)} %collective-permute-done.35.rest_0_, ...), custom_call_target="tpu_custom_call" | custom-call | flops 199999995904 | bytes 20000000 | tf_op jit(solution)/shard_map/weight_grad/pallas_call | solution.py:524
  237.9 4.0 %collective-permute-start.42 = (bf16[2,2,32,2048]{3,2,1,0:T(8,128)(2,1)}, bf16[2,2,32,2048]{3,2,1,0:T(8,128)(2,1)}, u32[]{:S(2)}, u32[]{:S(2)}) collective-permute-start(bf16[2,2,32,2048]{3,2,1,0:T(8,128)(2,1)} %get-tuple-element.191), channel_id=1, source_target_pairs={{0,1},{1,0},{2,3},{3,2},{4,5},{5,4},{6,7},{7,6},{8,9},{9,8},{10,11... | collective-permute-start | bytes 1572872 | tf_op jit(solution)/shard_map/ppermute | solution.py:635
  241.9 2.8 collective-permute-done.59
  244.8 2.1 maximum_select_fusion.10
  248.0 2.1 maximum_select_fusion.11
  250.1 5.6 %weight_grad.19 = bf16[256,1536]{1,0:T(8,128)(2,1)} custom-call(s32[2]{0:T(128)S(1)} %pad_add_fusion.5.index_ref, bf16[608,1024]{1,0:T(8,128)(2,1)S(1)} %copy-done.36, bf16[3,608,512]{2,1,0:T(8,128)(2,1)S(1)} %copy-done.21, bf16[256,1536]{1,0:T(8,128)(2,1)} %collective-permute-done.32.rest_0_), custom_call_target="tpu_custom_call" | custom-call | flops 199999995904 | bytes 20000000 | tf_op jit(solution)/shard_map/weight_grad/pallas_call | solution.py:524
  258.5 2.1 collective-permute-start.43
  260.6 2.6 out_grad.6
  264.3 8.8 %collective-permute-done.43 = bf16[2,1,32,2048]{3,2,1,0:T(8,128)(2,1)} collective-permute-done((bf16[2,1,32,2048]{3,2,1,0:T(8,128)(2,1)}, bf16[2,1,32,2048]{3,2,1,0:T(8,128)(2,1)}, u32[]{:S(2)}, u32[]{:S(2)}) %collective-permute-start.43) | collective-permute-done | bytes 262176 | tf_op jit(solution)/shard_map/ppermute | solution.py:635
  274.3 2.5 maximum_select_fusion.5
  278.9 5.2 %weight_grad.20 = bf16[256,1536]{1,0:T(8,128)(2,1)S(1)} custom-call(s32[2]{0:T(128)S(1)} %pad_add_fusion.4.index_ref, bf16[608,1024]{1,0:T(8,128)(2,1)S(1)} %copy-done.37, bf16[3,608,512]{2,1,0:T(8,128)(2,1)S(1)} %copy-done.21, bf16[256,1536]{1,0:T(8,128)(2,1)} %collective-permute-done.31.rest_0_, bf16[256,1536]{1,0:T(8,128)(2,1)} %collective-permute-done.33.rest_1_), custom_call_target="tpu_custom_call" | custom-call | flops 199999995904 | bytes 20000000 | tf_op jit(solution)/shard_map/weight_grad/pallas_call | solution.py:524
  285.0 2.7 collective-permute-start.47
  288.3 5.5 %collective-permute-done.45 = bf16[1,32,4096]{2,1,0:T(8,128)(2,1)} collective-permute-done((bf16[1,32,4096]{2,1,0:T(8,128)(2,1)}, bf16[1,32,4096]{2,1,0:T(8,128)(2,1)}, u32[]{:S(2)}, u32[]{:S(2)}) %collective-permute-start.45) | collective-permute-done | bytes 262176 | tf_op jit(solution)/shard_map/ppermute | solution.py:635
  293.7 2.2 maximum_select_fusion.8
  295.9 2.0 maximum_select_fusion.9
  299.4 1.9 out_grad.7
  301.4 2.1 collective-permute-start.40
  304.9 16.0 %collective-permute-done.40 = bf16[1,2,40,1024]{3,2,1,0:T(8,128)(2,1)S(1)} collective-permute-done((bf16[1,2,40,1024]{3,2,1,0:T(8,128)(2,1)S(1)}, bf16[1,2,40,1024]{3,2,1,0:T(8,128)(2,1)S(1)}, u32[]{:S(2)}, u32[]{:S(2)}) %collective-permute-start.40) | collective-permute-done | bytes 163872 | tf_op jit(solution)/shard_map/ppermute | solution.py:635
  321.1 2.6 maximum_select_fusion.1
  323.7 2.6 bitcast_convert_fusion
  327.2 2.1 collective-permute-start.54
  329.5 4.8 %collective-permute-done.54 = bf16[1,40,1024]{2,1,0:T(8,128)(2,1)S(1)} collective-permute-done((bf16[1,40,1024]{2,1,0:T(8,128)(2,1)S(1)}, bf16[1,40,1024]{2,1,0:T(8,128)(2,1)S(1)}, u32[]{:S(2)}, u32[]{:S(2)}) %collective-permute-start.54) | collective-permute-done | bytes 81952 | tf_op jit(solution)/shard_map/ppermute | solution.py:635
  337.1 2.3 collective-permute-start.50
  339.4 2.1 fusion.2
  343.3 5.0 %collective-permute-done.50 = bf16[1,32,3072]{2,1,0:T(8,128)(2,1)S(1)} collective-permute-done((bf16[1,32,3072]{2,1,0:T(8,128)(2,1)S(1)}, bf16[1,32,3072]{2,1,0:T(8,128)(2,1)S(1)}, u32[]{:S(2)}, u32[]{:S(2)}) %collective-permute-start.50) | collective-permute-done | bytes 196640 | tf_op jit(solution)/shard_map/ppermute | solution.py:635
  349.2 18.5 %collective-permute-done.56 = bf16[4,40,1024]{2,1,0:T(8,128)(2,1)S(1)} collective-permute-done((bf16[4,40,1024]{2,1,0:T(8,128)(2,1)S(1)}, bf16[4,40,1024]{2,1,0:T(8,128)(2,1)S(1)}, u32[]{:S(2)}, u32[]{:S(2)}) %collective-permute-start.56) | collective-permute-done | bytes 327712 | tf_op jit(solution)/shard_map/ppermute | solution.py:632
  370.2 2.4 collective-permute-start.53
  372.8 2.2 copy.38
  375.4 2.6 bitcast_convert_fusion.1
  378.0 13.1 %collective-permute-done.53 = bf16[4,32,3072]{2,1,0:T(8,128)(2,1)S(1)} collective-permute-done((bf16[4,32,3072]{2,1,0:T(8,128)(2,1)S(1)}, bf16[4,32,3072]{2,1,0:T(8,128)(2,1)S(1)}, u32[]{:S(2)}, u32[]{:S(2)}) %collective-permute-start.53) | collective-permute-done | bytes 786464 | tf_op jit(solution)/shard_map/ppermute | solution.py:632
  391.4 2.1 bitcast_convert_fusion.2
  (365 shorter events, 95.9 us)
Async XLA Ops:
  4.0 28.6 %collective-permute-start.2 = (bf16[304,1024]{1,0:T(8,128)(2,1)}, bf16[304,1024]{1,0:T(8,128)(2,1)}, u32[]{:S(2)}, u32[]{:S(2)}) collective-permute-start(bf16[304,1024]{1,0:T(8,128)(2,1)} %pad_maximum_fusion.2), channel_id=1, source_target_pairs={{4,16},{12,24},{16,4},{24,12},{5,17},{13,25},{17,5},{25,13},{6,18}... | collective-permute-start | bytes 1867784 | tf_op jit(solution)/shard_map/ppermute | solution.py:644
  9.9 20.2 %collective-permute-start.4 = (bf16[128,1536]{1,0:T(8,128)(2,1)}, bf16[128,1536]{1,0:T(8,128)(2,1)}, u32[]{:S(2)}, u32[]{:S(2)}) collective-permute-start(bf16[128,1536]{1,0:T(8,128)(2,1)} %get-tuple-element.96), channel_id=1, source_target_pairs={{0,8},{4,12},{8,0},{12,4},{1,9},{5,13},{9,1},{13,5},{2,10},{6,14},... | collective-permute-start | bytes 1179656 | tf_op jit(solution)/shard_map/ppermute | solution.py:625
  12.9 26.4 %collective-permute-start.6 = (bf16[128,1536]{1,0:T(8,128)(2,1)}, bf16[128,1536]{1,0:T(8,128)(2,1)}, u32[]{:S(2)}, u32[]{:S(2)}) collective-permute-start(bf16[128,1536]{1,0:T(8,128)(2,1)} %get-tuple-element.97), channel_id=1, source_target_pairs={{0,12},{4,8},{8,4},{12,0},{1,13},{5,9},{9,5},{13,1},{2,14},{6,10},... | collective-permute-start | bytes 1179656 | tf_op jit(solution)/shard_map/ppermute | solution.py:629
  15.7 14.4 %collective-permute-start = (bf16[16,256]{1,0:T(8,128)(2,1)}, bf16[16,256]{1,0:T(8,128)(2,1)}, u32[]{:S(2)}, u32[]{:S(2)}) collective-permute-start(bf16[16,256]{1,0:T(8,128)(2,1)} %select_select_fusion), channel_id=1, source_target_pairs={{0,8},{4,12},{8,0},{12,4},{1,9},{5,13},{9,1},{13,5},{2,10},{6,14},... | collective-permute-start | bytes 24584 | tf_op jit(solution)/shard_map/ppermute | solution.py:625
  19.3 21.1 %collective-permute-start.10 = (bf16[256,1536]{1,0:T(8,128)(2,1)S(1)}, bf16[256,1536]{1,0:T(8,128)(2,1)}, u32[]{:S(2)}, u32[]{:S(2)}) collective-permute-start(bf16[256,1536]{1,0:T(8,128)(2,1)S(1)} %get-tuple-element.117), channel_id=1, source_target_pairs={{0,4},{4,0},{8,12},{12,8},{1,5},{5,1},{9,13},{13,9},{2,6},{6,2},{1... | collective-permute-start | bytes 2359304 | tf_op jit(solution)/shard_map/ppermute | solution.py:622
  30.1 10.2 %collective-permute-start.5 = (bf16[256,2048]{1,0:T(8,128)(2,1)S(1)}, bf16[256,2048]{1,0:T(8,128)(2,1)S(1)}, u32[]{:S(2)}, u32[]{:S(2)}) collective-permute-start(bf16[256,2048]{1,0:T(8,128)(2,1)S(1)} %get-tuple-element.106), channel_id=1, source_target_pairs={{0,4},{4,0},{8,12},{12,8},{1,5},{5,1},{9,13},{13,9},{2,6},{6,2},{1... | collective-permute-start | bytes 3145736 | tf_op jit(solution)/shard_map/ppermute | solution.py:622
  32.5 2.1 collective-permute-start.1
  33.9 6.5 %collective-permute-start.3 = (bf16[304,1024]{1,0:T(8,128)(2,1)S(1)}, bf16[304,1024]{1,0:T(8,128)(2,1)}, u32[]{:S(2)}, u32[]{:S(2)}) collective-permute-start(bf16[304,1024]{1,0:T(8,128)(2,1)S(1)} %broadcast_select_fusion.1.own_ref), channel_id=1, source_target_pairs={{0,4},{4,0},{8,12},{12,8},{1,5},{5,1},{9,13},{13,9},{2,6},{6,2},{1... | collective-permute-start | bytes 1867784 | tf_op jit(solution)/shard_map/ppermute | solution.py:622
  38.3 16.5 %collective-permute-start.11 = (bf16[128,1536]{1,0:T(8,128)(2,1)}, bf16[128,1536]{1,0:T(8,128)(2,1)}, u32[]{:S(2)}, u32[]{:S(2)}) collective-permute-start(bf16[128,1536]{1,0:T(8,128)(2,1)} %collective-permute-done.4.refs_2_), channel_id=1, source_target_pairs={{0,16},{16,0},{1,17},{17,1},{2,18},{18,2},{3,19},{19,3},{4,20},{20... | collective-permute-start | bytes 1179656 | tf_op jit(solution)/shard_map/ppermute | solution.py:632
  39.3 19.8 %collective-permute-start.12 = (bf16[128,1536]{1,0:T(8,128)(2,1)}, bf16[128,1536]{1,0:T(8,128)(2,1)}, u32[]{:S(2)}, u32[]{:S(2)}) collective-permute-start(bf16[128,1536]{1,0:T(8,128)(2,1)} %collective-permute-done.6.refs_4_), channel_id=1, source_target_pairs={{0,16},{16,0},{1,17},{17,1},{2,18},{18,2},{3,19},{19,3},{4,20},{20... | collective-permute-start | bytes 1179656 | tf_op jit(solution)/shard_map/ppermute | solution.py:632
  43.9 8.3 %collective-permute-start.7 = (bf16[128,1024]{1,0:T(8,128)(2,1)}, bf16[128,1024]{1,0:T(8,128)(2,1)}, u32[]{:S(2)}, u32[]{:S(2)}) collective-permute-start(bf16[128,1024]{1,0:T(8,128)(2,1)} %dynamic-slice_bitcast_fusion.9), channel_id=1, source_target_pairs={{0,8},{4,12},{8,0},{12,4},{1,9},{5,13},{9,1},{13,5},{2,10},{6,14},... | collective-permute-start | bytes 786440 | tf_op jit(solution)/shard_map/ppermute | solution.py:625
  48.1 21.8 %copy-start.22 = (bf16[608,1024]{1,0:T(8,128)(2,1)}, bf16[608,1024]{1,0:T(8,128)(2,1)S(1)}, u32[]{:S(2)}) copy-start(bf16[608,1024]{1,0:T(8,128)(2,1)S(1)} %get-tuple-element.100.note_ref.image_ref) | copy-start | bytes 3735556
  51.7 15.2 %collective-permute-start.9 = (bf16[128,2048]{1,0:T(8,128)(2,1)}, bf16[128,2048]{1,0:T(8,128)(2,1)}, u32[]{:S(2)}, u32[]{:S(2)}) collective-permute-start(bf16[128,2048]{1,0:T(8,128)(2,1)} %pair_part.1), channel_id=1, source_target_pairs={{0,8},{4,12},{8,0},{12,4},{1,9},{5,13},{9,1},{13,5},{2,10},{6,14},... | collective-permute-start | bytes 1572872 | tf_op jit(solution)/shard_map/ppermute | solution.py:625
  52.2 27.9 %collective-permute-start.13 = (bf16[128,1024]{1,0:T(8,128)(2,1)}, bf16[128,1024]{1,0:T(8,128)(2,1)}, u32[]{:S(2)}, u32[]{:S(2)}) collective-permute-start(bf16[128,1024]{1,0:T(8,128)(2,1)} %collective-permute-done.7.refs_1_), channel_id=1, source_target_pairs={{0,16},{16,0},{1,17},{17,1},{2,18},{18,2},{3,19},{19,3},{4,20},{20... | collective-permute-start | bytes 786440 | tf_op jit(solution)/shard_map/ppermute | solution.py:632
  53.3 30.7 %collective-permute-start.8 = (bf16[256,1024]{1,0:T(8,128)(2,1)}, bf16[256,1024]{1,0:T(8,128)(2,1)}, u32[]{:S(2)}, u32[]{:S(2)}) collective-permute-start(bf16[256,1024]{1,0:T(8,128)(2,1)} %get-tuple-element.111), channel_id=1, source_target_pairs={{0,8},{4,12},{8,0},{12,4},{1,9},{5,13},{9,1},{13,5},{2,10},{6,14},... | collective-permute-start | bytes 1572872 | tf_op jit(solution)/shard_map/ppermute | solution.py:625
  65.4 18.6 %collective-permute-start.16 = (bf16[304,1024]{1,0:T(8,128)(2,1)}, bf16[304,1024]{1,0:T(8,128)(2,1)}, u32[]{:S(2)}, u32[]{:S(2)}) collective-permute-start(bf16[304,1024]{1,0:T(8,128)(2,1)} %concatenate.96), channel_id=1, source_target_pairs={{4,16},{12,24},{16,4},{24,12},{5,17},{13,25},{17,5},{25,13},{6,18}... | collective-permute-start | bytes 1867784 | tf_op jit(solution)/shard_map/ppermute | solution.py:644
  66.9 21.3 %collective-permute-start.18 = (bf16[128,2048]{1,0:T(8,128)(2,1)}, bf16[128,2048]{1,0:T(8,128)(2,1)}, u32[]{:S(2)}, u32[]{:S(2)}) collective-permute-start(bf16[128,2048]{1,0:T(8,128)(2,1)} %collective-permute-done.9.refs_2_), channel_id=1, source_target_pairs={{0,16},{16,0},{1,17},{17,1},{2,18},{18,2},{3,19},{19,3},{4,20},{20... | collective-permute-start | bytes 1572872 | tf_op jit(solution)/shard_map/ppermute | solution.py:632
  68.3 22.5 %collective-permute-start.20 = (bf16[128,2048]{1,0:T(8,128)(2,1)}, bf16[128,2048]{1,0:T(8,128)(2,1)}, u32[]{:S(2)}, u32[]{:S(2)}) collective-permute-start(bf16[128,2048]{1,0:T(8,128)(2,1)} %collective-permute-done.9.refs_2_), channel_id=1, source_target_pairs={{0,1},{1,0},{2,3},{3,2},{4,5},{5,4},{6,7},{7,6},{8,9},{9,8},{10,11... | collective-permute-start | bytes 1572872 | tf_op jit(solution)/shard_map/ppermute | solution.py:635
  84.0 20.4 %collective-permute-start.14 = (bf16[608,1024]{1,0:T(8,128)(2,1)S(1)}, bf16[608,1024]{1,0:T(8,128)(2,1)S(1)}, u32[]{:S(2)}, u32[]{:S(2)}) collective-permute-start(bf16[608,1024]{1,0:T(8,128)(2,1)S(1)} %get-tuple-element.122.own_ref), channel_id=1, source_target_pairs={{0,4},{4,0},{8,12},{12,8},{1,5},{5,1},{9,13},{13,9},{2,6},{6,2},{1... | collective-permute-start | bytes 3735560 | tf_op jit(solution)/shard_map/ppermute | solution.py:622
  85.1 17.3 %collective-permute-start.17 = (bf16[304,1024]{1,0:T(8,128)(2,1)}, bf16[304,1024]{1,0:T(8,128)(2,1)}, u32[]{:S(2)}, u32[]{:S(2)}) collective-permute-start(bf16[304,1024]{1,0:T(8,128)(2,1)} %broadcast_select_fusion), channel_id=1, source_target_pairs={{0,4},{4,0},{8,12},{12,8},{1,5},{5,1},{9,13},{13,9},{2,6},{6,2},{1... | collective-permute-start | bytes 1867784 | tf_op jit(solution)/shard_map/ppermute | solution.py:622
  86.7 14.1 %collective-permute-start.15 = (bf16[256,1024]{1,0:T(8,128)(2,1)}, bf16[256,1024]{1,0:T(8,128)(2,1)}, u32[]{:S(2)}, u32[]{:S(2)}) collective-permute-start(bf16[256,1024]{1,0:T(8,128)(2,1)} %get-tuple-element.124), channel_id=1, source_target_pairs={{0,8},{4,12},{8,0},{12,4},{1,9},{5,13},{9,1},{13,5},{2,10},{6,14},... | collective-permute-start | bytes 1572872 | tf_op jit(solution)/shard_map/ppermute | solution.py:625
  88.3 16.1 %collective-permute-start.19 = (bf16[128,2048]{1,0:T(8,128)(2,1)}, bf16[128,2048]{1,0:T(8,128)(2,1)S(1)}, u32[]{:S(2)}, u32[]{:S(2)}) collective-permute-start(bf16[128,2048]{1,0:T(8,128)(2,1)} %collective-permute-done.18.refs_4_), channel_id=1, source_target_pairs={{0,1},{1,0},{2,3},{3,2},{4,5},{5,4},{6,7},{7,6},{8,9},{9,8},{10,11... | collective-permute-start | bytes 1572872 | tf_op jit(solution)/shard_map/ppermute | solution.py:635
  90.8 32.3 %collective-permute-start.21 = (bf16[256,1024]{1,0:T(8,128)(2,1)}, bf16[256,1024]{1,0:T(8,128)(2,1)}, u32[]{:S(2)}, u32[]{:S(2)}) collective-permute-start(bf16[256,1024]{1,0:T(8,128)(2,1)} %collective-permute-done.8.refs_0_), channel_id=1, source_target_pairs={{0,16},{16,0},{1,17},{17,1},{2,18},{18,2},{3,19},{19,3},{4,20},{20... | collective-permute-start | bytes 1572872 | tf_op jit(solution)/shard_map/ppermute | solution.py:632
  100.8 22.3 %collective-permute-start.22 = (bf16[256,1024]{1,0:T(8,128)(2,1)}, bf16[256,1024]{1,0:T(8,128)(2,1)}, u32[]{:S(2)}, u32[]{:S(2)}) collective-permute-start(bf16[256,1024]{1,0:T(8,128)(2,1)} %collective-permute-done.15.refs_2_), channel_id=1, source_target_pairs={{0,16},{16,0},{1,17},{17,1},{2,18},{18,2},{3,19},{19,3},{4,20},{20... | collective-permute-start | bytes 1572872 | tf_op jit(solution)/shard_map/ppermute | solution.py:632
  106.5 38.9 %copy-start.25 = (bf16[608,1024]{1,0:T(8,128)(2,1)}, bf16[608,1024]{1,0:T(8,128)(2,1)S(1)}, u32[]{:S(2)}) copy-start(bf16[608,1024]{1,0:T(8,128)(2,1)S(1)} %get-tuple-element.129.left_ref) | copy-start | bytes 3735556
  119.4 32.7 %collective-permute-start.24 = (bf16[512,1024]{1,0:T(8,128)(2,1)}, bf16[512,1024]{1,0:T(8,128)(2,1)}, u32[]{:S(2)}, u32[]{:S(2)}) collective-permute-start(bf16[512,1024]{1,0:T(8,128)(2,1)} %weight_grad.12), channel_id=1, source_target_pairs={{0,8},{4,12},{8,0},{12,4},{1,9},{5,13},{9,1},{13,5},{2,10},{6,14},... | collective-permute-start | bytes 3145736 | tf_op jit(solution)/shard_map/ppermute | solution.py:625
  137.1 12.2 %collective-permute-start.23 = (bf16[304,1024]{1,0:T(8,128)(2,1)}, bf16[304,1024]{1,0:T(8,128)(2,1)}, u32[]{:S(2)}, u32[]{:S(2)}) collective-permute-start(bf16[304,1024]{1,0:T(8,128)(2,1)} %dynamic-slice_bitcast_fusion), channel_id=1, source_target_pairs={{0,4},{4,0},{8,12},{12,8},{1,5},{5,1},{9,13},{13,9},{2,6},{6,2},{1... | collective-permute-start | bytes 1867784 | tf_op jit(solution)/shard_map/ppermute | solution.py:622
  144.5 12.9 %collective-permute-start.25 = (bf16[608,1024]{1,0:T(8,128)(2,1)}, bf16[608,1024]{1,0:T(8,128)(2,1)}, u32[]{:S(2)}, u32[]{:S(2)}) collective-permute-start(bf16[608,1024]{1,0:T(8,128)(2,1)} %grad_second.1.own_ref), channel_id=1, source_target_pairs={{0,4},{4,0},{8,12},{12,8},{1,5},{5,1},{9,13},{13,9},{2,6},{6,2},{1... | collective-permute-start | bytes 3735560 | tf_op jit(solution)/shard_map/ppermute | solution.py:622
  145.0 44.5 %collective-permute-start.26 = (bf16[512,1024]{1,0:T(8,128)(2,1)}, bf16[512,1024]{1,0:T(8,128)(2,1)}, u32[]{:S(2)}, u32[]{:S(2)}) collective-permute-start(bf16[512,1024]{1,0:T(8,128)(2,1)} %weight_grad.14), channel_id=1, source_target_pairs={{0,8},{4,12},{8,0},{12,4},{1,9},{5,13},{9,1},{13,5},{2,10},{6,14},... | collective-permute-start | bytes 3145736 | tf_op jit(solution)/shard_map/ppermute | solution.py:625
  155.4 34.1 %collective-permute-start.27 = (bf16[512,1024]{1,0:T(8,128)(2,1)}, bf16[512,1024]{1,0:T(8,128)(2,1)}, u32[]{:S(2)}, u32[]{:S(2)}) collective-permute-start(bf16[512,1024]{1,0:T(8,128)(2,1)} %weight_grad.13), channel_id=1, source_target_pairs={{0,16},{16,0},{1,17},{17,1},{2,18},{18,2},{3,19},{19,3},{4,20},{20... | collective-permute-start | bytes 3145736 | tf_op jit(solution)/shard_map/ppermute | solution.py:632
  155.9 38.5 %collective-permute-start.36 = (bf16[256,2048]{1,0:T(8,128)(2,1)}, bf16[256,2048]{1,0:T(8,128)(2,1)}, u32[]{:S(2)}, u32[]{:S(2)}) collective-permute-start(bf16[256,2048]{1,0:T(8,128)(2,1)} %weight_grad.21), channel_id=1, source_target_pairs={{0,8},{4,12},{8,0},{12,4},{1,9},{5,13},{9,1},{13,5},{2,10},{6,14},... | collective-permute-start | bytes 3145736 | tf_op jit(solution)/shard_map/ppermute | solution.py:625
  185.6 15.2 %collective-permute-start.28 = (bf16[608,1024]{1,0:T(8,128)(2,1)}, bf16[608,1024]{1,0:T(8,128)(2,1)}, u32[]{:S(2)}, u32[]{:S(2)}) collective-permute-start(bf16[608,1024]{1,0:T(8,128)(2,1)} %grad_first.1.own_ref), channel_id=1, source_target_pairs={{0,4},{4,0},{8,12},{12,8},{1,5},{5,1},{9,13},{13,9},{2,6},{6,2},{1... | collective-permute-start | bytes 3735560 | tf_op jit(solution)/shard_map/ppermute | solution.py:622
  193.4 14.6 %collective-permute-start.29 = (bf16[1,2,128,1024]{3,2,1,0:T(8,128)(2,1)}, bf16[1,2,128,1024]{3,2,1,0:T(8,128)(2,1)}, u32[]{:S(2)}, u32[]{:S(2)}) collective-permute-start(bf16[1,2,128,1024]{3,2,1,0:T(8,128)(2,1)} %get-tuple-element.189), channel_id=1, source_target_pairs={{0,1},{1,0},{2,3},{3,2},{4,5},{5,4},{6,7},{7,6},{8,9},{9,8},{10,11... | collective-permute-start | bytes 1572872 | tf_op jit(solution)/shard_map/ppermute | solution.py:635
  193.8 38.0 %collective-permute-start.35 = (bf16[256,2048]{1,0:T(8,128)(2,1)}, bf16[256,2048]{1,0:T(8,128)(2,1)}, u32[]{:S(2)}, u32[]{:S(2)}) collective-permute-start(bf16[256,2048]{1,0:T(8,128)(2,1)} %weight_grad.16), channel_id=1, source_target_pairs={{0,8},{4,12},{8,0},{12,4},{1,9},{5,13},{9,1},{13,5},{2,10},{6,14},... | collective-permute-start | bytes 3145736 | tf_op jit(solution)/shard_map/ppermute | solution.py:625
  199.2 32.6 %collective-permute-start.37 = (bf16[256,2048]{1,0:T(8,128)(2,1)}, bf16[256,2048]{1,0:T(8,128)(2,1)}, u32[]{:S(2)}, u32[]{:S(2)}) collective-permute-start(bf16[256,2048]{1,0:T(8,128)(2,1)} %weight_grad.22), channel_id=1, source_target_pairs={{0,16},{16,0},{1,17},{17,1},{2,18},{18,2},{3,19},{19,3},{4,20},{20... | collective-permute-start | bytes 3145736 | tf_op jit(solution)/shard_map/ppermute | solution.py:632
  210.0 14.9 %collective-permute-start.30 = (bf16[1,1,128,1024]{3,2,1,0:T(8,128)(2,1)}, bf16[1,1,128,1024]{3,2,1,0:T(8,128)(2,1)}, u32[]{:S(2)}, u32[]{:S(2)}) collective-permute-start(bf16[1,1,128,1024]{3,2,1,0:T(8,128)(2,1)} %get-tuple-element.195), channel_id=1, source_target_pairs={{0,2},{1,3},{2,0},{3,1},{4,6},{5,7},{6,4},{7,5},{8,10},{9,11},{10,... | collective-permute-start | bytes 786440 | tf_op jit(solution)/shard_map/ppermute | solution.py:635
  213.6 36.5 %collective-permute-start.32 = (bf16[256,1536]{1,0:T(8,128)(2,1)}, bf16[256,1536]{1,0:T(8,128)(2,1)}, u32[]{:S(2)}, u32[]{:S(2)}) collective-permute-start(bf16[256,1536]{1,0:T(8,128)(2,1)} %weight_grad.18), channel_id=1, source_target_pairs={{0,8},{4,12},{8,0},{12,4},{1,9},{5,13},{9,1},{13,5},{2,10},{6,14},... | collective-permute-start | bytes 2359304 | tf_op jit(solution)/shard_map/ppermute | solution.py:625
  230.5 14.3 %collective-permute-start.59 = (bf16[1,128,1024]{2,1,0:T(8,128)(2,1)}, bf16[1,128,1024]{2,1,0:T(8,128)(2,1)}, u32[]{:S(2)}, u32[]{:S(2)}) collective-permute-start(bf16[1,128,1024]{2,1,0:T(8,128)(2,1)} %bitcast.114), channel_id=1, source_target_pairs={{0,2},{1,3},{2,0},{3,1},{4,6},{5,7},{6,4},{7,5},{8,10},{9,11},{10,... | collective-permute-start | bytes 786440 | tf_op jit(solution)/shard_map/ppermute | solution.py:635
  230.5 48.4 %collective-permute-start.31 = (bf16[256,1536]{1,0:T(8,128)(2,1)}, bf16[256,1536]{1,0:T(8,128)(2,1)}, u32[]{:S(2)}, u32[]{:S(2)}) collective-permute-start(bf16[256,1536]{1,0:T(8,128)(2,1)} %weight_grad.17), channel_id=1, source_target_pairs={{0,8},{4,12},{8,0},{12,4},{1,9},{5,13},{9,1},{13,5},{2,10},{6,14},... | collective-permute-start | bytes 2359304 | tf_op jit(solution)/shard_map/ppermute | solution.py:625
  237.9 18.5 %collective-permute-start.42 = (bf16[2,2,32,2048]{3,2,1,0:T(8,128)(2,1)}, bf16[2,2,32,2048]{3,2,1,0:T(8,128)(2,1)}, u32[]{:S(2)}, u32[]{:S(2)}) collective-permute-start(bf16[2,2,32,2048]{3,2,1,0:T(8,128)(2,1)} %get-tuple-element.191), channel_id=1, source_target_pairs={{0,1},{1,0},{2,3},{3,2},{4,5},{5,4},{6,7},{7,6},{8,9},{9,8},{10,11... | collective-permute-start | bytes 1572872 | tf_op jit(solution)/shard_map/ppermute | solution.py:635
  246.9 27.4 %collective-permute-start.60 = (bf16[2,128,1024]{2,1,0:T(8,128)(2,1)}, bf16[2,128,1024]{2,1,0:T(8,128)(2,1)}, u32[]{:S(2)}, u32[]{:S(2)}) collective-permute-start(bf16[2,128,1024]{2,1,0:T(8,128)(2,1)} %maximum_select_fusion.10), channel_id=1, source_target_pairs={{0,1},{1,0},{2,3},{3,2},{4,5},{5,4},{6,7},{7,6},{8,9},{9,8},{10,11... | collective-permute-start | bytes 1572872 | tf_op jit(solution)/shard_map/ppermute | solution.py:635
  246.9 13.7 %collective-permute-start.38 = (bf16[160,1024]{1,0:T(8,128)(2,1)}, bf16[160,1024]{1,0:T(8,128)(2,1)}, u32[]{:S(2)}, u32[]{:S(2)}) collective-permute-start(bf16[160,1024]{1,0:T(8,128)(2,1)} %out_grad.4), channel_id=1, source_target_pairs={{0,8},{4,12},{8,0},{12,4},{1,9},{5,13},{9,1},{13,5},{2,10},{6,14},... | collective-permute-start | bytes 983048 | tf_op jit(solution)/shard_map/ppermute | solution.py:625
  255.7 23.1 %collective-permute-start.33 = (bf16[256,1536]{1,0:T(8,128)(2,1)}, bf16[256,1536]{1,0:T(8,128)(2,1)}, u32[]{:S(2)}, u32[]{:S(2)}) collective-permute-start(bf16[256,1536]{1,0:T(8,128)(2,1)} %weight_grad.19), channel_id=1, source_target_pairs={{0,16},{16,0},{1,17},{17,1},{2,18},{18,2},{3,19},{19,3},{4,20},{20... | collective-permute-start | bytes 2359304 | tf_op jit(solution)/shard_map/ppermute | solution.py:632
  258.5 14.6 %collective-permute-start.43 = (bf16[2,1,32,2048]{3,2,1,0:T(8,128)(2,1)}, bf16[2,1,32,2048]{3,2,1,0:T(8,128)(2,1)}, u32[]{:S(2)}, u32[]{:S(2)}) collective-permute-start(bf16[2,1,32,2048]{3,2,1,0:T(8,128)(2,1)} %get-tuple-element.197), channel_id=1, source_target_pairs={{0,2},{1,3},{2,0},{3,1},{4,6},{5,7},{6,4},{7,5},{8,10},{9,11},{10,... | collective-permute-start | bytes 786440 | tf_op jit(solution)/shard_map/ppermute | solution.py:635
  263.3 34.7 %collective-permute-start.39 = (bf16[160,1024]{1,0:T(8,128)(2,1)}, bf16[160,1024]{1,0:T(8,128)(2,1)}, u32[]{:S(2)}, u32[]{:S(2)}) collective-permute-start(bf16[160,1024]{1,0:T(8,128)(2,1)} %out_grad.6), channel_id=1, source_target_pairs={{0,16},{16,0},{1,17},{17,1},{2,18},{18,2},{3,19},{19,3},{4,20},{20... | collective-permute-start | bytes 983048 | tf_op jit(solution)/shard_map/ppermute | solution.py:632
  274.2 3.8 collective-permute-start.44
  276.8 44.3 %collective-permute-start.61 = (bf16[4,128,1024]{2,1,0:T(8,128)(2,1)}, bf16[4,128,1024]{2,1,0:T(8,128)(2,1)}, u32[]{:S(2)}, u32[]{:S(2)}) collective-permute-start(bf16[4,128,1024]{2,1,0:T(8,128)(2,1)} %bitcast.120), channel_id=1, source_target_pairs={{0,16},{16,0},{1,17},{17,1},{2,18},{18,2},{3,19},{19,3},{4,20},{20... | collective-permute-start | bytes 3145736 | tf_op jit(solution)/shard_map/ppermute | solution.py:632
  278.9 14.9 %collective-permute-start.45 = (bf16[1,32,4096]{2,1,0:T(8,128)(2,1)}, bf16[1,32,4096]{2,1,0:T(8,128)(2,1)}, u32[]{:S(2)}, u32[]{:S(2)}) collective-permute-start(bf16[1,32,4096]{2,1,0:T(8,128)(2,1)} %get-tuple-element.203), channel_id=1, source_target_pairs={{0,2},{1,3},{2,0},{3,1},{4,6},{5,7},{6,4},{7,5},{8,10},{9,11},{10,... | collective-permute-start | bytes 786440 | tf_op jit(solution)/shard_map/ppermute | solution.py:635
  285.0 18.5 %collective-permute-start.47 = (bf16[2,2,32,1536]{3,2,1,0:T(8,128)(2,1)}, bf16[2,2,32,1536]{3,2,1,0:T(8,128)(2,1)}, u32[]{:S(2)}, u32[]{:S(2)}) collective-permute-start(bf16[2,2,32,1536]{3,2,1,0:T(8,128)(2,1)} %get-tuple-element.193), channel_id=1, source_target_pairs={{0,1},{1,0},{2,3},{3,2},{4,5},{5,4},{6,7},{7,6},{8,9},{9,8},{10,11... | collective-permute-start | bytes 1179656 | tf_op jit(solution)/shard_map/ppermute | solution.py:635
  287.8 11.7 %collective-permute-start.34 = (bf16[160,1024]{1,0:T(8,128)(2,1)S(1)}, bf16[160,1024]{1,0:T(8,128)(2,1)S(1)}, u32[]{:S(2)}, u32[]{:S(2)}) collective-permute-start(bf16[160,1024]{1,0:T(8,128)(2,1)S(1)} %out_grad.5), channel_id=1, source_target_pairs={{0,8},{4,12},{8,0},{12,4},{1,9},{5,13},{9,1},{13,5},{2,10},{6,14},... | collective-permute-start | bytes 983048 | tf_op jit(solution)/shard_map/ppermute | solution.py:625
  295.9 38.4 %collective-permute-start.57 = (bf16[2,32,4096]{2,1,0:T(8,128)(2,1)}, bf16[2,32,4096]{2,1,0:T(8,128)(2,1)}, u32[]{:S(2)}, u32[]{:S(2)}) collective-permute-start(bf16[2,32,4096]{2,1,0:T(8,128)(2,1)} %maximum_select_fusion.8), channel_id=1, source_target_pairs={{0,1},{1,0},{2,3},{3,2},{4,5},{5,4},{6,7},{7,6},{8,9},{9,8},{10,11... | collective-permute-start | bytes 1572872 | tf_op jit(solution)/shard_map/ppermute | solution.py:635
  297.9 41.5 %collective-permute-start.46 = (bf16[304,1024]{1,0:T(8,128)(2,1)}, bf16[304,1024]{1,0:T(8,128)(2,1)}, u32[]{:S(2)}, u32[]{:S(2)}) collective-permute-start(bf16[304,1024]{1,0:T(8,128)(2,1)} %add_convert_fusion), channel_id=1, source_target_pairs={{4,16},{12,24},{16,4},{24,12},{5,17},{13,25},{17,5},{25,13},{6,18}... | collective-permute-start | bytes 1867784 | tf_op jit(solution)/shard_map/ppermute | solution.py:644
  301.4 19.5 %collective-permute-start.40 = (bf16[1,2,40,1024]{3,2,1,0:T(8,128)(2,1)S(1)}, bf16[1,2,40,1024]{3,2,1,0:T(8,128)(2,1)S(1)}, u32[]{:S(2)}, u32[]{:S(2)}) collective-permute-start(bf16[1,2,40,1024]{3,2,1,0:T(8,128)(2,1)S(1)} %get-tuple-element.201), channel_id=1, source_target_pairs={{0,1},{1,0},{2,3},{3,2},{4,5},{5,4},{6,7},{7,6},{8,9},{9,8},{10,11... | collective-permute-start | bytes 491528 | tf_op jit(solution)/shard_map/ppermute | solution.py:635
  304.7 24.6 %collective-permute-start.48 = (bf16[2,1,32,1536]{3,2,1,0:T(8,128)(2,1)S(1)}, bf16[2,1,32,1536]{3,2,1,0:T(8,128)(2,1)S(1)}, u32[]{:S(2)}, u32[]{:S(2)}) collective-permute-start(bf16[2,1,32,1536]{3,2,1,0:T(8,128)(2,1)S(1)} %get-tuple-element.199), channel_id=1, source_target_pairs={{0,2},{1,3},{2,0},{3,1},{4,6},{5,7},{6,4},{7,5},{8,10},{9,11},{10,... | collective-permute-start | bytes 589832 | tf_op jit(solution)/shard_map/ppermute | solution.py:635
  321.0 6.2 %collective-permute-start.41 = (bf16[1,1,40,1024]{3,2,1,0:T(8,128)(2,1)S(1)}, bf16[1,1,40,1024]{3,2,1,0:T(8,128)(2,1)S(1)}, u32[]{:S(2)}, u32[]{:S(2)}) collective-permute-start(bf16[1,1,40,1024]{3,2,1,0:T(8,128)(2,1)S(1)} %get-tuple-element.213), channel_id=1, source_target_pairs={{0,2},{1,3},{2,0},{3,1},{4,6},{5,7},{6,4},{7,5},{8,10},{9,11},{10,... | collective-permute-start | bytes 245768 | tf_op jit(solution)/shard_map/ppermute | solution.py:635
  327.2 7.1 %collective-permute-start.54 = (bf16[1,40,1024]{2,1,0:T(8,128)(2,1)S(1)}, bf16[1,40,1024]{2,1,0:T(8,128)(2,1)S(1)}, u32[]{:S(2)}, u32[]{:S(2)}) collective-permute-start(bf16[1,40,1024]{2,1,0:T(8,128)(2,1)S(1)} %bitcast.224), channel_id=1, source_target_pairs={{0,2},{1,3},{2,0},{3,1},{4,6},{5,7},{6,4},{7,5},{8,10},{9,11},{10,... | collective-permute-start | bytes 245768 | tf_op jit(solution)/shard_map/ppermute | solution.py:635
  329.4 7.5 %collective-permute-start.49 = (bf16[32,1536]{1,0:T(8,128)(2,1)S(1)}, bf16[32,1536]{1,0:T(8,128)(2,1)S(1)}, u32[]{:S(2)}, u32[]{:S(2)}) collective-permute-start(bf16[32,1536]{1,0:T(8,128)(2,1)S(1)} %get-tuple-element.210), channel_id=1, source_target_pairs={{0,4},{4,0},{8,12},{12,8},{1,5},{5,1},{9,13},{13,9},{2,6},{6,2},{1... | collective-permute-start | bytes 294920 | tf_op jit(solution)/shard_map/ppermute | solution.py:622
  334.3 7.3 %collective-permute-start.55 = (bf16[2,40,1024]{2,1,0:T(8,128)(2,1)S(1)}, bf16[2,40,1024]{2,1,0:T(8,128)(2,1)S(1)}, u32[]{:S(2)}, u32[]{:S(2)}) collective-permute-start(bf16[2,40,1024]{2,1,0:T(8,128)(2,1)S(1)} %maximum_select_fusion.15), channel_id=1, source_target_pairs={{0,1},{1,0},{2,3},{3,2},{4,5},{5,4},{6,7},{7,6},{8,9},{9,8},{10,11... | collective-permute-start | bytes 491528 | tf_op jit(solution)/shard_map/ppermute | solution.py:635
  336.0 39.0 %collective-permute-start.58 = (bf16[4,32,4096]{2,1,0:T(8,128)(2,1)S(1)}, bf16[4,32,4096]{2,1,0:T(8,128)(2,1)S(1)}, u32[]{:S(2)}, u32[]{:S(2)}) collective-permute-start(bf16[4,32,4096]{2,1,0:T(8,128)(2,1)S(1)} %bitcast.207), channel_id=1, source_target_pairs={{0,16},{16,0},{1,17},{17,1},{2,18},{18,2},{3,19},{19,3},{4,20},{20... | collective-permute-start | bytes 3145736 | tf_op jit(solution)/shard_map/ppermute | solution.py:632
  337.1 11.2 %collective-permute-start.50 = (bf16[1,32,3072]{2,1,0:T(8,128)(2,1)S(1)}, bf16[1,32,3072]{2,1,0:T(8,128)(2,1)S(1)}, u32[]{:S(2)}, u32[]{:S(2)}) collective-permute-start(bf16[1,32,3072]{2,1,0:T(8,128)(2,1)S(1)} %bitcast.215), channel_id=1, source_target_pairs={{0,2},{1,3},{2,0},{3,1},{4,6},{5,7},{6,4},{7,5},{8,10},{9,11},{10,... | collective-permute-start | bytes 589832 | tf_op jit(solution)/shard_map/ppermute | solution.py:635
  341.6 26.1 %collective-permute-start.56 = (bf16[4,40,1024]{2,1,0:T(8,128)(2,1)S(1)}, bf16[4,40,1024]{2,1,0:T(8,128)(2,1)S(1)}, u32[]{:S(2)}, u32[]{:S(2)}) collective-permute-start(bf16[4,40,1024]{2,1,0:T(8,128)(2,1)S(1)} %bitcast.222), channel_id=1, source_target_pairs={{0,16},{16,0},{1,17},{17,1},{2,18},{18,2},{3,19},{19,3},{4,20},{20... | collective-permute-start | bytes 983048 | tf_op jit(solution)/shard_map/ppermute | solution.py:632
  348.3 21.7 %collective-permute-start.52 = (bf16[2,32,3072]{2,1,0:T(8,128)(2,1)S(1)}, bf16[2,32,3072]{2,1,0:T(8,128)(2,1)S(1)}, u32[]{:S(2)}, u32[]{:S(2)}) collective-permute-start(bf16[2,32,3072]{2,1,0:T(8,128)(2,1)S(1)} %maximum_select_fusion.12), channel_id=1, source_target_pairs={{0,1},{1,0},{2,3},{3,2},{4,5},{5,4},{6,7},{7,6},{8,9},{9,8},{10,11... | collective-permute-start | bytes 1179656 | tf_op jit(solution)/shard_map/ppermute | solution.py:635
  348.5 24.2 %collective-permute-start.51 = (bf16[304,1024]{1,0:T(8,128)(2,1)S(1)}, bf16[304,1024]{1,0:T(8,128)(2,1)S(1)}, u32[]{:S(2)}, u32[]{:S(2)}) collective-permute-start(bf16[304,1024]{1,0:T(8,128)(2,1)S(1)} %get-tuple-element.170), channel_id=1, source_target_pairs={{4,16},{12,24},{16,4},{24,12},{5,17},{13,25},{17,5},{25,13},{6,18}... | collective-permute-start | bytes 1867784 | tf_op jit(solution)/shard_map/ppermute | solution.py:644
  370.2 21.0 %collective-permute-start.53 = (bf16[4,32,3072]{2,1,0:T(8,128)(2,1)S(1)}, bf16[4,32,3072]{2,1,0:T(8,128)(2,1)S(1)}, u32[]{:S(2)}, u32[]{:S(2)}) collective-permute-start(bf16[4,32,3072]{2,1,0:T(8,128)(2,1)S(1)} %bitcast.209), channel_id=1, source_target_pairs={{0,16},{16,0},{1,17},{17,1},{2,18},{18,2},{3,19},{19,3},{4,20},{20... | collective-permute-start | bytes 2359304 | tf_op jit(solution)/shard_map/ppermute | solution.py:632
  (76 other events, 471.2 us)

commit v4 on v3

--- a/solution.py
+++ b/solution.py
@@ -657,16 +657,25 @@
     length = lengths[0]
     lane = lax.broadcasted_iota(jnp.int32, (padded - rows, width), 1)
     note = jnp.where(lane == 0, length // 16, jnp.where(lane == 1, length % 16, 0)).astype(BF16)
-    own_tokens = line.mark(jnp.concatenate([tokens[0], note], axis=0))
+    own_half = lambda shard: pick(
+        shard.reshape(halves, shard.shape[0] // halves, shard.shape[1]), half
+    )
+    source = lambda k: (column - k) % columns
+    part = owned // halves
+    eighth = owned // halves // 2
+    chunks = 2
+
+    def relay_qkv(index, c):
+        for k in steps:
+            value = line.pass_on(qkv_x[index][k - 1])
+            at = (2 * source(k) + c) * halves
+            qkv_pieces.append((value, 0, part, at + half))
+            qkv_pieces.append((over_y(value), 0, part, at + other_half))
+
+    qkv_x = {}
+
+    own_tokens = line.mark(jnp.concatenate([line.gate(tokens[0]), note], axis=0))
     other_tokens = swap(own_tokens)
-
-    qkv_keep, qkv_send, qkv_part, qkv_cross = line.mark(
-        split_columns(
-            line.gate(numbers(core, half)), qkv_weight, 3 * columns, owned // halves, "split_qkv"
-        )
-    )
-    qkv_x = [(over_x(qkv_part, k), over_x_core(qkv_cross, k)) for k in steps]
-
     singles = [
         query_bias,
         value_bias,
@@ -684,46 +693,38 @@
         vectors = jnp.where(row_of == i, jnp.broadcast_to(single[None], (16, owned)), vectors)
     vectors = line.mark(line.gate(vectors))
     vec_x = [over_x(vectors, k) for k in steps]
-
-    own_half = lambda shard: pick(
-        shard.reshape(halves, shard.shape[0] // halves, shard.shape[1]), half
-    )
-    up_keep, up_send = line.mark(
-        split_columns(line.gate(numbers(core, half)), up_weight, columns, 0, "split_up")
-    )
-    qkv_core = line.pass_on(over_core(line.gate(qkv_send)))
-    source = lambda k: (column - k) % columns
+    qkv_keep, qkv_send, qkv_part, qkv_cross = line.mark(
+        split_columns(
+            line.gate(numbers(core, half)), qkv_weight, 3 * columns, owned // halves, "split_qkv"
+        )
+    )
+    qkv_x[0] = [over_x(qkv_part, k) for k in steps]
+    qkv_x[1] = [over_x_core(line.gate(qkv_cross), k) for k in steps]
+    qkv_core = over_core(line.gate(qkv_send))
+    qkv_core = line.pass_on(qkv_core)
     qkv_pieces = [
         (qkv_keep, 0, owned, member),
         (qkv_core, 0, owned, member + 1 - 2 * core),
     ]
-    part = owned // halves
-
-    def relay_qkv(index, c):
-        for k in steps:
-            value = line.pass_on(qkv_x[k - 1][index])
-            at = (2 * source(k) + c) * halves
-            qkv_pieces.append((value, 0, part, at + half))
-            qkv_pieces.append((over_y(value), 0, part, at + other_half))
-
-    own_image = line.pass_on(jnp.where(half == core, own_tokens, line.pass_on(other_tokens)))
-    other_image = line.pass_on(over_core(own_image))
     relay_qkv(0, core)
-    up_core = line.pass_on(over_core(line.gate(up_send)))
-    eighth = owned // halves // 2
-    up_part = line.mark(pair_part(line.gate(numbers(core, quarter)), up_keep, up_core, eighth))
-    out_part = line.mark(own_half(line.gate(out_weight)))
-    relay_qkv(1, 1 - core)
-    out_x = [over_x(line.gate(out_part), k) for k in steps]
-
+    own_image = line.mark(jnp.where(half == core, own_tokens, line.pass_on(other_tokens)))
+    other_image = over_core(own_image)
+    other_image = line.pass_on(other_image)
+    up_keep, up_send = line.mark(
+        split_columns(line.gate(numbers(core, half)), up_weight, columns, 0, "split_up")
+    )
     gathered_vec = jnp.zeros((columns,) + vectors.shape, BF16)
     gathered_vec = place(gathered_vec, vectors, column)
     for k in steps:
         gathered_vec = place(gathered_vec, line.pass_on(vec_x[k - 1]), (column - k) % columns)
     line.mark(gathered_vec)
-    vec_core = line.pass_on(over_core(gathered_vec))
-    up_x = [over_x(line.gate(up_part), k) for k in steps]
-
+    vec_core = over_core(gathered_vec)
+    up_core = over_core(line.gate(up_send))
+    up_core = line.pass_on(up_core)
+    up_part = line.mark(pair_part(line.gate(numbers(core, quarter)), up_keep, up_core, eighth))
+    out_part = line.mark(own_half(line.gate(out_weight)))
+    out_x = [over_x(line.gate(out_part), k) for k in steps]
+    vec_core = line.pass_on(vec_core)
     mine_vec = gathered_vec.astype(F32)
     all_vec = by_core(gathered_vec, vec_core, 1).reshape(columns * 2, 16, owned)
     all_vec = all_vec.astype(F32)
@@ -735,26 +736,25 @@
     vec_qkv = jnp.concatenate(
         [own_vec(0), jnp.zeros((1, width // 2), F32), own_vec(1)], axis=1
     )
+    up_x = [over_x(line.gate(up_part), k) for k in steps]
     image, first_low = line.mark(
         norm_one(line.gate(numbers(core)), own_image, other_image, gain_one, shift_one)
     )
     own_cotangent = line.mark(
         jnp.concatenate([line.gate(cotangent[0]), jnp.zeros((padded - rows, width), BF16)], axis=0)
     )
-    chunks = 2
-    down_part = line.mark(
-        own_half(line.gate(down_weight)).reshape(chunks, -1, width)
-    )
+    down_part = line.mark(own_half(line.gate(down_weight)).reshape(chunks, -1, width))
+    relay_qkv(1, 1 - core)
     out_pieces = [(out_weight, 0, owned, column)]
     for k in steps:
         value = line.pass_on(out_x[k - 1])
         at = source(k) * halves
         out_pieces += [(value, 0, part, at + half), (over_y(value), 0, part, at + other_half)]
     down_x = [[over_x(line.gate(down_part[0]), k) for k in steps]]
-
     wqkv, qkv = join_dot(
         line, first_low, qkv_pieces, vec_qkv, lambda total: (total,), 1, width // 2, "project"
     )
+
     up_pieces = [(up_keep, 0, owned, member), (up_core, 0, owned, member + 1 - 2 * core)]
 
     def up_rows(value, k, h, s):
@@ -772,7 +772,6 @@
             down_others.append((value, at + half * chunks))
             down_others.append((over_y(value), at + other_half * chunks))
 
-    other_cotangent = swap(line.gate(own_cotangent))
     for k in steps:
         value = line.pass_on(up_x[k - 1])
         up_rows(value, k, half, side)
@@ -783,13 +782,14 @@
         line, mixed, out_pieces, no_bias, lambda total: (total,), 1, width // 2, "project_out"
     )
     branch_other = over_core(branch)
-    for k in steps:
-        up_rows(line.pass_on(up_z[k - 1]), k, half, 1 - side)
+    other_cotangent = swap(line.gate(own_cotangent))
     for k in steps:
         value = line.pass_on(up_y[k - 1])
         up_rows(value, k, other_half, side)
         up_y[k - 1] = over_z(value, 1)
     relay_down(0)
+    for k in steps:
+        up_rows(line.pass_on(up_z[k - 1]), k, half, 1 - side)
     line.tick()
     down_x.append([over_x(line.gate(down_part[1]), k) for k in steps])
     middle, second_low = line.mark(
@@ -807,8 +807,8 @@
     wup, act_low, slope = join_dot(line, second_low, up_pieces, vec_up, activate, 2, 512, "hidden")
 
     class Total:
-        def __init__(self, quadrant, lead, cross):
-            self.quadrant, self.lead, self.cross = quadrant, lead, cross
+        def __init__(self, quadrant, lead, cross, split=False):
+            self.quadrant, self.lead, self.cross, self.split = quadrant, lead, cross, split
             self.crossed = not cross
             self.halving, self.done, self.step = True, False, 1
 
@@ -850,6 +850,13 @@
         def double(self):
             self.step //= 2
             self.from_z = over_z(self.total, self.step)
+            if self.split and self.step == 1:
+                self.early = over_y(self.total)
+
+        def joined(self, own, got):
+            return jnp.where(
+                self.bit() == 0, jnp.stack([own, got], 1), jnp.stack([got, own], 1)
+            ).reshape((-1,) + own.shape[1:])
 
         def turn(self):
             line.tick()
@@ -874,13 +881,14 @@
                 self.total = line.mark(self.cross(own, got))[None]
                 self.double()
             elif self.step:
-                self.total = line.mark(
-                    jnp.where(
-                        self.bit() == 0,
-                        jnp.stack([line.gate(self.total), self.from_z], 1),
-                        jnp.stack([self.from_z, self.total], 1),
-                    ).reshape((-1,) + self.total.shape[1:])
-                )
+                if self.split and self.step == 1:
+                    self.from_z = line.mark(line.gate(self.from_z))
+                    late = over_y(self.from_z)
+                    self.total = self.joined(self.total, self.from_z)
+                    self.from_y = self.joined(self.early, late)
+                    self.step = 0
+                    return
+                self.total = line.mark(self.joined(line.gate(self.total), self.from_z))
                 if self.step > 1:
                     self.double()
                 else:
@@ -952,7 +960,7 @@
         dot_rows(line.gate(numbers(core)), hidden_low, wup, width // 2, "grad_second")
     )
     grad_second_other = over_core(grad_second)
-    total_up = Total(by_row(second_low, hidden_low), 2, cross_cores(columns))
+    total_up = Total(by_row(second_low, hidden_low), 2, cross_cores(columns), True)
     total_up.make_first()
     total_down.third()
     total_up.first()
@@ -964,7 +972,6 @@
     grad_mixed = line.mark(
         dot_rows(line.gate(numbers(core)), branch_low, wout, width // 2, "grad_mixed")
     )
-    total_up.make_second()
     grad_qkv, qv_sums = line.mark(
         attention_grad(line.gate(numbers(core)), image, qkv, grad_mixed, log_total, rows)
     )
@@ -972,9 +979,10 @@
         dot_rows(line.gate(numbers(core)), grad_qkv, wqkv, width // 2, "grad_first")
     )
     grad_first_other = over_core(grad_first)
-    total_qkv = Total(by_row(first_low, grad_qkv), 2, cross_cores(3 * columns))
+    total_qkv = Total(by_row(first_low, grad_qkv), 2, cross_cores(3 * columns), True)
     total_qkv.make_first()
     total_down.fourth()
+    total_up.make_second()
     total_up.second()
     own_grad, own_grad_low, sums_one = line.mark(
         norm_one_back(
@@ -1000,6 +1008,7 @@
     )
     total_out = Total(out_quadrant, 1, None)
     total_out.make_first()
+    total_qkv.make_second()
     total_out.make_second()
     total_down.turn()
     total_qkv.first()
@@ -1008,7 +1017,6 @@
     block = pick(halves_of(middle), core) + pick(halves_of(partial), core).astype(F32)
     block = line.mark((line.gate(block) + from_other.astype(F32) + vec_down).astype(BF16))
     total_down.turn()
-    total_qkv.make_second()
     total_qkv.second()
     total_qkv.third()
     total_up.third()
@@ -1020,10 +1028,10 @@
     total_up.turn()
     grad_down = total_down.finish().reshape(owned_hidden, width)
     total_qkv.fourth()
-    total_out.second()
     total_up.turn()
     total_up.turn()
     block_moved = swap(line.gate(block))
+    total_out.second()
     total_out.third()
     total_out.fourth()
     total_qkv.turn()
@@ -1034,18 +1042,18 @@
     total_qkv.turn()
     moved = swap(line.gate(own_grad_low))
     total_out.turn()
-    block_out = line.mark(jnp.where(half == core, line.gate(block), block_moved)[:rows][None])
     total_qkv.turn()
     total_out.turn()
-    grad_up = total_up.finish().reshape(owned, up_weight.shape[1])
-    token_grad = line.mark(
-        jnp.where(half == core, line.gate(own_grad), moved.astype(F32))[:rows][None]
-    )
+    block_out = line.mark(jnp.where(half == core, line.gate(block), block_moved)[:rows][None])
     grad_qkv_w = total_qkv.finish().reshape(owned, 3 * width)
     total_out.turn()
     out_rows = total_out.finish()
     height = out_rows.shape[2] - 8
     grad_out = out_rows[:, :, :height].reshape(owned, width)
+    token_grad = line.mark(
+        jnp.where(half == core, line.gate(own_grad), moved.astype(F32))[:rows][None]
+    )
+    grad_up = total_up.finish().reshape(owned, up_weight.shape[1])
 
     vec_out_grads = out_rows[:, :, height, : entries // pieces].reshape(entries)
     vec_of = lambda i: vec_out_grads[i * owned : (i + 1) * owned]

time: 400 us -> 383 us (0.958)
  waiting for transfers between devices: 109 us -> 92.2 us
    ppermute x14 -> x16, waiting for transfers between devices: 35.9 us -> 21.3 us  [over_y(): lax.ppermute(value, 'seq', [(i, halves - 1 - i) for i in range(halves)])]
    ppermute x11, starting transfers between devices: 4.7 us -> 14.5 us  [over_core(): return lax.ppermute(value, 'shard', [(i, i ^ 1) for i in range(group)])]
    ppermute x18, starting transfers between devices: 21.8 us -> 14.6 us  [over_z(): return lax.ppermute(value, 'rep', [(i, i ^ step) for i in range(replicas)])]
    ppermute x18, waiting for transfers between devices: 53.4 us -> 47.3 us  [over_z(): return lax.ppermute(value, 'rep', [(i, i ^ step) for i in range(replicas)])]
    ppermute x1, waiting for transfers between devices: 0.01 us -> 5.1 us  [over_x_core(): return lax.ppermute(value, 'shard', pairs)]
    ppermute x14 -> x16, starting transfers between devices: 16.4 us -> 17.1 us  [over_y(): lax.ppermute(value, 'seq', [(i, halves - 1 - i) for i in range(halves)])]
    unnamed x175 -> x145, local copies, waits for them, and re-layouts: 19.3 us -> 20 us
  transfers between devices with their start and end apart: 62 -> 64, of which waited for: 14 -> 21; matrix products, arithmetic and copies ran while one was open for 15% -> 16% of each run, Pallas kernels for 34% -> 35%
where the time goes in v4:
time: 383 us; the launch traced here: 376 us
  Pallas kernels  132 us (34%)
  waiting for transfers between devices  92.2 us (24%)
  starting transfers between devices  68.1 us (18%)
  other arithmetic  44.6 us (12%)
  local copies, waits for them, and re-layouts  35.7 us (9%)
    pallas_call x21, Pallas kernels, run(): pl.pallas_call(body, grid_spec=pltpu.PrefetchScalarGridSpec(num_scalar_pr...  86.7 us
    ppermute x18, waiting for transfers between devices, over_z(): return lax.ppermute(value, 'rep', [(i, i ^ step) for i in range(replicas)])  47.3 us
    pallas_call x12, Pallas kernels, weight_grad(): pl.pallas_call(functools.partial(weight_grad_body, len(added)), grid_spec...  45.8 us
    ppermute x16, waiting for transfers between devices, over_y(): lax.ppermute(value, 'seq', [(i, halves - 1 - i) for i in range(halves)])  21.3 us
    unnamed x145, local copies, waits for them, and re-layouts  20 us
    ppermute x14, waiting for transfers between devices, over_x(): lax.ppermute(value, 'shard', [(i, (i + 2 * step) % group) for i in range(...  17.3 us
    ppermute x16, starting transfers between devices, over_y(): lax.ppermute(value, 'seq', [(i, halves - 1 - i) for i in range(halves)])  17.1 us
    ppermute x14, starting transfers between devices, over_x(): lax.ppermute(value, 'shard', [(i, (i + 2 * step) % group) for i in range(...  15.6 us
  transfers between devices with their start and end apart: 64, of which 21 were waited for; matrix products, arithmetic and copies ran while one was open for 16% of the time, Pallas kernels for 35%

profile of v4, /device:TPU:0, one launch (start us, length us, event | category | flops | bytes accessed | tf_op | source)
XLA Modules:
  0.0 376.3 jit_solution(6126425558334532277)
XLA Ops:
  7.8 3.0 collective-permute-start.2
  12.3 3.0 split_qkv.1
  16.2 2.0 collective-permute-start.8
  31.8 5.1 %collective-permute-done.11.refs_4_ = bf16[128,1536]{1,0:T(8,128)(2,1)} collective-permute-done((bf16[128,1536]{1,0:T(8,128)(2,1)}, bf16[128,1536]{1,0:T(8,128)(2,1)}, u32[]{:S(2)}, u32[]{:S(2)}) %collective-permute-start.11) | collective-permute-done | bytes 393248 | tf_op jit(solution)/shard_map/ppermute | solution.py:629
  42.8 2.7 dynamic-slice_bitcast_fusion.1
  47.5 2.5 collective-permute-done.7.refs_1_
  51.2 6.3 %project.1 = (bf16[1024,1536]{1,0:T(8,128)(2,1)}, bf16[608,1536]{1,0:T(8,128)(2,1)}) custom-call(s32[6]{0:T(128)S(1)} %stack.433.place_ref, bf16[608,1024]{1,0:T(8,128)(2,1)S(1)} %get-tuple-element.109.left_ref, f32[1,1536]{1,0:T(1,128)S(1)} %fusion.5.bias_ref, bf16[256,1536]{1,0:T(8,128)(2,1)S(1)} %copy-done.42, ...), custom_call_target="tpu_custom_call" | custom-call | flops 199999995904 | bytes 20000000 | tf_op jit(solution)/shard_map/project/pallas_call | solution.py:31
  57.5 3.6 collective-permute-done.5.refs_2_
  66.2 8.5 %attention.1 = (bf16[608,512]{1,0:T(8,128)(2,1)S(1)}, f32[4,2,608]{2,1,0:T(2,128)S(1)}) custom-call(s32[1]{0:T(128)} %bitcast.place_ref, bf16[608,1024]{1,0:T(8,128)(2,1)S(1)} %get-tuple-element.105.note_ref.image_ref, bf16[608,1536]{1,0:T(8,128)(2,1)S(1)} %copy-done.20, bf16[608,1536]{1,0:T(8,128)(2,1)S(1)} %copy-done.20, bf16[608,1536]{1,0:T(8,128)(2,1)S(1)} %copy-done.20), custom_call_target="tpu_custom_call" | custom-call | flops 199999995904 | bytes 20000000 | tf_op jit(solution)/shard_map/attention/pallas_call | solution.py:31
  74.8 2.8 project_out.1
  83.5 2.6 collective-permute-start.21
  86.0 2.1 broadcast_select_fusion
  88.2 9.7 %collective-permute-start.17 = (bf16[304,1024]{1,0:T(8,128)(2,1)}, bf16[304,1024]{1,0:T(8,128)(2,1)}, u32[]{:S(2)}, u32[]{:S(2)}) collective-permute-start(bf16[304,1024]{1,0:T(8,128)(2,1)} %broadcast_select_fusion), channel_id=1, source_target_pairs={{0,4},{4,0},{8,12},{12,8},{1,5},{5,1},{9,13},{13,9},{2,6},{6,2},{1... | collective-permute-start | bytes 1867784 | tf_op jit(solution)/shard_map/ppermute | solution.py:622
  97.9 2.1 norm_two.1
  100.0 8.4 %hidden.1 = (bf16[1024,2048]{1,0:T(8,128)(2,1)}, bf16[608,2048]{1,0:T(8,128)(2,1)}, bf16[608,2048]{1,0:T(8,128)(2,1)}) custom-call(s32[10]{0:T(128)S(1)} %stack.455.place_ref, bf16[608,1024]{1,0:T(8,128)(2,1)S(1)} %get-tuple-element.130.left_ref, f32[1,2048]{1,0:T(1,128)S(1)} %reshape.414.bias_ref, bf16[256,2048]{1,0:T(8,128)(2,1)S(1)} %copy-done.38, ...), custom_call_target="tpu_custom_call" | custom-call | flops 199999995904 | bytes 20000000 | tf_op jit(solution)/shard_map/hidden/pallas_call | solution.py:31
  108.4 2.0 maximum_select_fusion.3
  110.9 2.2 weight_grad.12
  113.1 2.2 weight_grad.14
  115.3 2.4 collective-permute-start.24
  117.7 12.1 %feed_back.1 = (bf16[608,2048]{1,0:T(8,128)(2,1)}, f32[1,2048]{1,0:T(1,128)S(1)}, bf16[608,1024]{1,0:T(8,128)(2,1)S(1)}) custom-call(s32[8]{0:T(128)S(1)} %stack.442.place_ref, bf16[608,1024]{1,0:T(8,128)(2,1)S(1)} %bitcast.187, bf16[608,2048]{1,0:T(8,128)(2,1)} %get-tuple-element.131.act_ref.left_ref, bf16[608,2048]{1,0:T(8,128)(2,1)} %get-tuple-element.132.slope_ref, ...), custom_call_target="tpu_custom_call" | custom-call | flops 199999995904 | bytes 20000000 | tf_op jit(solution)/shard_map/feed_back/pallas_call | solution.py:31
  133.4 5.7 %grad_second.1.own_ref = bf16[608,1024]{1,0:T(8,128)(2,1)} custom-call(s32[1]{0:T(128)} %bitcast.place_ref, bf16[608,2048]{1,0:T(8,128)(2,1)S(1)} %copy-done.16, bf16[1024,2048]{1,0:T(8,128)(2,1)} %get-tuple-element.136.weight_ref), custom_call_target="tpu_custom_call" | custom-call | flops 199999995904 | bytes 20000000 | tf_op jit(solution)/shard_map/grad_second/pallas_call | solution.py:31
  139.6 3.5 weight_grad.18
  143.8 2.4 add_convert_fusion
  146.3 3.2 weight_grad.13
  149.5 2.0 collective-permute-start.27
  153.2 5.2 %norm_two_back.1 = (f32[608,1024]{1,0:T(8,128)}, bf16[608,1024]{1,0:T(8,128)(2,1)S(1)}, f32[8,1024]{1,0:T(8,128)S(1)}) custom-call(s32[1]{0:T(128)} %bitcast.place_ref, bf16[608,1024]{1,0:T(8,128)(2,1)S(1)} %bitcast.189, bf16[608,1024]{1,0:T(8,128)(2,1)} %grad_second.1.own_ref, bf16[608,1024]{1,0:T(8,128)(2,1)} %collective-permute-done.25.other_ref, ...), custom_call_target="tpu_custom_call" | custom-call | flops 199999995904 | bytes 20000000 | tf_op jit(solution)/shard_map/norm_two_back/pallas_call | solution.py:31
  160.4 12.1 %attention_grad.1 = (bf16[3,608,512]{2,1,0:T(8,128)(2,1)S(1)}, f32[4,8,128]{2,1,0:T(8,128)S(1)}) custom-call(s32[1]{0:T(128)} %bitcast.place_ref, bf16[608,1024]{1,0:T(8,128)(2,1)S(1)} %copy-done.24, bf16[608,1536]{1,0:T(8,128)(2,1)S(1)} %copy-done.21, bf16[608,1536]{1,0:T(8,128)(2,1)S(1)} %copy-done.21, bf16[608,1536]{1,0:T(8,128)(2,1)S(1)} %copy-done.21, ...), custom_call_target="tpu_custom_call" | custom-call | flops 199999995904 | bytes 20000000 | tf_op jit(solution)/shard_map/attention_grad/pallas_call | solution.py:31
  172.6 4.7 %grad_first.1.own_ref = bf16[608,1024]{1,0:T(8,128)(2,1)} custom-call(s32[1]{0:T(128)} %bitcast.place_ref, bf16[3,608,512]{2,1,0:T(8,128)(2,1)S(1)} %get-tuple-element.152.left_ref.right_ref, bf16[1024,1536]{1,0:T(8,128)(2,1)} %get-tuple-element.155.weight_ref), custom_call_target="tpu_custom_call" | custom-call | flops 199999995904 | bytes 20000000 | tf_op jit(solution)/shard_map/grad_first/pallas_call | solution.py:31
  177.3 3.9 %weight_grad.21 = bf16[256,1536]{1,0:T(8,128)(2,1)} custom-call(s32[2]{0:T(128)S(1)} %get-tuple-element.172.index_ref, bf16[608,1024]{1,0:T(8,128)(2,1)S(1)} %copy-done.33, bf16[3,608,512]{2,1,0:T(8,128)(2,1)S(1)} %get-tuple-element.152.left_ref.right_ref), custom_call_target="tpu_custom_call" | custom-call | flops 199999995904 | bytes 20000000 | tf_op jit(solution)/shard_map/weight_grad/pallas_call | solution.py:524
  181.1 2.8 weight_grad.15
  185.7 3.5 weight_grad.16
  189.5 4.9 %weight_grad.19 = bf16[256,2048]{1,0:T(8,128)(2,1)} custom-call(s32[2]{0:T(128)S(1)} %pad_add_fusion.5.index_ref, bf16[608,1024]{1,0:T(8,128)(2,1)S(1)} %copy-done.28, bf16[608,2048]{1,0:T(8,128)(2,1)S(1)} %copy-done.17, bf16[256,2048]{1,0:T(8,128)(2,1)} %collective-permute-done.30.rest_0_), custom_call_target="tpu_custom_call" | custom-call | flops 199999995904 | bytes 20000000 | tf_op jit(solution)/shard_map/weight_grad/pallas_call | solution.py:524
  194.4 9.5 %collective-permute-done.45 = bf16[1,2,128,1024]{3,2,1,0:T(8,128)(2,1)} collective-permute-done((bf16[1,2,128,1024]{3,2,1,0:T(8,128)(2,1)}, bf16[1,2,128,1024]{3,2,1,0:T(8,128)(2,1)}, u32[]{:S(2)}, u32[]{:S(2)}) %collective-permute-start.45) | collective-permute-done | bytes 524320 | tf_op jit(solution)/shard_map/ppermute | solution.py:635
  205.9 2.5 collective-permute-start.46
  208.7 4.1 %norm_one_back.1 = (f32[304,1024]{1,0:T(8,128)S(1)}, bf16[304,1024]{1,0:T(8,128)(2,1)S(1)}, f32[8,1024]{1,0:T(8,128)S(1)}) custom-call(s32[1]{0:T(128)} %bitcast.place_ref, f32[608,1024]{1,0:T(8,128)} %get-tuple-element.148.grad_ref, bf16[608,1024]{1,0:T(8,128)(2,1)} %grad_first.1.own_ref, bf16[608,1024]{1,0:T(8,128)(2,1)} %collective-permute-done.28.other_ref, ...), custom_call_target="tpu_custom_call" | custom-call | flops 199999995904 | bytes 20000000 | tf_op jit(solution)/shard_map/norm_one_back/pallas_call | solution.py:31
  215.9 3.8 %weight_grad.17 = bf16[256,1536]{1,0:T(8,128)(2,1)} custom-call(s32[2]{0:T(128)S(1)} %get-tuple-element.161.index_ref, bf16[608,1024]{1,0:T(8,128)(2,1)S(1)} %copy-done.34, bf16[3,608,512]{2,1,0:T(8,128)(2,1)S(1)} %get-tuple-element.152.left_ref.right_ref), custom_call_target="tpu_custom_call" | custom-call | flops 199999995904 | bytes 20000000 | tf_op jit(solution)/shard_map/weight_grad/pallas_call | solution.py:524
  224.7 5.0 %weight_grad.20 = bf16[256,2048]{1,0:T(8,128)(2,1)S(1)} custom-call(s32[2]{0:T(128)S(1)} %pad_add_fusion.4.index_ref, bf16[608,1024]{1,0:T(8,128)(2,1)S(1)} %copy-done.28, bf16[608,2048]{1,0:T(8,128)(2,1)} %get-tuple-element.140.left_ref.right_ref, bf16[256,2048]{1,0:T(8,128)(2,1)} %collective-permute-done.29.rest_0_, ...), custom_call_target="tpu_custom_call" | custom-call | flops 199999995904 | bytes 20000000 | tf_op jit(solution)/shard_map/weight_grad/pallas_call | solution.py:524
  231.7 5.0 %collective-permute-done.61 = bf16[1,128,1024]{2,1,0:T(8,128)(2,1)} collective-permute-done((bf16[1,128,1024]{2,1,0:T(8,128)(2,1)}, bf16[1,128,1024]{2,1,0:T(8,128)(2,1)}, u32[]{:S(2)}, u32[]{:S(2)}) %collective-permute-start.61) | collective-permute-done | bytes 262176 | tf_op jit(solution)/shard_map/ppermute | solution.py:635
  236.7 2.1 maximum_select_fusion.12
  240.5 5.6 %weight_grad.22 = bf16[256,1536]{1,0:T(8,128)(2,1)} custom-call(s32[2]{0:T(128)S(1)} %pad_add_fusion.5.index_ref, bf16[608,1024]{1,0:T(8,128)(2,1)S(1)} %copy-done.35, bf16[3,608,512]{2,1,0:T(8,128)(2,1)S(1)} %get-tuple-element.152.left_ref.right_ref, bf16[256,1536]{1,0:T(8,128)(2,1)} %collective-permute-done.48.rest_0_), custom_call_target="tpu_custom_call" | custom-call | flops 199999995904 | bytes 20000000 | tf_op jit(solution)/shard_map/weight_grad/pallas_call | solution.py:524
  250.4 5.4 %collective-permute-done.37.rest_0_ = bf16[160,1024]{1,0:T(8,128)(2,1)} collective-permute-done((bf16[160,1024]{1,0:T(8,128)(2,1)}, bf16[160,1024]{1,0:T(8,128)(2,1)}, u32[]{:S(2)}, u32[]{:S(2)}) %collective-permute-start.37) | collective-permute-done | bytes 327712 | tf_op jit(solution)/shard_map/ppermute | solution.py:625
  255.8 2.6 out_grad.6
  258.5 6.5 %collective-permute-done.33 = bf16[2,1,32,2048]{3,2,1,0:T(8,128)(2,1)} collective-permute-done((bf16[2,1,32,2048]{3,2,1,0:T(8,128)(2,1)}, bf16[2,1,32,2048]{3,2,1,0:T(8,128)(2,1)}, u32[]{:S(2)}, u32[]{:S(2)}) %collective-permute-start.33) | collective-permute-done | bytes 262176 | tf_op jit(solution)/shard_map/ppermute | solution.py:635
  266.2 2.9 maximum_select_fusion.6
  269.9 5.2 %weight_grad.23 = bf16[256,1536]{1,0:T(8,128)(2,1)S(1)} custom-call(s32[2]{0:T(128)S(1)} %pad_add_fusion.4.index_ref, bf16[608,1024]{1,0:T(8,128)(2,1)S(1)} %copy-done.35, bf16[3,608,512]{2,1,0:T(8,128)(2,1)S(1)} %get-tuple-element.152.left_ref.right_ref, bf16[256,1536]{1,0:T(8,128)(2,1)} %collective-permute-done.47.rest_0_, ...), custom_call_target="tpu_custom_call" | custom-call | flops 199999995904 | bytes 20000000 | tf_op jit(solution)/shard_map/weight_grad/pallas_call | solution.py:524
  275.1 2.4 collective-permute-start.50
  277.5 7.1 %collective-permute-done.35 = bf16[1,32,4096]{2,1,0:T(8,128)(2,1)} collective-permute-done((bf16[1,32,4096]{2,1,0:T(8,128)(2,1)}, bf16[1,32,4096]{2,1,0:T(8,128)(2,1)}, u32[]{:S(2)}, u32[]{:S(2)}) %collective-permute-start.35) | collective-permute-done | bytes 262176 | tf_op jit(solution)/shard_map/ppermute | solution.py:635
  284.6 2.1 maximum_select_fusion.10
  288.4 2.1 maximum_select_fusion.11
  290.5 2.4 collective-permute-done.50
  296.1 5.7 %collective-permute-done.36.rest_0_ = bf16[160,1024]{1,0:T(8,128)(2,1)S(1)} collective-permute-done((bf16[160,1024]{1,0:T(8,128)(2,1)S(1)}, bf16[160,1024]{1,0:T(8,128)(2,1)S(1)}, u32[]{:S(2)}, u32[]{:S(2)}) %collective-permute-start.36) | collective-permute-done | bytes 327712 | tf_op jit(solution)/shard_map/ppermute | solution.py:625
  304.2 2.4 collective-permute-start.39
  306.6 2.5 maximum_select_fusion.1
  309.2 2.6 bitcast_convert_fusion
  317.2 3.0 collective-permute-done.40
  320.3 2.9 collective-permute-start.53
  323.3 7.8 %collective-permute-done.41 = bf16[1,40,1024]{2,1,0:T(8,128)(2,1)S(1)} collective-permute-done((bf16[1,40,1024]{2,1,0:T(8,128)(2,1)S(1)}, bf16[1,40,1024]{2,1,0:T(8,128)(2,1)S(1)}, u32[]{:S(2)}, u32[]{:S(2)}) %collective-permute-start.41) | collective-permute-done | bytes 81952 | tf_op jit(solution)/shard_map/ppermute | solution.py:635
  331.1 2.1 fusion.2
  339.6 3.0 collective-permute-start.44
  344.3 2.6 bitcast_convert_fusion.1
  347.0 13.1 %collective-permute-done.44 = bf16[4,40,1024]{2,1,0:T(8,128)(2,1)S(1)} collective-permute-done((bf16[4,40,1024]{2,1,0:T(8,128)(2,1)S(1)}, bf16[4,40,1024]{2,1,0:T(8,128)(2,1)S(1)}, u32[]{:S(2)}, u32[]{:S(2)}) %collective-permute-start.44) | collective-permute-done | bytes 327712 | tf_op jit(solution)/shard_map/ppermute | solution.py:632
  362.9 2.2 copy.42
  365.2 8.2 %collective-permute-done.57 = bf16[2,32,3072]{2,1,0:T(8,128)(2,1)S(1)} collective-permute-done((bf16[2,32,3072]{2,1,0:T(8,128)(2,1)S(1)}, bf16[2,32,3072]{2,1,0:T(8,128)(2,1)S(1)}, u32[]{:S(2)}, u32[]{:S(2)}) %collective-permute-start.57) | collective-permute-done | bytes 393248 | tf_op jit(solution)/shard_map/ppermute | solution.py:632
  373.7 2.1 bitcast_convert_fusion.2
  (340 shorter events, 97.4 us)
Async XLA Ops:
  4.0 15.4 %collective-permute-start = (bf16[304,1024]{1,0:T(8,128)(2,1)}, bf16[304,1024]{1,0:T(8,128)(2,1)}, u32[]{:S(2)}, u32[]{:S(2)}) collective-permute-start(bf16[304,1024]{1,0:T(8,128)(2,1)} %pad_maximum_fusion.1), channel_id=1, source_target_pairs={{4,16},{12,24},{16,4},{24,12},{5,17},{13,25},{17,5},{25,13},{6,18}... | collective-permute-start | bytes 1867784 | tf_op jit(solution)/shard_map/ppermute | solution.py:644
  7.8 14.4 %collective-permute-start.2 = (bf16[16,256]{1,0:T(8,128)(2,1)}, bf16[16,256]{1,0:T(8,128)(2,1)}, u32[]{:S(2)}, u32[]{:S(2)}) collective-permute-start(bf16[16,256]{1,0:T(8,128)(2,1)} %select_select_fusion), channel_id=1, source_target_pairs={{0,8},{4,12},{8,0},{12,4},{1,9},{5,13},{9,1},{13,5},{2,10},{6,14},... | collective-permute-start | bytes 24584 | tf_op jit(solution)/shard_map/ppermute | solution.py:625
  16.2 14.7 %collective-permute-start.9 = (bf16[128,1536]{1,0:T(8,128)(2,1)}, bf16[128,1536]{1,0:T(8,128)(2,1)}, u32[]{:S(2)}, u32[]{:S(2)}) collective-permute-start(bf16[128,1536]{1,0:T(8,128)(2,1)} %get-tuple-element.113), channel_id=1, source_target_pairs={{0,8},{4,12},{8,0},{12,4},{1,9},{5,13},{9,1},{13,5},{2,10},{6,14},... | collective-permute-start | bytes 1179656 | tf_op jit(solution)/shard_map/ppermute | solution.py:625
  16.2 20.7 %collective-permute-start.8 = (bf16[256,1536]{1,0:T(8,128)(2,1)}, bf16[256,1536]{1,0:T(8,128)(2,1)}, u32[]{:S(2)}, u32[]{:S(2)}) collective-permute-start(bf16[256,1536]{1,0:T(8,128)(2,1)} %get-tuple-element.115), channel_id=1, source_target_pairs={{0,4},{4,0},{8,12},{12,8},{1,5},{5,1},{9,13},{13,9},{2,6},{6,2},{1... | collective-permute-start | bytes 2359304 | tf_op jit(solution)/shard_map/ppermute | solution.py:622
  18.2 18.7 %collective-permute-start.11 = (bf16[128,1536]{1,0:T(8,128)(2,1)}, bf16[128,1536]{1,0:T(8,128)(2,1)}, u32[]{:S(2)}, u32[]{:S(2)}) collective-permute-start(bf16[128,1536]{1,0:T(8,128)(2,1)} %get-tuple-element.116), channel_id=1, source_target_pairs={{0,12},{4,8},{8,4},{12,0},{1,13},{5,9},{9,5},{13,1},{2,14},{6,10},... | collective-permute-start | bytes 1179656 | tf_op jit(solution)/shard_map/ppermute | solution.py:629
  19.6 3.3 collective-permute-start.1
  26.6 10.3 %collective-permute-start.3 = (bf16[256,2048]{1,0:T(8,128)(2,1)S(1)}, bf16[256,2048]{1,0:T(8,128)(2,1)S(1)}, u32[]{:S(2)}, u32[]{:S(2)}) collective-permute-start(bf16[256,2048]{1,0:T(8,128)(2,1)S(1)} %get-tuple-element.98), channel_id=1, source_target_pairs={{0,4},{4,0},{8,12},{12,8},{1,5},{5,1},{9,13},{13,9},{2,6},{6,2},{1... | collective-permute-start | bytes 3145736 | tf_op jit(solution)/shard_map/ppermute | solution.py:622
  27.3 2.0 collective-permute-start.4
  30.9 20.3 %collective-permute-start.10 = (bf16[128,1536]{1,0:T(8,128)(2,1)}, bf16[128,1536]{1,0:T(8,128)(2,1)}, u32[]{:S(2)}, u32[]{:S(2)}) collective-permute-start(bf16[128,1536]{1,0:T(8,128)(2,1)} %collective-permute-done.9.refs_2_), channel_id=1, source_target_pairs={{0,16},{16,0},{1,17},{17,1},{2,18},{18,2},{3,19},{19,3},{4,20},{20... | collective-permute-start | bytes 1179656 | tf_op jit(solution)/shard_map/ppermute | solution.py:632
  36.9 14.3 %collective-permute-start.12 = (bf16[128,1536]{1,0:T(8,128)(2,1)}, bf16[128,1536]{1,0:T(8,128)(2,1)}, u32[]{:S(2)}, u32[]{:S(2)}) collective-permute-start(bf16[128,1536]{1,0:T(8,128)(2,1)} %collective-permute-done.11.refs_4_), channel_id=1, source_target_pairs={{0,16},{16,0},{1,17},{17,1},{2,18},{18,2},{3,19},{19,3},{4,20},{20... | collective-permute-start | bytes 1179656 | tf_op jit(solution)/shard_map/ppermute | solution.py:632
  40.8 9.2 %collective-permute-start.7 = (bf16[128,1024]{1,0:T(8,128)(2,1)}, bf16[128,1024]{1,0:T(8,128)(2,1)}, u32[]{:S(2)}, u32[]{:S(2)}) collective-permute-start(bf16[128,1024]{1,0:T(8,128)(2,1)} %dynamic-slice_bitcast_fusion.9), channel_id=1, source_target_pairs={{0,8},{4,12},{8,0},{12,4},{1,9},{5,13},{9,1},{13,5},{2,10},{6,14},... | collective-permute-start | bytes 786440 | tf_op jit(solution)/shard_map/ppermute | solution.py:625
  45.5 15.7 %collective-permute-start.5 = (bf16[128,2048]{1,0:T(8,128)(2,1)}, bf16[128,2048]{1,0:T(8,128)(2,1)}, u32[]{:S(2)}, u32[]{:S(2)}) collective-permute-start(bf16[128,2048]{1,0:T(8,128)(2,1)} %pair_part.1), channel_id=1, source_target_pairs={{0,8},{4,12},{8,0},{12,4},{1,9},{5,13},{9,1},{13,5},{2,10},{6,14},... | collective-permute-start | bytes 1572872 | tf_op jit(solution)/shard_map/ppermute | solution.py:625
  50.0 24.7 %collective-permute-start.13 = (bf16[128,1024]{1,0:T(8,128)(2,1)}, bf16[128,1024]{1,0:T(8,128)(2,1)}, u32[]{:S(2)}, u32[]{:S(2)}) collective-permute-start(bf16[128,1024]{1,0:T(8,128)(2,1)} %collective-permute-done.7.refs_1_), channel_id=1, source_target_pairs={{0,16},{16,0},{1,17},{17,1},{2,18},{18,2},{3,19},{19,3},{4,20},{20... | collective-permute-start | bytes 786440 | tf_op jit(solution)/shard_map/ppermute | solution.py:632
  51.2 32.2 %collective-permute-start.20 = (bf16[256,1024]{1,0:T(8,128)(2,1)}, bf16[256,1024]{1,0:T(8,128)(2,1)}, u32[]{:S(2)}, u32[]{:S(2)}) collective-permute-start(bf16[256,1024]{1,0:T(8,128)(2,1)} %get-tuple-element.133), channel_id=1, source_target_pairs={{0,8},{4,12},{8,0},{12,4},{1,9},{5,13},{9,1},{13,5},{2,10},{6,14},... | collective-permute-start | bytes 1572872 | tf_op jit(solution)/shard_map/ppermute | solution.py:625
  61.2 19.0 %collective-permute-start.6 = (bf16[128,2048]{1,0:T(8,128)(2,1)}, bf16[128,2048]{1,0:T(8,128)(2,1)}, u32[]{:S(2)}, u32[]{:S(2)}) collective-permute-start(bf16[128,2048]{1,0:T(8,128)(2,1)} %collective-permute-done.5.refs_2_), channel_id=1, source_target_pairs={{0,1},{1,0},{2,3},{3,2},{4,5},{5,4},{6,7},{7,6},{8,9},{9,8},{10,11... | collective-permute-start | bytes 1572872 | tf_op jit(solution)/shard_map/ppermute | solution.py:635
  62.8 19.0 %collective-permute-start.18 = (bf16[128,2048]{1,0:T(8,128)(2,1)}, bf16[128,2048]{1,0:T(8,128)(2,1)}, u32[]{:S(2)}, u32[]{:S(2)}) collective-permute-start(bf16[128,2048]{1,0:T(8,128)(2,1)} %collective-permute-done.5.refs_2_), channel_id=1, source_target_pairs={{0,16},{16,0},{1,17},{17,1},{2,18},{18,2},{3,19},{19,3},{4,20},{20... | collective-permute-start | bytes 1572872 | tf_op jit(solution)/shard_map/ppermute | solution.py:632
  78.6 19.3 %collective-permute-start.14 = (bf16[608,1024]{1,0:T(8,128)(2,1)S(1)}, bf16[608,1024]{1,0:T(8,128)(2,1)S(1)}, u32[]{:S(2)}, u32[]{:S(2)}) collective-permute-start(bf16[608,1024]{1,0:T(8,128)(2,1)S(1)} %get-tuple-element.121.own_ref), channel_id=1, source_target_pairs={{0,4},{4,0},{8,12},{12,8},{1,5},{5,1},{9,13},{13,9},{2,6},{6,2},{1... | collective-permute-start | bytes 3735560 | tf_op jit(solution)/shard_map/ppermute | solution.py:622
  78.6 7.5 %collective-permute-start.16 = (bf16[304,1024]{1,0:T(8,128)(2,1)}, bf16[304,1024]{1,0:T(8,128)(2,1)}, u32[]{:S(2)}, u32[]{:S(2)}) collective-permute-start(bf16[304,1024]{1,0:T(8,128)(2,1)} %concatenate.69), channel_id=1, source_target_pairs={{4,16},{12,24},{16,4},{24,12},{5,17},{13,25},{17,5},{25,13},{6,18}... | collective-permute-start | bytes 1867784 | tf_op jit(solution)/shard_map/ppermute | solution.py:644
  80.2 17.6 %collective-permute-start.15 = (bf16[256,1024]{1,0:T(8,128)(2,1)}, bf16[256,1024]{1,0:T(8,128)(2,1)}, u32[]{:S(2)}, u32[]{:S(2)}) collective-permute-start(bf16[256,1024]{1,0:T(8,128)(2,1)} %get-tuple-element.125), channel_id=1, source_target_pairs={{0,8},{4,12},{8,0},{12,4},{1,9},{5,13},{9,1},{13,5},{2,10},{6,14},... | collective-permute-start | bytes 1572872 | tf_op jit(solution)/shard_map/ppermute | solution.py:625
  81.8 16.1 %collective-permute-start.19 = (bf16[128,2048]{1,0:T(8,128)(2,1)}, bf16[128,2048]{1,0:T(8,128)(2,1)S(1)}, u32[]{:S(2)}, u32[]{:S(2)}) collective-permute-start(bf16[128,2048]{1,0:T(8,128)(2,1)} %collective-permute-done.18.refs_3_), channel_id=1, source_target_pairs={{0,1},{1,0},{2,3},{3,2},{4,5},{5,4},{6,7},{7,6},{8,9},{9,8},{10,11... | collective-permute-start | bytes 1572872 | tf_op jit(solution)/shard_map/ppermute | solution.py:635
  83.5 34.2 %collective-permute-start.21 = (bf16[256,1024]{1,0:T(8,128)(2,1)}, bf16[256,1024]{1,0:T(8,128)(2,1)}, u32[]{:S(2)}, u32[]{:S(2)}) collective-permute-start(bf16[256,1024]{1,0:T(8,128)(2,1)} %collective-permute-done.20.refs_0_), channel_id=1, source_target_pairs={{0,16},{16,0},{1,17},{17,1},{2,18},{18,2},{3,19},{19,3},{4,20},{20... | collective-permute-start | bytes 1572872 | tf_op jit(solution)/shard_map/ppermute | solution.py:632
  88.2 20.3 %collective-permute-start.17 = (bf16[304,1024]{1,0:T(8,128)(2,1)}, bf16[304,1024]{1,0:T(8,128)(2,1)}, u32[]{:S(2)}, u32[]{:S(2)}) collective-permute-start(bf16[304,1024]{1,0:T(8,128)(2,1)} %broadcast_select_fusion), channel_id=1, source_target_pairs={{0,4},{4,0},{8,12},{12,8},{1,5},{5,1},{9,13},{13,9},{2,6},{6,2},{1... | collective-permute-start | bytes 1867784 | tf_op jit(solution)/shard_map/ppermute | solution.py:622
  97.8 19.8 %collective-permute-start.22 = (bf16[256,1024]{1,0:T(8,128)(2,1)}, bf16[256,1024]{1,0:T(8,128)(2,1)}, u32[]{:S(2)}, u32[]{:S(2)}) collective-permute-start(bf16[256,1024]{1,0:T(8,128)(2,1)} %collective-permute-done.15.refs_2_), channel_id=1, source_target_pairs={{0,16},{16,0},{1,17},{17,1},{2,18},{18,2},{3,19},{19,3},{4,20},{20... | collective-permute-start | bytes 1572872 | tf_op jit(solution)/shard_map/ppermute | solution.py:632
  115.3 31.0 %collective-permute-start.24 = (bf16[512,1024]{1,0:T(8,128)(2,1)}, bf16[512,1024]{1,0:T(8,128)(2,1)}, u32[]{:S(2)}, u32[]{:S(2)}) collective-permute-start(bf16[512,1024]{1,0:T(8,128)(2,1)} %weight_grad.12), channel_id=1, source_target_pairs={{0,8},{4,12},{8,0},{12,4},{1,9},{5,13},{9,1},{13,5},{2,10},{6,14},... | collective-permute-start | bytes 3145736 | tf_op jit(solution)/shard_map/ppermute | solution.py:625
  131.7 11.7 %collective-permute-start.23 = (bf16[304,1024]{1,0:T(8,128)(2,1)}, bf16[304,1024]{1,0:T(8,128)(2,1)}, u32[]{:S(2)}, u32[]{:S(2)}) collective-permute-start(bf16[304,1024]{1,0:T(8,128)(2,1)} %dynamic-slice_bitcast_fusion), channel_id=1, source_target_pairs={{0,4},{4,0},{8,12},{12,8},{1,5},{5,1},{9,13},{13,9},{2,6},{6,2},{1... | collective-permute-start | bytes 1867784 | tf_op jit(solution)/shard_map/ppermute | solution.py:622
  131.7 49.4 %collective-permute-start.26 = (bf16[512,1024]{1,0:T(8,128)(2,1)}, bf16[512,1024]{1,0:T(8,128)(2,1)}, u32[]{:S(2)}, u32[]{:S(2)}) collective-permute-start(bf16[512,1024]{1,0:T(8,128)(2,1)} %weight_grad.14), channel_id=1, source_target_pairs={{0,8},{4,12},{8,0},{12,4},{1,9},{5,13},{9,1},{13,5},{2,10},{6,14},... | collective-permute-start | bytes 3145736 | tf_op jit(solution)/shard_map/ppermute | solution.py:625
  139.1 14.1 %collective-permute-start.25 = (bf16[608,1024]{1,0:T(8,128)(2,1)}, bf16[608,1024]{1,0:T(8,128)(2,1)}, u32[]{:S(2)}, u32[]{:S(2)}) collective-permute-start(bf16[608,1024]{1,0:T(8,128)(2,1)} %grad_second.1.own_ref), channel_id=1, source_target_pairs={{0,4},{4,0},{8,12},{12,8},{1,5},{5,1},{9,13},{13,9},{2,6},{6,2},{1... | collective-permute-start | bytes 3735560 | tf_op jit(solution)/shard_map/ppermute | solution.py:622
  149.5 31.7 %collective-permute-start.27 = (bf16[512,1024]{1,0:T(8,128)(2,1)}, bf16[512,1024]{1,0:T(8,128)(2,1)}, u32[]{:S(2)}, u32[]{:S(2)}) collective-permute-start(bf16[512,1024]{1,0:T(8,128)(2,1)} %weight_grad.13), channel_id=1, source_target_pairs={{0,16},{16,0},{1,17},{17,1},{2,18},{18,2},{3,19},{19,3},{4,20},{20... | collective-permute-start | bytes 3145736 | tf_op jit(solution)/shard_map/ppermute | solution.py:632
  151.5 38.0 %collective-permute-start.30 = (bf16[256,2048]{1,0:T(8,128)(2,1)}, bf16[256,2048]{1,0:T(8,128)(2,1)}, u32[]{:S(2)}, u32[]{:S(2)}) collective-permute-start(bf16[256,2048]{1,0:T(8,128)(2,1)} %weight_grad.18), channel_id=1, source_target_pairs={{0,8},{4,12},{8,0},{12,4},{1,9},{5,13},{9,1},{13,5},{2,10},{6,14},... | collective-permute-start | bytes 3145736 | tf_op jit(solution)/shard_map/ppermute | solution.py:625
  177.3 31.4 %collective-permute-start.28 = (bf16[608,1024]{1,0:T(8,128)(2,1)}, bf16[608,1024]{1,0:T(8,128)(2,1)}, u32[]{:S(2)}, u32[]{:S(2)}) collective-permute-start(bf16[608,1024]{1,0:T(8,128)(2,1)} %grad_first.1.own_ref), channel_id=1, source_target_pairs={{0,4},{4,0},{8,12},{12,8},{1,5},{5,1},{9,13},{13,9},{2,6},{6,2},{1... | collective-permute-start | bytes 3735560 | tf_op jit(solution)/shard_map/ppermute | solution.py:622
  189.2 14.6 %collective-permute-start.45 = (bf16[1,2,128,1024]{3,2,1,0:T(8,128)(2,1)}, bf16[1,2,128,1024]{3,2,1,0:T(8,128)(2,1)}, u32[]{:S(2)}, u32[]{:S(2)}) collective-permute-start(bf16[1,2,128,1024]{3,2,1,0:T(8,128)(2,1)} %get-tuple-element.193), channel_id=1, source_target_pairs={{0,1},{1,0},{2,3},{3,2},{4,5},{5,4},{6,7},{7,6},{8,9},{9,8},{10,11... | collective-permute-start | bytes 1572872 | tf_op jit(solution)/shard_map/ppermute | solution.py:635
  189.2 35.5 %collective-permute-start.29 = (bf16[256,2048]{1,0:T(8,128)(2,1)}, bf16[256,2048]{1,0:T(8,128)(2,1)}, u32[]{:S(2)}, u32[]{:S(2)}) collective-permute-start(bf16[256,2048]{1,0:T(8,128)(2,1)} %weight_grad.16), channel_id=1, source_target_pairs={{0,8},{4,12},{8,0},{12,4},{1,9},{5,13},{9,1},{13,5},{2,10},{6,14},... | collective-permute-start | bytes 3145736 | tf_op jit(solution)/shard_map/ppermute | solution.py:625
  194.4 30.3 %collective-permute-start.31 = (bf16[256,2048]{1,0:T(8,128)(2,1)}, bf16[256,2048]{1,0:T(8,128)(2,1)}, u32[]{:S(2)}, u32[]{:S(2)}) collective-permute-start(bf16[256,2048]{1,0:T(8,128)(2,1)} %weight_grad.19), channel_id=1, source_target_pairs={{0,16},{16,0},{1,17},{17,1},{2,18},{18,2},{3,19},{19,3},{4,20},{20... | collective-permute-start | bytes 3145736 | tf_op jit(solution)/shard_map/ppermute | solution.py:632
  205.9 14.8 %collective-permute-start.46 = (bf16[1,1,128,1024]{3,2,1,0:T(8,128)(2,1)}, bf16[1,1,128,1024]{3,2,1,0:T(8,128)(2,1)}, u32[]{:S(2)}, u32[]{:S(2)}) collective-permute-start(bf16[1,1,128,1024]{3,2,1,0:T(8,128)(2,1)} %get-tuple-element.199), channel_id=1, source_target_pairs={{0,2},{1,3},{2,0},{3,1},{4,6},{5,7},{6,4},{7,5},{8,10},{9,11},{10,... | collective-permute-start | bytes 786440 | tf_op jit(solution)/shard_map/ppermute | solution.py:635
  208.4 32.2 %collective-permute-start.48 = (bf16[256,1536]{1,0:T(8,128)(2,1)}, bf16[256,1536]{1,0:T(8,128)(2,1)}, u32[]{:S(2)}, u32[]{:S(2)}) collective-permute-start(bf16[256,1536]{1,0:T(8,128)(2,1)} %weight_grad.21), channel_id=1, source_target_pairs={{0,8},{4,12},{8,0},{12,4},{1,9},{5,13},{9,1},{13,5},{2,10},{6,14},... | collective-permute-start | bytes 2359304 | tf_op jit(solution)/shard_map/ppermute | solution.py:625
  222.5 14.3 %collective-permute-start.61 = (bf16[1,128,1024]{2,1,0:T(8,128)(2,1)}, bf16[1,128,1024]{2,1,0:T(8,128)(2,1)}, u32[]{:S(2)}, u32[]{:S(2)}) collective-permute-start(bf16[1,128,1024]{2,1,0:T(8,128)(2,1)} %bitcast.111), channel_id=1, source_target_pairs={{0,2},{1,3},{2,0},{3,1},{4,6},{5,7},{6,4},{7,5},{8,10},{9,11},{10,... | collective-permute-start | bytes 786440 | tf_op jit(solution)/shard_map/ppermute | solution.py:635
  222.9 47.0 %collective-permute-start.47 = (bf16[256,1536]{1,0:T(8,128)(2,1)}, bf16[256,1536]{1,0:T(8,128)(2,1)}, u32[]{:S(2)}, u32[]{:S(2)}) collective-permute-start(bf16[256,1536]{1,0:T(8,128)(2,1)} %weight_grad.17), channel_id=1, source_target_pairs={{0,8},{4,12},{8,0},{12,4},{1,9},{5,13},{9,1},{13,5},{2,10},{6,14},... | collective-permute-start | bytes 2359304 | tf_op jit(solution)/shard_map/ppermute | solution.py:625
  230.7 17.2 %collective-permute-start.32 = (bf16[2,2,32,2048]{3,2,1,0:T(8,128)(2,1)}, bf16[2,2,32,2048]{3,2,1,0:T(8,128)(2,1)}, u32[]{:S(2)}, u32[]{:S(2)}) collective-permute-start(bf16[2,2,32,2048]{3,2,1,0:T(8,128)(2,1)} %get-tuple-element.195), channel_id=1, source_target_pairs={{0,1},{1,0},{2,3},{3,2},{4,5},{5,4},{6,7},{7,6},{8,9},{9,8},{10,11... | collective-permute-start | bytes 1572872 | tf_op jit(solution)/shard_map/ppermute | solution.py:635
  238.8 27.4 %collective-permute-start.62 = (bf16[2,128,1024]{2,1,0:T(8,128)(2,1)}, bf16[2,128,1024]{2,1,0:T(8,128)(2,1)}, u32[]{:S(2)}, u32[]{:S(2)}) collective-permute-start(bf16[2,128,1024]{2,1,0:T(8,128)(2,1)} %maximum_select_fusion.12), channel_id=1, source_target_pairs={{0,1},{1,0},{2,3},{3,2},{4,5},{5,4},{6,7},{7,6},{8,9},{9,8},{10,11... | collective-permute-start | bytes 1572872 | tf_op jit(solution)/shard_map/ppermute | solution.py:635
  238.8 17.0 %collective-permute-start.37 = (bf16[160,1024]{1,0:T(8,128)(2,1)}, bf16[160,1024]{1,0:T(8,128)(2,1)}, u32[]{:S(2)}, u32[]{:S(2)}) collective-permute-start(bf16[160,1024]{1,0:T(8,128)(2,1)} %out_grad.4), channel_id=1, source_target_pairs={{0,8},{4,12},{8,0},{12,4},{1,9},{5,13},{9,1},{13,5},{2,10},{6,14},... | collective-permute-start | bytes 983048 | tf_op jit(solution)/shard_map/ppermute | solution.py:625
  246.2 23.7 %collective-permute-start.49 = (bf16[256,1536]{1,0:T(8,128)(2,1)}, bf16[256,1536]{1,0:T(8,128)(2,1)}, u32[]{:S(2)}, u32[]{:S(2)}) collective-permute-start(bf16[256,1536]{1,0:T(8,128)(2,1)} %weight_grad.22), channel_id=1, source_target_pairs={{0,16},{16,0},{1,17},{17,1},{2,18},{18,2},{3,19},{19,3},{4,20},{20... | collective-permute-start | bytes 2359304 | tf_op jit(solution)/shard_map/ppermute | solution.py:632
  250.0 15.0 %collective-permute-start.33 = (bf16[2,1,32,2048]{3,2,1,0:T(8,128)(2,1)}, bf16[2,1,32,2048]{3,2,1,0:T(8,128)(2,1)}, u32[]{:S(2)}, u32[]{:S(2)}) collective-permute-start(bf16[2,1,32,2048]{3,2,1,0:T(8,128)(2,1)} %get-tuple-element.201), channel_id=1, source_target_pairs={{0,2},{1,3},{2,0},{3,1},{4,6},{5,7},{6,4},{7,5},{8,10},{9,11},{10,... | collective-permute-start | bytes 786440 | tf_op jit(solution)/shard_map/ppermute | solution.py:635
  258.4 36.2 %collective-permute-start.38 = (bf16[160,1024]{1,0:T(8,128)(2,1)}, bf16[160,1024]{1,0:T(8,128)(2,1)}, u32[]{:S(2)}, u32[]{:S(2)}) collective-permute-start(bf16[160,1024]{1,0:T(8,128)(2,1)} %out_grad.6), channel_id=1, source_target_pairs={{0,16},{16,0},{1,17},{17,1},{2,18},{18,2},{3,19},{19,3},{4,20},{20... | collective-permute-start | bytes 983048 | tf_op jit(solution)/shard_map/ppermute | solution.py:632
  266.1 3.0 collective-permute-start.34
  269.1 35.1 %collective-permute-start.63 = (bf16[4,128,1024]{2,1,0:T(8,128)(2,1)}, bf16[4,128,1024]{2,1,0:T(8,128)(2,1)}, u32[]{:S(2)}, u32[]{:S(2)}) collective-permute-start(bf16[4,128,1024]{2,1,0:T(8,128)(2,1)} %bitcast.116), channel_id=1, source_target_pairs={{0,16},{16,0},{1,17},{17,1},{2,18},{18,2},{3,19},{19,3},{4,20},{20... | collective-permute-start | bytes 3145736 | tf_op jit(solution)/shard_map/ppermute | solution.py:632
  269.9 14.7 %collective-permute-start.35 = (bf16[1,32,4096]{2,1,0:T(8,128)(2,1)}, bf16[1,32,4096]{2,1,0:T(8,128)(2,1)}, u32[]{:S(2)}, u32[]{:S(2)}) collective-permute-start(bf16[1,32,4096]{2,1,0:T(8,128)(2,1)} %maximum_bitcast_fusion), channel_id=1, source_target_pairs={{0,2},{1,3},{2,0},{3,1},{4,6},{5,7},{6,4},{7,5},{8,10},{9,11},{10,... | collective-permute-start | bytes 786440 | tf_op jit(solution)/shard_map/ppermute | solution.py:635
  275.1 17.8 %collective-permute-start.50 = (bf16[2,2,32,1536]{3,2,1,0:T(8,128)(2,1)S(1)}, bf16[2,2,32,1536]{3,2,1,0:T(8,128)(2,1)S(1)}, u32[]{:S(2)}, u32[]{:S(2)}) collective-permute-start(bf16[2,2,32,1536]{3,2,1,0:T(8,128)(2,1)S(1)} %get-tuple-element.197), channel_id=1, source_target_pairs={{0,1},{1,0},{2,3},{3,2},{4,5},{5,4},{6,7},{7,6},{8,9},{9,8},{10,11... | collective-permute-start | bytes 1179656 | tf_op jit(solution)/shard_map/ppermute | solution.py:635
  286.7 27.1 %collective-permute-start.58 = (bf16[2,32,4096]{2,1,0:T(8,128)(2,1)}, bf16[2,32,4096]{2,1,0:T(8,128)(2,1)}, u32[]{:S(2)}, u32[]{:S(2)}) collective-permute-start(bf16[2,32,4096]{2,1,0:T(8,128)(2,1)} %maximum_select_fusion.10), channel_id=1, source_target_pairs={{0,1},{1,0},{2,3},{3,2},{4,5},{5,4},{6,7},{7,6},{8,9},{9,8},{10,11... | collective-permute-start | bytes 1572872 | tf_op jit(solution)/shard_map/ppermute | solution.py:635
  286.7 52.9 %collective-permute-start.59 = (bf16[2,32,4096]{2,1,0:T(8,128)(2,1)}, bf16[2,32,4096]{2,1,0:T(8,128)(2,1)}, u32[]{:S(2)}, u32[]{:S(2)}) collective-permute-start(bf16[2,32,4096]{2,1,0:T(8,128)(2,1)} %maximum_select_fusion.10), channel_id=1, source_target_pairs={{0,16},{16,0},{1,17},{17,1},{2,18},{18,2},{3,19},{19,3},{4,20},{20... | collective-permute-start | bytes 1572872 | tf_op jit(solution)/shard_map/ppermute | solution.py:632
  292.9 9.0 %collective-permute-start.36 = (bf16[160,1024]{1,0:T(8,128)(2,1)S(1)}, bf16[160,1024]{1,0:T(8,128)(2,1)S(1)}, u32[]{:S(2)}, u32[]{:S(2)}) collective-permute-start(bf16[160,1024]{1,0:T(8,128)(2,1)S(1)} %out_grad.5), channel_id=1, source_target_pairs={{0,8},{4,12},{8,0},{12,4},{1,9},{5,13},{9,1},{13,5},{2,10},{6,14},... | collective-permute-start | bytes 983048 | tf_op jit(solution)/shard_map/ppermute | solution.py:625
  294.7 36.5 %collective-permute-start.42 = (bf16[304,1024]{1,0:T(8,128)(2,1)}, bf16[304,1024]{1,0:T(8,128)(2,1)}, u32[]{:S(2)}, u32[]{:S(2)}) collective-permute-start(bf16[304,1024]{1,0:T(8,128)(2,1)} %add_convert_fusion), channel_id=1, source_target_pairs={{4,16},{12,24},{16,4},{24,12},{5,17},{13,25},{17,5},{25,13},{6,18}... | collective-permute-start | bytes 1867784 | tf_op jit(solution)/shard_map/ppermute | solution.py:644
  301.9 10.4 %collective-permute-start.51 = (bf16[2,1,32,1536]{3,2,1,0:T(8,128)(2,1)}, bf16[2,1,32,1536]{3,2,1,0:T(8,128)(2,1)}, u32[]{:S(2)}, u32[]{:S(2)}) collective-permute-start(bf16[2,1,32,1536]{3,2,1,0:T(8,128)(2,1)} %get-tuple-element.203), channel_id=1, source_target_pairs={{0,2},{1,3},{2,0},{3,1},{4,6},{5,7},{6,4},{7,5},{8,10},{9,11},{10,... | collective-permute-start | bytes 589832 | tf_op jit(solution)/shard_map/ppermute | solution.py:635
  304.2 9.4 %collective-permute-start.39 = (bf16[1,2,40,1024]{3,2,1,0:T(8,128)(2,1)S(1)}, bf16[1,2,40,1024]{3,2,1,0:T(8,128)(2,1)S(1)}, u32[]{:S(2)}, u32[]{:S(2)}) collective-permute-start(bf16[1,2,40,1024]{3,2,1,0:T(8,128)(2,1)S(1)} %get-tuple-element.205), channel_id=1, source_target_pairs={{0,1},{1,0},{2,3},{3,2},{4,5},{5,4},{6,7},{7,6},{8,9},{9,8},{10,11... | collective-permute-start | bytes 491528 | tf_op jit(solution)/shard_map/ppermute | solution.py:635
  313.3 3.8 collective-permute-start.52
  313.7 6.6 %collective-permute-start.40 = (bf16[1,1,40,1024]{3,2,1,0:T(8,128)(2,1)S(1)}, bf16[1,1,40,1024]{3,2,1,0:T(8,128)(2,1)S(1)}, u32[]{:S(2)}, u32[]{:S(2)}) collective-permute-start(bf16[1,1,40,1024]{3,2,1,0:T(8,128)(2,1)S(1)} %get-tuple-element.215), channel_id=1, source_target_pairs={{0,2},{1,3},{2,0},{3,1},{4,6},{5,7},{6,4},{7,5},{8,10},{9,11},{10,... | collective-permute-start | bytes 245768 | tf_op jit(solution)/shard_map/ppermute | solution.py:635
  313.8 28.8 %collective-permute-start.60 = (bf16[2,32,4096]{2,1,0:T(8,128)(2,1)}, bf16[2,32,4096]{2,1,0:T(8,128)(2,1)S(1)}, u32[]{:S(2)}, u32[]{:S(2)}) collective-permute-start(bf16[2,32,4096]{2,1,0:T(8,128)(2,1)} %collective-permute-done.58), channel_id=1, source_target_pairs={{0,16},{16,0},{1,17},{17,1},{2,18},{18,2},{3,19},{19,3},{4,20},{20... | collective-permute-start | bytes 1572872 | tf_op jit(solution)/shard_map/ppermute | solution.py:632
  320.3 10.8 %collective-permute-start.41 = (bf16[1,40,1024]{2,1,0:T(8,128)(2,1)S(1)}, bf16[1,40,1024]{2,1,0:T(8,128)(2,1)S(1)}, u32[]{:S(2)}, u32[]{:S(2)}) collective-permute-start(bf16[1,40,1024]{2,1,0:T(8,128)(2,1)S(1)} %fusion.3), channel_id=1, source_target_pairs={{0,2},{1,3},{2,0},{3,1},{4,6},{5,7},{6,4},{7,5},{8,10},{9,11},{10,... | collective-permute-start | bytes 245768 | tf_op jit(solution)/shard_map/ppermute | solution.py:635
  320.3 14.9 %collective-permute-start.53 = (bf16[1,32,3072]{2,1,0:T(8,128)(2,1)S(1)}, bf16[1,32,3072]{2,1,0:T(8,128)(2,1)S(1)}, u32[]{:S(2)}, u32[]{:S(2)}) collective-permute-start(bf16[1,32,3072]{2,1,0:T(8,128)(2,1)S(1)} %bitcast.216), channel_id=1, source_target_pairs={{0,2},{1,3},{2,0},{3,1},{4,6},{5,7},{6,4},{7,5},{8,10},{9,11},{10,... | collective-permute-start | bytes 589832 | tf_op jit(solution)/shard_map/ppermute | solution.py:635
  331.0 7.7 %collective-permute-start.43 = (bf16[2,40,1024]{2,1,0:T(8,128)(2,1)S(1)}, bf16[2,40,1024]{2,1,0:T(8,128)(2,1)S(1)}, u32[]{:S(2)}, u32[]{:S(2)}) collective-permute-start(bf16[2,40,1024]{2,1,0:T(8,128)(2,1)S(1)} %maximum_select_fusion.16), channel_id=1, source_target_pairs={{0,1},{1,0},{2,3},{3,2},{4,5},{5,4},{6,7},{7,6},{8,9},{9,8},{10,11... | collective-permute-start | bytes 491528 | tf_op jit(solution)/shard_map/ppermute | solution.py:635
  335.3 27.2 %collective-permute-start.55 = (bf16[2,32,3072]{2,1,0:T(8,128)(2,1)S(1)}, bf16[2,32,3072]{2,1,0:T(8,128)(2,1)S(1)}, u32[]{:S(2)}, u32[]{:S(2)}) collective-permute-start(bf16[2,32,3072]{2,1,0:T(8,128)(2,1)S(1)} %maximum_select_fusion.13), channel_id=1, source_target_pairs={{0,1},{1,0},{2,3},{3,2},{4,5},{5,4},{6,7},{7,6},{8,9},{9,8},{10,11... | collective-permute-start | bytes 1179656 | tf_op jit(solution)/shard_map/ppermute | solution.py:635
  335.4 29.8 %collective-permute-start.56 = (bf16[2,32,3072]{2,1,0:T(8,128)(2,1)S(1)}, bf16[2,32,3072]{2,1,0:T(8,128)(2,1)S(1)}, u32[]{:S(2)}, u32[]{:S(2)}) collective-permute-start(bf16[2,32,3072]{2,1,0:T(8,128)(2,1)S(1)} %maximum_select_fusion.13), channel_id=1, source_target_pairs={{0,16},{16,0},{1,17},{17,1},{2,18},{18,2},{3,19},{19,3},{4,20},{20... | collective-permute-start | bytes 1179656 | tf_op jit(solution)/shard_map/ppermute | solution.py:632
  338.8 24.0 %collective-permute-start.54 = (bf16[304,1024]{1,0:T(8,128)(2,1)S(1)}, bf16[304,1024]{1,0:T(8,128)(2,1)S(1)}, u32[]{:S(2)}, u32[]{:S(2)}) collective-permute-start(bf16[304,1024]{1,0:T(8,128)(2,1)S(1)} %get-tuple-element.174), channel_id=1, source_target_pairs={{4,16},{12,24},{16,4},{24,12},{5,17},{13,25},{17,5},{25,13},{6,18}... | collective-permute-start | bytes 1867784 | tf_op jit(solution)/shard_map/ppermute | solution.py:644
  339.6 20.5 %collective-permute-start.44 = (bf16[4,40,1024]{2,1,0:T(8,128)(2,1)S(1)}, bf16[4,40,1024]{2,1,0:T(8,128)(2,1)S(1)}, u32[]{:S(2)}, u32[]{:S(2)}) collective-permute-start(bf16[4,40,1024]{2,1,0:T(8,128)(2,1)S(1)} %bitcast.213), channel_id=1, source_target_pairs={{0,16},{16,0},{1,17},{17,1},{2,18},{18,2},{3,19},{19,3},{4,20},{20... | collective-permute-start | bytes 983048 | tf_op jit(solution)/shard_map/ppermute | solution.py:632
  362.5 10.9 %collective-permute-start.57 = (bf16[2,32,3072]{2,1,0:T(8,128)(2,1)S(1)}, bf16[2,32,3072]{2,1,0:T(8,128)(2,1)S(1)}, u32[]{:S(2)}, u32[]{:S(2)}) collective-permute-start(bf16[2,32,3072]{2,1,0:T(8,128)(2,1)S(1)} %collective-permute-done.55), channel_id=1, source_target_pairs={{0,16},{16,0},{1,17},{17,1},{2,18},{18,2},{3,19},{19,3},{4,20},{20... | collective-permute-start | bytes 1179656 | tf_op jit(solution)/shard_map/ppermute | solution.py:632
  (63 other events, 332.7 us)

commit v5 on v4

--- a/solution.py
+++ b/solution.py
@@ -62,7 +62,7 @@
     visible = key_visible(note_ref, padded_half, rows)
     for head in range(2):
         lanes = slice(head * HD, (head + 1) * HD)
-        scores = dims(k_ref[:, lanes], q_ref[:, lanes], 1, 1) * (HD ** -0.5)
+        scores = dims(k_ref[:, lanes], q_ref[:, lanes] * (HD ** -0.5), 1, 1)
         scores = jnp.where(visible, scores, -1000000000.0)
         top = jnp.max(scores, axis=0, keepdims=True)
         shifted = jnp.exp(scores - top)
@@ -80,18 +80,18 @@
     visible = key_visible(note_ref, padded_half, rows)
     for head in range(2):
         lanes = slice(head * HD, (head + 1) * HD)
-        queries, keys = q_ref[:, lanes], k_ref[:, lanes]
+        queries, keys = q_ref[:, lanes] * (HD ** -0.5), k_ref[:, lanes] * (HD ** -0.5)
         values, grads = v_ref[:, lanes], g_ref[:, lanes]
-        scores = dims(keys, queries, 1, 1) * (HD ** -0.5)
+        scores = dims(k_ref[:, lanes], queries, 1, 1)
         weights = jnp.where(visible, jnp.exp(scores - log_ref[0, head : head + 1, :]), 0.0)
         grad_weights = dims(values, grads, 1, 1)
         inner = jnp.sum(weights * grad_weights, axis=0, keepdims=True)
         grad_scores = (weights * (grad_weights - inner)).astype(BF16)
         keys_t = jnp.transpose(keys.astype(F32)).astype(BF16)
-        grad_q = (jnp.transpose(dims(keys_t, grad_scores, 1, 0)) * (HD ** -0.5)).astype(BF16)
+        grad_q = jnp.transpose(dims(keys_t, grad_scores, 1, 0)).astype(BF16)
         grad_v = dims(weights.astype(BF16), grads, 1, 0).astype(BF16)
         out_ref[0, :, lanes] = grad_q
-        out_ref[1, :, lanes] = (dims(grad_scores, queries, 1, 0) * (HD ** -0.5)).astype(BF16)
+        out_ref[1, :, lanes] = dims(grad_scores, queries, 1, 0).astype(BF16)
         out_ref[2, :, lanes] = grad_v
         sum_ref[0, 0:1, lanes] = jnp.sum(grad_q.astype(F32), axis=0, keepdims=True)
         sum_ref[0, 1:2, lanes] = jnp.sum(grad_v.astype(F32), axis=0, keepdims=True)
@@ -515,18 +515,18 @@
     parts = right.shape[0] if right.ndim == 3 else 1
     width = right.shape[-1]
     if right.ndim == 3:
-        right_spec = pl.BlockSpec((pl.Squeezed(), tokens, width), lambda i, j, n: (j, 0, 0))
+        right_spec = pl.BlockSpec((pl.Squeezed(), tokens, width), lambda j, i, n: (j, 0, 0))
     else:
         parts = 2
         width = width // parts
-        right_spec = pl.BlockSpec((tokens, width), lambda i, j, n: (0, j))
-    tile = pl.BlockSpec((height, width), lambda i, j, n: (i, j))
+        right_spec = pl.BlockSpec((tokens, width), lambda j, i, n: (0, j))
+    tile = pl.BlockSpec((height, width), lambda j, i, n: (i, j))
     return pl.pallas_call(
         functools.partial(weight_grad_body, len(added)),
         grid_spec=pltpu.PrefetchScalarGridSpec(
             num_scalar_prefetch=1,
-            grid=(number, parts),
-            in_specs=[pl.BlockSpec((tokens, height), lambda i, j, n: (0, n[i])), right_spec]
+            grid=(parts, number),
+            in_specs=[pl.BlockSpec((tokens, height), lambda j, i, n: (0, n[i])), right_spec]
             + [tile] * len(added),
             out_specs=tile,
         ),
@@ -1032,19 +1032,19 @@
     total_up.turn()
     block_moved = swap(line.gate(block))
     total_out.second()
+    total_qkv.turn()
     total_out.third()
     total_out.fourth()
-    total_qkv.turn()
-    total_up.turn()
     total_qkv.turn()
     total_qkv.turn()
     total_out.turn()
     total_qkv.turn()
+    block_out = line.mark(jnp.where(half == core, line.gate(block), block_moved)[:rows][None])
+    total_up.turn()
     moved = swap(line.gate(own_grad_low))
     total_out.turn()
     total_qkv.turn()
     total_out.turn()
-    block_out = line.mark(jnp.where(half == core, line.gate(block), block_moved)[:rows][None])
     grad_qkv_w = total_qkv.finish().reshape(owned, 3 * width)
     total_out.turn()
     out_rows = total_out.finish()

time: 383 us -> 384 us (level)
  transfers between devices with their start and end apart: 64 -> 64, of which waited for: 21 -> 20; matrix products, arithmetic and copies ran while one was open for 16% -> 16% of each run, Pallas kernels for 35% -> 35%
where the time goes in v5:
time: 384 us; the launch traced here: 376 us
  Pallas kernels  132 us (34%)
  waiting for transfers between devices  89.5 us (23%)
  starting transfers between devices  71.1 us (19%)
  other arithmetic  44.6 us (12%)
  local copies, waits for them, and re-layouts  35.7 us (9%)
    pallas_call x21, Pallas kernels, run(): pl.pallas_call(body, grid_spec=pltpu.PrefetchScalarGridSpec(num_scalar_pr...  86.7 us
    ppermute x18, waiting for transfers between devices, over_z(): return lax.ppermute(value, 'rep', [(i, i ^ step) for i in range(replicas)])  46.1 us
    pallas_call x12, Pallas kernels, weight_grad(): pl.pallas_call(functools.partial(weight_grad_body, len(added)), grid_spec...  45.8 us
    unnamed x145, local copies, waits for them, and re-layouts  20 us
    ppermute x16, waiting for transfers between devices, over_y(): lax.ppermute(value, 'seq', [(i, halves - 1 - i) for i in range(halves)])  19.4 us
    ppermute x16, starting transfers between devices, over_y(): lax.ppermute(value, 'seq', [(i, halves - 1 - i) for i in range(halves)])  18.3 us
    ppermute x14, waiting for transfers between devices, over_x(): lax.ppermute(value, 'shard', [(i, (i + 2 * step) % group) for i in range(...  17.7 us
    ppermute x18, starting transfers between devices, over_z(): return lax.ppermute(value, 'rep', [(i, i ^ step) for i in range(replicas)])  16.3 us
  transfers between devices with their start and end apart: 64, of which 20 were waited for; matrix products, arithmetic and copies ran while one was open for 16% of the time, Pallas kernels for 35%

profile of v5, /device:TPU:0, one launch (start us, length us, event | category | flops | bytes accessed | tf_op | source)
XLA Modules:
  0.0 376.5 jit_solution(3851292444422929283)
XLA Ops:
  7.8 3.0 collective-permute-start.2
  12.3 3.0 split_qkv.1
  16.2 2.0 collective-permute-start.8
  31.8 5.1 %collective-permute-done.11.refs_4_ = bf16[128,1536]{1,0:T(8,128)(2,1)} collective-permute-done((bf16[128,1536]{1,0:T(8,128)(2,1)}, bf16[128,1536]{1,0:T(8,128)(2,1)}, u32[]{:S(2)}, u32[]{:S(2)}) %collective-permute-start.11) | collective-permute-done | bytes 393248 | tf_op jit(solution)/shard_map/ppermute | solution.py:629
  42.8 2.7 dynamic-slice_bitcast_fusion.1
  47.5 2.5 collective-permute-done.7.refs_1_
  51.2 6.3 %project.1 = (bf16[1024,1536]{1,0:T(8,128)(2,1)}, bf16[608,1536]{1,0:T(8,128)(2,1)}) custom-call(s32[6]{0:T(128)S(1)} %stack.433.place_ref, bf16[608,1024]{1,0:T(8,128)(2,1)S(1)} %get-tuple-element.109.left_ref, f32[1,1536]{1,0:T(1,128)S(1)} %fusion.5.bias_ref, bf16[256,1536]{1,0:T(8,128)(2,1)S(1)} %copy-done.42, ...), custom_call_target="tpu_custom_call" | custom-call | flops 199999995904 | bytes 20000000 | tf_op jit(solution)/shard_map/project/pallas_call | solution.py:31
  57.5 3.6 collective-permute-done.5.refs_2_
  66.2 8.5 %attention.1 = (bf16[608,512]{1,0:T(8,128)(2,1)S(1)}, f32[4,2,608]{2,1,0:T(2,128)S(1)}) custom-call(s32[1]{0:T(128)} %bitcast.place_ref, bf16[608,1024]{1,0:T(8,128)(2,1)S(1)} %get-tuple-element.105.note_ref.image_ref, bf16[608,1536]{1,0:T(8,128)(2,1)S(1)} %copy-done.20, bf16[608,1536]{1,0:T(8,128)(2,1)S(1)} %copy-done.20, bf16[608,1536]{1,0:T(8,128)(2,1)S(1)} %copy-done.20), custom_call_target="tpu_custom_call" | custom-call | flops 199999995904 | bytes 20000000 | tf_op jit(solution)/shard_map/attention/pallas_call | solution.py:31
  74.8 2.8 project_out.1
  83.5 2.6 collective-permute-start.21
  86.0 2.1 broadcast_select_fusion
  88.2 9.7 %collective-permute-start.17 = (bf16[304,1024]{1,0:T(8,128)(2,1)}, bf16[304,1024]{1,0:T(8,128)(2,1)}, u32[]{:S(2)}, u32[]{:S(2)}) collective-permute-start(bf16[304,1024]{1,0:T(8,128)(2,1)} %broadcast_select_fusion), channel_id=1, source_target_pairs={{0,4},{4,0},{8,12},{12,8},{1,5},{5,1},{9,13},{13,9},{2,6},{6,2},{1... | collective-permute-start | bytes 1867784 | tf_op jit(solution)/shard_map/ppermute | solution.py:622
  97.9 2.1 norm_two.1
  100.1 8.4 %hidden.1 = (bf16[1024,2048]{1,0:T(8,128)(2,1)}, bf16[608,2048]{1,0:T(8,128)(2,1)}, bf16[608,2048]{1,0:T(8,128)(2,1)}) custom-call(s32[10]{0:T(128)S(1)} %stack.455.place_ref, bf16[608,1024]{1,0:T(8,128)(2,1)S(1)} %get-tuple-element.130.left_ref, f32[1,2048]{1,0:T(1,128)S(1)} %reshape.414.bias_ref, bf16[256,2048]{1,0:T(8,128)(2,1)S(1)} %copy-done.38, ...), custom_call_target="tpu_custom_call" | custom-call | flops 199999995904 | bytes 20000000 | tf_op jit(solution)/shard_map/hidden/pallas_call | solution.py:31
  108.4 2.0 maximum_select_fusion.3
  110.9 2.2 weight_grad.12
  113.1 2.2 weight_grad.14
  115.3 2.4 collective-permute-start.24
  117.7 12.1 %feed_back.1 = (bf16[608,2048]{1,0:T(8,128)(2,1)}, f32[1,2048]{1,0:T(1,128)S(1)}, bf16[608,1024]{1,0:T(8,128)(2,1)S(1)}) custom-call(s32[8]{0:T(128)S(1)} %stack.442.place_ref, bf16[608,1024]{1,0:T(8,128)(2,1)S(1)} %bitcast.187, bf16[608,2048]{1,0:T(8,128)(2,1)} %get-tuple-element.131.act_ref.left_ref, bf16[608,2048]{1,0:T(8,128)(2,1)} %get-tuple-element.132.slope_ref, ...), custom_call_target="tpu_custom_call" | custom-call | flops 199999995904 | bytes 20000000 | tf_op jit(solution)/shard_map/feed_back/pallas_call | solution.py:31
  133.5 5.7 %grad_second.1.own_ref = bf16[608,1024]{1,0:T(8,128)(2,1)} custom-call(s32[1]{0:T(128)} %bitcast.place_ref, bf16[608,2048]{1,0:T(8,128)(2,1)S(1)} %copy-done.16, bf16[1024,2048]{1,0:T(8,128)(2,1)} %get-tuple-element.136.weight_ref), custom_call_target="tpu_custom_call" | custom-call | flops 199999995904 | bytes 20000000 | tf_op jit(solution)/shard_map/grad_second/pallas_call | solution.py:31
  139.6 3.5 weight_grad.21
  143.8 2.4 add_convert_fusion
  146.3 3.2 weight_grad.13
  149.5 2.0 collective-permute-start.27
  153.2 5.2 %norm_two_back.1 = (f32[608,1024]{1,0:T(8,128)}, bf16[608,1024]{1,0:T(8,128)(2,1)S(1)}, f32[8,1024]{1,0:T(8,128)S(1)}) custom-call(s32[1]{0:T(128)} %bitcast.place_ref, bf16[608,1024]{1,0:T(8,128)(2,1)S(1)} %bitcast.189, bf16[608,1024]{1,0:T(8,128)(2,1)} %grad_second.1.own_ref, bf16[608,1024]{1,0:T(8,128)(2,1)} %collective-permute-done.25.other_ref, ...), custom_call_target="tpu_custom_call" | custom-call | flops 199999995904 | bytes 20000000 | tf_op jit(solution)/shard_map/norm_two_back/pallas_call | solution.py:31
  160.4 12.1 %attention_grad.1 = (bf16[3,608,512]{2,1,0:T(8,128)(2,1)S(1)}, f32[4,8,128]{2,1,0:T(8,128)S(1)}) custom-call(s32[1]{0:T(128)} %bitcast.place_ref, bf16[608,1024]{1,0:T(8,128)(2,1)S(1)} %copy-done.24, bf16[608,1536]{1,0:T(8,128)(2,1)S(1)} %copy-done.21, bf16[608,1536]{1,0:T(8,128)(2,1)S(1)} %copy-done.21, bf16[608,1536]{1,0:T(8,128)(2,1)S(1)} %copy-done.21, ...), custom_call_target="tpu_custom_call" | custom-call | flops 199999995904 | bytes 20000000 | tf_op jit(solution)/shard_map/attention_grad/pallas_call | solution.py:31
  172.6 4.7 %grad_first.1.own_ref = bf16[608,1024]{1,0:T(8,128)(2,1)} custom-call(s32[1]{0:T(128)} %bitcast.place_ref, bf16[3,608,512]{2,1,0:T(8,128)(2,1)S(1)} %get-tuple-element.148.left_ref.right_ref, bf16[1024,1536]{1,0:T(8,128)(2,1)} %get-tuple-element.155.weight_ref), custom_call_target="tpu_custom_call" | custom-call | flops 199999995904 | bytes 20000000 | tf_op jit(solution)/shard_map/grad_first/pallas_call | solution.py:31
  177.3 4.0 %weight_grad.18 = bf16[256,1536]{1,0:T(8,128)(2,1)} custom-call(s32[2]{0:T(128)S(1)} %get-tuple-element.163.index_ref, bf16[608,1024]{1,0:T(8,128)(2,1)S(1)} %copy-done.33, bf16[3,608,512]{2,1,0:T(8,128)(2,1)S(1)} %get-tuple-element.148.left_ref.right_ref), custom_call_target="tpu_custom_call" | custom-call | flops 199999995904 | bytes 20000000 | tf_op jit(solution)/shard_map/weight_grad/pallas_call | solution.py:524
  181.2 2.8 weight_grad.15
  185.7 3.5 weight_grad.16
  189.5 4.8 %weight_grad.22 = bf16[256,2048]{1,0:T(8,128)(2,1)} custom-call(s32[2]{0:T(128)S(1)} %pad_add_fusion.5.index_ref, bf16[608,1024]{1,0:T(8,128)(2,1)S(1)} %copy-done.28, bf16[608,2048]{1,0:T(8,128)(2,1)S(1)} %copy-done.17, bf16[256,2048]{1,0:T(8,128)(2,1)} %collective-permute-done.39.rest_0_), custom_call_target="tpu_custom_call" | custom-call | flops 199999995904 | bytes 20000000 | tf_op jit(solution)/shard_map/weight_grad/pallas_call | solution.py:524
  194.4 9.5 %collective-permute-done.29 = bf16[1,2,128,1024]{3,2,1,0:T(8,128)(2,1)} collective-permute-done((bf16[1,2,128,1024]{3,2,1,0:T(8,128)(2,1)}, bf16[1,2,128,1024]{3,2,1,0:T(8,128)(2,1)}, u32[]{:S(2)}, u32[]{:S(2)}) %collective-permute-start.29) | collective-permute-done | bytes 524320 | tf_op jit(solution)/shard_map/ppermute | solution.py:635
  206.0 2.4 collective-permute-start.30
  208.7 4.1 %norm_one_back.1 = (f32[304,1024]{1,0:T(8,128)S(1)}, bf16[304,1024]{1,0:T(8,128)(2,1)S(1)}, f32[8,1024]{1,0:T(8,128)S(1)}) custom-call(s32[1]{0:T(128)} %bitcast.place_ref, f32[608,1024]{1,0:T(8,128)} %get-tuple-element.143.grad_ref, bf16[608,1024]{1,0:T(8,128)(2,1)} %grad_first.1.own_ref, bf16[608,1024]{1,0:T(8,128)(2,1)} %collective-permute-done.28.other_ref, ...), custom_call_target="tpu_custom_call" | custom-call | flops 199999995904 | bytes 20000000 | tf_op jit(solution)/shard_map/norm_one_back/pallas_call | solution.py:31
  215.9 3.9 %weight_grad.17 = bf16[256,1536]{1,0:T(8,128)(2,1)} custom-call(s32[2]{0:T(128)S(1)} %get-tuple-element.161.index_ref, bf16[608,1024]{1,0:T(8,128)(2,1)S(1)} %copy-done.34, bf16[3,608,512]{2,1,0:T(8,128)(2,1)S(1)} %get-tuple-element.148.left_ref.right_ref), custom_call_target="tpu_custom_call" | custom-call | flops 199999995904 | bytes 20000000 | tf_op jit(solution)/shard_map/weight_grad/pallas_call | solution.py:524
  224.8 4.8 %weight_grad.23 = bf16[256,2048]{1,0:T(8,128)(2,1)S(1)} custom-call(s32[2]{0:T(128)S(1)} %pad_add_fusion.3.index_ref, bf16[608,1024]{1,0:T(8,128)(2,1)S(1)} %copy-done.28, bf16[608,2048]{1,0:T(8,128)(2,1)} %get-tuple-element.140.left_ref.right_ref, bf16[256,2048]{1,0:T(8,128)(2,1)} %collective-permute-done.38.rest_0_, ...), custom_call_target="tpu_custom_call" | custom-call | flops 199999995904 | bytes 20000000 | tf_op jit(solution)/shard_map/weight_grad/pallas_call | solution.py:524
  231.6 5.3 %collective-permute-done.61 = bf16[1,128,1024]{2,1,0:T(8,128)(2,1)} collective-permute-done((bf16[1,128,1024]{2,1,0:T(8,128)(2,1)}, bf16[1,128,1024]{2,1,0:T(8,128)(2,1)}, u32[]{:S(2)}, u32[]{:S(2)}) %collective-permute-start.61) | collective-permute-done | bytes 262176 | tf_op jit(solution)/shard_map/ppermute | solution.py:635
  236.8 2.1 maximum_select_fusion.12
  240.6 5.6 %weight_grad.19 = bf16[256,1536]{1,0:T(8,128)(2,1)} custom-call(s32[2]{0:T(128)S(1)} %pad_add_fusion.5.index_ref, bf16[608,1024]{1,0:T(8,128)(2,1)S(1)} %copy-done.35, bf16[3,608,512]{2,1,0:T(8,128)(2,1)S(1)} %get-tuple-element.148.left_ref.right_ref, bf16[256,1536]{1,0:T(8,128)(2,1)} %collective-permute-done.32.rest_0_), custom_call_target="tpu_custom_call" | custom-call | flops 199999995904 | bytes 20000000 | tf_op jit(solution)/shard_map/weight_grad/pallas_call | solution.py:524
  250.3 5.6 %collective-permute-done.47.rest_0_ = bf16[160,1024]{1,0:T(8,128)(2,1)} collective-permute-done((bf16[160,1024]{1,0:T(8,128)(2,1)}, bf16[160,1024]{1,0:T(8,128)(2,1)}, u32[]{:S(2)}, u32[]{:S(2)}) %collective-permute-start.47) | collective-permute-done | bytes 327712 | tf_op jit(solution)/shard_map/ppermute | solution.py:625
  255.9 2.6 out_grad.6
  258.5 6.6 %collective-permute-done.42 = bf16[2,1,32,2048]{3,2,1,0:T(8,128)(2,1)} collective-permute-done((bf16[2,1,32,2048]{3,2,1,0:T(8,128)(2,1)}, bf16[2,1,32,2048]{3,2,1,0:T(8,128)(2,1)}, u32[]{:S(2)}, u32[]{:S(2)}) %collective-permute-start.42) | collective-permute-done | bytes 262176 | tf_op jit(solution)/shard_map/ppermute | solution.py:635
  266.3 2.9 maximum_select_fusion.6
  270.0 5.2 %weight_grad.20 = bf16[256,1536]{1,0:T(8,128)(2,1)S(1)} custom-call(s32[2]{0:T(128)S(1)} %pad_add_fusion.3.index_ref, bf16[608,1024]{1,0:T(8,128)(2,1)S(1)} %copy-done.35, bf16[3,608,512]{2,1,0:T(8,128)(2,1)S(1)} %get-tuple-element.148.left_ref.right_ref, bf16[256,1536]{1,0:T(8,128)(2,1)} %collective-permute-done.31.rest_0_, ...), custom_call_target="tpu_custom_call" | custom-call | flops 199999995904 | bytes 20000000 | tf_op jit(solution)/shard_map/weight_grad/pallas_call | solution.py:524
  275.4 2.3 collective-permute-start.34
  277.6 7.0 %collective-permute-done.44 = bf16[1,32,4096]{2,1,0:T(8,128)(2,1)} collective-permute-done((bf16[1,32,4096]{2,1,0:T(8,128)(2,1)}, bf16[1,32,4096]{2,1,0:T(8,128)(2,1)}, u32[]{:S(2)}, u32[]{:S(2)}) %collective-permute-start.44) | collective-permute-done | bytes 262176 | tf_op jit(solution)/shard_map/ppermute | solution.py:635
  284.6 2.1 maximum_select_fusion.10
  288.5 2.1 maximum_select_fusion.11
  290.6 2.4 collective-permute-done.34
  296.2 5.9 %collective-permute-done.46.rest_0_ = bf16[160,1024]{1,0:T(8,128)(2,1)S(1)} collective-permute-done((bf16[160,1024]{1,0:T(8,128)(2,1)S(1)}, bf16[160,1024]{1,0:T(8,128)(2,1)S(1)}, u32[]{:S(2)}, u32[]{:S(2)}) %collective-permute-start.46) | collective-permute-done | bytes 327712 | tf_op jit(solution)/shard_map/ppermute | solution.py:625
  304.3 2.6 collective-permute-start.49
  306.9 2.5 maximum_select_fusion.1
  309.4 2.6 bitcast_convert_fusion
  316.1 2.9 collective-permute-start.37
  322.2 10.3 %collective-permute-done.51 = bf16[1,40,1024]{2,1,0:T(8,128)(2,1)S(1)} collective-permute-done((bf16[1,40,1024]{2,1,0:T(8,128)(2,1)S(1)}, bf16[1,40,1024]{2,1,0:T(8,128)(2,1)S(1)}, u32[]{:S(2)}, u32[]{:S(2)}) %collective-permute-start.51) | collective-permute-done | bytes 81952 | tf_op jit(solution)/shard_map/ppermute | solution.py:635
  333.4 2.1 collective-permute-start.56
  335.5 2.1 fusion.2
  338.6 4.7 %collective-permute-start.57 = (bf16[2,32,3072]{2,1,0:T(8,128)(2,1)S(1)}, bf16[2,32,3072]{2,1,0:T(8,128)(2,1)S(1)}, u32[]{:S(2)}, u32[]{:S(2)}) collective-permute-start(bf16[2,32,3072]{2,1,0:T(8,128)(2,1)S(1)} %maximum_select_fusion.13), channel_id=1, source_target_pairs={{0,16},{16,0},{1,17},{17,1},{2,18},{18,2},{3,19},{19,3},{4,20},{20... | collective-permute-start | bytes 1179656 | tf_op jit(solution)/shard_map/ppermute | solution.py:632
  345.3 2.6 bitcast_convert_fusion.1
  347.9 12.1 %collective-permute-done.53 = bf16[4,40,1024]{2,1,0:T(8,128)(2,1)S(1)} collective-permute-done((bf16[4,40,1024]{2,1,0:T(8,128)(2,1)S(1)}, bf16[4,40,1024]{2,1,0:T(8,128)(2,1)S(1)}, u32[]{:S(2)}, u32[]{:S(2)}) %collective-permute-start.53) | collective-permute-done | bytes 327712 | tf_op jit(solution)/shard_map/ppermute | solution.py:632
  363.8 2.2 copy.42
  366.2 7.3 %collective-permute-done.58 = bf16[2,32,3072]{2,1,0:T(8,128)(2,1)S(1)} collective-permute-done((bf16[2,32,3072]{2,1,0:T(8,128)(2,1)S(1)}, bf16[2,32,3072]{2,1,0:T(8,128)(2,1)S(1)}, u32[]{:S(2)}, u32[]{:S(2)}) %collective-permute-start.58) | collective-permute-done | bytes 393248 | tf_op jit(solution)/shard_map/ppermute | solution.py:632
  373.9 2.1 bitcast_convert_fusion.2
  (340 shorter events, 95.5 us)
Async XLA Ops:
  4.0 15.4 %collective-permute-start = (bf16[304,1024]{1,0:T(8,128)(2,1)}, bf16[304,1024]{1,0:T(8,128)(2,1)}, u32[]{:S(2)}, u32[]{:S(2)}) collective-permute-start(bf16[304,1024]{1,0:T(8,128)(2,1)} %pad_maximum_fusion.1), channel_id=1, source_target_pairs={{4,16},{12,24},{16,4},{24,12},{5,17},{13,25},{17,5},{25,13},{6,18}... | collective-permute-start | bytes 1867784 | tf_op jit(solution)/shard_map/ppermute | solution.py:644
  7.8 14.4 %collective-permute-start.2 = (bf16[16,256]{1,0:T(8,128)(2,1)}, bf16[16,256]{1,0:T(8,128)(2,1)}, u32[]{:S(2)}, u32[]{:S(2)}) collective-permute-start(bf16[16,256]{1,0:T(8,128)(2,1)} %select_select_fusion), channel_id=1, source_target_pairs={{0,8},{4,12},{8,0},{12,4},{1,9},{5,13},{9,1},{13,5},{2,10},{6,14},... | collective-permute-start | bytes 24584 | tf_op jit(solution)/shard_map/ppermute | solution.py:625
  16.2 14.7 %collective-permute-start.9 = (bf16[128,1536]{1,0:T(8,128)(2,1)}, bf16[128,1536]{1,0:T(8,128)(2,1)}, u32[]{:S(2)}, u32[]{:S(2)}) collective-permute-start(bf16[128,1536]{1,0:T(8,128)(2,1)} %get-tuple-element.113), channel_id=1, source_target_pairs={{0,8},{4,12},{8,0},{12,4},{1,9},{5,13},{9,1},{13,5},{2,10},{6,14},... | collective-permute-start | bytes 1179656 | tf_op jit(solution)/shard_map/ppermute | solution.py:625
  16.2 20.7 %collective-permute-start.8 = (bf16[256,1536]{1,0:T(8,128)(2,1)}, bf16[256,1536]{1,0:T(8,128)(2,1)}, u32[]{:S(2)}, u32[]{:S(2)}) collective-permute-start(bf16[256,1536]{1,0:T(8,128)(2,1)} %get-tuple-element.115), channel_id=1, source_target_pairs={{0,4},{4,0},{8,12},{12,8},{1,5},{5,1},{9,13},{13,9},{2,6},{6,2},{1... | collective-permute-start | bytes 2359304 | tf_op jit(solution)/shard_map/ppermute | solution.py:622
  18.2 18.7 %collective-permute-start.11 = (bf16[128,1536]{1,0:T(8,128)(2,1)}, bf16[128,1536]{1,0:T(8,128)(2,1)}, u32[]{:S(2)}, u32[]{:S(2)}) collective-permute-start(bf16[128,1536]{1,0:T(8,128)(2,1)} %get-tuple-element.116), channel_id=1, source_target_pairs={{0,12},{4,8},{8,4},{12,0},{1,13},{5,9},{9,5},{13,1},{2,14},{6,10},... | collective-permute-start | bytes 1179656 | tf_op jit(solution)/shard_map/ppermute | solution.py:629
  19.6 3.3 collective-permute-start.1
  26.6 10.3 %collective-permute-start.3 = (bf16[256,2048]{1,0:T(8,128)(2,1)S(1)}, bf16[256,2048]{1,0:T(8,128)(2,1)S(1)}, u32[]{:S(2)}, u32[]{:S(2)}) collective-permute-start(bf16[256,2048]{1,0:T(8,128)(2,1)S(1)} %get-tuple-element.98), channel_id=1, source_target_pairs={{0,4},{4,0},{8,12},{12,8},{1,5},{5,1},{9,13},{13,9},{2,6},{6,2},{1... | collective-permute-start | bytes 3145736 | tf_op jit(solution)/shard_map/ppermute | solution.py:622
  27.3 2.0 collective-permute-start.4
  30.9 20.3 %collective-permute-start.10 = (bf16[128,1536]{1,0:T(8,128)(2,1)}, bf16[128,1536]{1,0:T(8,128)(2,1)}, u32[]{:S(2)}, u32[]{:S(2)}) collective-permute-start(bf16[128,1536]{1,0:T(8,128)(2,1)} %collective-permute-done.9.refs_2_), channel_id=1, source_target_pairs={{0,16},{16,0},{1,17},{17,1},{2,18},{18,2},{3,19},{19,3},{4,20},{20... | collective-permute-start | bytes 1179656 | tf_op jit(solution)/shard_map/ppermute | solution.py:632
  36.9 14.3 %collective-permute-start.12 = (bf16[128,1536]{1,0:T(8,128)(2,1)}, bf16[128,1536]{1,0:T(8,128)(2,1)}, u32[]{:S(2)}, u32[]{:S(2)}) collective-permute-start(bf16[128,1536]{1,0:T(8,128)(2,1)} %collective-permute-done.11.refs_4_), channel_id=1, source_target_pairs={{0,16},{16,0},{1,17},{17,1},{2,18},{18,2},{3,19},{19,3},{4,20},{20... | collective-permute-start | bytes 1179656 | tf_op jit(solution)/shard_map/ppermute | solution.py:632
  40.8 9.2 %collective-permute-start.7 = (bf16[128,1024]{1,0:T(8,128)(2,1)}, bf16[128,1024]{1,0:T(8,128)(2,1)}, u32[]{:S(2)}, u32[]{:S(2)}) collective-permute-start(bf16[128,1024]{1,0:T(8,128)(2,1)} %dynamic-slice_bitcast_fusion.9), channel_id=1, source_target_pairs={{0,8},{4,12},{8,0},{12,4},{1,9},{5,13},{9,1},{13,5},{2,10},{6,14},... | collective-permute-start | bytes 786440 | tf_op jit(solution)/shard_map/ppermute | solution.py:625
  45.5 15.7 %collective-permute-start.5 = (bf16[128,2048]{1,0:T(8,128)(2,1)}, bf16[128,2048]{1,0:T(8,128)(2,1)}, u32[]{:S(2)}, u32[]{:S(2)}) collective-permute-start(bf16[128,2048]{1,0:T(8,128)(2,1)} %pair_part.1), channel_id=1, source_target_pairs={{0,8},{4,12},{8,0},{12,4},{1,9},{5,13},{9,1},{13,5},{2,10},{6,14},... | collective-permute-start | bytes 1572872 | tf_op jit(solution)/shard_map/ppermute | solution.py:625
  50.0 24.8 %collective-permute-start.13 = (bf16[128,1024]{1,0:T(8,128)(2,1)}, bf16[128,1024]{1,0:T(8,128)(2,1)}, u32[]{:S(2)}, u32[]{:S(2)}) collective-permute-start(bf16[128,1024]{1,0:T(8,128)(2,1)} %collective-permute-done.7.refs_1_), channel_id=1, source_target_pairs={{0,16},{16,0},{1,17},{17,1},{2,18},{18,2},{3,19},{19,3},{4,20},{20... | collective-permute-start | bytes 786440 | tf_op jit(solution)/shard_map/ppermute | solution.py:632
  51.2 32.3 %collective-permute-start.20 = (bf16[256,1024]{1,0:T(8,128)(2,1)}, bf16[256,1024]{1,0:T(8,128)(2,1)}, u32[]{:S(2)}, u32[]{:S(2)}) collective-permute-start(bf16[256,1024]{1,0:T(8,128)(2,1)} %get-tuple-element.133), channel_id=1, source_target_pairs={{0,8},{4,12},{8,0},{12,4},{1,9},{5,13},{9,1},{13,5},{2,10},{6,14},... | collective-permute-start | bytes 1572872 | tf_op jit(solution)/shard_map/ppermute | solution.py:625
  61.2 19.0 %collective-permute-start.6 = (bf16[128,2048]{1,0:T(8,128)(2,1)}, bf16[128,2048]{1,0:T(8,128)(2,1)}, u32[]{:S(2)}, u32[]{:S(2)}) collective-permute-start(bf16[128,2048]{1,0:T(8,128)(2,1)} %collective-permute-done.5.refs_2_), channel_id=1, source_target_pairs={{0,1},{1,0},{2,3},{3,2},{4,5},{5,4},{6,7},{7,6},{8,9},{9,8},{10,11... | collective-permute-start | bytes 1572872 | tf_op jit(solution)/shard_map/ppermute | solution.py:635
  62.8 19.0 %collective-permute-start.18 = (bf16[128,2048]{1,0:T(8,128)(2,1)}, bf16[128,2048]{1,0:T(8,128)(2,1)}, u32[]{:S(2)}, u32[]{:S(2)}) collective-permute-start(bf16[128,2048]{1,0:T(8,128)(2,1)} %collective-permute-done.5.refs_2_), channel_id=1, source_target_pairs={{0,16},{16,0},{1,17},{17,1},{2,18},{18,2},{3,19},{19,3},{4,20},{20... | collective-permute-start | bytes 1572872 | tf_op jit(solution)/shard_map/ppermute | solution.py:632
  78.6 19.3 %collective-permute-start.14 = (bf16[608,1024]{1,0:T(8,128)(2,1)S(1)}, bf16[608,1024]{1,0:T(8,128)(2,1)S(1)}, u32[]{:S(2)}, u32[]{:S(2)}) collective-permute-start(bf16[608,1024]{1,0:T(8,128)(2,1)S(1)} %get-tuple-element.121.own_ref), channel_id=1, source_target_pairs={{0,4},{4,0},{8,12},{12,8},{1,5},{5,1},{9,13},{13,9},{2,6},{6,2},{1... | collective-permute-start | bytes 3735560 | tf_op jit(solution)/shard_map/ppermute | solution.py:622
  78.6 7.5 %collective-permute-start.16 = (bf16[304,1024]{1,0:T(8,128)(2,1)}, bf16[304,1024]{1,0:T(8,128)(2,1)}, u32[]{:S(2)}, u32[]{:S(2)}) collective-permute-start(bf16[304,1024]{1,0:T(8,128)(2,1)} %concatenate.69), channel_id=1, source_target_pairs={{4,16},{12,24},{16,4},{24,12},{5,17},{13,25},{17,5},{25,13},{6,18}... | collective-permute-start | bytes 1867784 | tf_op jit(solution)/shard_map/ppermute | solution.py:644
  80.2 17.6 %collective-permute-start.15 = (bf16[256,1024]{1,0:T(8,128)(2,1)}, bf16[256,1024]{1,0:T(8,128)(2,1)}, u32[]{:S(2)}, u32[]{:S(2)}) collective-permute-start(bf16[256,1024]{1,0:T(8,128)(2,1)} %get-tuple-element.125), channel_id=1, source_target_pairs={{0,8},{4,12},{8,0},{12,4},{1,9},{5,13},{9,1},{13,5},{2,10},{6,14},... | collective-permute-start | bytes 1572872 | tf_op jit(solution)/shard_map/ppermute | solution.py:625
  81.8 16.0 %collective-permute-start.19 = (bf16[128,2048]{1,0:T(8,128)(2,1)}, bf16[128,2048]{1,0:T(8,128)(2,1)S(1)}, u32[]{:S(2)}, u32[]{:S(2)}) collective-permute-start(bf16[128,2048]{1,0:T(8,128)(2,1)} %collective-permute-done.18.refs_3_), channel_id=1, source_target_pairs={{0,1},{1,0},{2,3},{3,2},{4,5},{5,4},{6,7},{7,6},{8,9},{9,8},{10,11... | collective-permute-start | bytes 1572872 | tf_op jit(solution)/shard_map/ppermute | solution.py:635
  83.5 34.2 %collective-permute-start.21 = (bf16[256,1024]{1,0:T(8,128)(2,1)}, bf16[256,1024]{1,0:T(8,128)(2,1)}, u32[]{:S(2)}, u32[]{:S(2)}) collective-permute-start(bf16[256,1024]{1,0:T(8,128)(2,1)} %collective-permute-done.20.refs_0_), channel_id=1, source_target_pairs={{0,16},{16,0},{1,17},{17,1},{2,18},{18,2},{3,19},{19,3},{4,20},{20... | collective-permute-start | bytes 1572872 | tf_op jit(solution)/shard_map/ppermute | solution.py:632
  88.2 20.2 %collective-permute-start.17 = (bf16[304,1024]{1,0:T(8,128)(2,1)}, bf16[304,1024]{1,0:T(8,128)(2,1)}, u32[]{:S(2)}, u32[]{:S(2)}) collective-permute-start(bf16[304,1024]{1,0:T(8,128)(2,1)} %broadcast_select_fusion), channel_id=1, source_target_pairs={{0,4},{4,0},{8,12},{12,8},{1,5},{5,1},{9,13},{13,9},{2,6},{6,2},{1... | collective-permute-start | bytes 1867784 | tf_op jit(solution)/shard_map/ppermute | solution.py:622
  97.9 19.8 %collective-permute-start.22 = (bf16[256,1024]{1,0:T(8,128)(2,1)}, bf16[256,1024]{1,0:T(8,128)(2,1)}, u32[]{:S(2)}, u32[]{:S(2)}) collective-permute-start(bf16[256,1024]{1,0:T(8,128)(2,1)} %collective-permute-done.15.refs_2_), channel_id=1, source_target_pairs={{0,16},{16,0},{1,17},{17,1},{2,18},{18,2},{3,19},{19,3},{4,20},{20... | collective-permute-start | bytes 1572872 | tf_op jit(solution)/shard_map/ppermute | solution.py:632
  115.3 31.0 %collective-permute-start.24 = (bf16[512,1024]{1,0:T(8,128)(2,1)}, bf16[512,1024]{1,0:T(8,128)(2,1)}, u32[]{:S(2)}, u32[]{:S(2)}) collective-permute-start(bf16[512,1024]{1,0:T(8,128)(2,1)} %weight_grad.12), channel_id=1, source_target_pairs={{0,8},{4,12},{8,0},{12,4},{1,9},{5,13},{9,1},{13,5},{2,10},{6,14},... | collective-permute-start | bytes 3145736 | tf_op jit(solution)/shard_map/ppermute | solution.py:625
  131.7 11.6 %collective-permute-start.23 = (bf16[304,1024]{1,0:T(8,128)(2,1)}, bf16[304,1024]{1,0:T(8,128)(2,1)}, u32[]{:S(2)}, u32[]{:S(2)}) collective-permute-start(bf16[304,1024]{1,0:T(8,128)(2,1)} %dynamic-slice_bitcast_fusion), channel_id=1, source_target_pairs={{0,4},{4,0},{8,12},{12,8},{1,5},{5,1},{9,13},{13,9},{2,6},{6,2},{1... | collective-permute-start | bytes 1867784 | tf_op jit(solution)/shard_map/ppermute | solution.py:622
  131.7 49.5 %collective-permute-start.26 = (bf16[512,1024]{1,0:T(8,128)(2,1)}, bf16[512,1024]{1,0:T(8,128)(2,1)}, u32[]{:S(2)}, u32[]{:S(2)}) collective-permute-start(bf16[512,1024]{1,0:T(8,128)(2,1)} %weight_grad.14), channel_id=1, source_target_pairs={{0,8},{4,12},{8,0},{12,4},{1,9},{5,13},{9,1},{13,5},{2,10},{6,14},... | collective-permute-start | bytes 3145736 | tf_op jit(solution)/shard_map/ppermute | solution.py:625
  139.1 14.1 %collective-permute-start.25 = (bf16[608,1024]{1,0:T(8,128)(2,1)}, bf16[608,1024]{1,0:T(8,128)(2,1)}, u32[]{:S(2)}, u32[]{:S(2)}) collective-permute-start(bf16[608,1024]{1,0:T(8,128)(2,1)} %grad_second.1.own_ref), channel_id=1, source_target_pairs={{0,4},{4,0},{8,12},{12,8},{1,5},{5,1},{9,13},{13,9},{2,6},{6,2},{1... | collective-permute-start | bytes 3735560 | tf_op jit(solution)/shard_map/ppermute | solution.py:622
  149.5 31.8 %collective-permute-start.27 = (bf16[512,1024]{1,0:T(8,128)(2,1)}, bf16[512,1024]{1,0:T(8,128)(2,1)}, u32[]{:S(2)}, u32[]{:S(2)}) collective-permute-start(bf16[512,1024]{1,0:T(8,128)(2,1)} %weight_grad.13), channel_id=1, source_target_pairs={{0,16},{16,0},{1,17},{17,1},{2,18},{18,2},{3,19},{19,3},{4,20},{20... | collective-permute-start | bytes 3145736 | tf_op jit(solution)/shard_map/ppermute | solution.py:632
  151.5 38.0 %collective-permute-start.39 = (bf16[256,2048]{1,0:T(8,128)(2,1)}, bf16[256,2048]{1,0:T(8,128)(2,1)}, u32[]{:S(2)}, u32[]{:S(2)}) collective-permute-start(bf16[256,2048]{1,0:T(8,128)(2,1)} %weight_grad.21), channel_id=1, source_target_pairs={{0,8},{4,12},{8,0},{12,4},{1,9},{5,13},{9,1},{13,5},{2,10},{6,14},... | collective-permute-start | bytes 3145736 | tf_op jit(solution)/shard_map/ppermute | solution.py:625
  177.3 31.4 %collective-permute-start.28 = (bf16[608,1024]{1,0:T(8,128)(2,1)}, bf16[608,1024]{1,0:T(8,128)(2,1)}, u32[]{:S(2)}, u32[]{:S(2)}) collective-permute-start(bf16[608,1024]{1,0:T(8,128)(2,1)} %grad_first.1.own_ref), channel_id=1, source_target_pairs={{0,4},{4,0},{8,12},{12,8},{1,5},{5,1},{9,13},{13,9},{2,6},{6,2},{1... | collective-permute-start | bytes 3735560 | tf_op jit(solution)/shard_map/ppermute | solution.py:622
  189.2 14.7 %collective-permute-start.29 = (bf16[1,2,128,1024]{3,2,1,0:T(8,128)(2,1)}, bf16[1,2,128,1024]{3,2,1,0:T(8,128)(2,1)}, u32[]{:S(2)}, u32[]{:S(2)}) collective-permute-start(bf16[1,2,128,1024]{3,2,1,0:T(8,128)(2,1)} %get-tuple-element.193), channel_id=1, source_target_pairs={{0,1},{1,0},{2,3},{3,2},{4,5},{5,4},{6,7},{7,6},{8,9},{9,8},{10,11... | collective-permute-start | bytes 1572872 | tf_op jit(solution)/shard_map/ppermute | solution.py:635
  189.2 35.6 %collective-permute-start.38 = (bf16[256,2048]{1,0:T(8,128)(2,1)}, bf16[256,2048]{1,0:T(8,128)(2,1)}, u32[]{:S(2)}, u32[]{:S(2)}) collective-permute-start(bf16[256,2048]{1,0:T(8,128)(2,1)} %weight_grad.16), channel_id=1, source_target_pairs={{0,8},{4,12},{8,0},{12,4},{1,9},{5,13},{9,1},{13,5},{2,10},{6,14},... | collective-permute-start | bytes 3145736 | tf_op jit(solution)/shard_map/ppermute | solution.py:625
  194.4 30.5 %collective-permute-start.40 = (bf16[256,2048]{1,0:T(8,128)(2,1)}, bf16[256,2048]{1,0:T(8,128)(2,1)}, u32[]{:S(2)}, u32[]{:S(2)}) collective-permute-start(bf16[256,2048]{1,0:T(8,128)(2,1)} %weight_grad.22), channel_id=1, source_target_pairs={{0,16},{16,0},{1,17},{17,1},{2,18},{18,2},{3,19},{19,3},{4,20},{20... | collective-permute-start | bytes 3145736 | tf_op jit(solution)/shard_map/ppermute | solution.py:632
  206.0 14.8 %collective-permute-start.30 = (bf16[1,1,128,1024]{3,2,1,0:T(8,128)(2,1)}, bf16[1,1,128,1024]{3,2,1,0:T(8,128)(2,1)}, u32[]{:S(2)}, u32[]{:S(2)}) collective-permute-start(bf16[1,1,128,1024]{3,2,1,0:T(8,128)(2,1)} %get-tuple-element.199), channel_id=1, source_target_pairs={{0,2},{1,3},{2,0},{3,1},{4,6},{5,7},{6,4},{7,5},{8,10},{9,11},{10,... | collective-permute-start | bytes 786440 | tf_op jit(solution)/shard_map/ppermute | solution.py:635
  208.4 32.2 %collective-permute-start.32 = (bf16[256,1536]{1,0:T(8,128)(2,1)}, bf16[256,1536]{1,0:T(8,128)(2,1)}, u32[]{:S(2)}, u32[]{:S(2)}) collective-permute-start(bf16[256,1536]{1,0:T(8,128)(2,1)} %weight_grad.18), channel_id=1, source_target_pairs={{0,8},{4,12},{8,0},{12,4},{1,9},{5,13},{9,1},{13,5},{2,10},{6,14},... | collective-permute-start | bytes 2359304 | tf_op jit(solution)/shard_map/ppermute | solution.py:625
  222.6 14.2 %collective-permute-start.61 = (bf16[1,128,1024]{2,1,0:T(8,128)(2,1)}, bf16[1,128,1024]{2,1,0:T(8,128)(2,1)}, u32[]{:S(2)}, u32[]{:S(2)}) collective-permute-start(bf16[1,128,1024]{2,1,0:T(8,128)(2,1)} %bitcast.111), channel_id=1, source_target_pairs={{0,2},{1,3},{2,0},{3,1},{4,6},{5,7},{6,4},{7,5},{8,10},{9,11},{10,... | collective-permute-start | bytes 786440 | tf_op jit(solution)/shard_map/ppermute | solution.py:635
  223.1 46.9 %collective-permute-start.31 = (bf16[256,1536]{1,0:T(8,128)(2,1)}, bf16[256,1536]{1,0:T(8,128)(2,1)}, u32[]{:S(2)}, u32[]{:S(2)}) collective-permute-start(bf16[256,1536]{1,0:T(8,128)(2,1)} %weight_grad.17), channel_id=1, source_target_pairs={{0,8},{4,12},{8,0},{12,4},{1,9},{5,13},{9,1},{13,5},{2,10},{6,14},... | collective-permute-start | bytes 2359304 | tf_op jit(solution)/shard_map/ppermute | solution.py:625
  230.7 17.4 %collective-permute-start.41 = (bf16[2,2,32,2048]{3,2,1,0:T(8,128)(2,1)}, bf16[2,2,32,2048]{3,2,1,0:T(8,128)(2,1)}, u32[]{:S(2)}, u32[]{:S(2)}) collective-permute-start(bf16[2,2,32,2048]{3,2,1,0:T(8,128)(2,1)} %get-tuple-element.195), channel_id=1, source_target_pairs={{0,1},{1,0},{2,3},{3,2},{4,5},{5,4},{6,7},{7,6},{8,9},{9,8},{10,11... | collective-permute-start | bytes 1572872 | tf_op jit(solution)/shard_map/ppermute | solution.py:635
  238.9 27.4 %collective-permute-start.62 = (bf16[2,128,1024]{2,1,0:T(8,128)(2,1)}, bf16[2,128,1024]{2,1,0:T(8,128)(2,1)}, u32[]{:S(2)}, u32[]{:S(2)}) collective-permute-start(bf16[2,128,1024]{2,1,0:T(8,128)(2,1)} %maximum_select_fusion.12), channel_id=1, source_target_pairs={{0,1},{1,0},{2,3},{3,2},{4,5},{5,4},{6,7},{7,6},{8,9},{9,8},{10,11... | collective-permute-start | bytes 1572872 | tf_op jit(solution)/shard_map/ppermute | solution.py:635
  238.9 16.9 %collective-permute-start.47 = (bf16[160,1024]{1,0:T(8,128)(2,1)}, bf16[160,1024]{1,0:T(8,128)(2,1)}, u32[]{:S(2)}, u32[]{:S(2)}) collective-permute-start(bf16[160,1024]{1,0:T(8,128)(2,1)} %out_grad.4), channel_id=1, source_target_pairs={{0,8},{4,12},{8,0},{12,4},{1,9},{5,13},{9,1},{13,5},{2,10},{6,14},... | collective-permute-start | bytes 983048 | tf_op jit(solution)/shard_map/ppermute | solution.py:625
  246.3 23.8 %collective-permute-start.33 = (bf16[256,1536]{1,0:T(8,128)(2,1)}, bf16[256,1536]{1,0:T(8,128)(2,1)}, u32[]{:S(2)}, u32[]{:S(2)}) collective-permute-start(bf16[256,1536]{1,0:T(8,128)(2,1)} %weight_grad.19), channel_id=1, source_target_pairs={{0,16},{16,0},{1,17},{17,1},{2,18},{18,2},{3,19},{19,3},{4,20},{20... | collective-permute-start | bytes 2359304 | tf_op jit(solution)/shard_map/ppermute | solution.py:632
  250.1 15.0 %collective-permute-start.42 = (bf16[2,1,32,2048]{3,2,1,0:T(8,128)(2,1)}, bf16[2,1,32,2048]{3,2,1,0:T(8,128)(2,1)}, u32[]{:S(2)}, u32[]{:S(2)}) collective-permute-start(bf16[2,1,32,2048]{3,2,1,0:T(8,128)(2,1)} %get-tuple-element.201), channel_id=1, source_target_pairs={{0,2},{1,3},{2,0},{3,1},{4,6},{5,7},{6,4},{7,5},{8,10},{9,11},{10,... | collective-permute-start | bytes 786440 | tf_op jit(solution)/shard_map/ppermute | solution.py:635
  258.5 36.2 %collective-permute-start.48 = (bf16[160,1024]{1,0:T(8,128)(2,1)}, bf16[160,1024]{1,0:T(8,128)(2,1)}, u32[]{:S(2)}, u32[]{:S(2)}) collective-permute-start(bf16[160,1024]{1,0:T(8,128)(2,1)} %out_grad.6), channel_id=1, source_target_pairs={{0,16},{16,0},{1,17},{17,1},{2,18},{18,2},{3,19},{19,3},{4,20},{20... | collective-permute-start | bytes 983048 | tf_op jit(solution)/shard_map/ppermute | solution.py:632
  266.2 3.1 collective-permute-start.43
  269.2 35.1 %collective-permute-start.63 = (bf16[4,128,1024]{2,1,0:T(8,128)(2,1)}, bf16[4,128,1024]{2,1,0:T(8,128)(2,1)}, u32[]{:S(2)}, u32[]{:S(2)}) collective-permute-start(bf16[4,128,1024]{2,1,0:T(8,128)(2,1)} %bitcast.116), channel_id=1, source_target_pairs={{0,16},{16,0},{1,17},{17,1},{2,18},{18,2},{3,19},{19,3},{4,20},{20... | collective-permute-start | bytes 3145736 | tf_op jit(solution)/shard_map/ppermute | solution.py:632
  270.0 14.6 %collective-permute-start.44 = (bf16[1,32,4096]{2,1,0:T(8,128)(2,1)}, bf16[1,32,4096]{2,1,0:T(8,128)(2,1)}, u32[]{:S(2)}, u32[]{:S(2)}) collective-permute-start(bf16[1,32,4096]{2,1,0:T(8,128)(2,1)} %maximum_bitcast_fusion), channel_id=1, source_target_pairs={{0,2},{1,3},{2,0},{3,1},{4,6},{5,7},{6,4},{7,5},{8,10},{9,11},{10,... | collective-permute-start | bytes 786440 | tf_op jit(solution)/shard_map/ppermute | solution.py:635
  275.4 17.6 %collective-permute-start.34 = (bf16[2,2,32,1536]{3,2,1,0:T(8,128)(2,1)S(1)}, bf16[2,2,32,1536]{3,2,1,0:T(8,128)(2,1)S(1)}, u32[]{:S(2)}, u32[]{:S(2)}) collective-permute-start(bf16[2,2,32,1536]{3,2,1,0:T(8,128)(2,1)S(1)} %get-tuple-element.197), channel_id=1, source_target_pairs={{0,1},{1,0},{2,3},{3,2},{4,5},{5,4},{6,7},{7,6},{8,9},{9,8},{10,11... | collective-permute-start | bytes 1179656 | tf_op jit(solution)/shard_map/ppermute | solution.py:635
  286.7 27.4 %collective-permute-start.54 = (bf16[2,32,4096]{2,1,0:T(8,128)(2,1)}, bf16[2,32,4096]{2,1,0:T(8,128)(2,1)}, u32[]{:S(2)}, u32[]{:S(2)}) collective-permute-start(bf16[2,32,4096]{2,1,0:T(8,128)(2,1)} %maximum_select_fusion.10), channel_id=1, source_target_pairs={{0,1},{1,0},{2,3},{3,2},{4,5},{5,4},{6,7},{7,6},{8,9},{9,8},{10,11... | collective-permute-start | bytes 1572872 | tf_op jit(solution)/shard_map/ppermute | solution.py:635
  286.7 56.7 %collective-permute-start.59 = (bf16[2,32,4096]{2,1,0:T(8,128)(2,1)}, bf16[2,32,4096]{2,1,0:T(8,128)(2,1)}, u32[]{:S(2)}, u32[]{:S(2)}) collective-permute-start(bf16[2,32,4096]{2,1,0:T(8,128)(2,1)} %maximum_select_fusion.10), channel_id=1, source_target_pairs={{0,16},{16,0},{1,17},{17,1},{2,18},{18,2},{3,19},{19,3},{4,20},{20... | collective-permute-start | bytes 1572872 | tf_op jit(solution)/shard_map/ppermute | solution.py:632
  293.0 9.2 %collective-permute-start.46 = (bf16[160,1024]{1,0:T(8,128)(2,1)S(1)}, bf16[160,1024]{1,0:T(8,128)(2,1)S(1)}, u32[]{:S(2)}, u32[]{:S(2)}) collective-permute-start(bf16[160,1024]{1,0:T(8,128)(2,1)S(1)} %out_grad.5), channel_id=1, source_target_pairs={{0,8},{4,12},{8,0},{12,4},{1,9},{5,13},{9,1},{13,5},{2,10},{6,14},... | collective-permute-start | bytes 983048 | tf_op jit(solution)/shard_map/ppermute | solution.py:625
  294.7 38.7 %collective-permute-start.45 = (bf16[304,1024]{1,0:T(8,128)(2,1)}, bf16[304,1024]{1,0:T(8,128)(2,1)}, u32[]{:S(2)}, u32[]{:S(2)}) collective-permute-start(bf16[304,1024]{1,0:T(8,128)(2,1)} %add_convert_fusion), channel_id=1, source_target_pairs={{4,16},{12,24},{16,4},{24,12},{5,17},{13,25},{17,5},{25,13},{6,18}... | collective-permute-start | bytes 1867784 | tf_op jit(solution)/shard_map/ppermute | solution.py:644
  302.1 10.6 %collective-permute-start.35 = (bf16[2,1,32,1536]{3,2,1,0:T(8,128)(2,1)}, bf16[2,1,32,1536]{3,2,1,0:T(8,128)(2,1)}, u32[]{:S(2)}, u32[]{:S(2)}) collective-permute-start(bf16[2,1,32,1536]{3,2,1,0:T(8,128)(2,1)} %get-tuple-element.203), channel_id=1, source_target_pairs={{0,2},{1,3},{2,0},{3,1},{4,6},{5,7},{6,4},{7,5},{8,10},{9,11},{10,... | collective-permute-start | bytes 589832 | tf_op jit(solution)/shard_map/ppermute | solution.py:635
  304.3 9.6 %collective-permute-start.49 = (bf16[1,2,40,1024]{3,2,1,0:T(8,128)(2,1)S(1)}, bf16[1,2,40,1024]{3,2,1,0:T(8,128)(2,1)S(1)}, u32[]{:S(2)}, u32[]{:S(2)}) collective-permute-start(bf16[1,2,40,1024]{3,2,1,0:T(8,128)(2,1)S(1)} %get-tuple-element.205), channel_id=1, source_target_pairs={{0,1},{1,0},{2,3},{3,2},{4,5},{5,4},{6,7},{7,6},{8,9},{9,8},{10,11... | collective-permute-start | bytes 491528 | tf_op jit(solution)/shard_map/ppermute | solution.py:635
  313.7 2.2 collective-permute-start.36
  314.0 6.5 %collective-permute-start.50 = (bf16[1,1,40,1024]{3,2,1,0:T(8,128)(2,1)S(1)}, bf16[1,1,40,1024]{3,2,1,0:T(8,128)(2,1)S(1)}, u32[]{:S(2)}, u32[]{:S(2)}) collective-permute-start(bf16[1,1,40,1024]{3,2,1,0:T(8,128)(2,1)S(1)} %get-tuple-element.215), channel_id=1, source_target_pairs={{0,2},{1,3},{2,0},{3,1},{4,6},{5,7},{6,4},{7,5},{8,10},{9,11},{10,... | collective-permute-start | bytes 245768 | tf_op jit(solution)/shard_map/ppermute | solution.py:635
  314.1 29.4 %collective-permute-start.60 = (bf16[2,32,4096]{2,1,0:T(8,128)(2,1)}, bf16[2,32,4096]{2,1,0:T(8,128)(2,1)S(1)}, u32[]{:S(2)}, u32[]{:S(2)}) collective-permute-start(bf16[2,32,4096]{2,1,0:T(8,128)(2,1)} %collective-permute-done.54), channel_id=1, source_target_pairs={{0,16},{16,0},{1,17},{17,1},{2,18},{18,2},{3,19},{19,3},{4,20},{20... | collective-permute-start | bytes 1572872 | tf_op jit(solution)/shard_map/ppermute | solution.py:632
  316.1 17.1 %collective-permute-start.37 = (bf16[1,32,3072]{2,1,0:T(8,128)(2,1)S(1)}, bf16[1,32,3072]{2,1,0:T(8,128)(2,1)S(1)}, u32[]{:S(2)}, u32[]{:S(2)}) collective-permute-start(bf16[1,32,3072]{2,1,0:T(8,128)(2,1)S(1)} %bitcast.216), channel_id=1, source_target_pairs={{0,2},{1,3},{2,0},{3,1},{4,6},{5,7},{6,4},{7,5},{8,10},{9,11},{10,... | collective-permute-start | bytes 589832 | tf_op jit(solution)/shard_map/ppermute | solution.py:635
  320.6 11.9 %collective-permute-start.51 = (bf16[1,40,1024]{2,1,0:T(8,128)(2,1)S(1)}, bf16[1,40,1024]{2,1,0:T(8,128)(2,1)S(1)}, u32[]{:S(2)}, u32[]{:S(2)}) collective-permute-start(bf16[1,40,1024]{2,1,0:T(8,128)(2,1)S(1)} %fusion.3), channel_id=1, source_target_pairs={{0,2},{1,3},{2,0},{3,1},{4,6},{5,7},{6,4},{7,5},{8,10},{9,11},{10,... | collective-permute-start | bytes 245768 | tf_op jit(solution)/shard_map/ppermute | solution.py:635
  332.4 31.2 %collective-permute-start.55 = (bf16[304,1024]{1,0:T(8,128)(2,1)S(1)}, bf16[304,1024]{1,0:T(8,128)(2,1)S(1)}, u32[]{:S(2)}, u32[]{:S(2)}) collective-permute-start(bf16[304,1024]{1,0:T(8,128)(2,1)S(1)} %get-tuple-element.174), channel_id=1, source_target_pairs={{4,16},{12,24},{16,4},{24,12},{5,17},{13,25},{17,5},{25,13},{6,18}... | collective-permute-start | bytes 1867784 | tf_op jit(solution)/shard_map/ppermute | solution.py:644
  333.2 5.4 %collective-permute-start.52 = (bf16[2,40,1024]{2,1,0:T(8,128)(2,1)S(1)}, bf16[2,40,1024]{2,1,0:T(8,128)(2,1)S(1)}, u32[]{:S(2)}, u32[]{:S(2)}) collective-permute-start(bf16[2,40,1024]{2,1,0:T(8,128)(2,1)S(1)} %maximum_select_fusion.16), channel_id=1, source_target_pairs={{0,1},{1,0},{2,3},{3,2},{4,5},{5,4},{6,7},{7,6},{8,9},{9,8},{10,11... | collective-permute-start | bytes 491528 | tf_op jit(solution)/shard_map/ppermute | solution.py:635
  333.4 29.0 %collective-permute-start.56 = (bf16[2,32,3072]{2,1,0:T(8,128)(2,1)S(1)}, bf16[2,32,3072]{2,1,0:T(8,128)(2,1)S(1)}, u32[]{:S(2)}, u32[]{:S(2)}) collective-permute-start(bf16[2,32,3072]{2,1,0:T(8,128)(2,1)S(1)} %maximum_select_fusion.13), channel_id=1, source_target_pairs={{0,1},{1,0},{2,3},{3,2},{4,5},{5,4},{6,7},{7,6},{8,9},{9,8},{10,11... | collective-permute-start | bytes 1179656 | tf_op jit(solution)/shard_map/ppermute | solution.py:635
  338.6 27.7 %collective-permute-start.57 = (bf16[2,32,3072]{2,1,0:T(8,128)(2,1)S(1)}, bf16[2,32,3072]{2,1,0:T(8,128)(2,1)S(1)}, u32[]{:S(2)}, u32[]{:S(2)}) collective-permute-start(bf16[2,32,3072]{2,1,0:T(8,128)(2,1)S(1)} %maximum_select_fusion.13), channel_id=1, source_target_pairs={{0,16},{16,0},{1,17},{17,1},{2,18},{18,2},{3,19},{19,3},{4,20},{20... | collective-permute-start | bytes 1179656 | tf_op jit(solution)/shard_map/ppermute | solution.py:632
  343.4 16.6 %collective-permute-start.53 = (bf16[4,40,1024]{2,1,0:T(8,128)(2,1)S(1)}, bf16[4,40,1024]{2,1,0:T(8,128)(2,1)S(1)}, u32[]{:S(2)}, u32[]{:S(2)}) collective-permute-start(bf16[4,40,1024]{2,1,0:T(8,128)(2,1)S(1)} %bitcast.213), channel_id=1, source_target_pairs={{0,16},{16,0},{1,17},{17,1},{2,18},{18,2},{3,19},{19,3},{4,20},{20... | collective-permute-start | bytes 983048 | tf_op jit(solution)/shard_map/ppermute | solution.py:632
  362.3 11.2 %collective-permute-start.58 = (bf16[2,32,3072]{2,1,0:T(8,128)(2,1)S(1)}, bf16[2,32,3072]{2,1,0:T(8,128)(2,1)S(1)}, u32[]{:S(2)}, u32[]{:S(2)}) collective-permute-start(bf16[2,32,3072]{2,1,0:T(8,128)(2,1)S(1)} %collective-permute-done.56), channel_id=1, source_target_pairs={{0,16},{16,0},{1,17},{17,1},{2,18},{18,2},{3,19},{19,3},{4,20},{20... | collective-permute-start | bytes 1179656 | tf_op jit(solution)/shard_map/ppermute | solution.py:632
  (63 other events, 338.0 us)
